TPU v7x, 32 devices: a whole 2x2x4 slice. The times are simulated.
32 devices in a mesh: row: 8 (over z, y), col: 4 (over x, core).
Axes of the slice: x: 2, y: 2, z: 4, core: 2. Of those that a mesh axis runs over, the one named last changes fastest.
Arguments:
- tokens: bfloat16 [8192, 2048], P('row', 'col'), may hold values from -6 to 6
- segments: int32 [8, 1024], P('row'), may hold values from 0 to 3, never falling along the last dimension, each value on 1 to 800 neighbouring positions
- gains: float32 [2, 2048], P(None, 'col'), may hold values from 0.5 to 1.5
- shifts: float32 [2, 2048], P(None, 'col'), may hold values from -1.8 to 1.8
- biases: float32 [4, 2048], P(None, 'col'), may hold values from -3 to 3
- mixing: bfloat16 [2048, 3, 2048], P('row', None, 'col'), may hold values from -0.125 to 0.125
- projection: bfloat16 [2048, 2048], P('row', 'col'), may hold values from -0.5 to 0.5
- expand: bfloat16 [2048, 8192], P('row', 'col'), may hold values from -0.125 to 0.125
- thresholds: float32 [8192], P('col'), may hold values from -3 to 3
- contract: bfloat16 [2048, 8192], P('row', 'col'), may hold values from -0.0625 to 0.0625
- cotangent: bfloat16 [8192, 2048], P('row', 'col'), may hold values from -6 to 6
Outputs:
- layer_out: bfloat16 [8192, 2048], P('row', 'col')
- tokens_grad: float32 [8192, 2048], P('row', 'col')
- gains_grad: float32 [2, 2048], P(None, 'col')
- shifts_grad: float32 [2, 2048], P(None, 'col')
- biases_grad: float32 [4, 2048], P(None, 'col')
- mixing_grad: float32 [2048, 3, 2048], P('row', None, 'col')
- projection_grad: float32 [2048, 2048], P('row', 'col')
- expand_grad: float32 [2048, 8192], P('row', 'col')
- thresholds_grad: float32 [8192], P('col')
- contract_grad: float32 [2048, 8192], P('row', 'col')
Inputs may be any that keep to these rules, and one draw needn't show every extreme that they name: `segments`: within a sequence the document numbers never fall and every number from 0 to 3 occurs; a document holds at most 800 tokens.
All inputs are finite; a program needn't handle non-finite values.
Results may differ from a plain program's by a relative error of at most 0.0095.
Values may be sent and summed in bfloat16 or wider, within the bound.
No kernel may reach another device: no remote copies, remote signals or barrier semaphores. Data moves between devices by JAX's collectives and lax.ppermute only.
A program may use at most 192 MiB of HBM per device.

v0:
```python
from functools import partial

import jax
import jax.numpy as jnp
from jax import lax
from jax.sharding import PartitionSpec as P

HD = 64


norm_eps = 1e-05
sqrt_half = 0.7071067811865476
inverse_root = 0.3989422804014327
masked_score = -1e30
contract_last = (((1,), (1,)), ((), ()))
contract_first = (((0,), (0,)), ((), ()))


def normalize(resid, gain_row, shift_row, full_width):
    row_sums = lax.psum((jnp.sum(resid, axis=1), jnp.sum(resid * resid, axis=1)), "col")
    row_mean = row_sums[0][:, None] / full_width
    spread = row_sums[1][:, None] / full_width - row_mean * row_mean
    row_scale = lax.rsqrt(spread + norm_eps)
    centred = (resid - row_mean) * row_scale
    return (centred, row_scale, (centred * gain_row + shift_row).astype(jnp.bfloat16))


def normalize_back(upstream, centred, row_scale, gain_row, full_width):
    scaled = upstream * gain_row
    row_sums = lax.psum((jnp.sum(scaled, axis=1), jnp.sum(scaled * centred, axis=1)), "col")
    result = row_scale * (
        scaled - row_sums[0][:, None] / full_width - centred * (row_sums[1][:, None] / full_width)
    )
    return (result, jnp.sum(upstream * centred, axis=0), jnp.sum(upstream, axis=0))


def gather_features(local_part):
    return lax.all_gather(local_part, "col", axis=1, tiled=True)


def gather_grads(local_part):
    return lax.all_gather(local_part, "col", axis=1, tiled=True)


def sum_forward(partial_term):
    return lax.psum_scatter(partial_term, "col", scatter_dimension=1, tiled=True)


def sum_backward(partial_term):
    return lax.psum_scatter(partial_term, "col", scatter_dimension=1, tiled=True)


def to_heads(matrix, seq_count, head_count):
    return (
        matrix.reshape(seq_count, -1, head_count, HD)
        .transpose(2, 0, 1, 3)
        .reshape(head_count * seq_count, -1, HD)
    )


def from_heads(stacked, seq_count, head_count):
    return (
        stacked.reshape(head_count, seq_count, -1, HD)
        .transpose(1, 2, 0, 3)
        .reshape(-1, head_count * HD)
    )


def block_scores(
    row_block, key_matrix, row_segments, segment_row, first_row, decay_slope, score_scale
):
    raw_scores = lax.dot_general(
        row_block, key_matrix, contract_last, preferred_element_type=jnp.float32
    )
    row_places = first_row + jnp.arange(row_block.shape[0])
    col_places = jnp.arange(key_matrix.shape[0])
    distance = (row_places[:, None] - col_places[None, :]).astype(jnp.float32)
    allowed = (row_segments[:, None] == segment_row[None, :]) & (
        col_places[None, :] <= row_places[:, None]
    )
    return jnp.where(allowed, (raw_scores - decay_slope * distance) * score_scale, masked_score)


def attend_forward(element, block_rows, score_scale):
    query_matrix, key_matrix, value_matrix, segment_row, decay_slope = element
    seq_length = key_matrix.shape[0]

    def one_block(first_row):
        row_block = lax.dynamic_slice_in_dim(query_matrix, first_row, block_rows, 0)
        row_segments = lax.dynamic_slice_in_dim(segment_row, first_row, block_rows, 0)
        scores = block_scores(
            row_block, key_matrix, row_segments, segment_row, first_row, decay_slope, score_scale
        )
        row_max = jnp.max(scores, axis=1, keepdims=True)
        weights = jnp.exp(scores - row_max)
        row_total = jnp.sum(weights, axis=1, keepdims=True)
        probabilities = (weights / row_total).astype(jnp.bfloat16)
        attended = jnp.dot(probabilities, value_matrix, preferred_element_type=jnp.float32).astype(
            jnp.bfloat16
        )
        return (attended, (row_max + jnp.log(row_total))[:, 0])

    attended, log_totals = lax.map(one_block, jnp.arange(0, seq_length, block_rows))
    return (attended.reshape(seq_length, -1), log_totals.reshape(seq_length))


def attend_backward(element, block_rows, score_scale):
    query_matrix, key_matrix, value_matrix, segment_row, decay_slope, log_totals, grad_matrix = (
        element
    )
    seq_length = key_matrix.shape[0]
    head_size = key_matrix.shape[1]

    def one_block(running, first_row):
        key_total, value_total = running
        row_block = lax.dynamic_slice_in_dim(query_matrix, first_row, block_rows, 0)
        row_segments = lax.dynamic_slice_in_dim(segment_row, first_row, block_rows, 0)
        row_logs = lax.dynamic_slice_in_dim(log_totals, first_row, block_rows, 0)
        row_grads = lax.dynamic_slice_in_dim(grad_matrix, first_row, block_rows, 0)
        scores = block_scores(
            row_block, key_matrix, row_segments, segment_row, first_row, decay_slope, score_scale
        )
        probabilities = jnp.exp(scores - row_logs[:, None])
        value_total = value_total + lax.dot_general(
            probabilities.astype(jnp.bfloat16),
            row_grads,
            contract_first,
            preferred_element_type=jnp.float32,
        )
        prob_grads = lax.dot_general(
            row_grads, value_matrix, contract_last, preferred_element_type=jnp.float32
        )
        centre = jnp.sum(probabilities * prob_grads, axis=1, keepdims=True)
        score_grads = (probabilities * (prob_grads - centre)).astype(jnp.bfloat16)
        key_total = (
            key_total
            + lax.dot_general(
                score_grads, row_block, contract_first, preferred_element_type=jnp.float32
            )
            * score_scale
        )
        query_grads = (
            jnp.dot(score_grads, key_matrix, preferred_element_type=jnp.float32) * score_scale
        )
        return ((key_total, value_total), query_grads)

    zero_block = jnp.zeros((seq_length, head_size), jnp.float32)
    (key_total, value_total), query_grads = lax.scan(
        one_block, (zero_block, zero_block), jnp.arange(0, seq_length, block_rows)
    )
    return (query_grads.reshape(seq_length, head_size), key_total, value_total)


def on_device(
    tokens,
    segments,
    gains,
    shifts,
    biases,
    mixing,
    projection,
    expand,
    thresholds,
    contract,
    cotangent,
):
    seq_count = segments.shape[0]
    seq_length = segments.shape[1]
    col_parts = lax.axis_size("col")
    full_width = tokens.shape[1] * col_parts
    head_count = mixing.shape[2] // HD
    score_scale = HD ** (-0.5)
    block_rows = min(512, seq_length)
    head_ids = (lax.axis_index("col") * head_count + jnp.arange(head_count)).astype(jnp.float32)
    slopes = jnp.exp2(-8.0 * (head_ids + 1.0) / (head_count * col_parts))
    slope_items = jnp.repeat(slopes, seq_count)
    segment_items = jnp.tile(segments, (head_count, 1))
    full_mix, full_proj, full_expand, full_contract = (
        lax.all_gather(mixing, "row", axis=0, tiled=True),
        lax.all_gather(projection, "row", axis=0, tiled=True),
        lax.all_gather(expand, "row", axis=0, tiled=True),
        lax.all_gather(contract, "row", axis=0, tiled=True),
    )
    resid_in = tokens.astype(jnp.float32)
    first_centred, first_scale, first_normed = normalize(resid_in, gains[0], shifts[0], full_width)
    first_full = gather_features(first_normed)
    mixed_rows = jnp.einsum("td,dcf->tcf", first_full, full_mix, preferred_element_type=jnp.float32)
    query_part = (mixed_rows[:, 0] + biases[0]).astype(jnp.bfloat16)
    key_part = mixed_rows[:, 1].astype(jnp.bfloat16)
    value_part = (mixed_rows[:, 2] + biases[1]).astype(jnp.bfloat16)
    query_heads = to_heads(query_part, seq_count, head_count)
    key_heads = to_heads(key_part, seq_count, head_count)
    value_heads = to_heads(value_part, seq_count, head_count)
    head_out, log_totals = lax.map(
        partial(attend_forward, block_rows=block_rows, score_scale=score_scale),
        (query_heads, key_heads, value_heads, segment_items, slope_items),
    )
    attended = from_heads(head_out, seq_count, head_count)
    proj_term = lax.dot_general(
        attended, full_proj, contract_last, preferred_element_type=jnp.float32
    )
    middle = resid_in + (sum_forward(proj_term) + biases[2])
    second_centred, second_scale, second_normed = normalize(middle, gains[1], shifts[1], full_width)
    second_full = gather_features(second_normed)
    hidden = jnp.dot(second_full, full_expand, preferred_element_type=jnp.float32) + thresholds
    erf_part = jax.scipy.special.erf(hidden * sqrt_half)
    active = (0.5 * hidden * (1.0 + erf_part)).astype(jnp.bfloat16)
    mlp_term = lax.dot_general(
        active, full_contract, contract_last, preferred_element_type=jnp.float32
    )
    layer_out = (middle + (sum_forward(mlp_term) + biases[3])).astype(jnp.bfloat16)
    back_mix, back_proj, back_expand, back_contract = (
        lax.all_gather(mixing, "row", axis=0, tiled=True),
        lax.all_gather(projection, "row", axis=0, tiled=True),
        lax.all_gather(expand, "row", axis=0, tiled=True),
        lax.all_gather(contract, "row", axis=0, tiled=True),
    )
    cot_full = gather_grads(cotangent)
    columns = cot_full
    contract_grad = lax.psum_scatter(
        lax.dot_general(columns, active, contract_first, preferred_element_type=jnp.float32),
        "row",
        scatter_dimension=0,
        tiled=True,
    )
    active_grad = jnp.dot(cot_full, back_contract, preferred_element_type=jnp.float32)
    density = jnp.exp(-0.5 * hidden * hidden) * inverse_root
    hidden_grad = (active_grad * (0.5 * (1.0 + erf_part) + hidden * density)).astype(jnp.bfloat16)
    columns = second_full
    expand_grad = lax.psum_scatter(
        lax.dot_general(columns, hidden_grad, contract_first, preferred_element_type=jnp.float32),
        "row",
        scatter_dimension=0,
        tiled=True,
    )
    thresholds_part = jnp.sum(hidden_grad.astype(jnp.float32), axis=0)
    second_back = sum_backward(
        lax.dot_general(hidden_grad, back_expand, contract_last, preferred_element_type=jnp.float32)
    )
    second_input, second_gain_part, second_shift_part = normalize_back(
        second_back, second_centred, second_scale, gains[1], full_width
    )
    cot_float = cotangent.astype(jnp.float32)
    middle_grad = cot_float + second_input
    branch_grad = middle_grad.astype(jnp.bfloat16)
    branch_full = gather_grads(branch_grad)
    columns = branch_full
    projection_grad = lax.psum_scatter(
        lax.dot_general(columns, attended, contract_first, preferred_element_type=jnp.float32),
        "row",
        scatter_dimension=0,
        tiled=True,
    )
    attended_grad = jnp.dot(branch_full, back_proj, preferred_element_type=jnp.float32).astype(
        jnp.bfloat16
    )
    query_back, key_back, value_back = lax.map(
        partial(attend_backward, block_rows=block_rows, score_scale=score_scale),
        (
            query_heads,
            key_heads,
            value_heads,
            segment_items,
            slope_items,
            log_totals,
            to_heads(attended_grad, seq_count, head_count),
        ),
    )
    mixed_grad = jnp.stack(
        [
            from_heads(query_back, seq_count, head_count),
            from_heads(key_back, seq_count, head_count),
            from_heads(value_back, seq_count, head_count),
        ],
        axis=1,
    ).astype(jnp.bfloat16)
    columns = first_full
    mixing_grad = lax.psum_scatter(
        jnp.einsum("tc,tkf->ckf", columns, mixed_grad, preferred_element_type=jnp.float32),
        "row",
        scatter_dimension=0,
        tiled=True,
    )
    mixed_float = mixed_grad.astype(jnp.float32)
    query_bias_part = jnp.sum(mixed_float[:, 0], axis=0)
    value_bias_part = jnp.sum(mixed_float[:, 2], axis=0)
    first_back = sum_backward(
        jnp.einsum("tkf,dkf->td", mixed_grad, back_mix, preferred_element_type=jnp.float32)
    )
    first_input, first_gain_part, first_shift_part = normalize_back(
        first_back, first_centred, first_scale, gains[0], full_width
    )
    tokens_grad = middle_grad + first_input
    gains_grad, shifts_grad, biases_grad, thresholds_grad = lax.psum(
        (
            jnp.stack([first_gain_part, second_gain_part]),
            jnp.stack([first_shift_part, second_shift_part]),
            jnp.stack(
                [
                    query_bias_part,
                    value_bias_part,
                    jnp.sum(branch_grad.astype(jnp.float32), axis=0),
                    jnp.sum(cot_float, axis=0),
                ]
            ),
            thresholds_part,
        ),
        "row",
    )
    return (
        layer_out,
        tokens_grad,
        gains_grad,
        shifts_grad,
        biases_grad,
        mixing_grad,
        projection_grad,
        expand_grad,
        thresholds_grad,
        contract_grad,
    )


def solution(mesh):
    return jax.shard_map(
        on_device,
        mesh=mesh,
        in_specs=(
            P("row", "col"),
            P("row", None),
            P(None, "col"),
            P(None, "col"),
            P(None, "col"),
            P("row", None, "col"),
            P("row", "col"),
            P("row", "col"),
            P("col"),
            P("row", "col"),
            P("row", "col"),
        ),
        out_specs=(
            P("row", "col"),
            P("row", "col"),
            P(None, "col"),
            P(None, "col"),
            P(None, "col"),
            P("row", None, "col"),
            P("row", "col"),
            P("row", "col"),
            P("col"),
            P("row", "col"),
        ),
        check_vma=False,
    )
```

profile of v0, /device:TPU:0, one launch (start us, length us, event | category | flops | bytes accessed | tf_op | source)
XLA Modules:
  0.0 1903.3 jit_solution(4557955186555000541)
XLA Ops:
  10.4 8.5 all-reduce.4
  19.5 2.6 fusion.36
  25.0 32.1 %all-gather.9.cloned.1.call-done = bf16[1024,2048]{1,0:T(8,128)(2,1)} async-done(((bf16[1024,512]{1,0:T(8,128)(2,1)}), bf16[1024,2048]{1,0:T(8,128)(2,1)}) %all-gather.9.cloned.1.call-update) | async-done | bytes 4194320 | tf_op jit(solution)/shard_map/all_gather | solution.py:38
  57.2 102.6 %all-gather.11.cloned.1.call-done = bf16[2048,3,512]{0,2,1:T(8,128)(2,1)} async-done(((bf16[256,3,512]{0,2,1:T(8,128)(2,1)}), bf16[2048,3,512]{0,2,1:T(8,128)(2,1)}) %all-gather.11.cloned.1.call-update) | async-done | bytes 6291472 | tf_op jit(solution)/shard_map/all_gather | solution.py:179
  159.7 10.1 fusion.28
  171.7 3.8 copy.39
  175.5 2.7 copy.41
  180.0 6.5 fusion.43
  186.5 137.3 %while.54 = (s32[]{:T(128)}, bf16[8,1024,64]{1,2,0:T(8,128)(2,1)}, f32[8,1024]{1,0:T(8,128)}, bf16[8,1024,64]{2,1,0:T(8,128)(2,1)}, s32[8,1024]{1,0:T(8,128)S(1)...) while((s32[]{:T(128)}, bf16[8,1024,64]{1,2,0:T(8,128)(2,1)}, ...), condition=%wide.region_9.10_spmd, body=%wide.region_4.9_spmd.sunk | while | flops 142114816 | bytes 8645572 | solution.py:194
  189.2 12.1 while.57
  206.4 12.1 while.57
  223.6 12.1 while.57
  240.7 12.1 while.57
  257.9 12.1 while.57
  275.0 12.1 while.57
  292.2 12.1 while.57
  309.4 12.1 while.57
  323.9 7.5 fusion.51
  332.1 69.4 %reduce-scatter.9.cloned.1.call-done = f32[1024,512]{1,0:T(8,128)} async-done(((f32[1024,2048]{1,0:T(8,128)}), f32[1024,512]{1,0:T(8,128)}) %reduce-scatter.9.cloned.1.call-update) | async-done | bytes 2097168 | tf_op jit(solution)/shard_map/reduce_scatter | solution.py:46
  403.6 5.9 all-reduce.3
  412.4 116.3 %all-gather.17.cloned.1.call-done = bf16[2048,2048]{1,0:T(8,128)(2,1)} async-done(((bf16[256,2048]{1,0:T(8,128)(2,1)}), bf16[2048,2048]{1,0:T(8,128)(2,1)}) %all-gather.17.cloned.1.call-update) | async-done | bytes 8388624 | tf_op jit(solution)/shard_map/all_gather | solution.py:181
  528.7 34.8 %all-gather.15.cloned.1.call-done = bf16[1024,2048]{1,0:T(8,128)(2,1)} async-done(((bf16[1024,512]{1,0:T(8,128)(2,1)}), bf16[1024,2048]{1,0:T(8,128)(2,1)}) %all-gather.15.cloned.1.call-update) | async-done | bytes 4194320 | tf_op jit(solution)/shard_map/all_gather | solution.py:38
  563.4 16.2 multiply_convert_fusion.1
  579.6 20.0 %all-gather.21.cloned.1.call-done = bf16[1024,2048]{1,0:T(8,128)(2,1)} async-done(((bf16[1024,512]{1,0:T(8,128)(2,1)}), bf16[1024,2048]{1,0:T(8,128)(2,1)}) %all-gather.21.cloned.1.call-update) | async-done | bytes 4194320 | tf_op jit(solution)/shard_map/all_gather | solution.py:42
  599.6 127.3 %all-gather.19.cloned.1.call-done = bf16[2048,2048]{1,0:T(8,128)(2,1)} async-done(((bf16[256,2048]{1,0:T(8,128)(2,1)}), bf16[2048,2048]{1,0:T(8,128)(2,1)}) %all-gather.19.cloned.1.call-update) | async-done | bytes 8388624 | tf_op jit(solution)/shard_map/all_gather | solution.py:182
  726.9 16.9 convert_reduce_fusion
  745.7 11.0 fusion.53
  756.9 14.7 fusion.52
  771.7 55.1 %reduce-scatter.13.cloned.1.call-done = f32[1024,512]{1,0:T(8,128)} async-done(((f32[1024,2048]{1,0:T(8,128)}), f32[1024,512]{1,0:T(8,128)}) %reduce-scatter.13.cloned.1.call-update) | async-done | bytes 2097168 | tf_op jit(solution)/shard_map/reduce_scatter | solution.py:50
  826.8 3.2 multiply_reduce_fusion.1
  830.0 5.8 all-reduce.2
  835.9 65.1 %reduce-scatter.11.cloned.1.call-done = f32[1024,512]{1,0:T(8,128)} async-done(((f32[1024,2048]{1,0:T(8,128)}), f32[1024,512]{1,0:T(8,128)}) %reduce-scatter.11.cloned.1.call-update) | async-done | bytes 2097168 | tf_op jit(solution)/shard_map/reduce_scatter | solution.py:46
  901.0 4.7 convert_reduce_fusion.3
  905.9 15.2 convolution_bitcast_fusion
  921.3 19.1 %all-gather.23.cloned.1.call-done = bf16[1024,2048]{1,0:T(8,128)(2,1)} async-done(((bf16[1024,512]{1,0:T(8,128)(2,1)}), bf16[1024,2048]{1,0:T(8,128)(2,1)}) %all-gather.23.cloned.1.call-update) | async-done | bytes 4194320 | tf_op jit(solution)/shard_map/all_gather | solution.py:42
  940.4 4.6 convolution_convert_fusion.1
  946.8 272.2 %while.56 = (s32[]{:T(128)}, bf16[8,1024,64]{1,2,0:T(8,128)(2,1)}, bf16[8,1024,64]{1,2,0:T(8,128)(2,1)}, bf16[8,1024,64]{1,2,0:T(8,128)(2,1)}, bf16[8,1024,64]{2...) while((s32[]{:T(128)}, bf16[8,1024,64]{1,2,0:T(8,128)(2,1)}, ...), condition=%wide.region_25.26_spmd, body=%wide.region_21.25_spmd.sunk | while | flops 344293376 | bytes 23373520 | solution.py:257
  953.5 24.5 %while.58 = (s32[]{:T(128)}, f32[1024,64]{0,1:T(8,128)}, f32[1024,64]{0,1:T(8,128)S(1)}, bf16[2,512,64]{1,2,0:T(8,128)(2,1)S(1)}, s32[2]{0:T(128)S(1)}, /*index=...) while((s32[]{:T(128)}, f32[1024,64]{0,1:T(8,128)}, ...), condition=%wide.region_24.24_spmd.clone, body=%wide.region_22.23_spmd.clone.sunk | while | flops 344293376 | bytes 20210008 | solution.py:148
  973.2 2.1 fusion.110
  987.6 24.6 %while.58 = (s32[]{:T(128)}, f32[1024,64]{0,1:T(8,128)}, f32[1024,64]{0,1:T(8,128)S(1)}, bf16[2,512,64]{1,2,0:T(8,128)(2,1)S(1)}, s32[2]{0:T(128)S(1)}, /*index=...) while((s32[]{:T(128)}, f32[1024,64]{0,1:T(8,128)}, ...), condition=%wide.region_24.24_spmd.clone, body=%wide.region_22.23_spmd.clone.sunk | while | flops 344293376 | bytes 20210008 | solution.py:148
  1007.3 2.1 fusion.110
  1021.6 24.6 %while.58 = (s32[]{:T(128)}, f32[1024,64]{0,1:T(8,128)}, f32[1024,64]{0,1:T(8,128)S(1)}, bf16[2,512,64]{1,2,0:T(8,128)(2,1)S(1)}, s32[2]{0:T(128)S(1)}, /*index=...) while((s32[]{:T(128)}, f32[1024,64]{0,1:T(8,128)}, ...), condition=%wide.region_24.24_spmd.clone, body=%wide.region_22.23_spmd.clone.sunk | while | flops 344293376 | bytes 20210008 | solution.py:148
  1041.3 2.1 fusion.110
  1055.7 24.6 %while.58 = (s32[]{:T(128)}, f32[1024,64]{0,1:T(8,128)}, f32[1024,64]{0,1:T(8,128)S(1)}, bf16[2,512,64]{1,2,0:T(8,128)(2,1)S(1)}, s32[2]{0:T(128)S(1)}, /*index=...) while((s32[]{:T(128)}, f32[1024,64]{0,1:T(8,128)}, ...), condition=%wide.region_24.24_spmd.clone, body=%wide.region_22.23_spmd.clone.sunk | while | flops 344293376 | bytes 20210008 | solution.py:148
  1075.4 2.1 fusion.110
  1089.7 24.5 %while.58 = (s32[]{:T(128)}, f32[1024,64]{0,1:T(8,128)}, f32[1024,64]{0,1:T(8,128)S(1)}, bf16[2,512,64]{1,2,0:T(8,128)(2,1)S(1)}, s32[2]{0:T(128)S(1)}, /*index=...) while((s32[]{:T(128)}, f32[1024,64]{0,1:T(8,128)}, ...), condition=%wide.region_24.24_spmd.clone, body=%wide.region_22.23_spmd.clone.sunk | while | flops 344293376 | bytes 20210008 | solution.py:148
  1109.4 2.1 fusion.110
  1123.7 24.5 %while.58 = (s32[]{:T(128)}, f32[1024,64]{0,1:T(8,128)}, f32[1024,64]{0,1:T(8,128)S(1)}, bf16[2,512,64]{1,2,0:T(8,128)(2,1)S(1)}, s32[2]{0:T(128)S(1)}, /*index=...) while((s32[]{:T(128)}, f32[1024,64]{0,1:T(8,128)}, ...), condition=%wide.region_24.24_spmd.clone, body=%wide.region_22.23_spmd.clone.sunk | while | flops 344293376 | bytes 20210008 | solution.py:148
  1143.4 2.1 fusion.110
  1157.8 24.5 %while.58 = (s32[]{:T(128)}, f32[1024,64]{0,1:T(8,128)}, f32[1024,64]{0,1:T(8,128)S(1)}, bf16[2,512,64]{1,2,0:T(8,128)(2,1)S(1)}, s32[2]{0:T(128)S(1)}, /*index=...) while((s32[]{:T(128)}, f32[1024,64]{0,1:T(8,128)}, ...), condition=%wide.region_24.24_spmd.clone, body=%wide.region_22.23_spmd.clone.sunk | while | flops 344293376 | bytes 20210008 | solution.py:148
  1191.8 24.5 %while.58 = (s32[]{:T(128)}, f32[1024,64]{0,1:T(8,128)}, f32[1024,64]{0,1:T(8,128)S(1)}, bf16[2,512,64]{1,2,0:T(8,128)(2,1)S(1)}, s32[2]{0:T(128)S(1)}, /*index=...) while((s32[]{:T(128)}, f32[1024,64]{0,1:T(8,128)}, ...), condition=%wide.region_24.24_spmd.clone, body=%wide.region_22.23_spmd.clone.sunk | while | flops 344293376 | bytes 20210008 | solution.py:148
  1222.7 10.7 convolution_bitcast_fusion.1
  1233.5 6.8 fusion.54
  1240.6 17.1 fusion.55
  1257.7 11.6 fusion.26
  1270.6 3.1 copy.52
  1273.7 31.6 %reduce-scatter.15.cloned.1.call-done = f32[1024,512]{1,0:T(8,128)} async-done(((f32[1024,2048]{1,0:T(8,128)}), f32[1024,512]{1,0:T(8,128)}) %reduce-scatter.15.cloned.1.call-update) | async-done | bytes 2097168 | tf_op jit(solution)/shard_map/reduce_scatter | solution.py:50
  1305.3 2.7 fusion.41
  1308.1 39.2 %all-reduce = (f32[2,512]{1,0:T(2,128)}, f32[2,512]{1,0:T(2,128)}, f32[4,512]{1,0:T(4,128)}, f32[2048]{0:T(1024)}) all-reduce(f32[2,512]{1,0:T(2,128)S(1)} %pad_maximum_fusion.2, f32[2,512]{1,0:T(2,128)S(1)} %pad_maximum_fusion.3, f32[4,512]{1,0:T(4,128)S(1)} %pad_maximum_fusion.1, ...), channel_id=1, replica_groups=mesh['row'=8,'col'=4] {'row'}, use_global_device_ids=true, to_apply=%region_33.34 | all-reduce | flops 6144 | bytes 49152 | tf_op jit(solution)/shard_map/psum | solution.py:294
  1347.3 6.1 all-reduce.1
  1353.5 3.1 fusion.40
  1356.6 41.8 %reduce-scatter.19.cloned.1.call-done = f32[256,512]{1,0:T(8,128)} async-done(((f32[2048,512]{1,0:T(8,128)}), f32[256,512]{1,0:T(8,128)}) %reduce-scatter.19.cloned.1.call-update) | async-done | bytes 524304 | tf_op jit(solution)/shard_map/reduce_scatter | solution.py:248
  1398.4 286.8 %reduce-scatter.21.cloned.1.call-done = f32[256,2048]{1,0:T(8,128)} async-done(((f32[2048,2048]{1,0:T(8,128)}), f32[256,2048]{1,0:T(8,128)}) %reduce-scatter.21.cloned.1.call-update) | async-done | bytes 2097168 | tf_op jit(solution)/shard_map/reduce_scatter | solution.py:230
  1685.1 211.2 %reduce-scatter.17.cloned.1.call-done = f32[256,3,512]{2,0,1:T(8,128)} async-done(((f32[2048,3,512]{2,0,1:T(8,128)}), f32[256,3,512]{2,0,1:T(8,128)}) %reduce-scatter.17.cloned.1.call-update) | async-done | bytes 1572880 | tf_op jit(solution)/shard_map/reduce_scatter | solution.py:278
  (774 shorter events, 356.0 us)
Async XLA Ops:
  7.2 15.1 copy-start.9
  7.2 50.0 %all-gather.9.cloned.1.call-start = ((), (), s32[]{:S(2)}) async-start(), calls=%async_computation.8 | async-start | bytes 5242880 | tf_op jit(solution)/shard_map/all_gather | solution.py:38
  9.7 13.8 copy-start.16
  22.2 137.5 %all-gather.11.cloned.1.call-start = ((), (), s32[]{:S(2)}) async-start(), calls=%async_computation.9 | async-start | bytes 7077888 | tf_op jit(solution)/shard_map/all_gather | solution.py:179
  23.4 300.4 %all-gather.13.cloned.1.call-start = ((), (), s32[]{:S(2)}) async-start(), calls=%async_computation.10 | async-start | bytes 2359296 | tf_op jit(solution)/shard_map/all_gather | solution.py:180
  24.2 377.3 %reduce-scatter.9.cloned.1.call-start = ((), (), s32[]{:S(2)}) async-start(), calls=%async_computation.11 | async-start | bytes 10485760 | tf_op jit(solution)/shard_map/reduce_scatter | solution.py:46
  331.4 70.1 %copy-start.4 = (bf16[1024,512]{1,0:T(8,128)(2,1)S(1)}, bf16[1024,512]{1,0:T(8,128)(2,1)}, u32[]{:S(2)}) copy-start(bf16[1024,512]{1,0:T(8,128)(2,1)} %param.19) | copy-start | bytes 3145732
  331.4 197.2 %all-gather.17.cloned.1.call-start = ((), (), s32[]{:S(2)}) async-start(), calls=%async_computation.13 | async-start | bytes 9437184 | tf_op jit(solution)/shard_map/all_gather | solution.py:181
  332.0 231.4 %all-gather.15.cloned.1.call-start = ((), (), s32[]{:S(2)}) async-start(), calls=%async_computation.12 | async-start | bytes 5242880 | tf_op jit(solution)/shard_map/all_gather | solution.py:38
  410.8 152.6 %copy-start.28 = (f32[2048]{0:T(1024)S(1)}, f32[2048]{0:T(1024)}, u32[]{:S(2)}) copy-start(f32[2048]{0:T(1024)} %param.27) | copy-start | bytes 24580
  410.8 188.7 %all-gather.21.cloned.1.call-start = ((), (), s32[]{:S(2)}) async-start(), calls=%async_computation.16 | async-start | bytes 5242880 | tf_op jit(solution)/shard_map/all_gather | solution.py:42
  411.6 315.3 %all-gather.19.cloned.1.call-start = ((), (), s32[]{:S(2)}) async-start(), calls=%async_computation.14 | async-start | bytes 9437184 | tf_op jit(solution)/shard_map/all_gather | solution.py:182
  412.3 414.5 %reduce-scatter.13.cloned.1.call-start = ((), (), s32[]{:S(2)}) async-start(), calls=%async_computation.17 | async-start | bytes 10485760 | tf_op jit(solution)/shard_map/reduce_scatter | solution.py:50
  726.9 18.8 copy-start.26
  756.8 144.2 %reduce-scatter.11.cloned.1.call-start = ((), (), s32[]{:S(2)}) async-start(), calls=%async_computation.15 | async-start | bytes 10485760 | tf_op jit(solution)/shard_map/reduce_scatter | solution.py:46
  771.6 129.4 %copy-start.7 = (bf16[1024,512]{1,0:T(8,128)(2,1)S(1)}, bf16[1024,512]{1,0:T(8,128)(2,1)}, u32[]{:S(2)}) copy-start(bf16[1024,512]{1,0:T(8,128)(2,1)} %param.29) | copy-start | bytes 3145732
  771.6 129.4 %copy-start.20 = (f32[1,512]{1,0:T(1,128)S(1)}, f32[1,512]{1,0:T(1,128)}, u32[]{:S(2)}) copy-start(f32[1,512]{1,0:T(1,128)} %get-tuple-element.434) | copy-start | bytes 6148
  771.6 168.8 %all-gather.23.cloned.1.call-start = ((), (), s32[]{:S(2)}) async-start(), calls=%async_computation.18 | async-start | bytes 5242880 | tf_op jit(solution)/shard_map/all_gather | solution.py:42
  905.8 364.8 %reduce-scatter.23.cloned.1.call-start = ((), (), s32[]{:S(2)}) async-start(), calls=%async_computation.23 | async-start | bytes 18874368 | tf_op jit(solution)/shard_map/reduce_scatter | solution.py:220
  921.1 19.4 %copy-start.27 = (bf16[2048,512]{1,0:T(8,128)(2,1)S(1)}, bf16[2048,512]{1,0:T(8,128)(2,1)}, u32[]{:S(2)}) copy-start(bf16[2048,512]{1,0:T(8,128)(2,1)} %all-gather.13.cloned.1.call-done) | copy-start | bytes 6291460
  921.1 384.2 %reduce-scatter.15.cloned.1.call-start = ((), (), s32[]{:S(2)}) async-start(), calls=%async_computation.19 | async-start | bytes 10485760 | tf_op jit(solution)/shard_map/reduce_scatter | solution.py:50
  953.5 7.2 copy-start
  953.6 7.2 copy-start.2
  965.8 7.2 copy-start
  965.8 7.2 copy-start.2
  987.6 7.2 copy-start
  987.6 7.2 copy-start.2
  999.8 7.2 copy-start
  999.8 7.2 copy-start.2
  1021.6 7.2 copy-start
  1021.6 7.2 copy-start.2
  1033.9 7.2 copy-start
  1033.9 7.2 copy-start.2
  1055.7 7.2 copy-start
  1055.7 7.2 copy-start.2
  1067.9 7.2 copy-start
  1067.9 7.2 copy-start.2
  1089.7 7.2 copy-start
  1089.7 7.2 copy-start.2
  1101.9 7.2 copy-start
  1101.9 7.2 copy-start.2
  1123.7 7.2 copy-start
  1123.7 7.2 copy-start.2
  1135.9 7.2 copy-start
  1135.9 7.2 copy-start.2
  1157.8 7.2 copy-start
  1157.8 7.2 copy-start.2
  1170.0 7.2 copy-start
  1170.0 7.2 copy-start.2
  1191.8 7.2 copy-start
  1191.8 7.2 copy-start.2
  1204.0 7.2 copy-start
  1204.0 7.2 copy-start.2
  1233.4 165.0 %reduce-scatter.19.cloned.1.call-start = ((), (), s32[]{:S(2)}) async-start(), calls=%async_computation.21 | async-start | bytes 4718592 | tf_op jit(solution)/shard_map/reduce_scatter | solution.py:248
  1240.3 444.8 %reduce-scatter.21.cloned.1.call-start = ((), (), s32[]{:S(2)}) async-start(), calls=%async_computation.22 | async-start | bytes 18874368 | tf_op jit(solution)/shard_map/reduce_scatter | solution.py:230
  1257.7 638.6 %reduce-scatter.17.cloned.1.call-start = ((), (), s32[]{:S(2)}) async-start(), calls=%async_computation.20 | async-start | bytes 14155776 | tf_op jit(solution)/shard_map/reduce_scatter | solution.py:278
  1270.6 34.7 %copy-start.5 = (bf16[1024,512]{1,0:T(8,128)(2,1)S(1)}, bf16[1024,512]{1,0:T(8,128)(2,1)}, u32[]{:S(2)}) copy-start(bf16[1024,512]{1,0:T(8,128)(2,1)} %param.19) | copy-start | bytes 3145732
  1270.6 34.7 %copy-start.13 = (f32[1024]{0:T(1024)S(1)}, f32[1024]{0:T(1024)}, u32[]{:S(2)}) copy-start(f32[1024]{0:T(1024)} %copy-done.12) | copy-start | bytes 12292
  1270.6 34.7 %copy-start.15 = (f32[1024]{0:T(1024)S(1)}, f32[1024]{0:T(1024)}, u32[]{:S(2)}) copy-start(f32[1024]{0:T(1024)} %copy-done.14) | copy-start | bytes 12292
  1270.6 34.7 %copy-start.17 = (f32[1,512]{1,0:T(1,128)S(1)}, f32[1,512]{1,0:T(1,128)}, u32[]{:S(2)}) copy-start(f32[1,512]{1,0:T(1,128)} %copy-done.16) | copy-start | bytes 6148
  1273.7 34.3 %copy-start.19 = (f32[512]{0:T(512)S(1)}, f32[512]{0:T(512)}, u32[]{:S(2)}) copy-start(f32[512]{0:T(512)} %get-tuple-element.319) | copy-start | bytes 6148
  1273.7 34.3 %copy-start.18 = (f32[512]{0:T(512)S(1)}, f32[512]{0:T(512)}, u32[]{:S(2)}) copy-start(f32[512]{0:T(512)} %get-tuple-element.312) | copy-start | bytes 6148
  1273.7 34.3 %copy-start.23 = (f32[2048]{0:T(1024)S(1)}, f32[2048]{0:T(1024)}, u32[]{:S(2)}) copy-start(f32[2048]{0:T(1024)} %get-tuple-element.446) | copy-start | bytes 24580
  1273.7 79.7 %copy-start.6 = (f32[1024,512]{1,0:T(8,128)S(1)}, f32[1024,512]{1,0:T(8,128)}, u32[]{:S(2)}) copy-start(f32[1024,512]{1,0:T(8,128)} %get-tuple-element.420) | copy-start | bytes 6291460
  (56 other events, 134.1 us)
Sparse Core Ops, SparseCore 0:
  22.3 34.7 all-gather.8
  59.8 99.9 all-gather.10
  161.9 47.4 all-gather.12
  331.5 69.8 reduce-scatter.8
  403.7 124.9 all-gather.16
  530.7 32.6 all-gather.14
  565.1 34.4 all-gather.20
  601.9 124.9 all-gather.18
  756.9 69.8 reduce-scatter.12
  829.3 71.7 reduce-scatter.10
  905.9 34.4 all-gather.22
  944.5 282.5 reduce-scatter.22
  1233.5 71.7 reduce-scatter.14
  1309.8 88.5 reduce-scatter.18
  1402.6 282.5 reduce-scatter.20
  1689.6 206.6 reduce-scatter.16
where the time goes:
time: 1920 us; the launch traced here: 1900 us
  waiting for transfers between devices  1220 us (64%)
  matrix products  310 us (16%)
  local copies, waits for them, and re-layouts  167 us (9%)
  loops' own time  66.5 us (3%)
  blocking collectives  65.6 us (3%)
  other arithmetic  61.9 us (3%)
    reduce_scatter x1, waiting for transfers between devices, on_device(): lax.psum_scatter(lax.dot_general(columns, hidden_grad, contract_first, pr...  287 us
    reduce_scatter x1, waiting for transfers between devices, on_device(): lax.psum_scatter(jnp.einsum('tc,tkf->ckf', columns, mixed_grad, preferred...  211 us
    reduce_scatter x2, waiting for transfers between devices, sum_forward(): lax.psum_scatter(partial_term, 'col', scatter_dimension=1, tiled=True)  135 us
    all_gather x1, waiting for transfers between devices, on_device(): lax.all_gather(contract, 'row', axis=0, tiled=True)  127 us
    all_gather x1, waiting for transfers between devices, on_device(): lax.all_gather(expand, 'row', axis=0, tiled=True)  116 us
    all_gather x1, waiting for transfers between devices, on_device(): lax.all_gather(mixing, 'row', axis=0, tiled=True)  103 us
    reduce_scatter x2, waiting for transfers between devices, sum_backward(): lax.psum_scatter(partial_term, 'col', scatter_dimension=1, tiled=True)  86.7 us
    all_gather x2, waiting for transfers between devices, gather_features(): return lax.all_gather(local_part, 'col', axis=1, tiled=True)  66.9 us
  transfers between devices with their start and end apart: 16, of which 14 were waited for; matrix products, arithmetic and copies ran while one was open for 26% of the time, Pallas kernels for 0%

commit v1 on v0

--- a/solution.py
+++ b/solution.py
@@ -3,6 +3,8 @@
 import jax
 import jax.numpy as jnp
 from jax import lax
+from jax.experimental import pallas as pl
+from jax.experimental.pallas import tpu as pltpu
 from jax.sharding import PartitionSpec as P
 
 HD = 64
@@ -50,105 +52,118 @@
     return lax.psum_scatter(partial_term, "col", scatter_dimension=1, tiled=True)
 
 
-def to_heads(matrix, seq_count, head_count):
-    return (
-        matrix.reshape(seq_count, -1, head_count, HD)
-        .transpose(2, 0, 1, 3)
-        .reshape(head_count * seq_count, -1, HD)
-    )
-
-
-def from_heads(stacked, seq_count, head_count):
-    return (
-        stacked.reshape(head_count, seq_count, -1, HD)
-        .transpose(1, 2, 0, 3)
-        .reshape(-1, head_count * HD)
-    )
-
-
-def block_scores(
-    row_block, key_matrix, row_segments, segment_row, first_row, decay_slope, score_scale
-):
-    raw_scores = lax.dot_general(
-        row_block, key_matrix, contract_last, preferred_element_type=jnp.float32
-    )
-    row_places = first_row + jnp.arange(row_block.shape[0])
-    col_places = jnp.arange(key_matrix.shape[0])
-    distance = (row_places[:, None] - col_places[None, :]).astype(jnp.float32)
-    allowed = (row_segments[:, None] == segment_row[None, :]) & (
-        col_places[None, :] <= row_places[:, None]
-    )
-    return jnp.where(allowed, (raw_scores - decay_slope * distance) * score_scale, masked_score)
-
-
-def attend_forward(element, block_rows, score_scale):
-    query_matrix, key_matrix, value_matrix, segment_row, decay_slope = element
-    seq_length = key_matrix.shape[0]
-
-    def one_block(first_row):
-        row_block = lax.dynamic_slice_in_dim(query_matrix, first_row, block_rows, 0)
-        row_segments = lax.dynamic_slice_in_dim(segment_row, first_row, block_rows, 0)
-        scores = block_scores(
-            row_block, key_matrix, row_segments, segment_row, first_row, decay_slope, score_scale
-        )
-        row_max = jnp.max(scores, axis=1, keepdims=True)
-        weights = jnp.exp(scores - row_max)
-        row_total = jnp.sum(weights, axis=1, keepdims=True)
-        probabilities = (weights / row_total).astype(jnp.bfloat16)
-        attended = jnp.dot(probabilities, value_matrix, preferred_element_type=jnp.float32).astype(
-            jnp.bfloat16
-        )
-        return (attended, (row_max + jnp.log(row_total))[:, 0])
-
-    attended, log_totals = lax.map(one_block, jnp.arange(0, seq_length, block_rows))
-    return (attended.reshape(seq_length, -1), log_totals.reshape(seq_length))
-
-
-def attend_backward(element, block_rows, score_scale):
-    query_matrix, key_matrix, value_matrix, segment_row, decay_slope, log_totals, grad_matrix = (
-        element
-    )
-    seq_length = key_matrix.shape[0]
-    head_size = key_matrix.shape[1]
-
-    def one_block(running, first_row):
-        key_total, value_total = running
-        row_block = lax.dynamic_slice_in_dim(query_matrix, first_row, block_rows, 0)
-        row_segments = lax.dynamic_slice_in_dim(segment_row, first_row, block_rows, 0)
-        row_logs = lax.dynamic_slice_in_dim(log_totals, first_row, block_rows, 0)
-        row_grads = lax.dynamic_slice_in_dim(grad_matrix, first_row, block_rows, 0)
-        scores = block_scores(
-            row_block, key_matrix, row_segments, segment_row, first_row, decay_slope, score_scale
-        )
-        probabilities = jnp.exp(scores - row_logs[:, None])
-        value_total = value_total + lax.dot_general(
-            probabilities.astype(jnp.bfloat16),
-            row_grads,
-            contract_first,
-            preferred_element_type=jnp.float32,
-        )
-        prob_grads = lax.dot_general(
-            row_grads, value_matrix, contract_last, preferred_element_type=jnp.float32
-        )
-        centre = jnp.sum(probabilities * prob_grads, axis=1, keepdims=True)
-        score_grads = (probabilities * (prob_grads - centre)).astype(jnp.bfloat16)
-        key_total = (
-            key_total
-            + lax.dot_general(
-                score_grads, row_block, contract_first, preferred_element_type=jnp.float32
-            )
-            * score_scale
-        )
-        query_grads = (
-            jnp.dot(score_grads, key_matrix, preferred_element_type=jnp.float32) * score_scale
-        )
-        return ((key_total, value_total), query_grads)
-
-    zero_block = jnp.zeros((seq_length, head_size), jnp.float32)
-    (key_total, value_total), query_grads = lax.scan(
-        one_block, (zero_block, zero_block), jnp.arange(0, seq_length, block_rows)
-    )
-    return (query_grads.reshape(seq_length, head_size), key_total, value_total)
+NT=(((1,),(1,)),((),()))
+TN=(((0,),(0,)),((),()))
+far=-1e33
+
+def pick_heads(pair):
+    lane=lax.broadcasted_iota(jnp.int32,pair.shape,1)
+    zero=jnp.zeros_like(pair)
+    return jnp.concatenate([jnp.where(lane<HD,pair,zero),jnp.where(lane<HD,zero,pair)],axis=0)
+
+def attend_kernel(slope_ref,start_ref,q_ref,k_ref,v_ref,out_ref,log_ref,dist_ref,*,rows,scale):
+    pair=pl.program_id(1)
+    length=k_ref.shape[0]
+    @pl.when(pair==0)
+    def _():
+        for r0 in range(0,length,rows):
+            shape=(rows,r0+rows)
+            i=lax.broadcasted_iota(jnp.int32,shape,0)+r0
+            j=lax.broadcasted_iota(jnp.int32,shape,1)
+            ok=(j<=i)&(j>=start_ref[0,r0:r0+rows,:])
+            dist_ref[r0:r0+rows,0:r0+rows]=jnp.where(ok,(j-i).astype(jnp.float32),far)
+    s0=slope_ref[2*pair]*scale; s1=slope_ref[2*pair+1]*scale
+    for r0 in range(0,length,rows):
+        r1=r0+rows
+        q=pick_heads(q_ref[r0:r1,:]*jnp.asarray(scale,jnp.bfloat16))
+        s=lax.dot_general(q,k_ref[0:r1,:],NT,preferred_element_type=jnp.float32)
+        d=dist_ref[r0:r1,0:r1]
+        s=jnp.concatenate([s[:rows]+d*s0,s[rows:]+d*s1],axis=0)
+        m=jnp.max(s,axis=1,keepdims=True)
+        e=jnp.exp(s-m)
+        l=jnp.sum(e,axis=1,keepdims=True)
+        p=(e*(1.0/l)).astype(jnp.bfloat16)
+        o=jnp.dot(p,v_ref[0:r1,:],preferred_element_type=jnp.float32)
+        lane=lax.broadcasted_iota(jnp.int32,(rows,2*HD),1)
+        out_ref[r0:r1,:]=jnp.where(lane<HD,o[:rows],o[rows:]).astype(jnp.bfloat16)
+        t=jnp.where(lane<HD,jnp.broadcast_to((m+jnp.log(l))[:rows],(rows,2*HD)),jnp.broadcast_to((m+jnp.log(l))[rows:],(rows,2*HD)))
+        t=t.T
+        log_ref[0,0:1,r0:r1]=t[0:1]
+        log_ref[0,1:2,r0:r1]=t[HD:HD+1]
+
+def attend_forward(q,k,v,start,slopes,seqs,rows=256):
+    length=q.shape[0]//seqs; pairs=q.shape[1]//(2*HD)
+    spec=pl.BlockSpec((length,2*HD),lambda s,p,*_:(s,p))
+    return pl.pallas_call(partial(attend_kernel,rows=rows,scale=HD**-0.5),
+        grid_spec=pltpu.PrefetchScalarGridSpec(num_scalar_prefetch=1,grid=(seqs,pairs),
+            in_specs=[pl.BlockSpec((1,length,1),lambda s,p,*_:(s,0,0)),spec,spec,spec],
+            out_specs=[spec,pl.BlockSpec((1,2,length),lambda s,p,*_:(s*pairs+p,0,0))],
+            scratch_shapes=[pltpu.VMEM((length,length),jnp.float32)]),
+        out_shape=[jax.ShapeDtypeStruct(q.shape,jnp.bfloat16),jax.ShapeDtypeStruct((seqs*pairs,2,length),jnp.float32)],
+        compiler_params=pltpu.CompilerParams(vmem_limit_bytes=40<<20),
+        cost_estimate=pl.CostEstimate(flops=4*seqs*pairs*2*length*length*HD,bytes_accessed=8*q.size,transcendentals=seqs*pairs*length*length),
+        name="attend_forward")(slopes,start[:,:,None],q,k,v)
+
+def attend_back_kernel(slope_ref,start_ref,log_ref,q_ref,k_ref,v_ref,g_ref,dq_ref,dk_ref,dv_ref,qs_ref,vs_ref,dist_ref,ka_ref,va_ref,*,rows,scale):
+    pair=pl.program_id(1)
+    length=k_ref.shape[0]
+    @pl.when(pair==0)
+    def _():
+        for r0 in range(0,length,rows):
+            shape=(r0+rows,rows)
+            i=lax.broadcasted_iota(jnp.int32,shape,1)+r0
+            j=lax.broadcasted_iota(jnp.int32,shape,0)
+            ok=(j<=i)&(j>=start_ref[0,:,r0:r0+rows])
+            dist_ref[0:r0+rows,r0:r0+rows]=jnp.where(ok,(j-i).astype(jnp.float32),far)
+    s0=slope_ref[2*pair]*scale; s1=slope_ref[2*pair+1]*scale
+    half=jnp.asarray(scale,jnp.bfloat16)
+    qsum=jnp.zeros((1,2*HD),jnp.float32)
+    for r0 in reversed(range(0,length,rows)):
+        r1=r0+rows
+        q=pick_heads(q_ref[r0:r1,:]*half)
+        g=pick_heads(g_ref[r0:r1,:])
+        k=k_ref[0:r1,:]; v=v_ref[0:r1,:]
+        s=lax.dot_general(k,q,NT,preferred_element_type=jnp.float32)
+        d=dist_ref[0:r1,r0:r1]
+        logs=jnp.concatenate([log_ref[0,0:1,r0:r1],log_ref[0,1:2,r0:r1]],axis=1)
+        s=jnp.concatenate([s[:,:rows]+d*s0,s[:,rows:]+d*s1],axis=1)
+        p=jnp.exp(s-logs)
+        t=lax.dot_general(v,g,NT,preferred_element_type=jnp.float32)
+        centre=jnp.sum(p*t,axis=0,keepdims=True)
+        ds=(p*(t-centre)).astype(jnp.bfloat16)
+        pb=p.astype(jnp.bfloat16)
+        va=jnp.dot(pb,g,preferred_element_type=jnp.float32)
+        ka=jnp.dot(ds,q,preferred_element_type=jnp.float32)
+        if r1==length:
+            va_ref[...]=va; ka_ref[...]=ka
+        else:
+            va_ref[0:r1,:]+=va; ka_ref[0:r1,:]+=ka
+        dq=lax.dot_general(ds,k,TN,preferred_element_type=jnp.float32)
+        lane=lax.broadcasted_iota(jnp.int32,(rows,2*HD),1)
+        dq=(jnp.where(lane<HD,dq[:rows],dq[rows:])*scale).astype(jnp.bfloat16)
+        dq_ref[r0:r1,:]=dq
+        qsum=qsum+jnp.sum(dq.astype(jnp.float32),axis=0,keepdims=True)
+    qs_ref[0]=qsum
+    dk_ref[...]=ka_ref[...].astype(jnp.bfloat16)
+    dv=va_ref[...].astype(jnp.bfloat16)
+    dv_ref[...]=dv
+    vs_ref[0]=jnp.sum(dv.astype(jnp.float32),axis=0,keepdims=True)
+
+def attend_backward(q,k,v,g,start,logs,slopes,seqs,rows=256):
+    length=q.shape[0]//seqs; pairs=q.shape[1]//(2*HD)
+    spec=pl.BlockSpec((length,2*HD),lambda s,p,*_:(s,p))
+    out=jax.ShapeDtypeStruct(q.shape,jnp.bfloat16)
+    sums=jax.ShapeDtypeStruct((seqs,1,q.shape[1]),jnp.float32)
+    sspec=pl.BlockSpec((1,1,2*HD),lambda s,p,*_:(s,0,p))
+    return pl.pallas_call(partial(attend_back_kernel,rows=rows,scale=HD**-0.5),
+        grid_spec=pltpu.PrefetchScalarGridSpec(num_scalar_prefetch=1,grid=(seqs,pairs),
+            in_specs=[pl.BlockSpec((1,1,length),lambda s,p,*_:(s,0,0)),pl.BlockSpec((1,2,length),lambda s,p,*_:(s*pairs+p,0,0)),spec,spec,spec,spec],
+            out_specs=[spec,spec,spec,sspec,sspec],
+            scratch_shapes=[pltpu.VMEM((length,length),jnp.float32),pltpu.VMEM((length,2*HD),jnp.float32),pltpu.VMEM((length,2*HD),jnp.float32)]),
+        out_shape=[out,out,out,sums,sums],
+        compiler_params=pltpu.CompilerParams(vmem_limit_bytes=40<<20),
+        cost_estimate=pl.CostEstimate(flops=10*seqs*pairs*2*length*length*HD,bytes_accessed=14*q.size,transcendentals=seqs*pairs*length*length),
+        name="attend_backward")(slopes,start[:,None,:],logs,q,k,v,g)
 
 
 def on_device(
@@ -165,16 +180,12 @@
     cotangent,
 ):
     seq_count = segments.shape[0]
-    seq_length = segments.shape[1]
     col_parts = lax.axis_size("col")
     full_width = tokens.shape[1] * col_parts
     head_count = mixing.shape[2] // HD
-    score_scale = HD ** (-0.5)
-    block_rows = min(512, seq_length)
     head_ids = (lax.axis_index("col") * head_count + jnp.arange(head_count)).astype(jnp.float32)
     slopes = jnp.exp2(-8.0 * (head_ids + 1.0) / (head_count * col_parts))
-    slope_items = jnp.repeat(slopes, seq_count)
-    segment_items = jnp.tile(segments, (head_count, 1))
+    starts = jnp.sum(segments[:, None, :] < segments[:, :, None], axis=2).astype(jnp.int32)
     full_mix, full_proj, full_expand, full_contract = (
         lax.all_gather(mixing, "row", axis=0, tiled=True),
         lax.all_gather(projection, "row", axis=0, tiled=True),
@@ -188,14 +199,9 @@
     query_part = (mixed_rows[:, 0] + biases[0]).astype(jnp.bfloat16)
     key_part = mixed_rows[:, 1].astype(jnp.bfloat16)
     value_part = (mixed_rows[:, 2] + biases[1]).astype(jnp.bfloat16)
-    query_heads = to_heads(query_part, seq_count, head_count)
-    key_heads = to_heads(key_part, seq_count, head_count)
-    value_heads = to_heads(value_part, seq_count, head_count)
-    head_out, log_totals = lax.map(
-        partial(attend_forward, block_rows=block_rows, score_scale=score_scale),
-        (query_heads, key_heads, value_heads, segment_items, slope_items),
-    )
-    attended = from_heads(head_out, seq_count, head_count)
+    attended, log_totals = attend_forward(
+        query_part, key_part, value_part, starts, slopes, seq_count
+    )
     proj_term = lax.dot_general(
         attended, full_proj, contract_last, preferred_element_type=jnp.float32
     )
@@ -254,26 +260,10 @@
     attended_grad = jnp.dot(branch_full, back_proj, preferred_element_type=jnp.float32).astype(
         jnp.bfloat16
     )
-    query_back, key_back, value_back = lax.map(
-        partial(attend_backward, block_rows=block_rows, score_scale=score_scale),
-        (
-            query_heads,
-            key_heads,
-            value_heads,
-            segment_items,
-            slope_items,
-            log_totals,
-            to_heads(attended_grad, seq_count, head_count),
-        ),
-    )
-    mixed_grad = jnp.stack(
-        [
-            from_heads(query_back, seq_count, head_count),
-            from_heads(key_back, seq_count, head_count),
-            from_heads(value_back, seq_count, head_count),
-        ],
-        axis=1,
-    ).astype(jnp.bfloat16)
+    query_back, key_back, value_back, query_bias_part, value_bias_part = attend_backward(
+        query_part, key_part, value_part, attended_grad, starts, log_totals, slopes, seq_count
+    )
+    mixed_grad = jnp.stack([query_back, key_back, value_back], axis=1)
     columns = first_full
     mixing_grad = lax.psum_scatter(
         jnp.einsum("tc,tkf->ckf", columns, mixed_grad, preferred_element_type=jnp.float32),
@@ -281,9 +271,8 @@
         scatter_dimension=0,
         tiled=True,
     )
-    mixed_float = mixed_grad.astype(jnp.float32)
-    query_bias_part = jnp.sum(mixed_float[:, 0], axis=0)
-    value_bias_part = jnp.sum(mixed_float[:, 2], axis=0)
+    query_bias_part = jnp.sum(query_bias_part, axis=(0, 1))
+    value_bias_part = jnp.sum(value_bias_part, axis=(0, 1))
     first_back = sum_backward(
         jnp.einsum("tkf,dkf->td", mixed_grad, back_mix, preferred_element_type=jnp.float32)
     )

time: 1920 us -> 1790 us (0.932)
  waiting for transfers between devices: 1220 us -> 1490 us
  matrix products: 310 us -> 140 us
  local copies, waits for them, and re-layouts: 167 us -> 14 us
  loops' own time: 66.5 us -> 0 us
  other arithmetic: 61.9 us -> 26.2 us
  Pallas kernels: 0 us -> 35 us
    reduce_scatter x1, waiting for transfers between devices: 0.02 us -> 214 us  [on_device(): lax.psum_scatter(lax.dot_general(columns, active, contract_first, preferr...]
    dot_general x112 -> x0, matrix products: 168 us -> none  [the longest x32 58.8 us: block_scores(): lax.dot_general(row_block, key_matrix, contract_last, preferred_element_t...]
    another operation x18 -> x0, loops' own time: 66.5 us -> none  [the longest x8 34.9 us: attend_backward(): lax.scan(one_block, (zero_block, zero_block), jnp.arange(0, seq_length, b...]
    squeeze x50 -> x0, local copies, waits for them, and re-layouts: 65.6 us -> none  [the longest x48 59 us: on_device(): lax.map(partial(attend_forward, block_rows=block_rows, score_scale=score_...]
    dynamic_slice x120 -> x0, local copies, waits for them, and re-layouts: 41.6 us -> none  [the longest x32 21.8 us: attend_forward(): lax.map(one_block, jnp.arange(0, seq_length, block_rows))]
    reduce_scatter x2, waiting for transfers between devices: 86.7 us -> 126 us  [sum_backward(): lax.psum_scatter(partial_term, 'col', scatter_dimension=1, tiled=True)]
    dynamic_update_slice x64 -> x0, local copies, waits for them, and re-layouts: 38.1 us -> none  [the longest x24 19.9 us: on_device(): lax.map(partial(attend_backward, block_rows=block_rows, score_scale=score...]
    pallas_call x0 -> x2, Pallas kernels: none -> 35 us  [the longest x1 19.4 us: attend_backward(): pl.pallas_call(partial(attend_back_kernel, rows=rows, scale=HD ** (-0.5))...]
  transfers between devices with their start and end apart: 16 -> 16, of which waited for: 14 -> 16; matrix products, arithmetic and copies ran while one was open for 26% -> 7% of each run, Pallas kernels for 0% -> 2%
where the time goes in v1:
time: 1790 us; the launch traced here: 1780 us
  waiting for transfers between devices  1490 us (83%)
  matrix products  140 us (8%)
  blocking collectives  65.9 us (4%)
  Pallas kernels  35 us (2%)
  other arithmetic  26.2 us (1%)
    reduce_scatter x1, waiting for transfers between devices, on_device(): lax.psum_scatter(lax.dot_general(columns, hidden_grad, contract_first, pr...  287 us
    reduce_scatter x1, waiting for transfers between devices, on_device(): lax.psum_scatter(lax.dot_general(columns, active, contract_first, preferr...  214 us
    reduce_scatter x1, waiting for transfers between devices, on_device(): lax.psum_scatter(jnp.einsum('tc,tkf->ckf', columns, mixed_grad, preferred...  211 us
    reduce_scatter x2, waiting for transfers between devices, sum_forward(): lax.psum_scatter(partial_term, 'col', scatter_dimension=1, tiled=True)  135 us
    all_gather x1, waiting for transfers between devices, on_device(): lax.all_gather(contract, 'row', axis=0, tiled=True)  127 us
    reduce_scatter x2, waiting for transfers between devices, sum_backward(): lax.psum_scatter(partial_term, 'col', scatter_dimension=1, tiled=True)  126 us
    all_gather x1, waiting for transfers between devices, on_device(): lax.all_gather(expand, 'row', axis=0, tiled=True)  113 us
    all_gather x1, waiting for transfers between devices, on_device(): lax.all_gather(mixing, 'row', axis=0, tiled=True)  101 us
  transfers between devices with their start and end apart: 16, of which 16 were waited for; matrix products, arithmetic and copies ran while one was open for 7% of the time, Pallas kernels for 2%

profile of v1, /device:TPU:0, one launch (start us, length us, event | category | flops | bytes accessed | tf_op | source)
XLA Modules:
  0.0 1782.7 jit_solution(3541737117785044592)
XLA Ops:
  7.2 0.8 fusion.32
  8.0 0.8 fusion.33
  8.8 1.6 convert_reduce_fusion.2
  10.4 8.5 all-reduce.4
  18.9 0.6 copy-done.11
  19.5 2.6 fusion.16
  22.2 0.7 all-gather.11.cloned.1.call-update
  23.0 0.7 all-gather.13.cloned.1.call-update
  23.7 0.6 convert_reduce_fusion.1
  24.3 1.0 copy.26.start_ref
  25.3 31.8 %all-gather.9.cloned.1.call-done = bf16[1024,2048]{1,0:T(8,128)(2,1)} async-done(((bf16[1024,512]{1,0:T(8,128)(2,1)}), bf16[1024,2048]{1,0:T(8,128)(2,1)}) %all-gather.9.cloned.1.call-update) | async-done | bytes 4194320 | tf_op jit(solution)/shard_map/all_gather | solution.py:40
  57.1 101.3 %all-gather.11.cloned.1.call-done = bf16[2048,3,512]{2,0,1:T(8,128)(2,1)} async-done(((bf16[256,3,512]{2,0,1:T(8,128)(2,1)}), bf16[2048,3,512]{2,0,1:T(8,128)(2,1)}) %all-gather.11.cloned.1.call-update) | async-done | bytes 6291472 | tf_op jit(solution)/shard_map/all_gather | solution.py:190
  158.4 10.2 fusion.8
  168.7 0.6 fusion.24
  169.3 0.3 copy-done
  169.6 15.6 attend_forward.1
  185.2 1.0 copy-done.7
  186.2 21.8 %all-gather.13.cloned.1.call-done = bf16[2048,512]{1,0:T(8,128)(2,1)} async-done(((bf16[256,512]{1,0:T(8,128)(2,1)}), bf16[2048,512]{1,0:T(8,128)(2,1)}) %all-gather.13.cloned.1.call-update) | async-done | bytes 2097168 | tf_op jit(solution)/shard_map/all_gather | solution.py:191
  208.0 7.5 fusion.34
  215.6 0.5 all-gather.17.cloned.1.call-update
  216.2 69.7 %reduce-scatter.9.cloned.1.call-done = f32[1024,512]{1,0:T(8,128)} async-done(((f32[1024,2048]{1,0:T(8,128)}), f32[1024,512]{1,0:T(8,128)}) %reduce-scatter.9.cloned.1.call-update) | async-done | bytes 2097168 | tf_op jit(solution)/shard_map/reduce_scatter | solution.py:48
  285.9 3.4 fusion.30
  289.4 6.0 all-reduce.3
  295.4 3.2 add_convert_fusion.1
  298.7 0.7 all-gather.21.cloned.1.call-update
  299.4 0.7 all-gather.19.cloned.1.call-update
  300.2 112.9 %all-gather.17.cloned.1.call-done = bf16[2048,2048]{1,0:T(8,128)(2,1)} async-done(((bf16[256,2048]{1,0:T(8,128)(2,1)}), bf16[2048,2048]{1,0:T(8,128)(2,1)}) %all-gather.17.cloned.1.call-update) | async-done | bytes 8388624 | tf_op jit(solution)/shard_map/all_gather | solution.py:192
  413.1 34.8 %all-gather.15.cloned.1.call-done = bf16[1024,2048]{1,0:T(8,128)(2,1)} async-done(((bf16[1024,512]{1,0:T(8,128)(2,1)}), bf16[1024,2048]{1,0:T(8,128)(2,1)}) %all-gather.15.cloned.1.call-update) | async-done | bytes 4194320 | tf_op jit(solution)/shard_map/all_gather | solution.py:40
  447.8 16.1 multiply_convert_fusion
  463.9 20.1 %all-gather.21.cloned.1.call-done = bf16[1024,2048]{1,0:T(8,128)(2,1)} async-done(((bf16[1024,512]{1,0:T(8,128)(2,1)}), bf16[1024,2048]{1,0:T(8,128)(2,1)}) %all-gather.21.cloned.1.call-update) | async-done | bytes 4194320 | tf_op jit(solution)/shard_map/all_gather | solution.py:44
  484.0 127.3 %all-gather.19.cloned.1.call-done = bf16[2048,2048]{1,0:T(8,128)(2,1)} async-done(((bf16[256,2048]{1,0:T(8,128)(2,1)}), bf16[2048,2048]{1,0:T(8,128)(2,1)}) %all-gather.19.cloned.1.call-update) | async-done | bytes 8388624 | tf_op jit(solution)/shard_map/all_gather | solution.py:193
  611.3 16.3 convert_reduce_fusion
  627.6 1.9 copy-done.21
  629.6 11.1 fusion.36
  640.8 14.8 fusion.35
  655.7 55.1 %reduce-scatter.13.cloned.1.call-done = f32[1024,512]{1,0:T(8,128)} async-done(((f32[1024,2048]{1,0:T(8,128)}), f32[1024,512]{1,0:T(8,128)}) %reduce-scatter.13.cloned.1.call-update) | async-done | bytes 2097168 | tf_op jit(solution)/shard_map/reduce_scatter | solution.py:52
  710.8 3.2 multiply_reduce_fusion
  714.0 5.9 all-reduce.2
  719.9 65.1 %reduce-scatter.11.cloned.1.call-done = f32[1024,512]{1,0:T(8,128)} async-done(((f32[1024,2048]{1,0:T(8,128)}), f32[1024,512]{1,0:T(8,128)}) %reduce-scatter.11.cloned.1.call-update) | async-done | bytes 2097168 | tf_op jit(solution)/shard_map/reduce_scatter | solution.py:48
  785.0 5.0 convert_reduce_fusion.4
  790.1 15.3 convolution_bitcast_fusion
  805.4 19.2 %all-gather.23.cloned.1.call-done = bf16[1024,2048]{1,0:T(8,128)(2,1)} async-done(((bf16[1024,512]{1,0:T(8,128)(2,1)}), bf16[1024,2048]{1,0:T(8,128)(2,1)}) %all-gather.23.cloned.1.call-update) | async-done | bytes 4194320 | tf_op jit(solution)/shard_map/all_gather | solution.py:44
  824.7 5.3 convolution_convert_fusion.g_ref
  830.0 19.4 %attend_backward.1 = (bf16[1024,512]{1,0:T(8,128)(2,1)S(1)}, bf16[1024,512]{1,0:T(8,128)(2,1)S(1)}, bf16[1024,512]{1,0:T(8,128)(2,1)S(1)}, f32[1,1,512]{2,1,0:T(1,128)S(1)}, f32[1,1,512]{2,1,0:T(1,128)S(1)}) custom-call(f32[8]{0:T(128)S(1)} %multiply_exponential_fusion.slope_ref, s32[1,1,1024]{2,1,0:T(1,128)S(1)} %bitcast.67, ...), custom_call_target="tpu_custom_call" | custom-call | flops 5368709120 | bytes 7340032 | tf_op jit(solution)/shard_map/attend_backward/pallas_call | solution.py:158
  849.4 1.0 copy-done.1
  850.7 0.3 copy-done.5
  851.1 9.0 convolution_bitcast_fusion.1
  860.1 1.2 copy-done.8
  861.3 6.5 fusion.37
  867.9 15.8 fusion.38
  883.7 1.1 copy-done.2
  884.9 0.3 copy-done.4
  885.2 0.3 copy-done.6
  885.5 11.7 fusion.6
  897.3 214.2 %reduce-scatter.23.cloned.1.call-done = f32[256,2048]{0,1:T(8,128)} async-done(((f32[2048,2048]{0,1:T(8,128)}), f32[256,2048]{0,1:T(8,128)}) %reduce-scatter.23.cloned.1.call-update) | async-done | bytes 2097168 | tf_op jit(solution)/shard_map/reduce_scatter | solution.py:226
  1111.5 2.9 copy.28
  1114.4 70.5 %reduce-scatter.15.cloned.1.call-done = f32[1024,512]{1,0:T(8,128)} async-done(((f32[1024,2048]{1,0:T(8,128)}), f32[1024,512]{1,0:T(8,128)}) %reduce-scatter.15.cloned.1.call-update) | async-done | bytes 2097168 | tf_op jit(solution)/shard_map/reduce_scatter | solution.py:52
  1184.9 2.7 fusion.21
  1187.7 39.5 %all-reduce = (f32[2,512]{1,0:T(2,128)}, f32[2,512]{1,0:T(2,128)}, f32[4,512]{1,0:T(4,128)}, f32[2048]{0:T(1024)}) all-reduce(f32[2,512]{1,0:T(2,128)S(1)} %pad_maximum_fusion.4, f32[2,512]{1,0:T(2,128)S(1)} %pad_maximum_fusion.5, f32[4,512]{1,0:T(4,128)S(1)} %pad_maximum_fusion.3, ...), channel_id=1, replica_groups=mesh['row'=8,'col'=4] {'row'}, use_global_device_ids=true, to_apply=%region_23.0 | all-reduce | flops 6144 | bytes 49152 | tf_op jit(solution)/shard_map/psum | solution.py:283
  1227.1 6.1 all-reduce.1
  1233.3 3.1 fusion.20
  1236.4 41.5 %reduce-scatter.19.cloned.1.call-done = f32[256,512]{1,0:T(8,128)} async-done(((f32[2048,512]{1,0:T(8,128)}), f32[256,512]{1,0:T(8,128)}) %reduce-scatter.19.cloned.1.call-update) | async-done | bytes 524304 | tf_op jit(solution)/shard_map/reduce_scatter | solution.py:254
  1278.0 286.6 %reduce-scatter.21.cloned.1.call-done = f32[256,2048]{1,0:T(8,128)} async-done(((f32[2048,2048]{1,0:T(8,128)}), f32[256,2048]{1,0:T(8,128)}) %reduce-scatter.21.cloned.1.call-update) | async-done | bytes 2097168 | tf_op jit(solution)/shard_map/reduce_scatter | solution.py:236
  1564.5 211.2 %reduce-scatter.17.cloned.1.call-done = f32[256,3,512]{2,0,1:T(8,128)} async-done(((f32[2048,3,512]{2,0,1:T(8,128)}), f32[256,3,512]{2,0,1:T(8,128)}) %reduce-scatter.17.cloned.1.call-update) | async-done | bytes 1572880 | tf_op jit(solution)/shard_map/reduce_scatter | solution.py:268
  (77 shorter events, 1.4 us)
Async XLA Ops:
  7.2 16.5 copy-start.17
  7.2 18.1 %copy-start.18 = (f32[4,512]{1,0:T(4,128)S(1)}, f32[4,512]{1,0:T(4,128)}, u32[]{:S(2)}) copy-start(f32[4,512]{1,0:T(4,128)} %param.15) | copy-start | bytes 24580
  7.2 49.9 %all-gather.9.cloned.1.call-start = ((), (), s32[]{:S(2)}) async-start(), calls=%async_computation.8 | async-start | bytes 5242880 | tf_op jit(solution)/shard_map/all_gather | solution.py:40
  8.0 15.7 copy-start.15
  18.9 0.6 copy-start.11
  18.9 0.6 copy-start.13
  22.2 136.2 %all-gather.11.cloned.1.call-start = ((), (), s32[]{:S(2)}) async-start(), calls=%async_computation.9 | async-start | bytes 7077888 | tf_op jit(solution)/shard_map/all_gather | solution.py:190
  22.9 185.1 %all-gather.13.cloned.1.call-start = ((), (), s32[]{:S(2)}) async-start(), calls=%async_computation.10 | async-start | bytes 2359296 | tf_op jit(solution)/shard_map/all_gather | solution.py:191
  23.6 262.3 %reduce-scatter.9.cloned.1.call-start = ((), (), s32[]{:S(2)}) async-start(), calls=%async_computation.11 | async-start | bytes 10485760 | tf_op jit(solution)/shard_map/reduce_scatter | solution.py:48
  168.6 1.0 copy-start
  185.2 1.0 copy-start.7
  215.6 197.5 %all-gather.17.cloned.1.call-start = ((), (), s32[]{:S(2)}) async-start(), calls=%async_computation.13 | async-start | bytes 9437184 | tf_op jit(solution)/shard_map/all_gather | solution.py:192
  216.1 231.7 %all-gather.15.cloned.1.call-start = ((), (), s32[]{:S(2)}) async-start(), calls=%async_computation.12 | async-start | bytes 5242880 | tf_op jit(solution)/shard_map/all_gather | solution.py:40
  289.4 158.5 %copy-start.20 = (f32[2048]{0:T(1024)S(1)}, f32[2048]{0:T(1024)}, u32[]{:S(2)}) copy-start(f32[2048]{0:T(1024)} %param.19) | copy-start | bytes 24580
  298.6 185.4 %all-gather.21.cloned.1.call-start = ((), (), s32[]{:S(2)}) async-start(), calls=%async_computation.16 | async-start | bytes 5242880 | tf_op jit(solution)/shard_map/all_gather | solution.py:44
  299.4 311.9 %all-gather.19.cloned.1.call-start = ((), (), s32[]{:S(2)}) async-start(), calls=%async_computation.14 | async-start | bytes 9437184 | tf_op jit(solution)/shard_map/all_gather | solution.py:193
  300.1 410.6 %reduce-scatter.13.cloned.1.call-start = ((), (), s32[]{:S(2)}) async-start(), calls=%async_computation.17 | async-start | bytes 10485760 | tf_op jit(solution)/shard_map/reduce_scatter | solution.py:52
  611.3 18.3 %copy-start.19 = (bf16[2048,2048]{1,0:T(8,128)(2,1)S(1)}, bf16[2048,2048]{1,0:T(8,128)(2,1)}, u32[]{:S(2)}) copy-start(bf16[2048,2048]{1,0:T(8,128)(2,1)} %all-gather.17.cloned.1.call-done) | copy-start | bytes 25165828
  627.6 2.0 copy-start.21
  640.7 144.2 %reduce-scatter.11.cloned.1.call-start = ((), (), s32[]{:S(2)}) async-start(), calls=%async_computation.15 | async-start | bytes 10485760 | tf_op jit(solution)/shard_map/reduce_scatter | solution.py:48
  655.6 169.0 %all-gather.23.cloned.1.call-start = ((), (), s32[]{:S(2)}) async-start(), calls=%async_computation.18 | async-start | bytes 5242880 | tf_op jit(solution)/shard_map/all_gather | solution.py:44
  790.0 321.5 %reduce-scatter.23.cloned.1.call-start = ((), (), s32[]{:S(2)}) async-start(), calls=%async_computation.23 | async-start | bytes 18874368 | tf_op jit(solution)/shard_map/reduce_scatter | solution.py:226
  805.4 379.5 %reduce-scatter.15.cloned.1.call-start = ((), (), s32[]{:S(2)}) async-start(), calls=%async_computation.19 | async-start | bytes 10485760 | tf_op jit(solution)/shard_map/reduce_scatter | solution.py:52
  824.7 26.4 %slice-start = ((s8[6291456]{0:T(1024)(128)(4,1)}), s8[4194304]{0:T(1024)(128)(4,1)S(1)}, s32[]{:S(2)}) async-start(s8[6291456]{0:T(1024)(128)(4,1)} %bitcast.95), calls=%async_computation.24 | async-start | bytes 8388608
  830.0 21.1 %slice-start.1 = ((s8[6291456]{0:T(1024)(128)(4,1)}), s8[2097152]{0:T(1024)(128)(4,1)S(1)}, s32[]{:S(2)}) async-start(s8[6291456]{0:T(1024)(128)(4,1)} %bitcast.95), calls=%async_computation.25 | async-start | bytes 4194304
  849.4 1.0 copy-start.1
  849.4 1.3 copy-start.3
  849.4 1.6 copy-start.5
  860.1 1.2 copy-start.8
  860.1 417.9 %reduce-scatter.19.cloned.1.call-start = ((), (), s32[]{:S(2)}) async-start(), calls=%async_computation.21 | async-start | bytes 4718592 | tf_op jit(solution)/shard_map/reduce_scatter | solution.py:254
  867.9 696.7 %reduce-scatter.21.cloned.1.call-start = ((), (), s32[]{:S(2)}) async-start(), calls=%async_computation.22 | async-start | bytes 18874368 | tf_op jit(solution)/shard_map/reduce_scatter | solution.py:236
  883.7 1.2 copy-start.2
  883.7 1.5 copy-start.4
  883.7 1.9 copy-start.6
  883.7 892.1 %reduce-scatter.17.cloned.1.call-start = ((), (), s32[]{:S(2)}) async-start(), calls=%async_computation.20 | async-start | bytes 14155776 | tf_op jit(solution)/shard_map/reduce_scatter | solution.py:268
  897.2 287.7 %copy-start.9 = (bf16[1024,512]{1,0:T(8,128)(2,1)S(1)}, bf16[1024,512]{1,0:T(8,128)(2,1)}, u32[]{:S(2)}) copy-start(bf16[1024,512]{1,0:T(8,128)(2,1)} %param.11) | copy-start | bytes 3145732
  897.2 287.7 %copy-start.12 = (f32[1024]{0:T(1024)S(1)}, f32[1024]{0:T(1024)}, u32[]{:S(2)}) copy-start(f32[1024]{0:T(1024)} %copy-done.11) | copy-start | bytes 12292
  897.2 287.7 %copy-start.14 = (f32[1024]{0:T(1024)S(1)}, f32[1024]{0:T(1024)}, u32[]{:S(2)}) copy-start(f32[1024]{0:T(1024)} %copy-done.13) | copy-start | bytes 12292
  897.2 287.7 %copy-start.16 = (f32[1,512]{1,0:T(1,128)S(1)}, f32[1,512]{1,0:T(1,128)}, u32[]{:S(2)}) copy-start(f32[1,512]{1,0:T(1,128)} %copy-done.15) | copy-start | bytes 6148
  897.2 336.0 %copy-start.10 = (f32[1024,512]{1,0:T(8,128)S(1)}, f32[1024,512]{1,0:T(8,128)}, u32[]{:S(2)}) copy-start(f32[1024,512]{1,0:T(8,128)} %get-tuple-element.80) | copy-start | bytes 6291460
Sparse Core Ops, SparseCore 0:
  22.3 34.7 all-gather.8
  59.3 99.0 all-gather.10
  160.5 47.4 all-gather.12
  215.7 70.1 reduce-scatter.8
  288.1 124.9 all-gather.16
  415.2 32.6 all-gather.14
  449.5 34.4 all-gather.20
  486.3 124.9 all-gather.18
  640.8 69.8 reduce-scatter.12
  713.2 71.7 reduce-scatter.10
  790.1 34.4 all-gather.22
  828.8 282.6 reduce-scatter.22
  1114.1 70.7 reduce-scatter.14
  1189.4 88.5 reduce-scatter.18
  1282.2 282.3 reduce-scatter.20
  1569.0 206.6 reduce-scatter.16

commit v2 on v1

v2 whole, which is shorter than its diff:
```python
import math
from functools import partial

import jax
import jax.numpy as jnp
from jax import lax
from jax.experimental import pallas as pl
from jax.experimental.pallas import tpu as pltpu
from jax.sharding import PartitionSpec as P

HD = 64
BLOCK = 256

norm_eps = 1e-05
sqrt_half = 0.7071067811865476
inverse_root = 0.3989422804014327
far = -1e33
NT = (((1,), (1,)), ((), ()))
TN = (((0,), (0,)), ((), ()))
VMEM_LIMIT = 48 << 20
f32 = jnp.float32
bf16 = jnp.bfloat16


def pick_heads(pair):
    lane = lax.broadcasted_iota(jnp.int32, pair.shape, 1)
    zero = jnp.zeros_like(pair)
    return jnp.concatenate(
        [jnp.where(lane < HD, pair, zero), jnp.where(lane < HD, zero, pair)], axis=0
    )


def attend_kernel(
    slope_ref, start_ref, q_ref, k_ref, v_ref, out_ref, log_ref, dist_ref, *, rows, scale
):
    pair = pl.program_id(1)
    length = k_ref.shape[0]

    @pl.when(pair == 0)
    def _():
        for r0 in range(0, length, rows):
            shape = (rows, r0 + rows)
            i = lax.broadcasted_iota(jnp.int32, shape, 0) + r0
            j = lax.broadcasted_iota(jnp.int32, shape, 1)
            allowed = (j <= i) & (j >= start_ref[0, r0 : r0 + rows, :])
            dist_ref[r0 : r0 + rows, 0 : r0 + rows] = jnp.where(allowed, (j - i).astype(f32), far)

    slope_a, slope_b = slope_ref[2 * pair] * scale, slope_ref[2 * pair + 1] * scale
    for r0 in range(0, length, rows):
        r1 = r0 + rows
        q = pick_heads(q_ref[r0:r1, :] * jnp.asarray(scale, bf16))
        s = lax.dot_general(q, k_ref[0:r1, :], NT, preferred_element_type=f32)
        d = dist_ref[r0:r1, 0:r1]
        s = jnp.concatenate([s[:rows] + d * slope_a, s[rows:] + d * slope_b], axis=0)
        row_max = jnp.max(s, axis=1, keepdims=True)
        weights = jnp.exp(s - row_max)
        row_total = jnp.sum(weights, axis=1, keepdims=True)
        probs = (weights * (1.0 / row_total)).astype(bf16)
        o = jnp.dot(probs, v_ref[0:r1, :], preferred_element_type=f32)
        lane = lax.broadcasted_iota(jnp.int32, (rows, 2 * HD), 1)
        out_ref[r0:r1, :] = jnp.where(lane < HD, o[:rows], o[rows:]).astype(bf16)
        logs = row_max + jnp.log(row_total)
        logs = jnp.where(
            lane < HD,
            jnp.broadcast_to(logs[:rows], (rows, 2 * HD)),
            jnp.broadcast_to(logs[rows:], (rows, 2 * HD)),
        ).T
        log_ref[0, 0:1, r0:r1] = logs[0:1]
        log_ref[0, 1:2, r0:r1] = logs[HD : HD + 1]


def attend_forward(mixed, starts, slopes, seqs, rows=256):
    length, pairs = mixed.shape[0] // seqs, mixed.shape[1] // (6 * HD)

    def part(i):
        return pl.BlockSpec((length, 2 * HD), lambda s, p, *_: (s, i * pairs + p))

    return pl.pallas_call(
        partial(attend_kernel, rows=rows, scale=HD**-0.5),
        grid_spec=pltpu.PrefetchScalarGridSpec(
            num_scalar_prefetch=1,
            grid=(seqs, pairs),
            in_specs=[
                pl.BlockSpec((1, length, 1), lambda s, p, *_: (s, 0, 0)),
                part(0),
                part(1),
                part(2),
            ],
            out_specs=[part(0), pl.BlockSpec((1, 2, length), lambda s, p, *_: (s * pairs + p, 0, 0))],
            scratch_shapes=[pltpu.VMEM((length, length), f32)],
        ),
        out_shape=[
            jax.ShapeDtypeStruct((mixed.shape[0], 2 * HD * pairs), bf16),
            jax.ShapeDtypeStruct((seqs * pairs, 2, length), f32),
        ],
        compiler_params=pltpu.CompilerParams(vmem_limit_bytes=40 << 20),
        cost_estimate=pl.CostEstimate(
            flops=8 * seqs * pairs * length * length * HD * 3,
            bytes_accessed=4 * mixed.size,
            transcendentals=seqs * pairs * length * length,
        ),
        name="attend_forward",
    )(slopes, starts[:, :, None], mixed, mixed, mixed)


def attend_back_kernel(
    slope_ref,
    start_ref,
    log_ref,
    q_ref,
    k_ref,
    v_ref,
    g_ref,
    dq_ref,
    dk_ref,
    dv_ref,
    qs_ref,
    vs_ref,
    dist_ref,
    ka_ref,
    va_ref,
    *,
    rows,
    scale,
):
    pair = pl.program_id(1)
    length = k_ref.shape[0]

    @pl.when(pair == 0)
    def _():
        for r0 in range(0, length, rows):
            shape = (r0 + rows, rows)
            i = lax.broadcasted_iota(jnp.int32, shape, 1) + r0
            j = lax.broadcasted_iota(jnp.int32, shape, 0)
            allowed = (j <= i) & (j >= start_ref[0, :, r0 : r0 + rows])
            dist_ref[0 : r0 + rows, r0 : r0 + rows] = jnp.where(allowed, (j - i).astype(f32), far)

    slope_a, slope_b = slope_ref[2 * pair] * scale, slope_ref[2 * pair + 1] * scale
    query_sum = jnp.zeros((1, 2 * HD), f32)
    for r0 in reversed(range(0, length, rows)):
        r1 = r0 + rows
        q = pick_heads(q_ref[r0:r1, :] * jnp.asarray(scale, bf16))
        g = pick_heads(g_ref[r0:r1, :])
        k, v = k_ref[0:r1, :], v_ref[0:r1, :]
        s = lax.dot_general(k, q, NT, preferred_element_type=f32)
        d = dist_ref[0:r1, r0:r1]
        logs = jnp.concatenate([log_ref[0, 0:1, r0:r1], log_ref[0, 1:2, r0:r1]], axis=1)
        s = jnp.concatenate([s[:, :rows] + d * slope_a, s[:, rows:] + d * slope_b], axis=1)
        probs = jnp.exp(s - logs)
        t = lax.dot_general(v, g, NT, preferred_element_type=f32)
        centre = jnp.sum(probs * t, axis=0, keepdims=True)
        score_grad = (probs * (t - centre)).astype(bf16)
        value_part = jnp.dot(probs.astype(bf16), g, preferred_element_type=f32)
        key_part = jnp.dot(score_grad, q, preferred_element_type=f32)
        if r1 == length:
            va_ref[...] = value_part
            ka_ref[...] = key_part
        else:
            va_ref[0:r1, :] += value_part
            ka_ref[0:r1, :] += key_part
        dq = lax.dot_general(score_grad, k, TN, preferred_element_type=f32)
        lane = lax.broadcasted_iota(jnp.int32, (rows, 2 * HD), 1)
        dq = (jnp.where(lane < HD, dq[:rows], dq[rows:]) * scale).astype(bf16)
        dq_ref[r0:r1, :] = dq
        query_sum = query_sum + jnp.sum(dq.astype(f32), axis=0, keepdims=True)
    qs_ref[0] = query_sum
    dk_ref[...] = ka_ref[...].astype(bf16)
    dv = va_ref[...].astype(bf16)
    dv_ref[...] = dv
    vs_ref[0] = jnp.sum(dv.astype(f32), axis=0, keepdims=True)


def attend_backward(mixed, grads, starts, logs, slopes, seqs, rows=256):
    length, pairs = mixed.shape[0] // seqs, mixed.shape[1] // (6 * HD)

    def part(i):
        return pl.BlockSpec((length, 2 * HD), lambda s, p, *_: (s, i * pairs + p))

    out = jax.ShapeDtypeStruct(grads.shape, bf16)
    sums = jax.ShapeDtypeStruct((seqs, 1, grads.shape[1]), f32)
    sum_spec = pl.BlockSpec((1, 1, 2 * HD), lambda s, p, *_: (s, 0, p))
    return pl.pallas_call(
        partial(attend_back_kernel, rows=rows, scale=HD**-0.5),
        grid_spec=pltpu.PrefetchScalarGridSpec(
            num_scalar_prefetch=1,
            grid=(seqs, pairs),
            in_specs=[
                pl.BlockSpec((1, 1, length), lambda s, p, *_: (s, 0, 0)),
                pl.BlockSpec((1, 2, length), lambda s, p, *_: (s * pairs + p, 0, 0)),
                part(0),
                part(1),
                part(2),
                part(0),
            ],
            out_specs=[part(0), part(0), part(0), sum_spec, sum_spec],
            scratch_shapes=[
                pltpu.VMEM((length, length), f32),
                pltpu.VMEM((length, 2 * HD), f32),
                pltpu.VMEM((length, 2 * HD), f32),
            ],
        ),
        out_shape=[out, out, out, sums, sums],
        compiler_params=pltpu.CompilerParams(vmem_limit_bytes=40 << 20),
        cost_estimate=pl.CostEstimate(
            flops=20 * seqs * pairs * length * length * HD * 2,
            bytes_accessed=14 * grads.size,
            transcendentals=seqs * pairs * length * length,
        ),
        name="attend_backward",
    )(slopes, starts[:, None, :], logs, mixed, mixed, mixed, grads)


def resident(shape):
    return pl.BlockSpec(shape, lambda *_: (0,) * len(shape))


def flat_rows(ws):
    return jnp.concatenate([w[...] for w in ws], axis=0)


def matmul_call(kernel, grid, ins, outs, scratch, flops, name, prefetch=()):
    moved = sum(a.size * a.dtype.itemsize for a, _ in ins)
    moved += sum(jnp.dtype(t).itemsize * math.prod(s) for s, t, _ in outs)
    return pl.pallas_call(
        kernel,
        grid_spec=pltpu.PrefetchScalarGridSpec(
            num_scalar_prefetch=len(prefetch),
            grid=grid,
            in_specs=[s for _, s in ins],
            out_specs=[s for _, _, s in outs],
            scratch_shapes=scratch,
        ),
        out_shape=[jax.ShapeDtypeStruct(s, t) for s, t, _ in outs],
        compiler_params=pltpu.CompilerParams(vmem_limit_bytes=VMEM_LIMIT),
        cost_estimate=pl.CostEstimate(flops=flops, bytes_accessed=moved, transcendentals=0),
        name=name,
    )(*prefetch, *[a for a, _ in ins])


def times_rows(x, ws, extras, outs, finish, name, tn, tm=256):
    tokens, depth = x.shape
    width = ws[0].shape[1]
    tn, tm = min(tn, width), min(tm, tokens)
    n_ws, n_ex = len(ws), len(extras)

    def kernel(*refs):
        x_ref, w_refs = refs[0], refs[1 : 1 + n_ws]
        extra, out = refs[1 + n_ws : 1 + n_ws + n_ex], refs[1 + n_ws + n_ex :]
        rows = pl.ds(pl.multiple_of(pl.program_id(1) * tm, tm), tm)
        acc = jnp.dot(x_ref[rows, :], flat_rows(w_refs), preferred_element_type=f32)
        finish(acc, extra, out)

    def spec(shape):
        if shape[0] == 1:
            return pl.BlockSpec((1, tn), lambda n, m: (0, n))
        return pl.BlockSpec((tm, tn), lambda n, m: (m, n))

    ins = [(x, resident(x.shape))]
    ins += [(w, pl.BlockSpec((w.shape[0], tn), lambda n, m: (0, n))) for w in ws]
    ins += [(e, spec(e.shape)) for e in extras]
    return matmul_call(
        kernel,
        (width // tn, tokens // tm),
        ins,
        [(s, t, spec(s)) for s, t in outs],
        [],
        2 * tokens * depth * width,
        name,
    )


def times_columns(xs, ws, slots, name, tm=256):
    tokens = xs[0].shape[0]
    tm = min(tm, tokens)
    blocks = sum(w.shape[0] for w in ws) // BLOCK
    half = blocks // 2
    n_xs = len(xs)

    def kernel(slot_ref, *refs):
        x_refs, w_refs = refs[:n_xs], refs[n_xs : n_xs + len(ws)]
        sent_ref, kept_ref = refs[n_xs + len(ws) :]
        x = jnp.concatenate([r[...] for r in x_refs], axis=1)
        at = 0
        for w_ref in w_refs:
            for r0 in range(0, w_ref.shape[0], BLOCK):
                acc = lax.dot_general(x, w_ref[r0 : r0 + BLOCK, :], NT, preferred_element_type=f32)
                slot = slot_ref[at]

                @pl.when(slot < half)
                def _():
                    place = pl.ds(pl.multiple_of(slot * BLOCK, BLOCK), BLOCK)
                    sent_ref[:, place] = acc.astype(bf16)

                @pl.when(slot >= half)
                def _():
                    place = pl.ds(pl.multiple_of((slot - half) * BLOCK, BLOCK), BLOCK)
                    kept_ref[:, place] = acc

                at += 1

    ins = [(x, pl.BlockSpec((tm, x.shape[1]), lambda m, *_: (m, 0))) for x in xs]
    ins += [(w, resident(w.shape)) for w in ws]
    out_spec = pl.BlockSpec((tm, half * BLOCK), lambda m, *_: (m, 0))
    return matmul_call(
        kernel,
        (tokens // tm,),
        ins,
        [((tokens, half * BLOCK), bf16, out_spec), ((tokens, half * BLOCK), f32, out_spec)],
        [],
        2 * tokens * blocks * BLOCK * ws[0].shape[1],
        name,
        prefetch=(slots,),
    )


def weight_parts(a, first, count, gs, dtype, name):
    tokens = a.shape[0]
    width = sum(g.shape[1] for g in gs)
    n_gs = len(gs)

    def kernel(a_ref, *refs):
        g_refs, out_refs = refs[:n_gs], refs[n_gs:]
        g = jnp.concatenate([r[...] for r in g_refs], axis=1)
        acc = lax.dot_general(a_ref[...], g, TN, preferred_element_type=f32).astype(dtype)
        for i in range(count):

            @pl.when(pl.program_id(0) == i)
            def _(i=i):
                out_refs[i][...] = acc

    ins = [(a, pl.BlockSpec((tokens, BLOCK), lambda i: (0, first + i)))]
    ins += [(g, resident(g.shape)) for g in gs]
    return matmul_call(
        kernel,
        (count,),
        ins,
        [((BLOCK, width), dtype, resident((BLOCK, width))) for _ in range(count)],
        [],
        2 * tokens * BLOCK * count * width,
        name,
    )


def place_blocks(values, place_ref, out_ref):
    at = 0
    for value in values:
        for c0 in range(0, value.shape[1], BLOCK):
            place = pl.ds(pl.multiple_of(place_ref[at] * BLOCK, BLOCK), BLOCK)
            out_ref[:, place] = value[:, c0 : c0 + BLOCK]
            at += 1


def lay_out(parts, places, name, tm=256):
    tokens, width = parts[0].shape
    full = width * len(parts)

    def kernel(place_ref, *refs):
        place_blocks([r[...] for r in refs[:-1]], place_ref, refs[-1])

    return matmul_call(
        kernel,
        (tokens // tm,),
        [(p, pl.BlockSpec((tm, width), lambda m, *_: (m, 0))) for p in parts],
        [((tokens, full), bf16, pl.BlockSpec((tm, full), lambda m, *_: (m, 0)))],
        [],
        tokens * full,
        name,
        prefetch=(places,),
    )[0]


def normalize(parts, gain, shift, places, name, tm=256):
    tokens, width = parts[0].shape
    n = len(parts)
    full = width * n

    def kernel(place_ref, *refs):
        gain_ref, shift_ref, out_ref, mean_ref, scale_ref = refs[n:]
        rows = [r[...].astype(f32) for r in refs[:n]]
        mean = sum(jnp.sum(v, axis=1, keepdims=True) for v in rows) / full
        square = sum(jnp.sum(v * v, axis=1, keepdims=True) for v in rows) / full
        scale = lax.rsqrt(square - mean * mean + norm_eps)
        mean_ref[...] = mean
        scale_ref[...] = scale
        done = []
        for i, v in enumerate(rows):
            cols = slice(i * width, (i + 1) * width)
            done.append(((v - mean) * scale * gain_ref[:, cols] + shift_ref[:, cols]).astype(bf16))
        place_blocks(done, place_ref, out_ref)

    ins = [(p, pl.BlockSpec((tm, width), lambda m, *_: (m, 0))) for p in parts]
    ins += [(gain, resident(gain.shape)), (shift, resident(shift.shape))]
    column = pl.BlockSpec((tm, 1), lambda m, *_: (m, 0))
    return matmul_call(
        kernel,
        (tokens // tm,),
        ins,
        [
            ((tokens, full), bf16, pl.BlockSpec((tm, full), lambda m, *_: (m, 0))),
            ((tokens, 1), f32, column),
            ((tokens, 1), f32, column),
        ],
        [],
        8 * tokens * full,
        name,
        prefetch=(places,),
    )


def swap(x, axis, bit):
    return lax.ppermute(x, axis, [(i, i ^ bit) for i in range(lax.axis_size(axis))])


def turn(x, steps):
    count = lax.axis_size("row")
    return lax.ppermute(x, "row", [(i, (i + 2 * steps) % count) for i in range(count)])


def gather_columns(x):
    near, across = swap(x, "col", 1), swap(x, "col", 2)
    return [x, near, across, swap(across, "col", 1)]


def sum_columns(sent, kept):
    half = kept.shape[1] // 2
    got = swap(sent, "col", 1)
    across = swap((kept[:, half:] + got[:, half:].astype(f32)).astype(bf16), "col", 2)
    return kept[:, :half] + got[:, :half].astype(f32) + across.astype(f32)


def sum_col_stats(stats):
    stats = stats + swap(stats, "col", 1)
    return stats + swap(stats, "col", 2)


def sum_rows(x):
    bit = 1
    while bit < lax.axis_size("row"):
        x = x + swap(x, "row", bit)
        bit *= 2
    return x


def gather_rows(w, stepped):
    if not stepped:
        return [lax.all_gather(w, "row", axis=0, tiled=True)]
    own = [w] + [turn(w, k) for k in range(1, lax.axis_size("row") // 2)]
    return own + [swap(v, "row", 1) for v in own]


def sum_weight(a, gs, stepped, name):
    if not stepped:
        whole = weight_parts(a, 0, a.shape[1] // BLOCK, gs, f32, name)
        return lax.psum_scatter(
            jnp.concatenate(whole, axis=0), "row", scatter_dimension=0, tiled=True
        )
    count = lax.axis_size("row") // 2
    other = weight_parts(a, count, count, gs, bf16, name + "_other")
    got = [None] * count
    for k in reversed(range(count)):
        got[k] = swap(other[k], "row", 1)
    mine = weight_parts(a, 0, count, gs, f32, name + "_mine")
    total = None
    for k in reversed(range(count)):
        term = mine[k] + got[k].astype(f32)
        if k:
            term = turn(term.astype(bf16), -k).astype(f32)
        total = term if total is None else total + term
    return total


def on_device(
    tokens,
    segments,
    gains,
    shifts,
    biases,
    mixing,
    projection,
    expand,
    thresholds,
    contract,
    cotangent,
):
    seqs = segments.shape[0]
    rows, cols = lax.axis_size("row"), lax.axis_size("col")
    row, col = lax.axis_index("row"), lax.axis_index("col")
    tokens_here, width = tokens.shape
    full = width * cols
    heads = width // HD
    stepped = full // rows == BLOCK and rows == 2 * cols
    blocks = full // BLOCK
    per_col = width // BLOCK
    at = jnp.arange(blocks)
    if stepped:
        outer, inner = row // 2, row % 2
        ids = 2 * ((outer - at % (rows // 2)) % (rows // 2)) + (inner ^ (at // (rows // 2)))
        mine = (at // per_col) ^ col
        places = ((at % per_col) ^ inner) * (rows // 2) + (outer - mine) % (rows // 2)
    else:
        ids = at
        places = ((at // per_col) ^ col) * per_col + at % per_col
    away = (ids // per_col) ^ col
    slots = (away // 2 + (1 - away % 2) * 2) * per_col + ids % per_col
    places, slots = places.astype(jnp.int32), slots.astype(jnp.int32)

    head_ids = (col * heads + jnp.arange(heads)).astype(f32)
    slopes = jnp.exp2(-8.0 * (head_ids + 1.0) / (heads * cols))
    starts = jnp.sum(segments[:, None, :] < segments[:, :, None], axis=2).astype(jnp.int32)

    full_mix = gather_rows(mixing.reshape(mixing.shape[0], -1), stepped)
    token_parts = gather_columns(tokens)
    norms = gather_columns(jnp.concatenate([gains, shifts], axis=0))
    norms = jnp.concatenate(norms, axis=1)
    full_proj = gather_rows(projection, stepped)
    full_expand = gather_rows(expand, stepped)
    full_contract = gather_rows(contract, stepped)
    cot_parts = gather_columns(cotangent)

    first_full, first_mean, first_scale = normalize(
        token_parts, norms[0:1], norms[2:3], places, "first_norm"
    )
    mixed_bias = jnp.concatenate([biases[0:1], jnp.zeros((1, width), f32), biases[1:2]], axis=1)

    def add_bias(acc, extra, out):
        out[0][...] = (acc + extra[0][...]).astype(bf16)

    (mixed,) = times_rows(
        first_full,
        full_mix,
        [mixed_bias],
        [((tokens_here, 3 * width), bf16)],
        add_bias,
        "mix",
        tn=512,
    )
    attended, logs = attend_forward(mixed, starts, slopes, seqs)
    resid = tokens.astype(f32)
    middle = resid + (
        sum_columns(*times_columns([attended], full_proj, slots, "project")) + biases[2]
    )
    second_full, second_mean, second_scale = normalize(
        gather_columns(middle.astype(bf16)), norms[1:2], norms[3:4], places, "second_norm"
    )

    def activate(acc, extra, out):
        hidden = acc + extra[0][...]
        bell = 0.5 * (1.0 + lax.erf(hidden * sqrt_half))
        out[0][...] = (hidden * bell).astype(bf16)
        out[1][...] = bell + hidden * (jnp.exp(-0.5 * hidden * hidden) * inverse_root)

    hidden_shape = (tokens_here, expand.shape[1])
    active, slope = times_rows(
        second_full,
        full_expand,
        [thresholds[None]],
        [(hidden_shape, bf16), (hidden_shape, f32)],
        activate,
        "expand",
        tn=512,
    )
    cot_full = lay_out(cot_parts, places, "cotangent_rows")
    contract_grad = sum_weight(cot_full, [active], stepped, "contract_grad")

    def back_activate(acc, extra, out):
        grad = (acc * extra[0][...]).astype(bf16)
        out[0][...] = grad
        total = jnp.sum(grad.astype(f32), axis=0, keepdims=True)

        @pl.when(pl.program_id(1) == 0)
        def _():
            out[1][...] = total

        @pl.when(pl.program_id(1) > 0)
        def _():
            out[1][...] += total

    hidden_grad, thresholds_part = times_rows(
        cot_full,
        full_contract,
        [slope],
        [(hidden_shape, bf16), ((1, hidden_shape[1]), f32)],
        back_activate,
        "contract_back",
        tn=512,
    )
    second_back = sum_columns(*times_columns([hidden_grad], full_expand, slots, "expand_back"))
    layer_out = (
        middle + (sum_columns(*times_columns([active], full_contract, slots, "contract")) + biases[3])
    ).astype(bf16)
    expand_grad = sum_weight(second_full, [hidden_grad], stepped, "expand_grad")

    def norm_back(upstream, centred, scale, gain):
        scaled = upstream * gain
        sums = sum_col_stats(
            jnp.stack([jnp.sum(scaled, axis=1), jnp.sum(scaled * centred, axis=1)])
        )
        result = scale * (
            scaled - sums[0][:, None] / full - centred * (sums[1][:, None] / full)
        )
        return result, jnp.sum(upstream * centred, axis=0), jnp.sum(upstream, axis=0)

    second_centred = (middle - second_mean) * second_scale
    second_input, second_gain, second_shift = norm_back(
        second_back, second_centred, second_scale, gains[1]
    )
    cot_float = cotangent.astype(f32)
    middle_grad = cot_float + second_input
    branch_grad = middle_grad.astype(bf16)
    branch_full = lay_out(gather_columns(branch_grad), places, "branch_rows")

    def store(acc, extra, out):
        out[0][...] = acc.astype(bf16)

    (attended_grad,) = times_rows(
        branch_full,
        full_proj,
        [],
        [((tokens_here, width), bf16)],
        store,
        "project_back",
        tn=512,
    )
    projection_grad = sum_weight(branch_full, [attended], stepped, "projection_grad")
    query_back, key_back, value_back, query_sum, value_sum = attend_backward(
        mixed, attended_grad, starts, logs, slopes, seqs
    )
    mixed_grads = [query_back, key_back, value_back]
    mixing_grad = sum_weight(first_full, mixed_grads, stepped, "mixing_grad")
    first_back = sum_columns(*times_columns(mixed_grads, full_mix, slots, "mix_back"))
    first_centred = (resid - first_mean) * first_scale
    first_input, first_gain, first_shift = norm_back(
        first_back, first_centred, first_scale, gains[0]
    )
    tokens_grad = middle_grad + first_input
    small = jnp.stack(
        [
            first_gain,
            second_gain,
            first_shift,
            second_shift,
            jnp.sum(query_sum, axis=(0, 1)),
            jnp.sum(value_sum, axis=(0, 1)),
            jnp.sum(branch_grad.astype(f32), axis=0),
            jnp.sum(cot_float, axis=0),
        ]
    )
    small = sum_rows(jnp.concatenate([small, thresholds_part.reshape(-1, width)], axis=0))
    return (
        layer_out,
        tokens_grad,
        small[0:2],
        small[2:4],
        small[4:8],
        mixing_grad.reshape(mixing.shape),
        projection_grad,
        expand_grad,
        small[8:].reshape(thresholds.shape),
        contract_grad,
    )


def solution(mesh):
    return jax.shard_map(
        on_device,
        mesh=mesh,
        in_specs=(
            P("row", "col"),
            P("row", None),
            P(None, "col"),
            P(None, "col"),
            P(None, "col"),
            P("row", None, "col"),
            P("row", "col"),
            P("row", "col"),
            P("col"),
            P("row", "col"),
            P("row", "col"),
        ),
        out_specs=(
            P("row", "col"),
            P("row", "col"),
            P(None, "col"),
            P(None, "col"),
            P(None, "col"),
            P("row", None, "col"),
            P("row", "col"),
            P("row", "col"),
            P("col"),
            P("row", "col"),
        ),
        check_vma=False,
    )
```

time: 1790 us -> 1170 us (0.65)
  waiting for transfers between devices: 1490 us -> 585 us
  Pallas kernels: 35 us -> 265 us
  starting transfers between devices: 0.65 us -> 221 us
  matrix products: 140 us -> 0 us
  blocking collectives: 65.9 us -> 0 us
  other arithmetic: 26.2 us -> 50.1 us
  local copies, waits for them, and re-layouts: 14 us -> 37.3 us
    reduce_scatter x8 -> x0, waiting for transfers between devices: 1010 us -> none  [the longest x1 287 us: on_device(): lax.psum_scatter(lax.dot_general(columns, hidden_grad, contract_first, pr...]
    ppermute x0 -> x86, waiting for transfers between devices: none -> 585 us  [the longest x62 335 us: swap(): lax.ppermute(x, axis, [(i, i ^ bit) for i in range(lax.axis_size(axis))])]
    all_gather x8 -> x0, waiting for transfers between devices: 469 us -> none  [the longest x1 127 us: on_device(): lax.all_gather(contract, 'row', axis=0, tiled=True)]
    pallas_call x0 -> x20, Pallas kernels: none -> 231 us  [matmul_call(): pl.pallas_call(kernel, grid_spec=pltpu.PrefetchScalarGridSpec(num_scalar_...]
    ppermute x0 -> x86, starting transfers between devices: none -> 221 us  [the longest x24 149 us: turn(): lax.ppermute(x, 'row', [(i, (i + 2 * steps) % count) for i in range(count)])]
    dot_general x12 -> x0, matrix products: 140 us -> none  [the longest x1 16.3 us: on_device(): jnp.dot(cot_full, back_contract, preferred_element_type=jnp.float32)]
    psum x5 -> x0, blocking collectives: 65.9 us -> none  [the longest x1 39.5 us: on_device(): lax.psum((jnp.stack([first_gain_part, second_gain_part]), jnp.stack([firs...]
    unnamed x49 -> x176, local copies, waits for them, and re-layouts: 11.3 us -> 31 us
  transfers between devices with their start and end apart: 16 -> 86, of which waited for: 16 -> 37; matrix products, arithmetic and copies ran while one was open for 7% -> 5% of each run, Pallas kernels for 2% -> 11%
where the time goes in v2:
time: 1170 us; the launch traced here: 1160 us
  waiting for transfers between devices  585 us (50%)
  Pallas kernels  265 us (23%)
  starting transfers between devices  221 us (19%)
  other arithmetic  50.1 us (4%)
  local copies, waits for them, and re-layouts  37.3 us (3%)
    ppermute x62, waiting for transfers between devices, swap(): lax.ppermute(x, axis, [(i, i ^ bit) for i in range(lax.axis_size(axis))])  335 us
    ppermute x24, waiting for transfers between devices, turn(): lax.ppermute(x, 'row', [(i, (i + 2 * steps) % count) for i in range(count)])  251 us
    pallas_call x20, Pallas kernels, matmul_call(): pl.pallas_call(kernel, grid_spec=pltpu.PrefetchScalarGridSpec(num_scalar_...  231 us
    ppermute x24, starting transfers between devices, turn(): lax.ppermute(x, 'row', [(i, (i + 2 * steps) % count) for i in range(count)])  149 us
    ppermute x62, starting transfers between devices, swap(): lax.ppermute(x, axis, [(i, i ^ bit) for i in range(lax.axis_size(axis))])  72.1 us
    unnamed x176, local copies, waits for them, and re-layouts  31 us
  transfers between devices with their start and end apart: 86, of which 37 were waited for; matrix products, arithmetic and copies ran while one was open for 5% of the time, Pallas kernels for 11%

profile of v2, /device:TPU:0, one launch (start us, length us, event | category | flops | bytes accessed | tf_op | source)
XLA Modules:
  0.0 1161.7 jit_solution(15629808731683726621)
XLA Ops:
  3.7 3.6 collective-permute-start.15
  8.6 18.6 %collective-permute-done.4 = f32[4,512]{1,0:T(4,128)S(1)} collective-permute-done((f32[4,512]{1,0:T(4,128)S(1)}, f32[4,512]{1,0:T(4,128)S(1)}, u32[]{:S(2)}, u32[]{:S(2)}) %collective-permute-start.4) | collective-permute-done | bytes 8224 | tf_op jit(solution)/shard_map/ppermute | solution.py:411
  33.2 3.9 collective-permute-start.8
  40.8 14.6 %collective-permute-done.8.refs_4_.refs_6_ = bf16[256,1536]{1,0:T(8,128)(2,1)} collective-permute-done((bf16[256,1536]{1,0:T(8,128)(2,1)}, bf16[256,1536]{1,0:T(8,128)(2,1)}, u32[]{:S(2)}, u32[]{:S(2)}) %collective-permute-start.8) | collective-permute-done | bytes 786464 | tf_op jit(solution)/shard_map/ppermute | solution.py:416
  56.9 48.3 %collective-permute-done.7.refs_3_.refs_5_ = bf16[256,1536]{1,0:T(8,128)(2,1)} collective-permute-done((bf16[256,1536]{1,0:T(8,128)(2,1)}, bf16[256,1536]{1,0:T(8,128)(2,1)}, u32[]{:S(2)}, u32[]{:S(2)}) %collective-permute-start.7) | collective-permute-done | bytes 786464 | tf_op jit(solution)/shard_map/ppermute | solution.py:416
  112.3 6.4 first_norm.1
  122.3 3.5 collective-permute-done.12.refs_8_.refs_10_
  127.4 15.3 %collective-permute-done.11.refs_7_.refs_9_ = bf16[256,1536]{1,0:T(8,128)(2,1)S(1)} collective-permute-done((bf16[256,1536]{1,0:T(8,128)(2,1)}, bf16[256,1536]{1,0:T(8,128)(2,1)S(1)}, u32[]{:S(2)}, u32[]{:S(2)}) %collective-permute-start.11) | collective-permute-done | bytes 786464 | tf_op jit(solution)/shard_map/ppermute | solution.py:411
  144.2 15.3 %collective-permute-done.10.refs_6_.refs_8_ = bf16[256,1536]{1,0:T(8,128)(2,1)S(1)} collective-permute-done((bf16[256,1536]{1,0:T(8,128)(2,1)}, bf16[256,1536]{1,0:T(8,128)(2,1)S(1)}, u32[]{:S(2)}, u32[]{:S(2)}) %collective-permute-start.10) | collective-permute-done | bytes 786464 | tf_op jit(solution)/shard_map/ppermute | solution.py:411
  159.6 13.6 %mix.1.q_ref.k_ref.v_ref = bf16[1024,1536]{1,0:T(8,128)(2,1)} custom-call(bf16[1024,2048]{1,0:T(8,128)(2,1)} %get-tuple-element.67.refs_0_.a_ref, bf16[256,1536]{1,0:T(8,128)(2,1)S(1)} %copy-done.15, bf16[256,1536]{1,0:T(8,128)(2,1)} %collective-permute-done.6.refs_2_.refs_4_, bf16[256,1536]{1,0:T(8,128)(2,1)} %collective-permute-done.7.refs_3_.refs_5_, ...), custom_call_target="tpu_custom_call" | custom-call | flops 6442450944 | bytes 13637632 | tf_op jit(solution)/shard_map/mix/pallas_call | solution.py:224
  175.1 15.7 %attend_forward.1 = (bf16[1024,512]{1,0:T(8,128)(2,1)S(1)}, f32[4,2,1024]{2,1,0:T(2,128)S(1)}) custom-call(f32[8]{0:T(128)S(1)} %multiply_exponential_fusion.slope_ref, s32[1,1024,1]{2,1,0:T(8,128)S(1)} %copy-done.21, bf16[1024,1536]{1,0:T(8,128)(2,1)S(1)} %copy-done.61, bf16[1024,1536]{1,0:T(8,128)(2,1)S(1)} %copy-done.61, bf16[1024,1536]{1,0:T(8,128)(2,1)S(1)} %copy-done.61), custom_call_target="tpu_custom_call" | custom-call | flops 6442450944 | bytes 6291456 | tf_op jit(solution)/shard_map/attend_forward/pallas_call | solution.py:78
  190.9 13.3 %project.1 = (bf16[1024,1024]{1,0:T(8,128)(2,1)S(1)}, f32[1024,1024]{1,0:T(8,128)}) custom-call(s32[8]{0:T(128)S(1)} %fusion.10.slot_ref, bf16[1024,512]{1,0:T(8,128)(2,1)S(1)} %get-tuple-element.68.refs_0_, bf16[256,512]{1,0:T(8,128)(2,1)S(1)} %copy-done.43, bf16[256,512]{1,0:T(8,128)(2,1)S(1)} %collective-permute-done.13.refs_2_, ...), custom_call_target="tpu_custom_call" | custom-call | flops 2147483648 | bytes 9437184 | tf_op jit(solution)/shard_map/project/pallas_call | solution.py:224
  204.8 3.6 collective-permute-done.20
  214.1 22.4 %collective-permute-done.21 = bf16[1024,512]{1,0:T(8,128)(2,1)S(1)} collective-permute-done((bf16[1024,512]{1,0:T(8,128)(2,1)S(1)}, bf16[1024,512]{1,0:T(8,128)(2,1)S(1)}, u32[]{:S(2)}, u32[]{:S(2)}) %collective-permute-start.21) | collective-permute-done | bytes 1048608 | tf_op jit(solution)/shard_map/ppermute | solution.py:411
  236.6 3.7 fusion.25
  240.3 18.0 %collective-permute-done.42.refs_2_ = bf16[1024,512]{1,0:T(8,128)(2,1)S(1)} collective-permute-done((bf16[1024,512]{1,0:T(8,128)(2,1)S(1)}, bf16[1024,512]{1,0:T(8,128)(2,1)S(1)}, u32[]{:S(2)}, u32[]{:S(2)}) %collective-permute-start.42) | collective-permute-done | bytes 1048608 | tf_op jit(solution)/shard_map/ppermute | solution.py:411
  258.3 23.9 %collective-permute-start.32 = (bf16[256,2048]{1,0:T(8,128)(2,1)S(1)}, bf16[256,2048]{1,0:T(8,128)(2,1)}, u32[]{:S(2)}, u32[]{:S(2)}) collective-permute-start(bf16[256,2048]{1,0:T(8,128)(2,1)S(1)} %copy-done.23), channel_id=1, source_target_pairs={{0,8},{4,12},{8,16},{12,20},{16,24},{20,28},{24,0},{28,4},{1,9},{5... | collective-permute-start | bytes 3145736 | tf_op jit(solution)/shard_map/ppermute | solution.py:416
  282.2 67.9 %collective-permute-done.26.refs_3_ = bf16[256,2048]{1,0:T(8,128)(2,1)S(1)} collective-permute-done((bf16[256,2048]{1,0:T(8,128)(2,1)S(1)}, bf16[256,2048]{1,0:T(8,128)(2,1)S(1)}, u32[]{:S(2)}, u32[]{:S(2)}) %collective-permute-start.26) | collective-permute-done | bytes 1048608 | tf_op jit(solution)/shard_map/ppermute | solution.py:416
  352.2 41.5 %collective-permute-done.33.refs_3_ = bf16[256,2048]{1,0:T(8,128)(2,1)} collective-permute-done((bf16[256,2048]{1,0:T(8,128)(2,1)S(1)}, bf16[256,2048]{1,0:T(8,128)(2,1)}, u32[]{:S(2)}, u32[]{:S(2)}) %collective-permute-start.33) | collective-permute-done | bytes 1048608 | tf_op jit(solution)/shard_map/ppermute | solution.py:416
  397.8 22.1 %collective-permute-done.30.refs_7_ = bf16[256,2048]{1,0:T(8,128)(2,1)S(1)} collective-permute-done((bf16[256,2048]{1,0:T(8,128)(2,1)S(1)}, bf16[256,2048]{1,0:T(8,128)(2,1)S(1)}, u32[]{:S(2)}, u32[]{:S(2)}) %collective-permute-start.30) | collective-permute-done | bytes 1048608 | tf_op jit(solution)/shard_map/ppermute | solution.py:411
  425.6 5.2 second_norm.1
  432.4 10.0 collective-permute-done.29.refs_6_
  442.4 19.9 %expand.1 = (bf16[1024,2048]{1,0:T(8,128)(2,1)}, f32[1024,2048]{1,0:T(8,128)}) custom-call(bf16[1024,2048]{1,0:T(8,128)(2,1)} %get-tuple-element.71.refs_0_.a_ref, bf16[256,2048]{1,0:T(8,128)(2,1)S(1)} %copy-done.22, bf16[256,2048]{1,0:T(8,128)(2,1)} %collective-permute-done.25.refs_2_, bf16[256,2048]{1,0:T(8,128)(2,1)S(1)} %copy-done.32, ...), custom_call_target="tpu_custom_call" | custom-call | flops 8589934592 | bytes 25174016 | tf_op jit(solution)/shard_map/expand/pallas_call | solution.py:224
  464.9 22.5 %collective-permute-done.38.refs_8_ = bf16[256,2048]{1,0:T(8,128)(2,1)} collective-permute-done((bf16[256,2048]{1,0:T(8,128)(2,1)S(1)}, bf16[256,2048]{1,0:T(8,128)(2,1)}, u32[]{:S(2)}, u32[]{:S(2)}) %collective-permute-start.38) | collective-permute-done | bytes 1048608 | tf_op jit(solution)/shard_map/ppermute | solution.py:411
  487.3 22.5 %collective-permute-done.37.refs_7_ = bf16[256,2048]{1,0:T(8,128)(2,1)} collective-permute-done((bf16[256,2048]{1,0:T(8,128)(2,1)}, bf16[256,2048]{1,0:T(8,128)(2,1)}, u32[]{:S(2)}, u32[]{:S(2)}) %collective-permute-start.37) | collective-permute-done | bytes 1048608 | tf_op jit(solution)/shard_map/ppermute | solution.py:411
  509.8 20.1 %collective-permute-done.36.refs_6_ = bf16[256,2048]{1,0:T(8,128)(2,1)} collective-permute-done((bf16[256,2048]{1,0:T(8,128)(2,1)}, bf16[256,2048]{1,0:T(8,128)(2,1)}, u32[]{:S(2)}, u32[]{:S(2)}) %collective-permute-start.36) | collective-permute-done | bytes 1048608 | tf_op jit(solution)/shard_map/ppermute | solution.py:411
  529.9 19.9 %contract_back.1 = (bf16[1024,2048]{1,0:T(8,128)(2,1)}, f32[1,2048]{1,0:T(1,128)S(1)}) custom-call(bf16[1024,2048]{1,0:T(8,128)(2,1)} %cotangent_rows.1.refs_0_.a_ref, bf16[256,2048]{1,0:T(8,128)(2,1)S(1)} %copy-done.23, bf16[256,2048]{1,0:T(8,128)(2,1)} %collective-permute-done.32.refs_2_, bf16[256,2048]{1,0:T(8,128)(2,1)} %collective-permute-done.33.refs_3_, ...), custom_call_target="tpu_custom_call" | custom-call | flops 8589934592 | bytes 25174016 | tf_op jit(solution)/shard_map/contract_back/pallas_call | solution.py:224
  549.8 9.3 expand_grad_other.1
  561.1 10.2 expand_grad_mine.1
  573.9 28.0 %expand_back.1 = (bf16[1024,1024]{1,0:T(8,128)(2,1)}, f32[1024,1024]{1,0:T(8,128)}) custom-call(s32[8]{0:T(128)S(1)} %fusion.10.slot_ref, bf16[1024,2048]{1,0:T(8,128)(2,1)} %get-tuple-element.77.refs_0_, bf16[256,2048]{1,0:T(8,128)(2,1)S(1)} %copy-done.22, bf16[256,2048]{1,0:T(8,128)(2,1)} %collective-permute-done.25.refs_2_, ...), custom_call_target="tpu_custom_call" | custom-call | flops 8589934592 | bytes 18874368 | tf_op jit(solution)/shard_map/expand_back/pallas_call | solution.py:224
  603.9 8.0 contract_grad_other.1
  614.8 28.8 %contract.1 = (bf16[1024,1024]{1,0:T(8,128)(2,1)}, f32[1024,1024]{1,0:T(8,128)}) custom-call(s32[8]{0:T(128)S(1)} %fusion.10.slot_ref, bf16[1024,2048]{1,0:T(8,128)(2,1)} %get-tuple-element.72.refs_0_, bf16[256,2048]{1,0:T(8,128)(2,1)S(1)} %copy-done.23, bf16[256,2048]{1,0:T(8,128)(2,1)} %collective-permute-done.32.refs_2_, ...), custom_call_target="tpu_custom_call" | custom-call | flops 8589934592 | bytes 18874368 | tf_op jit(solution)/shard_map/contract/pallas_call | solution.py:224
  643.6 10.1 contract_grad_mine.1
  669.6 15.6 %collective-permute-done.76 = bf16[256,2048]{1,0:T(8,128)(2,1)S(1)} collective-permute-done((bf16[256,2048]{1,0:T(8,128)(2,1)}, bf16[256,2048]{1,0:T(8,128)(2,1)S(1)}, u32[]{:S(2)}, u32[]{:S(2)}) %collective-permute-start.76) | collective-permute-done | bytes 1048608 | tf_op jit(solution)/shard_map/ppermute | solution.py:411
  686.9 4.1 collective-permute-done.45
  698.1 31.9 %collective-permute-done.79 = bf16[256,2048]{1,0:T(8,128)(2,1)S(1)} collective-permute-done((bf16[256,2048]{1,0:T(8,128)(2,1)S(1)}, bf16[256,2048]{1,0:T(8,128)(2,1)S(1)}, u32[]{:S(2)}, u32[]{:S(2)}) %collective-permute-start.79) | collective-permute-done | bytes 1048608 | tf_op jit(solution)/shard_map/ppermute | solution.py:411
  737.7 14.9 %collective-permute-done.81 = bf16[256,2048]{1,0:T(8,128)(2,1)S(1)} collective-permute-done((bf16[256,2048]{1,0:T(8,128)(2,1)S(1)}, bf16[256,2048]{1,0:T(8,128)(2,1)S(1)}, u32[]{:S(2)}, u32[]{:S(2)}) %collective-permute-start.81) | collective-permute-done | bytes 1048608 | tf_op jit(solution)/shard_map/ppermute | solution.py:411
  752.6 22.5 %collective-permute-done.83 = bf16[256,2048]{1,0:T(8,128)(2,1)S(1)} collective-permute-done((bf16[256,2048]{1,0:T(8,128)(2,1)S(1)}, bf16[256,2048]{1,0:T(8,128)(2,1)S(1)}, u32[]{:S(2)}, u32[]{:S(2)}) %collective-permute-start.83) | collective-permute-done | bytes 1048608 | tf_op jit(solution)/shard_map/ppermute | solution.py:411
  779.7 17.3 %collective-permute-done.85 = bf16[256,2048]{1,0:T(8,128)(2,1)S(1)} collective-permute-done((bf16[256,2048]{1,0:T(8,128)(2,1)S(1)}, bf16[256,2048]{1,0:T(8,128)(2,1)S(1)}, u32[]{:S(2)}, u32[]{:S(2)}) %collective-permute-start.85) | collective-permute-done | bytes 1048608 | tf_op jit(solution)/shard_map/ppermute | solution.py:411
  797.5 6.3 collective-permute-start.82
  803.8 3.5 collective-permute-done.75
  807.3 55.1 %collective-permute-start.84 = (bf16[256,2048]{1,0:T(8,128)(2,1)}, bf16[256,2048]{1,0:T(8,128)(2,1)}, u32[]{:S(2)}, u32[]{:S(2)}) collective-permute-start(bf16[256,2048]{1,0:T(8,128)(2,1)} %add_convert_fusion), channel_id=1, source_target_pairs={{0,24},{4,28},{8,0},{12,4},{16,8},{20,12},{24,16},{28,20},{1,25},{... | collective-permute-start | bytes 3145736 | tf_op jit(solution)/shard_map/ppermute | solution.py:416
  866.7 5.1 add_add_fusion.1
  871.8 22.6 %collective-permute-done.82 = bf16[256,2048]{1,0:T(8,128)(2,1)} collective-permute-done((bf16[256,2048]{1,0:T(8,128)(2,1)}, bf16[256,2048]{1,0:T(8,128)(2,1)}, u32[]{:S(2)}, u32[]{:S(2)}) %collective-permute-start.82) | collective-permute-done | bytes 1048608 | tf_op jit(solution)/shard_map/ppermute | solution.py:416
  895.1 4.0 add_add_fusion
  899.2 4.9 branch_rows.1.refs_0_.a_ref
  904.2 5.3 project_back.1.g_ref
  909.6 19.3 %attend_backward.1 = (bf16[1024,512]{1,0:T(8,128)(2,1)S(1)}, bf16[1024,512]{1,0:T(8,128)(2,1)S(1)}, bf16[1024,512]{1,0:T(8,128)(2,1)S(1)}, f32[1,1,512]{2,1,0:T(1,128)S(1)}, f32[1,1,512]{2,1,0:T(1,128)S(1)}) custom-call(f32[8]{0:T(128)S(1)} %multiply_exponential_fusion.slope_ref, s32[1,1,1024]{2,1,0:T(1,128)S(1)} %bitcast.30, ...), custom_call_target="tpu_custom_call" | custom-call | flops 10737418240 | bytes 7340032 | tf_op jit(solution)/shard_map/attend_backward/pallas_call | solution.py:182
  931.8 23.3 %mix_back.1 = (bf16[1024,1024]{1,0:T(8,128)(2,1)}, f32[1024,1024]{1,0:T(8,128)}) custom-call(s32[8]{0:T(128)S(1)} %fusion.10.slot_ref, bf16[1024,512]{1,0:T(8,128)(2,1)} %copy-done.55, bf16[1024,512]{1,0:T(8,128)(2,1)} %copy-done.57, bf16[1024,512]{1,0:T(8,128)(2,1)} %copy-done.59, bf16[256,1536]{1,0:T(8,128)(2,1)S(1)} %copy-done.16, ...), custom_call_target="tpu_custom_call" | custom-call | flops 6442450944 | bytes 15728640 | tf_op jit(solution)/shard_map/mix_back/pallas_call | solution.py:224
  955.2 3.8 projection_grad_other.1
  961.1 5.8 mixing_grad_other.1
  968.6 7.8 mixing_grad_mine.1
  976.3 3.7 projection_grad_mine.1
  982.8 13.5 %collective-permute-done.69 = bf16[256,512]{1,0:T(8,128)(2,1)S(1)} collective-permute-done((bf16[256,512]{1,0:T(8,128)(2,1)S(1)}, bf16[256,512]{1,0:T(8,128)(2,1)S(1)}, u32[]{:S(2)}, u32[]{:S(2)}) %collective-permute-start.69) | collective-permute-done | bytes 262176 | tf_op jit(solution)/shard_map/ppermute | solution.py:411
  998.7 22.4 %collective-permute-start.66 = (bf16[256,512]{1,0:T(8,128)(2,1)S(1)}, bf16[256,512]{1,0:T(8,128)(2,1)S(1)}, u32[]{:S(2)}, u32[]{:S(2)}) collective-permute-start(bf16[256,512]{1,0:T(8,128)(2,1)S(1)} %add_convert_fusion.16), channel_id=1, source_target_pairs={{0,8},{4,12},{8,16},{12,20},{16,24},{20,28},{24,0},{28,4},{1,9},{5... | collective-permute-start | bytes 786440 | tf_op jit(solution)/shard_map/ppermute | solution.py:416
  1024.6 11.0 collective-permute-done.62
  1035.6 21.1 %collective-permute-start.68 = (bf16[256,512]{1,0:T(8,128)(2,1)S(1)}, bf16[256,512]{1,0:T(8,128)(2,1)S(1)}, u32[]{:S(2)}, u32[]{:S(2)}) collective-permute-start(bf16[256,512]{1,0:T(8,128)(2,1)S(1)} %add_convert_fusion.15), channel_id=1, source_target_pairs={{0,16},{4,20},{8,24},{12,28},{16,0},{20,4},{24,8},{28,12},{1,17},{... | collective-permute-start | bytes 786440 | tf_op jit(solution)/shard_map/ppermute | solution.py:416
  1057.0 3.4 collective-permute-start.70
  1060.4 9.4 collective-permute-done.68
  1069.8 7.5 collective-permute-start.63
  1077.3 3.4 fusion.8
  1083.6 6.4 collective-permute-done.59
  1090.0 35.8 %collective-permute-done.61 = bf16[256,1536]{1,0:T(8,128)(2,1)S(1)} collective-permute-done((bf16[256,1536]{1,0:T(8,128)(2,1)S(1)}, bf16[256,1536]{1,0:T(8,128)(2,1)S(1)}, u32[]{:S(2)}, u32[]{:S(2)}) %collective-permute-start.61) | collective-permute-done | bytes 786464 | tf_op jit(solution)/shard_map/ppermute | solution.py:416
  1135.1 15.9 %collective-permute-start.56 = (f32[12,512]{1,0:T(8,128)S(1)}, f32[12,512]{1,0:T(8,128)S(1)}, u32[]{:S(2)}, u32[]{:S(2)}) collective-permute-start(f32[12,512]{1,0:T(8,128)S(1)} %add.269), channel_id=1, source_target_pairs={{0,8},{4,12},{8,0},{12,4},{16,24},{20,28},{24,16},{28,20},{1,9},{5... | collective-permute-start | bytes 73736 | tf_op jit(solution)/shard_map/ppermute | solution.py:411
  (366 shorter events, 143.3 us)
Async XLA Ops:
  0.7 37.4 %collective-permute-start.1 = (bf16[1024,512]{1,0:T(8,128)(2,1)}, bf16[1024,512]{1,0:T(8,128)(2,1)S(1)}, u32[]{:S(2)}, u32[]{:S(2)}) collective-permute-start(bf16[1024,512]{1,0:T(8,128)(2,1)} %refs_0_.2), channel_id=1, source_target_pairs={{0,2},{1,3},{2,0},{3,1},{4,6},{5,7},{6,4},{7,5},{8,10},{9,11},{10,... | collective-permute-start | bytes 3145736 | tf_op jit(solution)/shard_map/ppermute | solution.py:411
  3.7 33.4 %collective-permute-start.15 = (bf16[256,512]{1,0:T(8,128)(2,1)}, bf16[256,512]{1,0:T(8,128)(2,1)}, u32[]{:S(2)}, u32[]{:S(2)}) collective-permute-start(bf16[256,512]{1,0:T(8,128)(2,1)} %refs_1_.11), channel_id=1, source_target_pairs={{0,24},{4,28},{8,0},{12,4},{16,8},{20,12},{24,16},{28,20},{1,25},{... | collective-permute-start | bytes 786440 | tf_op jit(solution)/shard_map/ppermute | solution.py:416
  7.3 29.8 %collective-permute-start.14 = (bf16[256,512]{1,0:T(8,128)(2,1)}, bf16[256,512]{1,0:T(8,128)(2,1)}, u32[]{:S(2)}, u32[]{:S(2)}) collective-permute-start(bf16[256,512]{1,0:T(8,128)(2,1)} %refs_1_.11), channel_id=1, source_target_pairs={{0,16},{4,20},{8,24},{12,28},{16,0},{20,4},{24,8},{28,12},{1,17},{... | collective-permute-start | bytes 786440 | tf_op jit(solution)/shard_map/ppermute | solution.py:416
  7.3 99.9 %collective-permute-start = (bf16[1024,512]{1,0:T(8,128)(2,1)}, bf16[1024,512]{1,0:T(8,128)(2,1)S(1)}, u32[]{:S(2)}, u32[]{:S(2)}) collective-permute-start(bf16[1024,512]{1,0:T(8,128)(2,1)} %refs_0_.2), channel_id=1, source_target_pairs={{0,1},{1,0},{2,3},{3,2},{4,5},{5,4},{6,7},{7,6},{8,9},{9,8},{10,11... | collective-permute-start | bytes 3145736 | tf_op jit(solution)/shard_map/ppermute | solution.py:411
  37.1 68.1 %collective-permute-start.7 = (bf16[256,1536]{1,0:T(8,128)(2,1)}, bf16[256,1536]{1,0:T(8,128)(2,1)}, u32[]{:S(2)}, u32[]{:S(2)}) collective-permute-start(bf16[256,1536]{1,0:T(8,128)(2,1)} %copy.38.refs_1_.refs_3_), channel_id=1, source_target_pairs={{0,16},{4,20},{8,24},{12,28},{16,0},{20,4},{24,8},{28,12},{1,17},{... | collective-permute-start | bytes 2359304 | tf_op jit(solution)/shard_map/ppermute | solution.py:416
  37.1 69.6 %collective-permute-start.6 = (bf16[256,1536]{1,0:T(8,128)(2,1)}, bf16[256,1536]{1,0:T(8,128)(2,1)}, u32[]{:S(2)}, u32[]{:S(2)}) collective-permute-start(bf16[256,1536]{1,0:T(8,128)(2,1)} %copy.38.refs_1_.refs_3_), channel_id=1, source_target_pairs={{0,8},{4,12},{8,16},{12,20},{16,24},{20,28},{24,0},{28,4},{1,9},{5... | collective-permute-start | bytes 2359304 | tf_op jit(solution)/shard_map/ppermute | solution.py:416
  38.1 71.6 %collective-permute-start.2 = (bf16[1024,512]{1,0:T(8,128)(2,1)S(1)}, bf16[1024,512]{1,0:T(8,128)(2,1)}, u32[]{:S(2)}, u32[]{:S(2)}) collective-permute-start(bf16[1024,512]{1,0:T(8,128)(2,1)S(1)} %collective-permute-done.1.refs_2_), channel_id=1, source_target_pairs={{0,1},{1,0},{2,3},{3,2},{4,5},{5,4},{6,7},{7,6},{8,9},{9,8},{10,11... | collective-permute-start | bytes 3145736 | tf_op jit(solution)/shard_map/ppermute | solution.py:411
  55.4 65.8 %collective-permute-start.9 = (bf16[256,1536]{1,0:T(8,128)(2,1)}, bf16[256,1536]{1,0:T(8,128)(2,1)S(1)}, u32[]{:S(2)}, u32[]{:S(2)}) collective-permute-start(bf16[256,1536]{1,0:T(8,128)(2,1)} %copy.38.refs_1_.refs_3_), channel_id=1, source_target_pairs={{0,4},{4,0},{8,12},{12,8},{16,20},{20,16},{24,28},{28,24},{1,5},{5... | collective-permute-start | bytes 2359304 | tf_op jit(solution)/shard_map/ppermute | solution.py:411
  106.7 36.0 %collective-permute-start.11 = (bf16[256,1536]{1,0:T(8,128)(2,1)}, bf16[256,1536]{1,0:T(8,128)(2,1)S(1)}, u32[]{:S(2)}, u32[]{:S(2)}) collective-permute-start(bf16[256,1536]{1,0:T(8,128)(2,1)} %collective-permute-done.7.refs_3_.refs_5_), channel_id=1, source_target_pairs={{0,4},{4,0},{8,12},{12,8},{16,20},{20,16},{24,28},{28,24},{1,5},{5... | collective-permute-start | bytes 2359304 | tf_op jit(solution)/shard_map/ppermute | solution.py:411
  108.2 51.4 %collective-permute-start.10 = (bf16[256,1536]{1,0:T(8,128)(2,1)}, bf16[256,1536]{1,0:T(8,128)(2,1)S(1)}, u32[]{:S(2)}, u32[]{:S(2)}) collective-permute-start(bf16[256,1536]{1,0:T(8,128)(2,1)} %collective-permute-done.6.refs_2_.refs_4_), channel_id=1, source_target_pairs={{0,4},{4,0},{8,12},{12,8},{16,20},{20,16},{24,28},{28,24},{1,5},{5... | collective-permute-start | bytes 2359304 | tf_op jit(solution)/shard_map/ppermute | solution.py:411
  120.3 70.5 %collective-permute-start.16 = (bf16[256,512]{1,0:T(8,128)(2,1)S(1)}, bf16[256,512]{1,0:T(8,128)(2,1)S(1)}, u32[]{:S(2)}, u32[]{:S(2)}) collective-permute-start(bf16[256,512]{1,0:T(8,128)(2,1)S(1)} %copy-done.43), channel_id=1, source_target_pairs={{0,4},{4,0},{8,12},{12,8},{16,20},{20,16},{24,28},{28,24},{1,5},{5... | collective-permute-start | bytes 786440 | tf_op jit(solution)/shard_map/ppermute | solution.py:411
  121.2 69.7 %collective-permute-start.19 = (bf16[256,512]{1,0:T(8,128)(2,1)}, bf16[256,512]{1,0:T(8,128)(2,1)S(1)}, u32[]{:S(2)}, u32[]{:S(2)}) collective-permute-start(bf16[256,512]{1,0:T(8,128)(2,1)} %collective-permute-done.15.refs_4_), channel_id=1, source_target_pairs={{0,4},{4,0},{8,12},{12,8},{16,20},{20,16},{24,28},{28,24},{1,5},{5... | collective-permute-start | bytes 786440 | tf_op jit(solution)/shard_map/ppermute | solution.py:411
  125.8 65.0 %collective-permute-start.18 = (bf16[256,512]{1,0:T(8,128)(2,1)}, bf16[256,512]{1,0:T(8,128)(2,1)S(1)}, u32[]{:S(2)}, u32[]{:S(2)}) collective-permute-start(bf16[256,512]{1,0:T(8,128)(2,1)} %collective-permute-done.14.refs_3_), channel_id=1, source_target_pairs={{0,4},{4,0},{8,12},{12,8},{16,20},{20,16},{24,28},{28,24},{1,5},{5... | collective-permute-start | bytes 786440 | tf_op jit(solution)/shard_map/ppermute | solution.py:411
  142.7 48.2 %collective-permute-start.17 = (bf16[256,512]{1,0:T(8,128)(2,1)S(1)}, bf16[256,512]{1,0:T(8,128)(2,1)S(1)}, u32[]{:S(2)}, u32[]{:S(2)}) collective-permute-start(bf16[256,512]{1,0:T(8,128)(2,1)S(1)} %collective-permute-done.13.refs_2_), channel_id=1, source_target_pairs={{0,4},{4,0},{8,12},{12,8},{16,20},{20,16},{24,28},{28,24},{1,5},{5... | collective-permute-start | bytes 786440 | tf_op jit(solution)/shard_map/ppermute | solution.py:411
  212.1 46.1 %collective-permute-start.42 = (bf16[1024,512]{1,0:T(8,128)(2,1)S(1)}, bf16[1024,512]{1,0:T(8,128)(2,1)S(1)}, u32[]{:S(2)}, u32[]{:S(2)}) collective-permute-start(bf16[1024,512]{1,0:T(8,128)(2,1)S(1)} %copy-done.1), channel_id=1, source_target_pairs={{0,2},{1,3},{2,0},{3,1},{4,6},{5,7},{6,4},{7,5},{8,10},{9,11},{10,... | collective-permute-start | bytes 3145736 | tf_op jit(solution)/shard_map/ppermute | solution.py:411
  212.6 45.7 %collective-permute-start.28 = (bf16[256,2048]{1,0:T(8,128)(2,1)S(1)}, bf16[256,2048]{1,0:T(8,128)(2,1)S(1)}, u32[]{:S(2)}, u32[]{:S(2)}) collective-permute-start(bf16[256,2048]{1,0:T(8,128)(2,1)S(1)} %copy-done.22), channel_id=1, source_target_pairs={{0,4},{4,0},{8,12},{12,8},{16,20},{20,16},{24,28},{28,24},{1,5},{5... | collective-permute-start | bytes 3145736 | tf_op jit(solution)/shard_map/ppermute | solution.py:411
  214.1 44.2 %collective-permute-start.27 = (bf16[256,2048]{1,0:T(8,128)(2,1)S(1)}, bf16[256,2048]{1,0:T(8,128)(2,1)S(1)}, u32[]{:S(2)}, u32[]{:S(2)}) collective-permute-start(bf16[256,2048]{1,0:T(8,128)(2,1)S(1)} %copy-done.22), channel_id=1, source_target_pairs={{0,24},{4,28},{8,0},{12,4},{16,8},{20,12},{24,16},{28,20},{1,25},{... | collective-permute-start | bytes 3145736 | tf_op jit(solution)/shard_map/ppermute | solution.py:416
  214.1 136.0 %collective-permute-start.26 = (bf16[256,2048]{1,0:T(8,128)(2,1)S(1)}, bf16[256,2048]{1,0:T(8,128)(2,1)S(1)}, u32[]{:S(2)}, u32[]{:S(2)}) collective-permute-start(bf16[256,2048]{1,0:T(8,128)(2,1)S(1)} %copy-done.22), channel_id=1, source_target_pairs={{0,16},{4,20},{8,24},{12,28},{16,0},{20,4},{24,8},{28,12},{1,17},{... | collective-permute-start | bytes 3145736 | tf_op jit(solution)/shard_map/ppermute | solution.py:416
  236.6 115.1 %collective-permute-start.25 = (bf16[256,2048]{1,0:T(8,128)(2,1)S(1)}, bf16[256,2048]{1,0:T(8,128)(2,1)}, u32[]{:S(2)}, u32[]{:S(2)}) collective-permute-start(bf16[256,2048]{1,0:T(8,128)(2,1)S(1)} %copy-done.22), channel_id=1, source_target_pairs={{0,8},{4,12},{8,16},{12,20},{16,24},{20,28},{24,0},{28,4},{1,9},{5... | collective-permute-start | bytes 3145736 | tf_op jit(solution)/shard_map/ppermute | solution.py:416
  258.2 93.4 %collective-permute-start.34 = (bf16[256,2048]{1,0:T(8,128)(2,1)S(1)}, bf16[256,2048]{1,0:T(8,128)(2,1)S(1)}, u32[]{:S(2)}, u32[]{:S(2)}) collective-permute-start(bf16[256,2048]{1,0:T(8,128)(2,1)S(1)} %copy-done.23), channel_id=1, source_target_pairs={{0,24},{4,28},{8,0},{12,4},{16,8},{20,12},{24,16},{28,20},{1,25},{... | collective-permute-start | bytes 3145736 | tf_op jit(solution)/shard_map/ppermute | solution.py:416
  258.3 135.5 %collective-permute-start.33 = (bf16[256,2048]{1,0:T(8,128)(2,1)S(1)}, bf16[256,2048]{1,0:T(8,128)(2,1)}, u32[]{:S(2)}, u32[]{:S(2)}) collective-permute-start(bf16[256,2048]{1,0:T(8,128)(2,1)S(1)} %copy-done.23), channel_id=1, source_target_pairs={{0,16},{4,20},{8,24},{12,28},{16,0},{20,4},{24,8},{28,12},{1,17},{... | collective-permute-start | bytes 3145736 | tf_op jit(solution)/shard_map/ppermute | solution.py:416
  258.3 136.9 %collective-permute-start.32 = (bf16[256,2048]{1,0:T(8,128)(2,1)S(1)}, bf16[256,2048]{1,0:T(8,128)(2,1)}, u32[]{:S(2)}, u32[]{:S(2)}) collective-permute-start(bf16[256,2048]{1,0:T(8,128)(2,1)S(1)} %copy-done.23), channel_id=1, source_target_pairs={{0,8},{4,12},{8,16},{12,20},{16,24},{20,28},{24,0},{28,4},{1,9},{5... | collective-permute-start | bytes 3145736 | tf_op jit(solution)/shard_map/ppermute | solution.py:416
  350.1 45.1 %collective-permute-start.23 = (bf16[1024,512]{1,0:T(8,128)(2,1)S(1)}, bf16[1024,512]{1,0:T(8,128)(2,1)S(1)}, u32[]{:S(2)}, u32[]{:S(2)}) collective-permute-start(bf16[1024,512]{1,0:T(8,128)(2,1)S(1)} %get-tuple-element.167.refs_0_), channel_id=1, source_target_pairs={{0,2},{1,3},{2,0},{3,1},{4,6},{5,7},{6,4},{7,5},{8,10},{9,11},{10,... | collective-permute-start | bytes 3145736 | tf_op jit(solution)/shard_map/ppermute | solution.py:411
  351.7 44.1 %collective-permute-start.43 = (bf16[1024,512]{1,0:T(8,128)(2,1)S(1)}, bf16[1024,512]{1,0:T(8,128)(2,1)S(1)}, u32[]{:S(2)}, u32[]{:S(2)}) collective-permute-start(bf16[1024,512]{1,0:T(8,128)(2,1)S(1)} %collective-permute-done.42.refs_2_), channel_id=1, source_target_pairs={{0,1},{1,0},{2,3},{3,2},{4,5},{5,4},{6,7},{7,6},{8,9},{9,8},{10,11... | collective-permute-start | bytes 3145736 | tf_op jit(solution)/shard_map/ppermute | solution.py:411
  351.7 45.6 %collective-permute-start.31 = (bf16[256,2048]{1,0:T(8,128)(2,1)S(1)}, bf16[256,2048]{1,0:T(8,128)(2,1)S(1)}, u32[]{:S(2)}, u32[]{:S(2)}) collective-permute-start(bf16[256,2048]{1,0:T(8,128)(2,1)S(1)} %collective-permute-done.27.refs_4_), channel_id=1, source_target_pairs={{0,4},{4,0},{8,12},{12,8},{16,20},{20,16},{24,28},{28,24},{1,5},{5... | collective-permute-start | bytes 3145736 | tf_op jit(solution)/shard_map/ppermute | solution.py:411
  395.2 26.6 %collective-permute-start.24 = (bf16[1024,512]{1,0:T(8,128)(2,1)S(1)}, bf16[1024,512]{1,0:T(8,128)(2,1)S(1)}, u32[]{:S(2)}, u32[]{:S(2)}) collective-permute-start(bf16[1024,512]{1,0:T(8,128)(2,1)S(1)} %collective-permute-done.23.refs_2_), channel_id=1, source_target_pairs={{0,1},{1,0},{2,3},{3,2},{4,5},{5,4},{6,7},{7,6},{8,9},{9,8},{10,11... | collective-permute-start | bytes 3145736 | tf_op jit(solution)/shard_map/ppermute | solution.py:411
  395.7 46.7 %collective-permute-start.29 = (bf16[256,2048]{1,0:T(8,128)(2,1)}, bf16[256,2048]{1,0:T(8,128)(2,1)}, u32[]{:S(2)}, u32[]{:S(2)}) collective-permute-start(bf16[256,2048]{1,0:T(8,128)(2,1)} %collective-permute-done.25.refs_2_), channel_id=1, source_target_pairs={{0,4},{4,0},{8,12},{12,8},{16,20},{20,16},{24,28},{28,24},{1,5},{5... | collective-permute-start | bytes 3145736 | tf_op jit(solution)/shard_map/ppermute | solution.py:411
  397.3 67.6 %collective-permute-start.35 = (bf16[256,2048]{1,0:T(8,128)(2,1)S(1)}, bf16[256,2048]{1,0:T(8,128)(2,1)}, u32[]{:S(2)}, u32[]{:S(2)}) collective-permute-start(bf16[256,2048]{1,0:T(8,128)(2,1)S(1)} %copy-done.23), channel_id=1, source_target_pairs={{0,4},{4,0},{8,12},{12,8},{16,20},{20,16},{24,28},{28,24},{1,5},{5... | collective-permute-start | bytes 3145736 | tf_op jit(solution)/shard_map/ppermute | solution.py:411
  419.8 67.5 %collective-permute-start.38 = (bf16[256,2048]{1,0:T(8,128)(2,1)S(1)}, bf16[256,2048]{1,0:T(8,128)(2,1)}, u32[]{:S(2)}, u32[]{:S(2)}) collective-permute-start(bf16[256,2048]{1,0:T(8,128)(2,1)S(1)} %collective-permute-done.34.refs_4_), channel_id=1, source_target_pairs={{0,4},{4,0},{8,12},{12,8},{16,20},{20,16},{24,28},{28,24},{1,5},{5... | collective-permute-start | bytes 3145736 | tf_op jit(solution)/shard_map/ppermute | solution.py:411
  420.3 89.5 %collective-permute-start.37 = (bf16[256,2048]{1,0:T(8,128)(2,1)}, bf16[256,2048]{1,0:T(8,128)(2,1)}, u32[]{:S(2)}, u32[]{:S(2)}) collective-permute-start(bf16[256,2048]{1,0:T(8,128)(2,1)} %collective-permute-done.33.refs_3_), channel_id=1, source_target_pairs={{0,4},{4,0},{8,12},{12,8},{16,20},{20,16},{24,28},{28,24},{1,5},{5... | collective-permute-start | bytes 3145736 | tf_op jit(solution)/shard_map/ppermute | solution.py:411
  421.9 108.0 %collective-permute-start.36 = (bf16[256,2048]{1,0:T(8,128)(2,1)}, bf16[256,2048]{1,0:T(8,128)(2,1)}, u32[]{:S(2)}, u32[]{:S(2)}) collective-permute-start(bf16[256,2048]{1,0:T(8,128)(2,1)} %collective-permute-done.32.refs_2_), channel_id=1, source_target_pairs={{0,4},{4,0},{8,12},{12,8},{16,20},{20,16},{24,28},{28,24},{1,5},{5... | collective-permute-start | bytes 3145736 | tf_op jit(solution)/shard_map/ppermute | solution.py:411
  601.9 61.5 %collective-permute-start.44 = (bf16[1024,1024]{1,0:T(8,128)(2,1)}, bf16[1024,1024]{1,0:T(8,128)(2,1)}, u32[]{:S(2)}, u32[]{:S(2)}) collective-permute-start(bf16[1024,1024]{1,0:T(8,128)(2,1)} %get-tuple-element.79), channel_id=1, source_target_pairs={{0,1},{1,0},{2,3},{3,2},{4,5},{5,4},{6,7},{7,6},{8,9},{9,8},{10,11... | collective-permute-start | bytes 6291464 | tf_op jit(solution)/shard_map/ppermute | solution.py:411
  601.9 57.6 %collective-permute-start.72 = (bf16[256,2048]{1,0:T(8,128)(2,1)}, bf16[256,2048]{1,0:T(8,128)(2,1)}, u32[]{:S(2)}, u32[]{:S(2)}) collective-permute-start(bf16[256,2048]{1,0:T(8,128)(2,1)} %get-tuple-element.109), channel_id=1, source_target_pairs={{0,4},{4,0},{8,12},{12,8},{16,20},{20,16},{24,28},{28,24},{1,5},{5... | collective-permute-start | bytes 3145736 | tf_op jit(solution)/shard_map/ppermute | solution.py:411
  602.4 63.9 %collective-permute-start.74 = (bf16[256,2048]{1,0:T(8,128)(2,1)}, bf16[256,2048]{1,0:T(8,128)(2,1)}, u32[]{:S(2)}, u32[]{:S(2)}) collective-permute-start(bf16[256,2048]{1,0:T(8,128)(2,1)} %get-tuple-element.111), channel_id=1, source_target_pairs={{0,4},{4,0},{8,12},{12,8},{16,20},{20,16},{24,28},{28,24},{1,5},{5... | collective-permute-start | bytes 3145736 | tf_op jit(solution)/shard_map/ppermute | solution.py:411
  658.8 36.6 %collective-permute-start.39 = (bf16[1024,1024]{1,0:T(8,128)(2,1)}, bf16[1024,1024]{1,0:T(8,128)(2,1)S(1)}, u32[]{:S(2)}, u32[]{:S(2)}) collective-permute-start(bf16[1024,1024]{1,0:T(8,128)(2,1)} %get-tuple-element.74), channel_id=1, source_target_pairs={{0,1},{1,0},{2,3},{3,2},{4,5},{5,4},{6,7},{7,6},{8,9},{9,8},{10,11... | collective-permute-start | bytes 6291464 | tf_op jit(solution)/shard_map/ppermute | solution.py:411
  658.9 26.2 %collective-permute-start.76 = (bf16[256,2048]{1,0:T(8,128)(2,1)}, bf16[256,2048]{1,0:T(8,128)(2,1)S(1)}, u32[]{:S(2)}, u32[]{:S(2)}) collective-permute-start(bf16[256,2048]{1,0:T(8,128)(2,1)} %copy-done.36), channel_id=1, source_target_pairs={{0,4},{4,0},{8,12},{12,8},{16,20},{20,16},{24,28},{28,24},{1,5},{5... | collective-permute-start | bytes 3145736 | tf_op jit(solution)/shard_map/ppermute | solution.py:411
  659.5 78.2 %collective-permute-start.78 = (bf16[256,2048]{1,0:T(8,128)(2,1)}, bf16[256,2048]{1,0:T(8,128)(2,1)S(1)}, u32[]{:S(2)}, u32[]{:S(2)}) collective-permute-start(bf16[256,2048]{1,0:T(8,128)(2,1)} %copy-done.24), channel_id=1, source_target_pairs={{0,4},{4,0},{8,12},{12,8},{16,20},{20,16},{24,28},{28,24},{1,5},{5... | collective-permute-start | bytes 3145736 | tf_op jit(solution)/shard_map/ppermute | solution.py:411
  663.4 66.7 %collective-permute-start.79 = (bf16[256,2048]{1,0:T(8,128)(2,1)S(1)}, bf16[256,2048]{1,0:T(8,128)(2,1)S(1)}, u32[]{:S(2)}, u32[]{:S(2)}) collective-permute-start(bf16[256,2048]{1,0:T(8,128)(2,1)S(1)} %copy-done.35), channel_id=1, source_target_pairs={{0,4},{4,0},{8,12},{12,8},{16,20},{20,16},{24,28},{28,24},{1,5},{5... | collective-permute-start | bytes 3145736 | tf_op jit(solution)/shard_map/ppermute | solution.py:411
  685.1 67.4 %collective-permute-start.81 = (bf16[256,2048]{1,0:T(8,128)(2,1)S(1)}, bf16[256,2048]{1,0:T(8,128)(2,1)S(1)}, u32[]{:S(2)}, u32[]{:S(2)}) collective-permute-start(bf16[256,2048]{1,0:T(8,128)(2,1)S(1)} %copy-done.30), channel_id=1, source_target_pairs={{0,4},{4,0},{8,12},{12,8},{16,20},{20,16},{24,28},{28,24},{1,5},{5... | collective-permute-start | bytes 3145736 | tf_op jit(solution)/shard_map/ppermute | solution.py:411
  691.0 84.0 %collective-permute-start.83 = (bf16[256,2048]{1,0:T(8,128)(2,1)S(1)}, bf16[256,2048]{1,0:T(8,128)(2,1)S(1)}, u32[]{:S(2)}, u32[]{:S(2)}) collective-permute-start(bf16[256,2048]{1,0:T(8,128)(2,1)S(1)} %copy-done.28), channel_id=1, source_target_pairs={{0,4},{4,0},{8,12},{12,8},{16,20},{20,16},{24,28},{28,24},{1,5},{5... | collective-permute-start | bytes 3145736 | tf_op jit(solution)/shard_map/ppermute | solution.py:411
  696.7 37.6 %collective-permute-start.40 = (bf16[1024,512]{1,0:T(8,128)(2,1)S(1)}, bf16[1024,512]{1,0:T(8,128)(2,1)S(1)}, u32[]{:S(2)}, u32[]{:S(2)}) collective-permute-start(bf16[1024,512]{1,0:T(8,128)(2,1)S(1)} %add_convert_fusion.9), channel_id=1, source_target_pairs={{0,2},{1,3},{2,0},{3,1},{4,6},{5,7},{6,4},{7,5},{8,10},{9,11},{10,... | collective-permute-start | bytes 3145736 | tf_op jit(solution)/shard_map/ppermute | solution.py:411
  733.7 63.3 %collective-permute-start.85 = (bf16[256,2048]{1,0:T(8,128)(2,1)S(1)}, bf16[256,2048]{1,0:T(8,128)(2,1)S(1)}, u32[]{:S(2)}, u32[]{:S(2)}) collective-permute-start(bf16[256,2048]{1,0:T(8,128)(2,1)S(1)} %copy-done.26), channel_id=1, source_target_pairs={{0,4},{4,0},{8,12},{12,8},{16,20},{20,16},{24,28},{28,24},{1,5},{5... | collective-permute-start | bytes 3145736 | tf_op jit(solution)/shard_map/ppermute | solution.py:411
  734.3 63.2 %collective-permute-start.73 = (bf16[256,2048]{1,0:T(8,128)(2,1)S(1)}, bf16[256,2048]{1,0:T(8,128)(2,1)S(1)}, u32[]{:S(2)}, u32[]{:S(2)}) collective-permute-start(bf16[256,2048]{1,0:T(8,128)(2,1)S(1)} %add_convert_fusion.5), channel_id=1, source_target_pairs={{0,8},{4,12},{8,16},{12,20},{16,24},{20,28},{24,0},{28,4},{1,9},{5... | collective-permute-start | bytes 3145736 | tf_op jit(solution)/shard_map/ppermute | solution.py:416
  737.7 69.6 %collective-permute-start.75 = (bf16[256,2048]{1,0:T(8,128)(2,1)S(1)}, bf16[256,2048]{1,0:T(8,128)(2,1)S(1)}, u32[]{:S(2)}, u32[]{:S(2)}) collective-permute-start(bf16[256,2048]{1,0:T(8,128)(2,1)S(1)} %add_convert_fusion.4), channel_id=1, source_target_pairs={{0,16},{4,20},{8,24},{12,28},{16,0},{20,4},{24,8},{28,12},{1,17},{... | collective-permute-start | bytes 3145736 | tf_op jit(solution)/shard_map/ppermute | solution.py:416
  752.5 113.5 %collective-permute-start.77 = (bf16[256,2048]{1,0:T(8,128)(2,1)}, bf16[256,2048]{1,0:T(8,128)(2,1)}, u32[]{:S(2)}, u32[]{:S(2)}) collective-permute-start(bf16[256,2048]{1,0:T(8,128)(2,1)} %add_convert_fusion.3), channel_id=1, source_target_pairs={{0,24},{4,28},{8,0},{12,4},{16,8},{20,12},{24,16},{28,20},{1,25},{... | collective-permute-start | bytes 3145736 | tf_op jit(solution)/shard_map/ppermute | solution.py:416
  775.0 91.2 %collective-permute-start.49 = (bf16[1024,512]{1,0:T(8,128)(2,1)}, bf16[1024,512]{1,0:T(8,128)(2,1)S(1)}, u32[]{:S(2)}, u32[]{:S(2)}) collective-permute-start(bf16[1024,512]{1,0:T(8,128)(2,1)} %get-tuple-element.163.refs_0_), channel_id=1, source_target_pairs={{0,2},{1,3},{2,0},{3,1},{4,6},{5,7},{6,4},{7,5},{8,10},{9,11},{10,... | collective-permute-start | bytes 3145736 | tf_op jit(solution)/shard_map/ppermute | solution.py:411
  797.0 74.7 %collective-permute-start.80 = (bf16[256,2048]{1,0:T(8,128)(2,1)}, bf16[256,2048]{1,0:T(8,128)(2,1)}, u32[]{:S(2)}, u32[]{:S(2)}) collective-permute-start(bf16[256,2048]{1,0:T(8,128)(2,1)} %add_convert_fusion.2), channel_id=1, source_target_pairs={{0,8},{4,12},{8,16},{12,20},{16,24},{20,28},{24,0},{28,4},{1,9},{5... | collective-permute-start | bytes 3145736 | tf_op jit(solution)/shard_map/ppermute | solution.py:416
  797.5 96.9 %collective-permute-start.82 = (bf16[256,2048]{1,0:T(8,128)(2,1)}, bf16[256,2048]{1,0:T(8,128)(2,1)}, u32[]{:S(2)}, u32[]{:S(2)}) collective-permute-start(bf16[256,2048]{1,0:T(8,128)(2,1)} %add_convert_fusion.1), channel_id=1, source_target_pairs={{0,16},{4,20},{8,24},{12,28},{16,0},{20,4},{24,8},{28,12},{1,17},{... | collective-permute-start | bytes 3145736 | tf_op jit(solution)/shard_map/ppermute | solution.py:416
  807.3 87.8 %collective-permute-start.84 = (bf16[256,2048]{1,0:T(8,128)(2,1)}, bf16[256,2048]{1,0:T(8,128)(2,1)}, u32[]{:S(2)}, u32[]{:S(2)}) collective-permute-start(bf16[256,2048]{1,0:T(8,128)(2,1)} %add_convert_fusion), channel_id=1, source_target_pairs={{0,24},{4,28},{8,0},{12,4},{16,8},{20,12},{24,16},{28,20},{1,25},{... | collective-permute-start | bytes 3145736 | tf_op jit(solution)/shard_map/ppermute | solution.py:416
  866.1 33.1 %collective-permute-start.48 = (bf16[1024,512]{1,0:T(8,128)(2,1)}, bf16[1024,512]{1,0:T(8,128)(2,1)S(1)}, u32[]{:S(2)}, u32[]{:S(2)}) collective-permute-start(bf16[1024,512]{1,0:T(8,128)(2,1)} %get-tuple-element.163.refs_0_), channel_id=1, source_target_pairs={{0,1},{1,0},{2,3},{3,2},{4,5},{5,4},{6,7},{7,6},{8,9},{9,8},{10,11... | collective-permute-start | bytes 3145736 | tf_op jit(solution)/shard_map/ppermute | solution.py:411
  866.2 33.0 %collective-permute-start.50 = (bf16[1024,512]{1,0:T(8,128)(2,1)S(1)}, bf16[1024,512]{1,0:T(8,128)(2,1)S(1)}, u32[]{:S(2)}, u32[]{:S(2)}) collective-permute-start(bf16[1024,512]{1,0:T(8,128)(2,1)S(1)} %collective-permute-done.49.refs_2_), channel_id=1, source_target_pairs={{0,1},{1,0},{2,3},{3,2},{4,5},{5,4},{6,7},{7,6},{8,9},{9,8},{10,11... | collective-permute-start | bytes 3145736 | tf_op jit(solution)/shard_map/ppermute | solution.py:411
  955.2 43.6 %collective-permute-start.51 = (bf16[1024,1024]{1,0:T(8,128)(2,1)}, bf16[1024,1024]{1,0:T(8,128)(2,1)}, u32[]{:S(2)}, u32[]{:S(2)}) collective-permute-start(bf16[1024,1024]{1,0:T(8,128)(2,1)} %get-tuple-element.87), channel_id=1, source_target_pairs={{0,1},{1,0},{2,3},{3,2},{4,5},{5,4},{6,7},{7,6},{8,9},{9,8},{10,11... | collective-permute-start | bytes 6291464 | tf_op jit(solution)/shard_map/ppermute | solution.py:411
  967.0 30.9 %collective-permute-start.58 = (bf16[256,1536]{1,0:T(8,128)(2,1)S(1)}, bf16[256,1536]{1,0:T(8,128)(2,1)S(1)}, u32[]{:S(2)}, u32[]{:S(2)}) collective-permute-start(bf16[256,1536]{1,0:T(8,128)(2,1)S(1)} %get-tuple-element.93), channel_id=1, source_target_pairs={{0,4},{4,0},{8,12},{12,8},{16,20},{20,16},{24,28},{28,24},{1,5},{5... | collective-permute-start | bytes 2359304 | tf_op jit(solution)/shard_map/ppermute | solution.py:411
  980.6 76.4 %collective-permute-start.71 = (bf16[256,512]{1,0:T(8,128)(2,1)S(1)}, bf16[256,512]{1,0:T(8,128)(2,1)S(1)}, u32[]{:S(2)}, u32[]{:S(2)}) collective-permute-start(bf16[256,512]{1,0:T(8,128)(2,1)S(1)} %get-tuple-element.107), channel_id=1, source_target_pairs={{0,4},{4,0},{8,12},{12,8},{16,20},{20,16},{24,28},{28,24},{1,5},{5... | collective-permute-start | bytes 786440 | tf_op jit(solution)/shard_map/ppermute | solution.py:411
  982.2 40.7 %collective-permute-start.60 = (bf16[256,1536]{1,0:T(8,128)(2,1)S(1)}, bf16[256,1536]{1,0:T(8,128)(2,1)S(1)}, u32[]{:S(2)}, u32[]{:S(2)}) collective-permute-start(bf16[256,1536]{1,0:T(8,128)(2,1)S(1)} %get-tuple-element.95), channel_id=1, source_target_pairs={{0,4},{4,0},{8,12},{12,8},{16,20},{20,16},{24,28},{28,24},{1,5},{5... | collective-permute-start | bytes 2359304 | tf_op jit(solution)/shard_map/ppermute | solution.py:411
  996.3 39.3 %collective-permute-start.62 = (bf16[256,1536]{1,0:T(8,128)(2,1)S(1)}, bf16[256,1536]{1,0:T(8,128)(2,1)S(1)}, u32[]{:S(2)}, u32[]{:S(2)}) collective-permute-start(bf16[256,1536]{1,0:T(8,128)(2,1)S(1)} %get-tuple-element.97), channel_id=1, source_target_pairs={{0,4},{4,0},{8,12},{12,8},{16,20},{20,16},{24,28},{28,24},{1,5},{5... | collective-permute-start | bytes 2359304 | tf_op jit(solution)/shard_map/ppermute | solution.py:411
  997.9 85.7 %collective-permute-start.64 = (bf16[256,1536]{1,0:T(8,128)(2,1)S(1)}, bf16[256,1536]{1,0:T(8,128)(2,1)S(1)}, u32[]{:S(2)}, u32[]{:S(2)}) collective-permute-start(bf16[256,1536]{1,0:T(8,128)(2,1)S(1)} %get-tuple-element.99), channel_id=1, source_target_pairs={{0,4},{4,0},{8,12},{12,8},{16,20},{20,16},{24,28},{28,24},{1,5},{5... | collective-permute-start | bytes 2359304 | tf_op jit(solution)/shard_map/ppermute | solution.py:411
  998.7 61.7 %collective-permute-start.66 = (bf16[256,512]{1,0:T(8,128)(2,1)S(1)}, bf16[256,512]{1,0:T(8,128)(2,1)S(1)}, u32[]{:S(2)}, u32[]{:S(2)}) collective-permute-start(bf16[256,512]{1,0:T(8,128)(2,1)S(1)} %add_convert_fusion.16), channel_id=1, source_target_pairs={{0,8},{4,12},{8,16},{12,20},{16,24},{20,28},{24,0},{28,4},{1,9},{5... | collective-permute-start | bytes 786440 | tf_op jit(solution)/shard_map/ppermute | solution.py:416
  1022.9 46.9 %collective-permute-start.52 = (bf16[1024,512]{1,0:T(8,128)(2,1)S(1)}, bf16[1024,512]{1,0:T(8,128)(2,1)S(1)}, u32[]{:S(2)}, u32[]{:S(2)}) collective-permute-start(bf16[1024,512]{1,0:T(8,128)(2,1)S(1)} %add_convert_fusion.6), channel_id=1, source_target_pairs={{0,2},{1,3},{2,0},{3,1},{4,6},{5,7},{6,4},{7,5},{8,10},{9,11},{10,... | collective-permute-start | bytes 3145736 | tf_op jit(solution)/shard_map/ppermute | solution.py:411
  1035.6 34.2 %collective-permute-start.68 = (bf16[256,512]{1,0:T(8,128)(2,1)S(1)}, bf16[256,512]{1,0:T(8,128)(2,1)S(1)}, u32[]{:S(2)}, u32[]{:S(2)}) collective-permute-start(bf16[256,512]{1,0:T(8,128)(2,1)S(1)} %add_convert_fusion.15), channel_id=1, source_target_pairs={{0,16},{4,20},{8,24},{12,28},{16,0},{20,4},{24,8},{28,12},{1,17},{... | collective-permute-start | bytes 786440 | tf_op jit(solution)/shard_map/ppermute | solution.py:416
  1060.4 29.5 %collective-permute-start.59 = (bf16[256,1536]{1,0:T(8,128)(2,1)S(1)}, bf16[256,1536]{1,0:T(8,128)(2,1)S(1)}, u32[]{:S(2)}, u32[]{:S(2)}) collective-permute-start(bf16[256,1536]{1,0:T(8,128)(2,1)S(1)} %add_convert_fusion.13), channel_id=1, source_target_pairs={{0,8},{4,12},{8,16},{12,20},{16,24},{20,28},{24,0},{28,4},{1,9},{5... | collective-permute-start | bytes 2359304 | tf_op jit(solution)/shard_map/ppermute | solution.py:416
  1069.8 56.0 %collective-permute-start.61 = (bf16[256,1536]{1,0:T(8,128)(2,1)S(1)}, bf16[256,1536]{1,0:T(8,128)(2,1)S(1)}, u32[]{:S(2)}, u32[]{:S(2)}) collective-permute-start(bf16[256,1536]{1,0:T(8,128)(2,1)S(1)} %add_convert_fusion.12), channel_id=1, source_target_pairs={{0,16},{4,20},{8,24},{12,28},{16,0},{20,4},{24,8},{28,12},{1,17},{... | collective-permute-start | bytes 2359304 | tf_op jit(solution)/shard_map/ppermute | solution.py:416
  1069.8 56.0 %collective-permute-start.63 = (bf16[256,1536]{1,0:T(8,128)(2,1)S(1)}, bf16[256,1536]{1,0:T(8,128)(2,1)S(1)}, u32[]{:S(2)}, u32[]{:S(2)}) collective-permute-start(bf16[256,1536]{1,0:T(8,128)(2,1)S(1)} %add_convert_fusion.11), channel_id=1, source_target_pairs={{0,24},{4,28},{8,0},{12,4},{16,8},{20,12},{24,16},{28,20},{1,25},{... | collective-permute-start | bytes 2359304 | tf_op jit(solution)/shard_map/ppermute | solution.py:416
  1082.1 50.7 %collective-permute-start.54 = (f32[2,1024]{1,0:T(2,128)S(1)}, f32[2,1024]{1,0:T(2,128)S(1)}, u32[]{:S(2)}, u32[]{:S(2)}) collective-permute-start(f32[2,1024]{1,0:T(2,128)S(1)} %fusion.23), channel_id=1, source_target_pairs={{0,2},{1,3},{2,0},{3,1},{4,6},{5,7},{6,4},{7,5},{8,10},{9,11},{10,... | collective-permute-start | bytes 24584 | tf_op jit(solution)/shard_map/ppermute | solution.py:411
  (108 other events, 1960.7 us)

commit v3 on v2

--- a/solution.py
+++ b/solution.py
@@ -17,7 +17,8 @@
 far = -1e33
 NT = (((1,), (1,)), ((), ()))
 TN = (((0,), (0,)), ((), ()))
-VMEM_LIMIT = 48 << 20
+VMEM_LIMIT = 56 << 20
+CHEAP = 64
 f32 = jnp.float32
 bf16 = jnp.bfloat16
 
@@ -93,11 +94,11 @@
             jax.ShapeDtypeStruct((mixed.shape[0], 2 * HD * pairs), bf16),
             jax.ShapeDtypeStruct((seqs * pairs, 2, length), f32),
         ],
-        compiler_params=pltpu.CompilerParams(vmem_limit_bytes=40 << 20),
+        compiler_params=pltpu.CompilerParams(vmem_limit_bytes=VMEM_LIMIT),
         cost_estimate=pl.CostEstimate(
-            flops=8 * seqs * pairs * length * length * HD * 3,
-            bytes_accessed=4 * mixed.size,
-            transcendentals=seqs * pairs * length * length,
+            flops=16 * seqs * pairs * length * length * HD // CHEAP,
+            bytes_accessed=4 * mixed.size // CHEAP,
+            transcendentals=seqs * pairs * length * length // CHEAP,
         ),
         name="attend_forward",
     )(slopes, starts[:, :, None], mixed, mixed, mixed)
@@ -200,17 +201,21 @@
             ],
         ),
         out_shape=[out, out, out, sums, sums],
-        compiler_params=pltpu.CompilerParams(vmem_limit_bytes=40 << 20),
+        compiler_params=pltpu.CompilerParams(vmem_limit_bytes=VMEM_LIMIT),
         cost_estimate=pl.CostEstimate(
-            flops=20 * seqs * pairs * length * length * HD * 2,
-            bytes_accessed=14 * grads.size,
-            transcendentals=seqs * pairs * length * length,
+            flops=40 * seqs * pairs * length * length * HD // CHEAP,
+            bytes_accessed=14 * grads.size // CHEAP,
+            transcendentals=seqs * pairs * length * length // CHEAP,
         ),
         name="attend_backward",
     )(slopes, starts[:, None, :], logs, mixed, mixed, mixed, grads)
 
 
 def resident(shape):
+    return pl.BlockSpec(shape, lambda *_: (0,) * len(shape), pipeline_mode=pl.Buffered(1))
+
+
+def kept_out(shape):
     return pl.BlockSpec(shape, lambda *_: (0,) * len(shape))
 
 
@@ -232,113 +237,124 @@
         ),
         out_shape=[jax.ShapeDtypeStruct(s, t) for s, t, _ in outs],
         compiler_params=pltpu.CompilerParams(vmem_limit_bytes=VMEM_LIMIT),
-        cost_estimate=pl.CostEstimate(flops=flops, bytes_accessed=moved, transcendentals=0),
+        cost_estimate=pl.CostEstimate(
+            flops=flops // CHEAP, bytes_accessed=moved // CHEAP, transcendentals=0
+        ),
         name=name,
     )(*prefetch, *[a for a, _ in ins])
 
 
-def times_rows(x, ws, extras, outs, finish, name, tn, tm=256):
+def times_rows(x, ws, extras, outs, finish, name, tn, window=None, joins=()):
     tokens, depth = x.shape
-    width = ws[0].shape[1]
-    tn, tm = min(tn, width), min(tm, tokens)
-    n_ws, n_ex = len(ws), len(extras)
+    first, width = window or (0, ws[0].shape[1])
+    first, tiles = first // tn, width // tn
+    n_ws, n_ex, n_out = len(ws), len(extras), len(outs)
+    steps = ws[0].shape[1] // tn if joins else tiles
 
     def kernel(*refs):
         x_ref, w_refs = refs[0], refs[1 : 1 + n_ws]
         extra, out = refs[1 + n_ws : 1 + n_ws + n_ex], refs[1 + n_ws + n_ex :]
-        rows = pl.ds(pl.multiple_of(pl.program_id(1) * tm, tm), tm)
-        acc = jnp.dot(x_ref[rows, :], flat_rows(w_refs), preferred_element_type=f32)
-        finish(acc, extra, out)
-
-    def spec(shape):
-        if shape[0] == 1:
-            return pl.BlockSpec((1, tn), lambda n, m: (0, n))
-        return pl.BlockSpec((tm, tn), lambda n, m: (m, n))
-
-    ins = [(x, resident(x.shape))]
-    ins += [(w, pl.BlockSpec((w.shape[0], tn), lambda n, m: (0, n))) for w in ws]
-    ins += [(e, spec(e.shape)) for e in extras]
-    return matmul_call(
-        kernel,
-        (width // tn, tokens // tm),
-        ins,
-        [(s, t, spec(s)) for s, t in outs],
-        [],
-        2 * tokens * depth * width,
-        name,
-    )
-
-
-def times_columns(xs, ws, slots, name, tm=256):
+        for places, joined in zip(joins, out[n_out:]):
+            at = 0
+            for i in places:
+                joined[at : at + ws[i].shape[0], :] = w_refs[i][...]
+                at += ws[i].shape[0]
+
+        def multiply():
+            acc = jnp.dot(x_ref[...], flat_rows(w_refs), preferred_element_type=f32)
+            finish(acc, extra, out[:n_out])
+
+        if steps == tiles:
+            multiply()
+        else:
+            pl.when(pl.program_id(0) < tiles)(multiply)
+
+    def spec(rows):
+        return pl.BlockSpec((rows, tn), lambda n: (0, jnp.minimum(n, tiles - 1)))
+
+    def tile(rows):
+        return pl.BlockSpec((rows, tn), lambda n: (0, n + first))
+
+    ins = [(x, resident(x.shape))] + [(w, tile(w.shape[0])) for w in ws]
+    ins += [(e, spec(e.shape[0])) for e in extras]
+    results = [(s, t, spec(s[0])) for s, t in outs]
+    for places in joins:
+        rows = sum(ws[i].shape[0] for i in places)
+        results.append(((rows, ws[0].shape[1]), bf16, tile(rows)))
+    return matmul_call(kernel, (steps,), ins, results, [], 2 * tokens * depth * width, name)
+
+
+def times_columns(xs, ws, order, side, dtype, name, first=0, added=None, block=0):
     tokens = xs[0].shape[0]
-    tm = min(tm, tokens)
-    blocks = sum(w.shape[0] for w in ws) // BLOCK
-    half = blocks // 2
+    count = order.shape[1]
     n_xs = len(xs)
-
-    def kernel(slot_ref, *refs):
-        x_refs, w_refs = refs[:n_xs], refs[n_xs : n_xs + len(ws)]
-        sent_ref, kept_ref = refs[n_xs + len(ws) :]
+    width = sum(x.shape[1] for x in xs)
+
+    def kernel(order_ref, side_ref, *refs):
+        x_refs, w_refs, rest, out_ref = refs[:n_xs], refs[n_xs : n_xs + 2], refs[n_xs + 2 :], refs[-1]
         x = jnp.concatenate([r[...] for r in x_refs], axis=1)
-        at = 0
-        for w_ref in w_refs:
-            for r0 in range(0, w_ref.shape[0], BLOCK):
-                acc = lax.dot_general(x, w_ref[r0 : r0 + BLOCK, :], NT, preferred_element_type=f32)
-                slot = slot_ref[at]
-
-                @pl.when(slot < half)
-                def _():
-                    place = pl.ds(pl.multiple_of(slot * BLOCK, BLOCK), BLOCK)
-                    sent_ref[:, place] = acc.astype(bf16)
-
-                @pl.when(slot >= half)
-                def _():
-                    place = pl.ds(pl.multiple_of((slot - half) * BLOCK, BLOCK), BLOCK)
-                    kept_ref[:, place] = acc
-
-                at += 1
-
-    ins = [(x, pl.BlockSpec((tm, x.shape[1]), lambda m, *_: (m, 0))) for x in xs]
-    ins += [(w, resident(w.shape)) for w in ws]
-    out_spec = pl.BlockSpec((tm, half * BLOCK), lambda m, *_: (m, 0))
-    return matmul_call(
-        kernel,
-        (tokens // tm,),
-        ins,
-        [((tokens, half * BLOCK), bf16, out_spec), ((tokens, half * BLOCK), f32, out_spec)],
-        [],
-        2 * tokens * blocks * BLOCK * ws[0].shape[1],
-        name,
-        prefetch=(slots,),
-    )
-
-
-def weight_parts(a, first, count, gs, dtype, name):
-    tokens = a.shape[0]
-    width = sum(g.shape[1] for g in gs)
-    n_gs = len(gs)
-
-    def kernel(a_ref, *refs):
-        g_refs, out_refs = refs[:n_gs], refs[n_gs:]
-        g = jnp.concatenate([r[...] for r in g_refs], axis=1)
-        acc = lax.dot_general(a_ref[...], g, TN, preferred_element_type=f32).astype(dtype)
-        for i in range(count):
-
-            @pl.when(pl.program_id(0) == i)
-            def _(i=i):
-                out_refs[i][...] = acc
-
-    ins = [(a, pl.BlockSpec((tokens, BLOCK), lambda i: (0, first + i)))]
-    ins += [(g, resident(g.shape)) for g in gs]
+        for i, w_ref in enumerate(w_refs):
+            acc = lax.dot_general(x, w_ref[...], NT, preferred_element_type=f32)
+            place = side_ref[0] if i == 0 else 1 - side_ref[0]
+            place = pl.ds(pl.multiple_of(place * BLOCK, BLOCK), BLOCK)
+            if added is not None:
+                acc = acc + rest[0][:, place].astype(f32)
+            out_ref[:, place] = acc.astype(dtype)
+
+    def rows(i):
+        return pl.BlockSpec((BLOCK, width), lambda n, order_ref, _: (order_ref[i, n], first // width))
+
+    def pair(start):
+        return pl.BlockSpec((tokens, 2 * BLOCK), lambda n, *_: (0, start + n))
+
+    ins = [(x, resident(x.shape)) for x in xs]
+    ins += [(w, rows(i)) for i, w in enumerate(ws)]
+    ins += [] if added is None else [(added, pair(block))]
     return matmul_call(
         kernel,
         (count,),
         ins,
-        [((BLOCK, width), dtype, resident((BLOCK, width))) for _ in range(count)],
+        [((tokens, 2 * BLOCK * count), dtype, pair(0))],
         [],
-        2 * tokens * BLOCK * count * width,
+        4 * tokens * BLOCK * count * width,
         name,
-    )
+        prefetch=(order, side),
+    )[0]
+
+
+def weight_rows(a, order, gs, name, added=(), apart=False, dtype=bf16):
+    tokens = a.shape[0]
+    width = sum(g.shape[1] for g in gs)
+    count = order.shape[0]
+    n_gs = len(gs)
+
+    def kernel(order_ref, a_ref, *refs):
+        g_refs, added_refs = refs[:n_gs], refs[n_gs : n_gs + len(added)]
+        out_refs = refs[n_gs + len(added) :]
+        g = jnp.concatenate([r[...] for r in g_refs], axis=1)
+        acc = lax.dot_general(a_ref[...], g, TN, preferred_element_type=f32)
+        if not apart and not added:
+            out_refs[0][...] = acc.astype(dtype)
+            return
+        for i in range(count):
+
+            @pl.when(pl.program_id(0) == i)
+            def _(i=i):
+                total = acc + added_refs[i][...].astype(f32) if added else acc
+                out_refs[i if apart else 0][...] = total.astype(dtype)
+
+    block = pl.BlockSpec((BLOCK, width), lambda i, *_: (i, 0))
+    ins = [(a, pl.BlockSpec((tokens, BLOCK), lambda i, order_ref: (0, order_ref[i])))]
+    ins += [(g, resident(g.shape)) for g in gs]
+    ins += [(b, resident(b.shape)) for b in added]
+    if apart:
+        outs = [((BLOCK, width), dtype, kept_out((BLOCK, width)))] * count
+    else:
+        outs = [((count * BLOCK, width), dtype, block)]
+    done = matmul_call(
+        kernel, (count,), ins, outs, [], 2 * tokens * BLOCK * count * width, name, prefetch=(order,)
+    )
+    return done if apart else done[0]
 
 
 def place_blocks(values, place_ref, out_ref):
@@ -416,18 +432,6 @@
     return lax.ppermute(x, "row", [(i, (i + 2 * steps) % count) for i in range(count)])
 
 
-def gather_columns(x):
-    near, across = swap(x, "col", 1), swap(x, "col", 2)
-    return [x, near, across, swap(across, "col", 1)]
-
-
-def sum_columns(sent, kept):
-    half = kept.shape[1] // 2
-    got = swap(sent, "col", 1)
-    across = swap((kept[:, half:] + got[:, half:].astype(f32)).astype(bf16), "col", 2)
-    return kept[:, :half] + got[:, :half].astype(f32) + across.astype(f32)
-
-
 def sum_col_stats(stats):
     stats = stats + swap(stats, "col", 1)
     return stats + swap(stats, "col", 2)
@@ -441,32 +445,42 @@
     return x
 
 
-def gather_rows(w, stepped):
-    if not stepped:
-        return [lax.all_gather(w, "row", axis=0, tiled=True)]
-    own = [w] + [turn(w, k) for k in range(1, lax.axis_size("row") // 2)]
-    return own + [swap(v, "row", 1) for v in own]
-
-
-def sum_weight(a, gs, stepped, name):
-    if not stepped:
-        whole = weight_parts(a, 0, a.shape[1] // BLOCK, gs, f32, name)
-        return lax.psum_scatter(
-            jnp.concatenate(whole, axis=0), "row", scatter_dimension=0, tiled=True
-        )
-    count = lax.axis_size("row") // 2
-    other = weight_parts(a, count, count, gs, bf16, name + "_other")
-    got = [None] * count
-    for k in reversed(range(count)):
-        got[k] = swap(other[k], "row", 1)
-    mine = weight_parts(a, 0, count, gs, f32, name + "_mine")
-    total = None
-    for k in reversed(range(count)):
-        term = mine[k] + got[k].astype(f32)
-        if k:
-            term = turn(term.astype(bf16), -k).astype(f32)
-        total = term if total is None else total + term
-    return total
+def after(x, *first):
+    return lax.optimization_barrier((x,) + first)[0] if first else x
+
+
+def outer_groups():
+    outer = lax.axis_size("row") // 2
+    return [[2 * i + inner for i in range(outer)] for inner in range(2)]
+
+
+def find(ids, wanted):
+    at = jnp.arange(ids.shape[0])
+    return jnp.sum(jnp.where(ids[None, :] == wanted[:, None], at[None, :], 0), axis=1).astype(
+        jnp.int32
+    )
+
+
+def gather_whole(w):
+    return [lax.all_gather(w, "row", axis=0, tiled=True)]
+
+
+def gather_outer(w):
+    return lax.all_gather(w, "row", axis=0, tiled=True, axis_index_groups=outer_groups())
+
+
+class Clock:
+    def __init__(self):
+        self.now, self.new = [], []
+
+    def at(self, x):
+        return after(x, *self.now)
+
+    def put(self, *xs):
+        self.new += xs
+
+    def tick(self):
+        self.now, self.new = self.new, []
 
 
 def on_device(
@@ -489,59 +503,185 @@
     full = width * cols
     heads = width // HD
     stepped = full // rows == BLOCK and rows == 2 * cols
-    blocks = full // BLOCK
-    per_col = width // BLOCK
+    blocks, per_col = full // BLOCK, width // BLOCK
     at = jnp.arange(blocks)
+    ours = per_col * ((at // per_col) ^ col) + at % per_col
+    place, side = row // 2, row % 2
+    steps = jnp.arange(max(rows // 2, 1))
+    back = (place - steps) % (rows // 2)
     if stepped:
-        outer, inner = row // 2, row % 2
-        ids = 2 * ((outer - at % (rows // 2)) % (rows // 2)) + (inner ^ (at // (rows // 2)))
-        mine = (at // per_col) ^ col
-        places = ((at % per_col) ^ inner) * (rows // 2) + (outer - mine) % (rows // 2)
+        ids_attend = jnp.concatenate([2 * back + side, 2 * back + 1 - side])
+        ids_expand = jnp.concatenate([2 * steps + side, 2 * steps + 1 - side])
+        ids_contract = jnp.stack([2 * steps + side, 2 * steps + 1 - side], axis=1).reshape(-1)
     else:
-        ids = at
-        places = ((at // per_col) ^ col) * per_col + at % per_col
-    away = (ids // per_col) ^ col
-    slots = (away // 2 + (1 - away % 2) * 2) * per_col + ids % per_col
-    places, slots = places.astype(jnp.int32), slots.astype(jnp.int32)
+        ids_attend = ids_expand = ids_contract = at
+        side = 0 * side
+    sides = jnp.reshape(side, (1,)).astype(jnp.int32)
+    away = jnp.array([1, 3, 0, 2]) ^ col
+    clock = Clock()
+    at_now, put, tick = clock.at, clock.put, clock.tick
+
+    def columns_order(ids, ws):
+        want = jnp.stack([2 * away + side, 2 * away + 1 - side]).reshape(-1)
+        order = find(ids, want).reshape(2, -1)
+        return order if len(ws) == 1 else order % (blocks // 2)
+
+    def two(ws):
+        return ws if len(ws) == 2 else [ws[0], ws[0]]
+
+    def columns_sent(xs, ws, ids, name, first=0):
+        order = columns_order(ids, ws)
+        xs = [at_now(xs[0])] + xs[1:]
+        sent = times_columns(xs, two(ws), order[:, :2], sides, bf16, name + "_sent", first)
+        return swap(sent, "col", 1)
+
+    def columns_part(xs, ws, ids, got, name, first=0):
+        order = columns_order(ids, ws)[:, 3:]
+        return times_columns(xs, two(ws), order, sides, bf16, name + "_part", first, got, 1)
+
+    def columns_base(xs, ws, ids, got, name, first=0):
+        order = columns_order(ids, ws)[:, 2:3]
+        xs = [at_now(xs[0])] + xs[1:]
+        return times_columns(xs, two(ws), order, sides, f32, name + "_base", first, got, 0)
+
+    def weight_other(a, ids, gs, name):
+        if not stepped:
+            return [weight_rows(at_now(a), find(ids, at), gs, name, dtype=f32)]
+        other = find(ids, 2 * steps + 1 - side)
+        return weight_rows(at_now(a), other, gs, name + "_other", apart=True)
+
+    def move(parts, k):
+        return swap(at_now(parts[k]), "row", 1) if stepped else parts[0]
+
+    def weight_mine(a, ids, gs, got, name):
+        if not stepped:
+            return lax.psum_scatter(got[0], "row", scatter_dimension=0, tiled=True)
+        mine = find(ids, 2 * steps + side)
+        total = weight_rows(at_now(a), mine, gs, name + "_mine", got)
+        return lax.psum_scatter(
+            total, "row", scatter_dimension=0, tiled=True, axis_index_groups=outer_groups()
+        ).astype(f32)
 
     head_ids = (col * heads + jnp.arange(heads)).astype(f32)
     slopes = jnp.exp2(-8.0 * (head_ids + 1.0) / (heads * cols))
     starts = jnp.sum(segments[:, None, :] < segments[:, :, None], axis=2).astype(jnp.int32)
-
-    full_mix = gather_rows(mixing.reshape(mixing.shape[0], -1), stepped)
-    token_parts = gather_columns(tokens)
-    norms = gather_columns(jnp.concatenate([gains, shifts], axis=0))
+    places_attend, places_expand = find(ids_attend, ours), find(ids_expand, ours)
+    places_contract = find(ids_contract, ours)
+    mix_width = 3 * width
+    mixed_bias = jnp.concatenate([biases[0:1], jnp.zeros((1, width), f32), biases[1:2]], axis=1)
+
+    attend_rows = jnp.concatenate([mixing.reshape(mixing.shape[0], -1), projection], axis=1)
+    small = jnp.concatenate([gains, shifts], axis=0)
+    put(attend_rows)
+    tick()
+    if stepped:
+        own, near = [attend_rows], []
+    else:
+        whole = gather_whole(attend_rows)[0]
+        own, near = [whole[: full // 2]], [whole[full // 2 :]]
+        full_expand = gather_whole(expand)
+        full_contract = gather_whole(contract)
+
+    def weight_step(k):
+        if stepped:
+            ready = at_now(own[k])
+            near.append(swap(ready, "row", 1))
+            put(near[k])
+            if k + 1 < rows // 2:
+                own.append(turn(ready, 1))
+                put(own[k + 1])
+
+    weight_step(0)
+    tokens_now = at_now(tokens)
+    token_parts = [tokens, swap(tokens_now, "col", 1), swap(tokens_now, "col", 2)]
+    put(*token_parts[1:])
+    tick()
+
+    weight_step(1)
+    cot_now = at_now(cotangent)
+    cot_parts = [cotangent, swap(cot_now, "col", 1), swap(cot_now, "col", 2)]
+    token_parts.append(swap(at_now(token_parts[2]), "col", 1))
+    put(*cot_parts[1:], token_parts[3])
+    if stepped:
+        expand_mine = gather_outer(at_now(expand))
+    tick()
+
+    weight_step(2)
+    small_now = at_now(small)
+    norms = [small, swap(small_now, "col", 1), swap(small_now, "col", 2)]
+    cot_parts.append(swap(at_now(cot_parts[2]), "col", 1))
+    put(*norms[1:], cot_parts[3])
+    tick()
+
+    weight_step(3)
+    norms.append(swap(at_now(norms[2]), "col", 1))
     norms = jnp.concatenate(norms, axis=1)
-    full_proj = gather_rows(projection, stepped)
-    full_expand = gather_rows(expand, stepped)
-    full_contract = gather_rows(contract, stepped)
-    cot_parts = gather_columns(cotangent)
-
     first_full, first_mean, first_scale = normalize(
-        token_parts, norms[0:1], norms[2:3], places, "first_norm"
-    )
-    mixed_bias = jnp.concatenate([biases[0:1], jnp.zeros((1, width), f32), biases[1:2]], axis=1)
+        token_parts, norms[0:1], norms[2:3], places_attend, "first_norm"
+    )
+    cot_full = lay_out([at_now(cot_parts[0])] + cot_parts[1:], places_contract, "cotangent_rows")
+    put(first_full, cot_full)
+    tick()
 
     def add_bias(acc, extra, out):
         out[0][...] = (acc + extra[0][...]).astype(bf16)
 
-    (mixed,) = times_rows(
-        first_full,
-        full_mix,
+    if stepped:
+        contract_pair = jnp.concatenate([contract, swap(at_now(contract), "row", 1)], axis=0)
+        put(contract_pair, expand_mine)
+    mixed, *full_attend = times_rows(
+        at_now(first_full),
+        own + near,
         [mixed_bias],
-        [((tokens_here, 3 * width), bf16)],
+        [((tokens_here, mix_width), bf16)],
         add_bias,
         "mix",
-        tn=512,
+        tn=width,
+        window=(0, mix_width),
+        joins=[range(len(own)), range(len(own), len(own) + len(near))],
     )
     attended, logs = attend_forward(mixed, starts, slopes, seqs)
+    put(attended)
+    tick()
+
+    if stepped:
+        full_contract = [gather_outer(at_now(contract_pair))]
+        expand_near = []
+
+    def expand_step(k):
+        if stepped:
+            block = expand_mine[k * BLOCK : (k + 1) * BLOCK]
+            expand_near.append(swap(at_now(block), "row", 1))
+            put(expand_near[k])
+
+    expand_step(0)
+    got = columns_sent([attended], full_attend, ids_attend, "project", mix_width)
+    part = columns_part([attended], full_attend, ids_attend, got, "project", mix_width)
+    put(part)
+    tick()
+
+    expand_step(1)
+    across = swap(at_now(part), "col", 2)
+    base = columns_base([attended], full_attend, ids_attend, got, "project", mix_width)
     resid = tokens.astype(f32)
-    middle = resid + (
-        sum_columns(*times_columns([attended], full_proj, slots, "project")) + biases[2]
-    )
+    middle = resid + (base + across.astype(f32) + biases[2])
+    middle_low = middle.astype(bf16)
+    put(middle_low)
+    tick()
+
+    expand_step(2)
+    middle_now = at_now(middle_low)
+    middle_parts = [middle_low, swap(middle_now, "col", 1), swap(middle_now, "col", 2)]
+    put(*middle_parts[1:])
+    tick()
+
+    expand_step(3)
+    middle_parts.append(swap(at_now(middle_parts[2]), "col", 1))
     second_full, second_mean, second_scale = normalize(
-        gather_columns(middle.astype(bf16)), norms[1:2], norms[3:4], places, "second_norm"
-    )
+        middle_parts, norms[1:2], norms[3:4], places_expand, "second_norm"
+    )
+    put(second_full)
+    tick()
 
     def activate(acc, extra, out):
         hidden = acc + extra[0][...]
@@ -550,33 +690,34 @@
         out[1][...] = bell + hidden * (jnp.exp(-0.5 * hidden * hidden) * inverse_root)
 
     hidden_shape = (tokens_here, expand.shape[1])
-    active, slope = times_rows(
-        second_full,
-        full_expand,
+    active, slope, *joined = times_rows(
+        at_now(second_full),
+        [expand_mine] + expand_near if stepped else full_expand,
         [thresholds[None]],
         [(hidden_shape, bf16), (hidden_shape, f32)],
         activate,
         "expand",
         tn=512,
-    )
-    cot_full = lay_out(cot_parts, places, "cotangent_rows")
-    contract_grad = sum_weight(cot_full, [active], stepped, "contract_grad")
+        joins=[range(1, 1 + rows // 2)] if stepped else [],
+    )
+    if stepped:
+        full_expand = [expand_mine] + joined
+    contract_other = weight_other(cot_full, ids_contract, [active], "contract_grad")
+    put(active, *contract_other)
+    tick()
+
+    contract_got = [move(contract_other, 0)]
+    put(contract_got[0], *full_contract)
+    tick()
 
     def back_activate(acc, extra, out):
         grad = (acc * extra[0][...]).astype(bf16)
         out[0][...] = grad
-        total = jnp.sum(grad.astype(f32), axis=0, keepdims=True)
-
-        @pl.when(pl.program_id(1) == 0)
-        def _():
-            out[1][...] = total
-
-        @pl.when(pl.program_id(1) > 0)
-        def _():
-            out[1][...] += total
-
+        out[1][...] = jnp.sum(grad.astype(f32), axis=0, keepdims=True)
+
+    contract_got.append(move(contract_other, 1))
     hidden_grad, thresholds_part = times_rows(
-        cot_full,
+        at_now(cot_full),
         full_contract,
         [slope],
         [(hidden_shape, bf16), ((1, hidden_shape[1]), f32)],
@@ -584,11 +725,18 @@
         "contract_back",
         tn=512,
     )
-    second_back = sum_columns(*times_columns([hidden_grad], full_expand, slots, "expand_back"))
-    layer_out = (
-        middle + (sum_columns(*times_columns([active], full_contract, slots, "contract")) + biases[3])
-    ).astype(bf16)
-    expand_grad = sum_weight(second_full, [hidden_grad], stepped, "expand_grad")
+    got = columns_sent([hidden_grad], full_expand, ids_expand, "expand_back")
+    part = columns_part([hidden_grad], full_expand, ids_expand, got, "expand_back")
+    put(contract_got[1], part)
+    tick()
+
+    contract_got.append(move(contract_other, 2))
+    across = swap(at_now(part), "col", 2)
+    base = columns_base([hidden_grad], full_expand, ids_expand, got, "expand_back")
+    expand_other = weight_other(second_full, ids_expand, [hidden_grad], "expand_grad")
+    second_back = base + across.astype(f32)
+    put(contract_got[2], second_back, *expand_other)
+    tick()
 
     def norm_back(upstream, centred, scale, gain):
         scaled = upstream * gain
@@ -600,39 +748,81 @@
         )
         return result, jnp.sum(upstream * centred, axis=0), jnp.sum(upstream, axis=0)
 
+    contract_got.append(move(contract_other, 3))
     second_centred = (middle - second_mean) * second_scale
     second_input, second_gain, second_shift = norm_back(
-        second_back, second_centred, second_scale, gains[1]
+        at_now(second_back), second_centred, second_scale, gains[1]
     )
     cot_float = cotangent.astype(f32)
     middle_grad = cot_float + second_input
     branch_grad = middle_grad.astype(bf16)
-    branch_full = lay_out(gather_columns(branch_grad), places, "branch_rows")
+    branch_parts = [branch_grad, swap(branch_grad, "col", 1), swap(branch_grad, "col", 2)]
+    out_got = columns_sent([after(active, branch_grad)], full_contract, ids_contract, "contract")
+    put(contract_got[3], *branch_parts[1:])
+    tick()
 
     def store(acc, extra, out):
         out[0][...] = acc.astype(bf16)
 
+    expand_got = [move(expand_other, 0)]
+    branch_parts.append(swap(at_now(branch_parts[2]), "col", 1))
+    contract_grad = weight_mine(cot_full, ids_contract, [active], contract_got, "contract_grad")
+    branch_full = lay_out(branch_parts, places_attend, "branch_rows")
     (attended_grad,) = times_rows(
         branch_full,
-        full_proj,
+        full_attend,
         [],
         [((tokens_here, width), bf16)],
         store,
         "project_back",
-        tn=512,
-    )
-    projection_grad = sum_weight(branch_full, [attended], stepped, "projection_grad")
+        tn=width,
+        window=(mix_width, width),
+    )
+    project_other = weight_other(branch_full, ids_attend, [attended], "projection_grad")
+    put(expand_got[0], attended_grad, project_other[0])
+    tick()
+
+    expand_got.append(move(expand_other, 1))
     query_back, key_back, value_back, query_sum, value_sum = attend_backward(
-        mixed, attended_grad, starts, logs, slopes, seqs
+        mixed, at_now(attended_grad), starts, logs, slopes, seqs
     )
     mixed_grads = [query_back, key_back, value_back]
-    mixing_grad = sum_weight(first_full, mixed_grads, stepped, "mixing_grad")
-    first_back = sum_columns(*times_columns(mixed_grads, full_mix, slots, "mix_back"))
+    put(expand_got[1], query_back)
+    tick()
+
+    expand_got.append(move(expand_other, 2))
+    got = columns_sent(mixed_grads, full_attend, ids_attend, "mix_back")
+    if stepped:
+        mine, other = find(ids_attend, 2 * back + side), find(ids_attend, 2 * back + 1 - side)
+        mixing_other = [
+            weight_rows(at_now(first_full), other[k : k + 2], mixed_grads, "mixing_grad_other")
+            for k in range(0, rows // 2, 2)
+        ]
+    else:
+        mixing_other = weight_other(first_full, ids_attend, mixed_grads, "mixing_grad")
+    part = columns_part(mixed_grads, full_attend, ids_attend, got, "mix_back")
+    put(expand_got[2], part, *mixing_other)
+    tick()
+
+    expand_got.append(move(expand_other, 3))
+    across = swap(at_now(part), "col", 2)
+    base = columns_base(mixed_grads, full_attend, ids_attend, got, "mix_back")
+    out_part = columns_part(
+        [at_now(active)], full_contract, ids_contract, out_got, "contract"
+    )
+    first_back = base + across.astype(f32)
+    put(expand_got[3], first_back, out_part)
+    tick()
+
+    project_got = [swap(at_now(v), "row", 1) for v in project_other] if stepped else project_other
+    expand_grad = weight_mine(second_full, ids_expand, [hidden_grad], expand_got, "expand_grad")
     first_centred = (resid - first_mean) * first_scale
     first_input, first_gain, first_shift = norm_back(
-        first_back, first_centred, first_scale, gains[0]
+        at_now(first_back), first_centred, first_scale, gains[0]
     )
     tokens_grad = middle_grad + first_input
+    out_across = swap(at_now(out_part), "col", 2)
+    out_base = columns_base([active], full_contract, ids_contract, out_got, "contract")
     small = jnp.stack(
         [
             first_gain,
@@ -645,14 +835,47 @@
             jnp.sum(cot_float, axis=0),
         ]
     )
-    small = sum_rows(jnp.concatenate([small, thresholds_part.reshape(-1, width)], axis=0))
+    small = jnp.concatenate([small, thresholds_part.reshape(-1, width)], axis=0)
+    put(small, out_base, out_across, *project_got)
+    tick()
+
+    layer_out = (middle + (out_base + out_across.astype(f32) + biases[3])).astype(bf16)
+    projection_grad = weight_mine(
+        branch_full, ids_attend, [attended], project_got, "projection_grad"
+    )
+    if stepped:
+        far = swap(at_now(mixing_other[1]), "row", 1)
+        small = sum_rows(at_now(small))
+        put(far, small)
+        tick()
+
+        def mixing_mine(k, got):
+            parts = [got[:BLOCK], got[BLOCK:]]
+            return weight_rows(
+                first_full, mine[k : k + 2], mixed_grads, "mixing_grad_mine", parts, True
+            )
+
+        nearer = swap(at_now(mixing_other[0]), "row", 1)
+        terms = mixing_mine(2, at_now(far))
+        terms = [turn(terms[1], -3), turn(terms[0], -2)]
+        put(nearer, *terms)
+        tick()
+        own_term, step_term = mixing_mine(0, at_now(nearer))
+        terms += [turn(step_term, -1), own_term]
+        mixing_grad = sum(t.astype(f32) for t in terms)
+    else:
+        small = sum_rows(at_now(small))
+        mixing_grad = weight_mine(None, None, None, mixing_other, None)
+    mixing_grad = jnp.stack(
+        [mixing_grad[:, i * width : (i + 1) * width] for i in range(3)], axis=1
+    )
     return (
         layer_out,
         tokens_grad,
         small[0:2],
         small[2:4],
         small[4:8],
-        mixing_grad.reshape(mixing.shape),
+        mixing_grad,
         projection_grad,
         expand_grad,
         small[8:].reshape(thresholds.shape),

time: 1170 us -> 867 us (0.74)
  waiting for transfers between devices: 585 us -> 420 us
  starting transfers between devices: 221 us -> 75.1 us
  Pallas kernels: 265 us -> 280 us
  between operations: 2.08 us -> 14.9 us
  other arithmetic: 50.1 us -> 38.1 us
    ppermute x24 -> x6, starting transfers between devices: 149 us -> 19.6 us  [turn(): lax.ppermute(x, 'row', [(i, (i + 2 * steps) % count) for i in range(count)])]
    ppermute x62 -> x53, waiting for transfers between devices: 335 us -> 245 us  [swap(): lax.ppermute(x, axis, [(i, i ^ bit) for i in range(lax.axis_size(axis))])]
    ppermute x24 -> x6, waiting for transfers between devices: 251 us -> 174 us  [turn(): lax.ppermute(x, 'row', [(i, (i + 2 * steps) % count) for i in range(count)])]
    ppermute x62 -> x53, starting transfers between devices: 72.1 us -> 55 us  [swap(): lax.ppermute(x, axis, [(i, i ^ bit) for i in range(lax.axis_size(axis))])]
    unnamed x176 -> x130, local copies, waits for them, and re-layouts: 31 us -> 15.1 us
    pallas_call x20 -> x30, Pallas kernels: 231 us -> 243 us  [matmul_call(): pl.pallas_call(kernel, grid_spec=pltpu.PrefetchScalarGridSpec(num_scalar_...]
  transfers between devices with their start and end apart: 86 -> 64, of which waited for: 37 -> 36; matrix products, arithmetic and copies ran while one was open for 5% -> 6% of each run, Pallas kernels for 11% -> 29%
where the time goes in v3:
time: 867 us; the launch traced here: 858 us
  waiting for transfers between devices  420 us (48%)
  Pallas kernels  280 us (32%)
  starting transfers between devices  75.1 us (9%)
  other arithmetic  38.1 us (4%)
  local copies, waits for them, and re-layouts  30.7 us (4%)
  between operations  14.9 us (2%)
    ppermute x53, waiting for transfers between devices, swap(): lax.ppermute(x, axis, [(i, i ^ bit) for i in range(lax.axis_size(axis))])  245 us
    pallas_call x30, Pallas kernels, matmul_call(): pl.pallas_call(kernel, grid_spec=pltpu.PrefetchScalarGridSpec(num_scalar_...  243 us
    ppermute x6, waiting for transfers between devices, turn(): lax.ppermute(x, 'row', [(i, (i + 2 * steps) % count) for i in range(count)])  174 us
    ppermute x53, starting transfers between devices, swap(): lax.ppermute(x, axis, [(i, i ^ bit) for i in range(lax.axis_size(axis))])  55 us
    pallas_call x1, Pallas kernels, attend_backward(): pl.pallas_call(partial(attend_back_kernel, rows=rows, scale=HD ** (-0.5))...  20.2 us
    ppermute x6, starting transfers between devices, turn(): lax.ppermute(x, 'row', [(i, (i + 2 * steps) % count) for i in range(count)])  19.6 us
  transfers between devices with their start and end apart: 64, of which 36 were waited for; matrix products, arithmetic and copies ran while one was open for 6% of the time, Pallas kernels for 29%

profile of v3, /device:TPU:0, one launch (start us, length us, event | category | flops | bytes accessed | tf_op | source)
XLA Modules:
  0.0 858.4 jit_solution(9003077904062889607)
XLA Ops:
  11.2 3.0 collective-permute-start.1
  17.3 20.1 %collective-permute-done.1.refs_2_ = bf16[1024,512]{1,0:T(8,128)(2,1)S(1)} collective-permute-done((bf16[1024,512]{1,0:T(8,128)(2,1)S(1)}, bf16[1024,512]{1,0:T(8,128)(2,1)S(1)}, u32[]{:S(2)}, u32[]{:S(2)}) %collective-permute-start.1) | collective-permute-done | bytes 1048608 | tf_op jit(solution)/shard_map/ppermute | solution.py:427
  37.4 4.3 collective-permute-done.3.refs_2_
  47.3 39.0 %collective-permute-done.6.refs_3_ = bf16[256,2048]{1,0:T(8,128)(2,1)S(1)} collective-permute-done((bf16[256,2048]{1,0:T(8,128)(2,1)}, bf16[256,2048]{1,0:T(8,128)(2,1)S(1)}, u32[]{:S(2)}, u32[]{:S(2)}) %collective-permute-start.6) | collective-permute-done | bytes 1048608 | tf_op jit(solution)/shard_map/ppermute | solution.py:432
  87.3 11.0 %collective-permute-start.12 = (bf16[256,2048]{1,0:T(8,128)(2,1)S(1)}, bf16[256,2048]{1,0:T(8,128)(2,1)S(1)}, u32[]{:S(2)}, u32[]{:S(2)}) collective-permute-start(bf16[256,2048]{1,0:T(8,128)(2,1)S(1)} %collective-permute-done.6.refs_3_), channel_id=1, source_target_pairs={{0,8},{4,12},{8,16},{12,20},{16,24},{20,28},{24,0},{28,4},{1,9},{5... | collective-permute-start | bytes 3145736 | tf_op jit(solution)/shard_map/ppermute | solution.py:432
  100.7 3.1 collective-permute-done.10
  103.7 43.8 %collective-permute-done.12.refs_4_ = bf16[256,2048]{1,0:T(8,128)(2,1)S(1)} collective-permute-done((bf16[256,2048]{1,0:T(8,128)(2,1)S(1)}, bf16[256,2048]{1,0:T(8,128)(2,1)S(1)}, u32[]{:S(2)}, u32[]{:S(2)}) %collective-permute-start.12) | collective-permute-done | bytes 1048608 | tf_op jit(solution)/shard_map/ppermute | solution.py:432
  150.3 5.5 cotangent_rows.1.a_ref.refs_0_
  156.5 7.3 first_norm.1
  169.6 13.3 %mix.1 = (bf16[1024,1536]{1,0:T(8,128)(2,1)}, bf16[1024,2048]{1,0:T(8,128)(2,1)}, bf16[1024,2048]{1,0:T(8,128)(2,1)}) custom-call(bf16[1024,2048]{1,0:T(8,128)(2,1)} %get-tuple-element.180.refs_0_.a_ref, bf16[256,2048]{1,0:T(8,128)(2,1)} %copy-done.15, bf16[256,2048]{1,0:T(8,128)(2,1)} %copy-done.17, bf16[256,2048]{1,0:T(8,128)(2,1)} %copy-done.18, ...), custom_call_target="tpu_custom_call" | custom-call | flops 100663296 | bytes 376928 | tf_op jit(solution)/shard_map/mix/pallas_call | solution.py:229
  182.9 17.3 %attend_forward.1 = (bf16[1024,512]{1,0:T(8,128)(2,1)}, f32[4,2,1024]{2,1,0:T(2,128)}) custom-call(f32[8]{0:T(128)} %multiply_exponential_fusion.slope_ref, s32[1,1024,1]{2,1,0:T(8,128)} %copy.28.start_ref, bf16[1024,1536]{1,0:T(8,128)(2,1)} %get-tuple-element.125.q_ref.k_ref.v_ref, bf16[1024,1536]{1,0:T(8,128)(2,1)} %get-tuple-element.125.q_ref.k_ref.v_ref, ...), custom_call_target="tpu_custom_call" | custom-call | flops 67108864 | bytes 98304 | tf_op jit(solution)/shard_map/attend_forward/pallas_call | solution.py:79
  203.8 5.2 project_sent.1
  214.7 4.1 project_part.1
  218.9 17.7 %collective-permute-done.17.refs_2_ = bf16[256,2048]{1,0:T(8,128)(2,1)S(1)} collective-permute-done((bf16[256,2048]{1,0:T(8,128)(2,1)S(1)}, bf16[256,2048]{1,0:T(8,128)(2,1)S(1)}, u32[]{:S(2)}, u32[]{:S(2)}) %collective-permute-start.17) | collective-permute-done | bytes 1048608 | tf_op jit(solution)/shard_map/ppermute | solution.py:427
  237.0 4.7 project_base.1
  241.7 19.9 %collective-permute-done.19 = bf16[1024,512]{1,0:T(8,128)(2,1)S(1)} collective-permute-done((bf16[1024,512]{1,0:T(8,128)(2,1)}, bf16[1024,512]{1,0:T(8,128)(2,1)S(1)}, u32[]{:S(2)}, u32[]{:S(2)}) %collective-permute-start.19) | collective-permute-done | bytes 1048608 | tf_op jit(solution)/shard_map/ppermute | solution.py:427
  264.7 23.4 %collective-permute-done.22.refs_2_ = bf16[1024,512]{1,0:T(8,128)(2,1)S(1)} collective-permute-done((bf16[1024,512]{1,0:T(8,128)(2,1)S(1)}, bf16[1024,512]{1,0:T(8,128)(2,1)S(1)}, u32[]{:S(2)}, u32[]{:S(2)}) %collective-permute-start.22) | collective-permute-done | bytes 1048608 | tf_op jit(solution)/shard_map/ppermute | solution.py:427
  294.5 7.3 second_norm.1
  301.7 15.0 %collective-permute-done.25.refs_5_ = bf16[256,2048]{1,0:T(8,128)(2,1)} collective-permute-done((bf16[256,2048]{1,0:T(8,128)(2,1)}, bf16[256,2048]{1,0:T(8,128)(2,1)}, u32[]{:S(2)}, u32[]{:S(2)}) %collective-permute-start.25) | collective-permute-done | bytes 1048608 | tf_op jit(solution)/shard_map/ppermute | solution.py:427
  316.7 17.7 %expand.1 = (bf16[1024,2048]{1,0:T(8,128)(2,1)}, f32[1024,2048]{1,0:T(8,128)}, bf16[1024,2048]{1,0:T(8,128)(2,1)}) custom-call(bf16[1024,2048]{1,0:T(8,128)(2,1)} %get-tuple-element.212.refs_0_.a_ref, bf16[1024,2048]{1,0:T(8,128)(2,1)} %all-gather.3.cloned.1.call-done.refs_1_, bf16[256,2048]{1,0:T(8,128)(2,1)} %copy-done.36, bf16[256,2048]{1,0:T(8,128)(2,1)} %copy-done.37, ...), custom_call_target="tpu_custom_call" | custom-call | flops 134217728 | bytes 458880 | tf_op jit(solution)/shard_map/expand/pallas_call | solution.py:229
  334.4 10.7 %contract_grad_other.1 = (bf16[256,2048]{1,0:T(8,128)(2,1)}, bf16[256,2048]{1,0:T(8,128)(2,1)}, bf16[256,2048]{1,0:T(8,128)(2,1)}, bf16[256,2048]{1,0:T(8,128)(2,1)}) custom-call(s32[4]{0:T(128)} %get-tuple-element.225.order_ref, bf16[1024,2048]{1,0:T(8,128)(2,1)} %cotangent_rows.1.a_ref.refs_0_, bf16[1024,2048]{1,0:T(8,128)(2,1)} %get-tuple-element.187.refs_0_), custom_call_target="tpu_custom_call" | custom-call | flops 67108864 | bytes 196608 | tf_op jit(solution)/shard_map/contract_grad_other/pallas_call | solution.py:229
  346.2 23.9 %collective-permute-done.26.refs_1_ = bf16[256,2048]{1,0:T(8,128)(2,1)} collective-permute-done((bf16[256,2048]{1,0:T(8,128)(2,1)}, bf16[256,2048]{1,0:T(8,128)(2,1)}, u32[]{:S(2)}, u32[]{:S(2)}) %collective-permute-start.26) | collective-permute-done | bytes 1048608 | tf_op jit(solution)/shard_map/ppermute | solution.py:427
  370.2 14.3 %contract_back.1 = (bf16[1024,2048]{1,0:T(8,128)(2,1)}, f32[1,2048]{1,0:T(1,128)}) custom-call(bf16[1024,2048]{1,0:T(8,128)(2,1)} %cotangent_rows.1.a_ref.refs_0_, bf16[2048,2048]{1,0:T(8,128)(2,1)} %all-gather.5.cloned.1.call-done.refs_1_.refs_2_, f32[1024,2048]{1,0:T(8,128)} %get-tuple-element.152.refs_2_), custom_call_target="tpu_custom_call" | custom-call | flops 134217728 | bytes 393344 | tf_op jit(solution)/shard_map/contract_back/pallas_call | solution.py:229
  384.5 9.9 %expand_back_sent.1 = bf16[1024,1024]{1,0:T(8,128)(2,1)} custom-call(s32[2,2]{1,0:T(2,128)} %bitcast.67, s32[1]{0:T(128)} %bitcast.2.side_ref, bf16[1024,2048]{1,0:T(8,128)(2,1)} %get-tuple-element.162.refs_0_, bf16[1024,2048]{1,0:T(8,128)(2,1)} %all-gather.3.cloned.1.call-done.refs_1_, bf16[1024,2048]{1,0:T(8,128)(2,1)} %get-tuple-element.154.refs_2_), custom_call_target="tpu_custom_call" | custom-call | flops 67108864 | bytes 229376 | tf_op jit(solution)/shard_map/expand_back_sent/pallas_call | solution.py:229
  395.7 3.1 collective-permute-done.28.refs_3_
  400.1 7.2 expand_back_part.1
  407.4 12.8 %collective-permute-done.27.refs_2_ = bf16[256,2048]{1,0:T(8,128)(2,1)} collective-permute-done((bf16[256,2048]{1,0:T(8,128)(2,1)S(1)}, bf16[256,2048]{1,0:T(8,128)(2,1)}, u32[]{:S(2)}, u32[]{:S(2)}) %collective-permute-start.27) | collective-permute-done | bytes 1048608 | tf_op jit(solution)/shard_map/ppermute | solution.py:427
  424.9 7.8 expand_back_base.1
  432.6 10.8 %expand_grad_other.1 = (bf16[256,2048]{1,0:T(8,128)(2,1)}, bf16[256,2048]{1,0:T(8,128)(2,1)}, bf16[256,2048]{1,0:T(8,128)(2,1)}, bf16[256,2048]{1,0:T(8,128)(2,1)}) custom-call(s32[4]{0:T(128)} %get-tuple-element.224.order_ref, bf16[1024,2048]{1,0:T(8,128)(2,1)} %get-tuple-element.212.refs_0_.a_ref, bf16[1024,2048]{1,0:T(8,128)(2,1)} %get-tuple-element.162.refs_0_), custom_call_target="tpu_custom_call" | custom-call | flops 67108864 | bytes 196608 | tf_op jit(solution)/shard_map/expand_grad_other/pallas_call | solution.py:229
  456.7 19.2 %collective-permute-done.31.refs_4_ = bf16[256,2048]{1,0:T(8,128)(2,1)S(1)} collective-permute-done((bf16[256,2048]{1,0:T(8,128)(2,1)S(1)}, bf16[256,2048]{1,0:T(8,128)(2,1)S(1)}, u32[]{:S(2)}, u32[]{:S(2)}) %collective-permute-start.31) | collective-permute-done | bytes 1048608 | tf_op jit(solution)/shard_map/ppermute | solution.py:427
  475.9 3.2 collective-permute-done.35.refs_2_
  481.0 11.2 %contract_grad_mine.1 = bf16[1024,2048]{1,0:T(8,128)(2,1)} custom-call(s32[4]{0:T(128)} %get-tuple-element.222.order_ref, bf16[1024,2048]{1,0:T(8,128)(2,1)} %cotangent_rows.1.a_ref.refs_0_, bf16[1024,2048]{1,0:T(8,128)(2,1)} %get-tuple-element.187.refs_0_, bf16[256,2048]{1,0:T(8,128)(2,1)} %collective-permute-done.26.refs_1_, ...), custom_call_target="tpu_custom_call" | custom-call | flops 67108864 | bytes 262144 | tf_op jit(solution)/shard_map/contract_grad_mine/pallas_call | solution.py:229
  496.3 5.6 branch_rows.1.refs_0_.a_ref
  501.9 5.7 projection_grad_other.1
  507.6 6.2 project_back.1.g_ref
  513.7 4.5 collective-permute-done.36.refs_1_
  518.9 20.2 %attend_backward.1 = (bf16[1024,512]{1,0:T(8,128)(2,1)}, bf16[1024,512]{1,0:T(8,128)(2,1)}, bf16[1024,512]{1,0:T(8,128)(2,1)}, f32[1,1,512]{2,1,0:T(1,128)}, f32[1,1,512]{2,1,0:T(1,128)}) custom-call(f32[8]{0:T(128)} %multiply_exponential_fusion.slope_ref, s32[1,1,1024]{2,1,0:T(1,128)} %bitcast.56, f32[4,2,1024]{2,1,0:T(2,128)} %get-tuple-element.173.log_ref, ...), custom_call_target="tpu_custom_call" | custom-call | flops 167772160 | bytes 114688 | tf_op jit(solution)/shard_map/attend_backward/pallas_call | solution.py:183
  539.2 3.9 collective-permute-done.38.refs_2_
  543.0 7.8 mix_back_sent.1
  551.5 9.6 %contract_sent.1 = bf16[1024,1024]{1,0:T(8,128)(2,1)} custom-call(s32[2,2]{1,0:T(2,128)} %bitcast.69, s32[1]{0:T(128)} %bitcast.2.side_ref, bf16[1024,2048]{1,0:T(8,128)(2,1)} %get-tuple-element.187.refs_0_, bf16[2048,2048]{1,0:T(8,128)(2,1)} %all-gather.5.cloned.1.call-done.refs_1_.refs_2_, bf16[2048,2048]{1,0:T(8,128)(2,1)} %all-gather.5.cloned.1.call-done.refs_1_.refs_2_), custom_call_target="tpu_custom_call" | custom-call | flops 67108864 | bytes 360448 | tf_op jit(solution)/shard_map/contract_sent/pallas_call | solution.py:229
  562.9 5.7 mixing_grad_other.3
  568.5 5.8 mixing_grad_other.2
  574.4 6.2 mix_back_part.1
  580.6 6.1 collective-permute-done.39.refs_3_
  589.6 6.6 mix_back_base.1
  597.5 7.4 contract_part.1
  604.9 6.5 collective-permute-done.42
  611.4 2.9 convert_add_fusion.2
  626.6 7.6 contract_base.1
  634.9 5.4 collective-permute-done.49.refs_3_
  643.2 5.9 projection_grad_mine.1
  649.1 11.5 %expand_grad_mine.1 = bf16[1024,2048]{1,0:T(8,128)(2,1)} custom-call(s32[4]{0:T(128)} %get-tuple-element.223.order_ref, bf16[1024,2048]{1,0:T(8,128)(2,1)} %get-tuple-element.212.refs_0_.a_ref, bf16[1024,2048]{1,0:T(8,128)(2,1)} %get-tuple-element.162.refs_0_, bf16[256,2048]{1,0:T(8,128)(2,1)} %copy-done.22, bf16[256,2048]{1,0:T(8,128)(2,1)} %copy-done.24, ...), custom_call_target="tpu_custom_call" | custom-call | flops 67108864 | bytes 262144 | tf_op jit(solution)/shard_map/expand_grad_mine/pallas_call | solution.py:229
  662.7 32.3 %collective-permute-done.51 = f32[12,512]{1,0:T(8,128)S(1)} collective-permute-done((f32[12,512]{1,0:T(8,128)S(1)}, f32[12,512]{1,0:T(8,128)S(1)}, u32[]{:S(2)}, u32[]{:S(2)}) %collective-permute-start.51) | collective-permute-done | bytes 24608 | tf_op jit(solution)/shard_map/ppermute | solution.py:427
  695.0 15.1 %collective-permute-start.52 = (f32[12,512]{1,0:T(8,128)S(1)}, f32[12,512]{1,0:T(8,128)S(1)}, u32[]{:S(2)}, u32[]{:S(2)}) collective-permute-start(f32[12,512]{1,0:T(8,128)S(1)} %add.291), channel_id=1, source_target_pairs={{0,8},{4,12},{8,0},{12,4},{16,24},{20,28},{24,16},{28,20},{1,9},{5... | collective-permute-start | bytes 73736 | tf_op jit(solution)/shard_map/ppermute | solution.py:427
  712.9 4.9 collective-permute-start.53
  718.4 4.9 collective-permute-done.53
  724.7 7.2 mixing_grad_mine.2
  734.0 3.4 collective-permute-start.56
  739.3 33.1 %collective-permute-done.55 = bf16[256,1536]{1,0:T(8,128)(2,1)S(1)} collective-permute-done((bf16[256,1536]{1,0:T(8,128)(2,1)}, bf16[256,1536]{1,0:T(8,128)(2,1)S(1)}, u32[]{:S(2)}, u32[]{:S(2)}) %collective-permute-start.55) | collective-permute-done | bytes 786464 | tf_op jit(solution)/shard_map/ppermute | solution.py:432
  772.5 47.0 %collective-permute-done.56 = bf16[256,1536]{1,0:T(8,128)(2,1)S(1)} collective-permute-done((bf16[256,1536]{1,0:T(8,128)(2,1)}, bf16[256,1536]{1,0:T(8,128)(2,1)S(1)}, u32[]{:S(2)}, u32[]{:S(2)}) %collective-permute-start.56) | collective-permute-done | bytes 786464 | tf_op jit(solution)/shard_map/ppermute | solution.py:432
  819.4 2.9 fusion.23
  822.3 6.8 mixing_grad_mine.3
  830.6 2.8 add_convert_fusion
  839.8 7.0 collective-permute-done.58
  (305 shorter events, 118.5 us)
Async XLA Ops:
  7.2 194.4 %all-gather.3.cloned.1.call-start = ((), (), s32[]{:S(2)}) async-start(), calls=%async_computation.3 | async-start | bytes 5242880 | tf_op jit(solution)/shard_map/all_gather | solution.py:469
  11.2 26.2 %collective-permute-start.1 = (bf16[1024,512]{1,0:T(8,128)(2,1)S(1)}, bf16[1024,512]{1,0:T(8,128)(2,1)S(1)}, u32[]{:S(2)}, u32[]{:S(2)}) collective-permute-start(bf16[1024,512]{1,0:T(8,128)(2,1)S(1)} %copy-done.2), channel_id=1, source_target_pairs={{0,2},{1,3},{2,0},{3,1},{4,6},{5,7},{6,4},{7,5},{8,10},{9,11},{10,... | collective-permute-start | bytes 3145736 | tf_op jit(solution)/shard_map/ppermute | solution.py:427
  14.2 23.2 %collective-permute-start = (bf16[1024,512]{1,0:T(8,128)(2,1)S(1)}, bf16[1024,512]{1,0:T(8,128)(2,1)S(1)}, u32[]{:S(2)}, u32[]{:S(2)}) collective-permute-start(bf16[1024,512]{1,0:T(8,128)(2,1)S(1)} %copy-done.2), channel_id=1, source_target_pairs={{0,1},{1,0},{2,3},{3,2},{4,5},{5,4},{6,7},{7,6},{8,9},{9,8},{10,11... | collective-permute-start | bytes 3145736 | tf_op jit(solution)/shard_map/ppermute | solution.py:427
  14.2 27.4 %collective-permute-start.3 = (bf16[256,2048]{1,0:T(8,128)(2,1)S(1)}, bf16[256,2048]{1,0:T(8,128)(2,1)S(1)}, u32[]{:S(2)}, u32[]{:S(2)}) collective-permute-start(bf16[256,2048]{1,0:T(8,128)(2,1)S(1)} %pad_maximum_fusion.1.refs_1_), channel_id=1, source_target_pairs={{0,8},{4,12},{8,16},{12,20},{16,24},{20,28},{24,0},{28,4},{1,9},{5... | collective-permute-start | bytes 3145736 | tf_op jit(solution)/shard_map/ppermute | solution.py:432
  15.8 26.8 %collective-permute-start.2 = (bf16[256,2048]{1,0:T(8,128)(2,1)S(1)}, bf16[256,2048]{1,0:T(8,128)(2,1)}, u32[]{:S(2)}, u32[]{:S(2)}) collective-permute-start(bf16[256,2048]{1,0:T(8,128)(2,1)S(1)} %pad_maximum_fusion.1.refs_1_), channel_id=1, source_target_pairs={{0,4},{4,0},{8,12},{12,8},{16,20},{20,16},{24,28},{28,24},{1,5},{5... | collective-permute-start | bytes 3145736 | tf_op jit(solution)/shard_map/ppermute | solution.py:427
  42.6 327.6 %all-gather.5.cloned.1.call-start = ((), (), s32[]{:S(2)}) async-start(), calls=%async_computation.4 | async-start | bytes 10485760 | tf_op jit(solution)/shard_map/all_gather | solution.py:469
  42.7 43.6 %collective-permute-start.6 = (bf16[256,2048]{1,0:T(8,128)(2,1)}, bf16[256,2048]{1,0:T(8,128)(2,1)S(1)}, u32[]{:S(2)}, u32[]{:S(2)}) collective-permute-start(bf16[256,2048]{1,0:T(8,128)(2,1)} %copy-done.17), channel_id=1, source_target_pairs={{0,8},{4,12},{8,16},{12,20},{16,24},{20,28},{24,0},{28,4},{1,9},{5... | collective-permute-start | bytes 3145736 | tf_op jit(solution)/shard_map/ppermute | solution.py:432
  42.9 43.4 %collective-permute-start.5 = (bf16[256,2048]{1,0:T(8,128)(2,1)}, bf16[256,2048]{1,0:T(8,128)(2,1)S(1)}, u32[]{:S(2)}, u32[]{:S(2)}) collective-permute-start(bf16[256,2048]{1,0:T(8,128)(2,1)} %copy-done.17), channel_id=1, source_target_pairs={{0,4},{4,0},{8,12},{12,8},{16,20},{20,16},{24,28},{28,24},{1,5},{5... | collective-permute-start | bytes 3145736 | tf_op jit(solution)/shard_map/ppermute | solution.py:427
  44.4 2.9 collective-permute-start.4
  44.4 41.9 %collective-permute-start.8 = (bf16[1024,512]{1,0:T(8,128)(2,1)S(1)}, bf16[1024,512]{1,0:T(8,128)(2,1)}, u32[]{:S(2)}, u32[]{:S(2)}) collective-permute-start(bf16[1024,512]{1,0:T(8,128)(2,1)S(1)} %copy-done.12), channel_id=1, source_target_pairs={{0,2},{1,3},{2,0},{3,1},{4,6},{5,7},{6,4},{7,5},{8,10},{9,11},{10,... | collective-permute-start | bytes 3145736 | tf_op jit(solution)/shard_map/ppermute | solution.py:427
  44.9 41.3 %collective-permute-start.7 = (bf16[1024,512]{1,0:T(8,128)(2,1)S(1)}, bf16[1024,512]{1,0:T(8,128)(2,1)S(1)}, u32[]{:S(2)}, u32[]{:S(2)}) collective-permute-start(bf16[1024,512]{1,0:T(8,128)(2,1)S(1)} %copy-done.12), channel_id=1, source_target_pairs={{0,1},{1,0},{2,3},{3,2},{4,5},{5,4},{6,7},{7,6},{8,9},{9,8},{10,11... | collective-permute-start | bytes 3145736 | tf_op jit(solution)/shard_map/ppermute | solution.py:427
  87.3 60.2 %collective-permute-start.12 = (bf16[256,2048]{1,0:T(8,128)(2,1)S(1)}, bf16[256,2048]{1,0:T(8,128)(2,1)S(1)}, u32[]{:S(2)}, u32[]{:S(2)}) collective-permute-start(bf16[256,2048]{1,0:T(8,128)(2,1)S(1)} %collective-permute-done.6.refs_3_), channel_id=1, source_target_pairs={{0,8},{4,12},{8,16},{12,20},{16,24},{20,28},{24,0},{28,4},{1,9},{5... | collective-permute-start | bytes 3145736 | tf_op jit(solution)/shard_map/ppermute | solution.py:432
  98.3 49.2 %collective-permute-start.11 = (bf16[256,2048]{1,0:T(8,128)(2,1)S(1)}, bf16[256,2048]{1,0:T(8,128)(2,1)}, u32[]{:S(2)}, u32[]{:S(2)}) collective-permute-start(bf16[256,2048]{1,0:T(8,128)(2,1)S(1)} %collective-permute-done.6.refs_3_), channel_id=1, source_target_pairs={{0,4},{4,0},{8,12},{12,8},{16,20},{20,16},{24,28},{28,24},{1,5},{5... | collective-permute-start | bytes 3145736 | tf_op jit(solution)/shard_map/ppermute | solution.py:427
  99.9 47.7 %collective-permute-start.13 = (bf16[1024,512]{1,0:T(8,128)(2,1)}, bf16[1024,512]{1,0:T(8,128)(2,1)}, u32[]{:S(2)}, u32[]{:S(2)}) collective-permute-start(bf16[1024,512]{1,0:T(8,128)(2,1)} %collective-permute-done.8.refs_2_), channel_id=1, source_target_pairs={{0,1},{1,0},{2,3},{3,2},{4,5},{5,4},{6,7},{7,6},{8,9},{9,8},{10,11... | collective-permute-start | bytes 3145736 | tf_op jit(solution)/shard_map/ppermute | solution.py:427
  100.0 3.7 collective-permute-start.10
  100.1 3.6 collective-permute-start.9
  147.5 17.6 %collective-permute-start.15 = (bf16[256,2048]{1,0:T(8,128)(2,1)S(1)}, bf16[256,2048]{1,0:T(8,128)(2,1)}, u32[]{:S(2)}, u32[]{:S(2)}) collective-permute-start(bf16[256,2048]{1,0:T(8,128)(2,1)S(1)} %collective-permute-done.12.refs_4_), channel_id=1, source_target_pairs={{0,4},{4,0},{8,12},{12,8},{16,20},{20,16},{24,28},{28,24},{1,5},{5... | collective-permute-start | bytes 3145736 | tf_op jit(solution)/shard_map/ppermute | solution.py:427
  149.5 6.3 collective-permute-start.14
  165.2 35.1 %collective-permute-start.16 = (bf16[256,2048]{1,0:T(8,128)(2,1)S(1)}, bf16[256,2048]{1,0:T(8,128)(2,1)}, u32[]{:S(2)}, u32[]{:S(2)}) collective-permute-start(bf16[256,2048]{1,0:T(8,128)(2,1)S(1)} %copy-done.35), channel_id=1, source_target_pairs={{0,4},{4,0},{8,12},{12,8},{16,20},{20,16},{24,28},{28,24},{1,5},{5... | collective-permute-start | bytes 3145736 | tf_op jit(solution)/shard_map/ppermute | solution.py:427
  202.9 632.3 %reduce-scatter.8.cloned.1.call-start = ((), (), s32[]{:S(2)}) async-start(), calls=%async_computation.7 | async-start | bytes 5242880 | tf_op jit(solution)/shard_map/reduce_scatter | solution.py:561
  209.0 4.4 collective-permute-start.18
  211.0 25.6 %collective-permute-start.17 = (bf16[256,2048]{1,0:T(8,128)(2,1)S(1)}, bf16[256,2048]{1,0:T(8,128)(2,1)S(1)}, u32[]{:S(2)}, u32[]{:S(2)}) collective-permute-start(bf16[256,2048]{1,0:T(8,128)(2,1)S(1)} %get-tuple-element.129), channel_id=1, source_target_pairs={{0,4},{4,0},{8,12},{12,8},{16,20},{20,16},{24,28},{28,24},{1,5},{5... | collective-permute-start | bytes 3145736 | tf_op jit(solution)/shard_map/ppermute | solution.py:427
  236.5 25.1 %collective-permute-start.19 = (bf16[1024,512]{1,0:T(8,128)(2,1)}, bf16[1024,512]{1,0:T(8,128)(2,1)S(1)}, u32[]{:S(2)}, u32[]{:S(2)}) collective-permute-start(bf16[1024,512]{1,0:T(8,128)(2,1)} %project_part.1), channel_id=1, source_target_pairs={{0,2},{1,3},{2,0},{3,1},{4,6},{5,7},{6,4},{7,5},{8,10},{9,11},{10,... | collective-permute-start | bytes 3145736 | tf_op jit(solution)/shard_map/ppermute | solution.py:427
  236.6 27.3 %collective-permute-start.20 = (bf16[256,2048]{1,0:T(8,128)(2,1)}, bf16[256,2048]{1,0:T(8,128)(2,1)S(1)}, u32[]{:S(2)}, u32[]{:S(2)}) collective-permute-start(bf16[256,2048]{1,0:T(8,128)(2,1)} %get-tuple-element.135), channel_id=1, source_target_pairs={{0,4},{4,0},{8,12},{12,8},{16,20},{20,16},{24,28},{28,24},{1,5},{5... | collective-permute-start | bytes 3145736 | tf_op jit(solution)/shard_map/ppermute | solution.py:427
  263.9 24.2 %collective-permute-start.22 = (bf16[1024,512]{1,0:T(8,128)(2,1)S(1)}, bf16[1024,512]{1,0:T(8,128)(2,1)S(1)}, u32[]{:S(2)}, u32[]{:S(2)}) collective-permute-start(bf16[1024,512]{1,0:T(8,128)(2,1)S(1)} %get-tuple-element.136.refs_0_), channel_id=1, source_target_pairs={{0,2},{1,3},{2,0},{3,1},{4,6},{5,7},{6,4},{7,5},{8,10},{9,11},{10,... | collective-permute-start | bytes 3145736 | tf_op jit(solution)/shard_map/ppermute | solution.py:427
  264.2 23.8 %collective-permute-start.21 = (bf16[1024,512]{1,0:T(8,128)(2,1)S(1)}, bf16[1024,512]{1,0:T(8,128)(2,1)S(1)}, u32[]{:S(2)}, u32[]{:S(2)}) collective-permute-start(bf16[1024,512]{1,0:T(8,128)(2,1)S(1)} %get-tuple-element.136.refs_0_), channel_id=1, source_target_pairs={{0,1},{1,0},{2,3},{3,2},{4,5},{5,4},{6,7},{7,6},{8,9},{9,8},{10,11... | collective-permute-start | bytes 3145736 | tf_op jit(solution)/shard_map/ppermute | solution.py:427
  264.2 25.6 %collective-permute-start.23 = (bf16[256,2048]{1,0:T(8,128)(2,1)S(1)}, bf16[256,2048]{1,0:T(8,128)(2,1)S(1)}, u32[]{:S(2)}, u32[]{:S(2)}) collective-permute-start(bf16[256,2048]{1,0:T(8,128)(2,1)S(1)} %copy-done.38), channel_id=1, source_target_pairs={{0,4},{4,0},{8,12},{12,8},{16,20},{20,16},{24,28},{28,24},{1,5},{5... | collective-permute-start | bytes 3145736 | tf_op jit(solution)/shard_map/ppermute | solution.py:427
  290.8 2.7 collective-permute-start.24
  290.8 25.9 %collective-permute-start.25 = (bf16[256,2048]{1,0:T(8,128)(2,1)}, bf16[256,2048]{1,0:T(8,128)(2,1)}, u32[]{:S(2)}, u32[]{:S(2)}) collective-permute-start(bf16[256,2048]{1,0:T(8,128)(2,1)} %get-tuple-element.140), channel_id=1, source_target_pairs={{0,4},{4,0},{8,12},{12,8},{16,20},{20,16},{24,28},{28,24},{1,5},{5... | collective-permute-start | bytes 3145736 | tf_op jit(solution)/shard_map/ppermute | solution.py:427
  345.1 25.1 %collective-permute-start.26 = (bf16[256,2048]{1,0:T(8,128)(2,1)}, bf16[256,2048]{1,0:T(8,128)(2,1)}, u32[]{:S(2)}, u32[]{:S(2)}) collective-permute-start(bf16[256,2048]{1,0:T(8,128)(2,1)} %get-tuple-element.148), channel_id=1, source_target_pairs={{0,4},{4,0},{8,12},{12,8},{16,20},{20,16},{24,28},{28,24},{1,5},{5... | collective-permute-start | bytes 3145736 | tf_op jit(solution)/shard_map/ppermute | solution.py:427
  394.4 4.4 collective-permute-start.28
  394.5 25.7 %collective-permute-start.27 = (bf16[256,2048]{1,0:T(8,128)(2,1)S(1)}, bf16[256,2048]{1,0:T(8,128)(2,1)}, u32[]{:S(2)}, u32[]{:S(2)}) collective-permute-start(bf16[256,2048]{1,0:T(8,128)(2,1)S(1)} %copy-done.62), channel_id=1, source_target_pairs={{0,4},{4,0},{8,12},{12,8},{16,20},{20,16},{24,28},{28,24},{1,5},{5... | collective-permute-start | bytes 3145736 | tf_op jit(solution)/shard_map/ppermute | solution.py:427
  420.2 25.0 %collective-permute-start.30 = (bf16[1024,512]{1,0:T(8,128)(2,1)}, bf16[1024,512]{1,0:T(8,128)(2,1)}, u32[]{:S(2)}, u32[]{:S(2)}) collective-permute-start(bf16[1024,512]{1,0:T(8,128)(2,1)} %expand_back_part.1), channel_id=1, source_target_pairs={{0,2},{1,3},{2,0},{3,1},{4,6},{5,7},{6,4},{7,5},{8,10},{9,11},{10,... | collective-permute-start | bytes 3145736 | tf_op jit(solution)/shard_map/ppermute | solution.py:427
  421.9 24.8 %collective-permute-start.29 = (bf16[256,2048]{1,0:T(8,128)(2,1)}, bf16[256,2048]{1,0:T(8,128)(2,1)}, u32[]{:S(2)}, u32[]{:S(2)}) collective-permute-start(bf16[256,2048]{1,0:T(8,128)(2,1)} %get-tuple-element.161), channel_id=1, source_target_pairs={{0,4},{4,0},{8,12},{12,8},{16,20},{20,16},{24,28},{28,24},{1,5},{5... | collective-permute-start | bytes 3145736 | tf_op jit(solution)/shard_map/ppermute | solution.py:427
  447.9 1.2 collective-permute-start.32
  449.1 3.7 collective-permute-start.33
  450.9 24.9 %collective-permute-start.31 = (bf16[256,2048]{1,0:T(8,128)(2,1)S(1)}, bf16[256,2048]{1,0:T(8,128)(2,1)S(1)}, u32[]{:S(2)}, u32[]{:S(2)}) collective-permute-start(bf16[256,2048]{1,0:T(8,128)(2,1)S(1)} %copy-done.60), channel_id=1, source_target_pairs={{0,4},{4,0},{8,12},{12,8},{16,20},{20,16},{24,28},{28,24},{1,5},{5... | collective-permute-start | bytes 3145736 | tf_op jit(solution)/shard_map/ppermute | solution.py:427
  455.0 24.1 %collective-permute-start.35 = (bf16[1024,512]{1,0:T(8,128)(2,1)S(1)}, bf16[1024,512]{1,0:T(8,128)(2,1)S(1)}, u32[]{:S(2)}, u32[]{:S(2)}) collective-permute-start(bf16[1024,512]{1,0:T(8,128)(2,1)S(1)} %get-tuple-element.237.refs_0_), channel_id=1, source_target_pairs={{0,2},{1,3},{2,0},{3,1},{4,6},{5,7},{6,4},{7,5},{8,10},{9,11},{10,... | collective-permute-start | bytes 3145736 | tf_op jit(solution)/shard_map/ppermute | solution.py:427
  456.7 22.3 %collective-permute-start.34 = (bf16[1024,512]{1,0:T(8,128)(2,1)S(1)}, bf16[1024,512]{1,0:T(8,128)(2,1)S(1)}, u32[]{:S(2)}, u32[]{:S(2)}) collective-permute-start(bf16[1024,512]{1,0:T(8,128)(2,1)S(1)} %get-tuple-element.237.refs_0_), channel_id=1, source_target_pairs={{0,1},{1,0},{2,3},{3,2},{4,5},{5,4},{6,7},{7,6},{8,9},{9,8},{10,11... | collective-permute-start | bytes 3145736 | tf_op jit(solution)/shard_map/ppermute | solution.py:427
  492.3 345.7 %reduce-scatter.4.cloned.1.call-start = ((), (), s32[]{:S(2)}) async-start(), calls=%async_computation.5 | async-start | bytes 1310720 | tf_op jit(solution)/shard_map/reduce_scatter | solution.py:561
  492.3 2.9 collective-permute-start.37
  492.4 25.8 %collective-permute-start.36 = (bf16[256,2048]{1,0:T(8,128)(2,1)}, bf16[256,2048]{1,0:T(8,128)(2,1)S(1)}, u32[]{:S(2)}, u32[]{:S(2)}) collective-permute-start(bf16[256,2048]{1,0:T(8,128)(2,1)} %get-tuple-element.168), channel_id=1, source_target_pairs={{0,4},{4,0},{8,12},{12,8},{16,20},{20,16},{24,28},{28,24},{1,5},{5... | collective-permute-start | bytes 3145736 | tf_op jit(solution)/shard_map/ppermute | solution.py:427
  518.2 24.8 %collective-permute-start.38 = (bf16[256,2048]{1,0:T(8,128)(2,1)S(1)}, bf16[256,2048]{1,0:T(8,128)(2,1)S(1)}, u32[]{:S(2)}, u32[]{:S(2)}) collective-permute-start(bf16[256,2048]{1,0:T(8,128)(2,1)S(1)} %copy-done.61), channel_id=1, source_target_pairs={{0,4},{4,0},{8,12},{12,8},{16,20},{20,16},{24,28},{28,24},{1,5},{5... | collective-permute-start | bytes 3145736 | tf_op jit(solution)/shard_map/ppermute | solution.py:427
  550.8 23.6 %collective-permute-start.40 = (bf16[1024,1024]{1,0:T(8,128)(2,1)}, bf16[1024,1024]{1,0:T(8,128)(2,1)}, u32[]{:S(2)}, u32[]{:S(2)}) collective-permute-start(bf16[1024,1024]{1,0:T(8,128)(2,1)} %mix_back_sent.1), channel_id=1, source_target_pairs={{0,1},{1,0},{2,3},{3,2},{4,5},{5,4},{6,7},{7,6},{8,9},{9,8},{10,11... | collective-permute-start | bytes 6291464 | tf_op jit(solution)/shard_map/ppermute | solution.py:427
  561.1 35.1 %collective-permute-start.43 = (bf16[1024,1024]{1,0:T(8,128)(2,1)}, bf16[1024,1024]{1,0:T(8,128)(2,1)S(1)}, u32[]{:S(2)}, u32[]{:S(2)}) collective-permute-start(bf16[1024,1024]{1,0:T(8,128)(2,1)} %contract_sent.1), channel_id=1, source_target_pairs={{0,1},{1,0},{2,3},{3,2},{4,5},{5,4},{6,7},{7,6},{8,9},{9,8},{10,11... | collective-permute-start | bytes 6291464 | tf_op jit(solution)/shard_map/ppermute | solution.py:427
  561.6 25.1 %collective-permute-start.39 = (bf16[256,2048]{1,0:T(8,128)(2,1)S(1)}, bf16[256,2048]{1,0:T(8,128)(2,1)S(1)}, u32[]{:S(2)}, u32[]{:S(2)}) collective-permute-start(bf16[256,2048]{1,0:T(8,128)(2,1)S(1)} %copy-done.59), channel_id=1, source_target_pairs={{0,4},{4,0},{8,12},{12,8},{16,20},{20,16},{24,28},{28,24},{1,5},{5... | collective-permute-start | bytes 3145736 | tf_op jit(solution)/shard_map/ppermute | solution.py:427
  586.7 24.6 %collective-permute-start.42 = (bf16[1024,512]{1,0:T(8,128)(2,1)}, bf16[1024,512]{1,0:T(8,128)(2,1)}, u32[]{:S(2)}, u32[]{:S(2)}) collective-permute-start(bf16[1024,512]{1,0:T(8,128)(2,1)} %mix_back_part.1), channel_id=1, source_target_pairs={{0,2},{1,3},{2,0},{3,1},{4,6},{5,7},{6,4},{7,5},{8,10},{9,11},{10,... | collective-permute-start | bytes 3145736 | tf_op jit(solution)/shard_map/ppermute | solution.py:427
  588.5 25.8 %collective-permute-start.41 = (bf16[256,2048]{1,0:T(8,128)(2,1)}, bf16[256,2048]{1,0:T(8,128)(2,1)}, u32[]{:S(2)}, u32[]{:S(2)}) collective-permute-start(bf16[256,2048]{1,0:T(8,128)(2,1)} %get-tuple-element.181), channel_id=1, source_target_pairs={{0,4},{4,0},{8,12},{12,8},{16,20},{20,16},{24,28},{28,24},{1,5},{5... | collective-permute-start | bytes 3145736 | tf_op jit(solution)/shard_map/ppermute | solution.py:427
  614.2 28.9 %collective-permute-start.44 = (bf16[1024,512]{1,0:T(8,128)(2,1)}, bf16[1024,512]{1,0:T(8,128)(2,1)}, u32[]{:S(2)}, u32[]{:S(2)}) collective-permute-start(bf16[1024,512]{1,0:T(8,128)(2,1)} %contract_part.1), channel_id=1, source_target_pairs={{0,2},{1,3},{2,0},{3,1},{4,6},{5,7},{6,4},{7,5},{8,10},{9,11},{10,... | collective-permute-start | bytes 3145736 | tf_op jit(solution)/shard_map/ppermute | solution.py:427
  619.7 14.5 %collective-permute-start.47 = (bf16[256,512]{1,0:T(8,128)(2,1)}, bf16[256,512]{1,0:T(8,128)(2,1)S(1)}, u32[]{:S(2)}, u32[]{:S(2)}) collective-permute-start(bf16[256,512]{1,0:T(8,128)(2,1)} %get-tuple-element.195), channel_id=1, source_target_pairs={{0,4},{4,0},{8,12},{12,8},{16,20},{20,16},{24,28},{28,24},{1,5},{5... | collective-permute-start | bytes 786440 | tf_op jit(solution)/shard_map/ppermute | solution.py:427
  620.2 14.7 %collective-permute-start.48 = (bf16[256,512]{1,0:T(8,128)(2,1)}, bf16[256,512]{1,0:T(8,128)(2,1)}, u32[]{:S(2)}, u32[]{:S(2)}) collective-permute-start(bf16[256,512]{1,0:T(8,128)(2,1)} %get-tuple-element.197), channel_id=1, source_target_pairs={{0,4},{4,0},{8,12},{12,8},{16,20},{20,16},{24,28},{28,24},{1,5},{5... | collective-permute-start | bytes 786440 | tf_op jit(solution)/shard_map/ppermute | solution.py:427
  621.8 18.6 %collective-permute-start.49 = (bf16[256,512]{1,0:T(8,128)(2,1)}, bf16[256,512]{1,0:T(8,128)(2,1)}, u32[]{:S(2)}, u32[]{:S(2)}) collective-permute-start(bf16[256,512]{1,0:T(8,128)(2,1)} %get-tuple-element.199), channel_id=1, source_target_pairs={{0,4},{4,0},{8,12},{12,8},{16,20},{20,16},{24,28},{28,24},{1,5},{5... | collective-permute-start | bytes 786440 | tf_op jit(solution)/shard_map/ppermute | solution.py:427
  622.3 20.9 %collective-permute-start.50 = (bf16[256,512]{1,0:T(8,128)(2,1)}, bf16[256,512]{1,0:T(8,128)(2,1)}, u32[]{:S(2)}, u32[]{:S(2)}) collective-permute-start(bf16[256,512]{1,0:T(8,128)(2,1)} %get-tuple-element.201), channel_id=1, source_target_pairs={{0,4},{4,0},{8,12},{12,8},{16,20},{20,16},{24,28},{28,24},{1,5},{5... | collective-permute-start | bytes 786440 | tf_op jit(solution)/shard_map/ppermute | solution.py:427
  649.1 199.5 %reduce-scatter.6.cloned.1.call-start = ((), (), s32[]{:S(2)}) async-start(), calls=%async_computation.6 | async-start | bytes 5242880 | tf_op jit(solution)/shard_map/reduce_scatter | solution.py:561
  660.6 62.7 %collective-permute-start.54 = (bf16[512,1536]{1,0:T(8,128)(2,1)}, bf16[512,1536]{1,0:T(8,128)(2,1)S(1)}, u32[]{:S(2)}, u32[]{:S(2)}) collective-permute-start(bf16[512,1536]{1,0:T(8,128)(2,1)} %mixing_grad_other.3), channel_id=1, source_target_pairs={{0,4},{4,0},{8,12},{12,8},{16,20},{20,16},{24,28},{28,24},{1,5},{5... | collective-permute-start | bytes 4718600 | tf_op jit(solution)/shard_map/ppermute | solution.py:427
  661.2 33.8 %collective-permute-start.51 = (f32[12,512]{1,0:T(8,128)S(1)}, f32[12,512]{1,0:T(8,128)S(1)}, u32[]{:S(2)}, u32[]{:S(2)}) collective-permute-start(f32[12,512]{1,0:T(8,128)S(1)} %concatenate.31), channel_id=1, source_target_pairs={{0,4},{4,0},{8,12},{12,8},{16,20},{20,16},{24,28},{28,24},{1,5},{5... | collective-permute-start | bytes 73736 | tf_op jit(solution)/shard_map/ppermute | solution.py:427
  695.0 17.9 %collective-permute-start.52 = (f32[12,512]{1,0:T(8,128)S(1)}, f32[12,512]{1,0:T(8,128)S(1)}, u32[]{:S(2)}, u32[]{:S(2)}) collective-permute-start(f32[12,512]{1,0:T(8,128)S(1)} %add.291), channel_id=1, source_target_pairs={{0,8},{4,12},{8,0},{12,4},{16,24},{20,28},{24,16},{28,20},{1,9},{5... | collective-permute-start | bytes 73736 | tf_op jit(solution)/shard_map/ppermute | solution.py:427
  710.1 13.3 %collective-permute-start.45 = (f32[2,1024]{1,0:T(2,128)S(1)}, f32[2,1024]{1,0:T(2,128)S(1)}, u32[]{:S(2)}, u32[]{:S(2)}) collective-permute-start(f32[2,1024]{1,0:T(2,128)S(1)} %pad_maximum_fusion.5), channel_id=1, source_target_pairs={{0,1},{1,0},{2,3},{3,2},{4,5},{5,4},{6,7},{7,6},{8,9},{9,8},{10,11... | collective-permute-start | bytes 24584 | tf_op jit(solution)/shard_map/ppermute | solution.py:427
  712.9 10.4 %collective-permute-start.53 = (f32[12,512]{1,0:T(8,128)S(1)}, f32[12,512]{1,0:T(8,128)S(1)}, u32[]{:S(2)}, u32[]{:S(2)}) collective-permute-start(f32[12,512]{1,0:T(8,128)S(1)} %add.292), channel_id=1, source_target_pairs={{0,16},{4,20},{8,24},{12,28},{16,0},{20,4},{24,8},{28,12},{1,17},{... | collective-permute-start | bytes 73736 | tf_op jit(solution)/shard_map/ppermute | solution.py:427
  723.3 96.1 %collective-permute-start.57 = (bf16[512,1536]{1,0:T(8,128)(2,1)}, bf16[512,1536]{1,0:T(8,128)(2,1)}, u32[]{:S(2)}, u32[]{:S(2)}) collective-permute-start(bf16[512,1536]{1,0:T(8,128)(2,1)} %mixing_grad_other.2), channel_id=1, source_target_pairs={{0,4},{4,0},{8,12},{12,8},{16,20},{20,16},{24,28},{28,24},{1,5},{5... | collective-permute-start | bytes 4718600 | tf_op jit(solution)/shard_map/ppermute | solution.py:427
  723.4 14.0 %collective-permute-start.46 = (f32[2,1024]{1,0:T(2,128)S(1)}, f32[2,1024]{1,0:T(2,128)S(1)}, u32[]{:S(2)}, u32[]{:S(2)}) collective-permute-start(f32[2,1024]{1,0:T(2,128)S(1)} %fusion.19), channel_id=1, source_target_pairs={{0,2},{1,3},{2,0},{3,1},{4,6},{5,7},{6,4},{7,5},{8,10},{9,11},{10,... | collective-permute-start | bytes 24584 | tf_op jit(solution)/shard_map/ppermute | solution.py:427
  732.0 40.5 %collective-permute-start.55 = (bf16[256,1536]{1,0:T(8,128)(2,1)}, bf16[256,1536]{1,0:T(8,128)(2,1)S(1)}, u32[]{:S(2)}, u32[]{:S(2)}) collective-permute-start(bf16[256,1536]{1,0:T(8,128)(2,1)} %get-tuple-element.205), channel_id=1, source_target_pairs={{0,8},{4,12},{8,16},{12,20},{16,24},{20,28},{24,0},{28,4},{1,9},{5... | collective-permute-start | bytes 2359304 | tf_op jit(solution)/shard_map/ppermute | solution.py:432
  734.0 85.4 %collective-permute-start.56 = (bf16[256,1536]{1,0:T(8,128)(2,1)}, bf16[256,1536]{1,0:T(8,128)(2,1)S(1)}, u32[]{:S(2)}, u32[]{:S(2)}) collective-permute-start(bf16[256,1536]{1,0:T(8,128)(2,1)} %get-tuple-element.206), channel_id=1, source_target_pairs={{0,16},{4,20},{8,24},{12,28},{16,0},{20,4},{24,8},{28,12},{1,17},{... | collective-permute-start | bytes 2359304 | tf_op jit(solution)/shard_map/ppermute | solution.py:432
  829.2 17.7 %collective-permute-start.58 = (bf16[256,1536]{1,0:T(8,128)(2,1)}, bf16[256,1536]{1,0:T(8,128)(2,1)S(1)}, u32[]{:S(2)}, u32[]{:S(2)}) collective-permute-start(bf16[256,1536]{1,0:T(8,128)(2,1)} %get-tuple-element.209), channel_id=1, source_target_pairs={{0,24},{4,28},{8,0},{12,4},{16,8},{20,12},{24,16},{28,20},{1,25},{... | collective-permute-start | bytes 2359304 | tf_op jit(solution)/shard_map/ppermute | solution.py:432
  (63 other events, 1081.1 us)
Sparse Core Ops, SparseCore 0:
  42.7 117.2 all-gather.2
  203.0 163.5 all-gather.4
  492.4 91.8 reduce-scatter.7
  649.2 41.0 reduce-scatter.3
  692.5 108.4 reduce-scatter.5

commit v4 on v3

--- a/solution.py
+++ b/solution.py
@@ -284,77 +284,79 @@
     return matmul_call(kernel, (steps,), ins, results, [], 2 * tokens * depth * width, name)
 
 
-def times_columns(xs, ws, order, side, dtype, name, first=0, added=None, block=0):
+def times_columns(xs, ws, order, side, dtype, name, first=0, added=(), block=0, chunks=1):
     tokens = xs[0].shape[0]
     count = order.shape[1]
     n_xs = len(xs)
     width = sum(x.shape[1] for x in xs)
+    rows = tokens // chunks
 
     def kernel(order_ref, side_ref, *refs):
-        x_refs, w_refs, rest, out_ref = refs[:n_xs], refs[n_xs : n_xs + 2], refs[n_xs + 2 :], refs[-1]
+        x_refs, w_refs = refs[:n_xs], refs[n_xs : n_xs + 2]
+        added_refs, out_refs = refs[n_xs + 2 : n_xs + 2 + len(added)], refs[-chunks:]
         x = jnp.concatenate([r[...] for r in x_refs], axis=1)
         for i, w_ref in enumerate(w_refs):
             acc = lax.dot_general(x, w_ref[...], NT, preferred_element_type=f32)
             place = side_ref[0] if i == 0 else 1 - side_ref[0]
             place = pl.ds(pl.multiple_of(place * BLOCK, BLOCK), BLOCK)
-            if added is not None:
-                acc = acc + rest[0][:, place].astype(f32)
-            out_ref[:, place] = acc.astype(dtype)
-
-    def rows(i):
+            if added:
+                acc = acc + jnp.concatenate([r[:, place] for r in added_refs]).astype(f32)
+            for c, out_ref in enumerate(out_refs):
+                out_ref[:, place] = acc[c * rows : (c + 1) * rows].astype(dtype)
+
+    def w_spec(i):
         return pl.BlockSpec((BLOCK, width), lambda n, order_ref, _: (order_ref[i, n], first // width))
 
-    def pair(start):
-        return pl.BlockSpec((tokens, 2 * BLOCK), lambda n, *_: (0, start + n))
+    def pair(height, start):
+        return pl.BlockSpec((height, 2 * BLOCK), lambda n, *_: (0, start + n))
 
     ins = [(x, resident(x.shape)) for x in xs]
-    ins += [(w, rows(i)) for i, w in enumerate(ws)]
-    ins += [] if added is None else [(added, pair(block))]
-    return matmul_call(
+    ins += [(w, w_spec(i)) for i, w in enumerate(ws)]
+    ins += [(b, pair(b.shape[0], block)) for b in added]
+    done = matmul_call(
         kernel,
         (count,),
         ins,
-        [((tokens, 2 * BLOCK * count), dtype, pair(0))],
+        [((rows, 2 * BLOCK * count), dtype, pair(rows, 0))] * chunks,
         [],
         4 * tokens * BLOCK * count * width,
         name,
         prefetch=(order, side),
-    )[0]
-
-
-def weight_rows(a, order, gs, name, added=(), apart=False, dtype=bf16):
+    )
+    return done if chunks > 1 else done[0]
+
+
+def weight_rows(a, order, gs, name, groups=None, dtype=bf16):
     tokens = a.shape[0]
     width = sum(g.shape[1] for g in gs)
     count = order.shape[0]
     n_gs = len(gs)
 
     def kernel(order_ref, a_ref, *refs):
-        g_refs, added_refs = refs[:n_gs], refs[n_gs : n_gs + len(added)]
-        out_refs = refs[n_gs + len(added) :]
+        g_refs, out_refs = refs[:n_gs], refs[n_gs:]
         g = jnp.concatenate([r[...] for r in g_refs], axis=1)
-        acc = lax.dot_general(a_ref[...], g, TN, preferred_element_type=f32)
-        if not apart and not added:
-            out_refs[0][...] = acc.astype(dtype)
+        acc = lax.dot_general(a_ref[...], g, TN, preferred_element_type=f32).astype(dtype)
+        if groups is None:
+            out_refs[0][...] = acc
             return
-        for i in range(count):
-
-            @pl.when(pl.program_id(0) == i)
-            def _(i=i):
-                total = acc + added_refs[i][...].astype(f32) if added else acc
-                out_refs[i if apart else 0][...] = total.astype(dtype)
-
-    block = pl.BlockSpec((BLOCK, width), lambda i, *_: (i, 0))
+        for out_ref, group in zip(out_refs, groups):
+            for j, i in enumerate(group):
+
+                @pl.when(pl.program_id(0) == i)
+                def _(out_ref=out_ref, rows=slice(j * BLOCK, (j + 1) * BLOCK)):
+                    out_ref[rows, :] = acc
+
     ins = [(a, pl.BlockSpec((tokens, BLOCK), lambda i, order_ref: (0, order_ref[i])))]
     ins += [(g, resident(g.shape)) for g in gs]
-    ins += [(b, resident(b.shape)) for b in added]
-    if apart:
-        outs = [((BLOCK, width), dtype, kept_out((BLOCK, width)))] * count
+    if groups is None:
+        outs = [((count * BLOCK, width), dtype, pl.BlockSpec((BLOCK, width), lambda i, *_: (i, 0)))]
     else:
-        outs = [((count * BLOCK, width), dtype, block)]
+        shapes = [(len(group) * BLOCK, width) for group in groups]
+        outs = [(shape, dtype, kept_out(shape)) for shape in shapes]
     done = matmul_call(
         kernel, (count,), ins, outs, [], 2 * tokens * BLOCK * count * width, name, prefetch=(order,)
     )
-    return done if apart else done[0]
+    return done[0] if groups is None else done
 
 
 def place_blocks(values, place_ref, out_ref):
@@ -510,8 +512,7 @@
     steps = jnp.arange(max(rows // 2, 1))
     back = (place - steps) % (rows // 2)
     if stepped:
-        ids_attend = jnp.concatenate([2 * back + side, 2 * back + 1 - side])
-        ids_expand = jnp.concatenate([2 * steps + side, 2 * steps + 1 - side])
+        ids_attend = ids_expand = jnp.concatenate([2 * back + side, 2 * back + 1 - side])
         ids_contract = jnp.stack([2 * steps + side, 2 * steps + 1 - side], axis=1).reshape(-1)
     else:
         ids_attend = ids_expand = ids_contract = at
@@ -529,11 +530,13 @@
     def two(ws):
         return ws if len(ws) == 2 else [ws[0], ws[0]]
 
-    def columns_sent(xs, ws, ids, name, first=0):
-        order = columns_order(ids, ws)
+    def columns_sent(xs, ws, ids, name, first=0, chunks=4):
+        order = columns_order(ids, ws)[:, :2]
         xs = [at_now(xs[0])] + xs[1:]
-        sent = times_columns(xs, two(ws), order[:, :2], sides, bf16, name + "_sent", first)
-        return swap(sent, "col", 1)
+        sent = times_columns(
+            xs, two(ws), order, sides, bf16, name + "_sent", first, chunks=chunks
+        )
+        return [swap(v, "col", 1) for v in (sent if chunks > 1 else [sent])]
 
     def columns_part(xs, ws, ids, got, name, first=0):
         order = columns_order(ids, ws)[:, 3:]
@@ -544,23 +547,57 @@
         xs = [at_now(xs[0])] + xs[1:]
         return times_columns(xs, two(ws), order, sides, f32, name + "_base", first, got, 0)
 
-    def weight_other(a, ids, gs, name):
-        if not stepped:
-            return [weight_rows(at_now(a), find(ids, at), gs, name, dtype=f32)]
-        other = find(ids, 2 * steps + 1 - side)
-        return weight_rows(at_now(a), other, gs, name + "_other", apart=True)
-
-    def move(parts, k):
-        return swap(at_now(parts[k]), "row", 1) if stepped else parts[0]
-
-    def weight_mine(a, ids, gs, got, name):
-        if not stepped:
-            return lax.psum_scatter(got[0], "row", scatter_dimension=0, tiled=True)
-        mine = find(ids, 2 * steps + side)
-        total = weight_rows(at_now(a), mine, gs, name + "_mine", got)
-        return lax.psum_scatter(
-            total, "row", scatter_dimension=0, tiled=True, axis_index_groups=outer_groups()
-        ).astype(f32)
+    class WeightSum:
+        def __init__(self, a, ids, gs, name, groups=None):
+            self.a, self.ids, self.gs, self.name = a, ids, gs, name
+            self.left = rows // 2
+            self.groups = groups or [[k] for k in reversed(range(self.left))]
+            self.got, self.carry, self.result = {}, None, None
+
+        def cut(self):
+            if stepped:
+                other = find(self.ids, 2 * back + 1 - side)
+                self.sent = list(
+                    weight_rows(at_now(self.a), other, self.gs, self.name + "_other", self.groups)
+                )
+            else:
+                self.sent = [
+                    weight_rows(at_now(self.a), find(self.ids, at), self.gs, self.name, dtype=f32)
+                ]
+            put(*self.sent)
+
+        def keep(self, *first):
+            if stepped:
+                mine = find(self.ids, 2 * back + side)
+                a = after(at_now(self.a), *first)
+                single = [[k] for k in range(rows // 2)]
+                self.kept = weight_rows(a, mine, self.gs, self.name + "_mine", single, f32)
+                put(*self.kept)
+
+        def move(self):
+            if stepped:
+                group = self.groups.pop(0)
+                got = swap(at_now(self.sent.pop(0)), "row", 1)
+                put(got)
+                for j, k in enumerate(group):
+                    self.got[k] = got[j * BLOCK : (j + 1) * BLOCK]
+
+        def add(self):
+            if not stepped:
+                if self.result is None:
+                    self.result = lax.psum_scatter(
+                        self.sent[0], "row", scatter_dimension=0, tiled=True
+                    )
+                return
+            self.left -= 1
+            total = self.kept[self.left] + at_now(self.got[self.left]).astype(f32)
+            if self.carry is not None:
+                total = total + self.carry.astype(f32)
+            if self.left == 0:
+                self.result = total
+            else:
+                self.carry = turn(total.astype(bf16), -1)
+                put(self.carry)
 
     head_ids = (col * heads + jnp.arange(heads)).astype(f32)
     slopes = jnp.exp2(-8.0 * (head_ids + 1.0) / (heads * cols))
@@ -602,8 +639,6 @@
     cot_parts = [cotangent, swap(cot_now, "col", 1), swap(cot_now, "col", 2)]
     token_parts.append(swap(at_now(token_parts[2]), "col", 1))
     put(*cot_parts[1:], token_parts[3])
-    if stepped:
-        expand_mine = gather_outer(at_now(expand))
     tick()
 
     weight_step(2)
@@ -621,14 +656,32 @@
     )
     cot_full = lay_out([at_now(cot_parts[0])] + cot_parts[1:], places_contract, "cotangent_rows")
     put(first_full, cot_full)
+    expand_own, expand_near = [expand], []
+
+    def expand_turn():
+        if stepped:
+            expand_own.append(turn(at_now(expand_own[-1]), 1))
+            put(expand_own[-1])
+
+    def expand_step(k):
+        if stepped:
+            expand_near.append(swap(at_now(expand_own[k]), "row", 1))
+            put(expand_near[k])
+
+    expand_turn()
+    expand_turn()
+    if stepped:
+        contract_pair = jnp.concatenate([contract, swap(at_now(contract), "row", 1)], axis=0)
+        put(contract_pair)
     tick()
 
     def add_bias(acc, extra, out):
         out[0][...] = (acc + extra[0][...]).astype(bf16)
 
+    expand_turn()
+    expand_step(0)
     if stepped:
-        contract_pair = jnp.concatenate([contract, swap(at_now(contract), "row", 1)], axis=0)
-        put(contract_pair, expand_mine)
+        full_contract = [gather_outer(at_now(contract_pair))]
     mixed, *full_attend = times_rows(
         at_now(first_full),
         own + near,
@@ -644,23 +697,13 @@
     put(attended)
     tick()
 
-    if stepped:
-        full_contract = [gather_outer(at_now(contract_pair))]
-        expand_near = []
-
-    def expand_step(k):
-        if stepped:
-            block = expand_mine[k * BLOCK : (k + 1) * BLOCK]
-            expand_near.append(swap(at_now(block), "row", 1))
-            put(expand_near[k])
-
-    expand_step(0)
+    expand_step(1)
     got = columns_sent([attended], full_attend, ids_attend, "project", mix_width)
     part = columns_part([attended], full_attend, ids_attend, got, "project", mix_width)
     put(part)
     tick()
 
-    expand_step(1)
+    expand_step(2)
     across = swap(at_now(part), "col", 2)
     base = columns_base([attended], full_attend, ids_attend, got, "project", mix_width)
     resid = tokens.astype(f32)
@@ -669,13 +712,12 @@
     put(middle_low)
     tick()
 
-    expand_step(2)
+    expand_step(3)
     middle_now = at_now(middle_low)
     middle_parts = [middle_low, swap(middle_now, "col", 1), swap(middle_now, "col", 2)]
     put(*middle_parts[1:])
     tick()
 
-    expand_step(3)
     middle_parts.append(swap(at_now(middle_parts[2]), "col", 1))
     second_full, second_mean, second_scale = normalize(
         middle_parts, norms[1:2], norms[3:4], places_expand, "second_norm"
@@ -692,22 +734,21 @@
     hidden_shape = (tokens_here, expand.shape[1])
     active, slope, *joined = times_rows(
         at_now(second_full),
-        [expand_mine] + expand_near if stepped else full_expand,
+        expand_own + expand_near if stepped else full_expand,
         [thresholds[None]],
         [(hidden_shape, bf16), (hidden_shape, f32)],
         activate,
         "expand",
         tn=512,
-        joins=[range(1, 1 + rows // 2)] if stepped else [],
+        joins=[range(rows // 2), range(rows // 2, rows)] if stepped else [],
     )
     if stepped:
-        full_expand = [expand_mine] + joined
-    contract_other = weight_other(cot_full, ids_contract, [active], "contract_grad")
-    put(active, *contract_other)
-    tick()
-
-    contract_got = [move(contract_other, 0)]
-    put(contract_got[0], *full_contract)
+        full_expand = joined
+    contract_sum = WeightSum(
+        cot_full, ids_contract, [active], "contract_grad", [[3, 2], [1], [0]]
+    )
+    contract_sum.cut()
+    put(active)
     tick()
 
     def back_activate(acc, extra, out):
@@ -715,7 +756,8 @@
         out[0][...] = grad
         out[1][...] = jnp.sum(grad.astype(f32), axis=0, keepdims=True)
 
-    contract_got.append(move(contract_other, 1))
+    contract_sum.move()
+    contract_sum.keep()
     hidden_grad, thresholds_part = times_rows(
         at_now(cot_full),
         full_contract,
@@ -727,15 +769,17 @@
     )
     got = columns_sent([hidden_grad], full_expand, ids_expand, "expand_back")
     part = columns_part([hidden_grad], full_expand, ids_expand, got, "expand_back")
-    put(contract_got[1], part)
-    tick()
-
-    contract_got.append(move(contract_other, 2))
+    put(part)
+    tick()
+
+    contract_sum.add()
+    contract_sum.move()
     across = swap(at_now(part), "col", 2)
     base = columns_base([hidden_grad], full_expand, ids_expand, got, "expand_back")
-    expand_other = weight_other(second_full, ids_expand, [hidden_grad], "expand_grad")
+    expand_sum = WeightSum(second_full, ids_expand, [hidden_grad], "expand_grad")
+    expand_sum.cut()
     second_back = base + across.astype(f32)
-    put(contract_got[2], second_back, *expand_other)
+    put(second_back)
     tick()
 
     def norm_back(upstream, centred, scale, gain):
@@ -748,7 +792,8 @@
         )
         return result, jnp.sum(upstream * centred, axis=0), jnp.sum(upstream, axis=0)
 
-    contract_got.append(move(contract_other, 3))
+    contract_sum.add()
+    contract_sum.move()
     second_centred = (middle - second_mean) * second_scale
     second_input, second_gain, second_shift = norm_back(
         at_now(second_back), second_centred, second_scale, gains[1]
@@ -757,16 +802,16 @@
     middle_grad = cot_float + second_input
     branch_grad = middle_grad.astype(bf16)
     branch_parts = [branch_grad, swap(branch_grad, "col", 1), swap(branch_grad, "col", 2)]
-    out_got = columns_sent([after(active, branch_grad)], full_contract, ids_contract, "contract")
-    put(contract_got[3], *branch_parts[1:])
+    expand_sum.keep(branch_grad)
+    put(*branch_parts[1:])
     tick()
 
     def store(acc, extra, out):
         out[0][...] = acc.astype(bf16)
 
-    expand_got = [move(expand_other, 0)]
+    contract_sum.add()
+    expand_sum.move()
     branch_parts.append(swap(at_now(branch_parts[2]), "col", 1))
-    contract_grad = weight_mine(cot_full, ids_contract, [active], contract_got, "contract_grad")
     branch_full = lay_out(branch_parts, places_attend, "branch_rows")
     (attended_grad,) = times_rows(
         branch_full,
@@ -778,51 +823,48 @@
         tn=width,
         window=(mix_width, width),
     )
-    project_other = weight_other(branch_full, ids_attend, [attended], "projection_grad")
-    put(expand_got[0], attended_grad, project_other[0])
-    tick()
-
-    expand_got.append(move(expand_other, 1))
+    project_sum = WeightSum(branch_full, ids_attend, [attended], "projection_grad", [[3, 2, 1, 0]])
+    project_sum.cut()
+    put(attended_grad)
+    tick()
+
+    expand_sum.add()
+    expand_sum.move()
     query_back, key_back, value_back, query_sum, value_sum = attend_backward(
         mixed, at_now(attended_grad), starts, logs, slopes, seqs
     )
     mixed_grads = [query_back, key_back, value_back]
-    put(expand_got[1], query_back)
-    tick()
-
-    expand_got.append(move(expand_other, 2))
+    put(query_back)
+    tick()
+
+    contract_sum.add()
+    expand_sum.add()
+    expand_sum.move()
     got = columns_sent(mixed_grads, full_attend, ids_attend, "mix_back")
-    if stepped:
-        mine, other = find(ids_attend, 2 * back + side), find(ids_attend, 2 * back + 1 - side)
-        mixing_other = [
-            weight_rows(at_now(first_full), other[k : k + 2], mixed_grads, "mixing_grad_other")
-            for k in range(0, rows // 2, 2)
-        ]
-    else:
-        mixing_other = weight_other(first_full, ids_attend, mixed_grads, "mixing_grad")
+    mixing_sum = WeightSum(first_full, ids_attend, mixed_grads, "mixing_grad")
+    mixing_sum.cut()
     part = columns_part(mixed_grads, full_attend, ids_attend, got, "mix_back")
-    put(expand_got[2], part, *mixing_other)
-    tick()
-
-    expand_got.append(move(expand_other, 3))
+    put(part)
+    tick()
+
+    expand_sum.add()
+    expand_sum.move()
     across = swap(at_now(part), "col", 2)
     base = columns_base(mixed_grads, full_attend, ids_attend, got, "mix_back")
-    out_part = columns_part(
-        [at_now(active)], full_contract, ids_contract, out_got, "contract"
-    )
+    out_got = columns_sent([active], full_contract, ids_contract, "contract", chunks=1)
     first_back = base + across.astype(f32)
-    put(expand_got[3], first_back, out_part)
-    tick()
-
-    project_got = [swap(at_now(v), "row", 1) for v in project_other] if stepped else project_other
-    expand_grad = weight_mine(second_full, ids_expand, [hidden_grad], expand_got, "expand_grad")
+    put(first_back, *out_got)
+    tick()
+
+    expand_sum.add()
+    project_sum.move()
+    project_sum.keep()
+    out_part = columns_part([at_now(active)], full_contract, ids_contract, out_got, "contract")
     first_centred = (resid - first_mean) * first_scale
     first_input, first_gain, first_shift = norm_back(
         at_now(first_back), first_centred, first_scale, gains[0]
     )
     tokens_grad = middle_grad + first_input
-    out_across = swap(at_now(out_part), "col", 2)
-    out_base = columns_base([active], full_contract, ids_contract, out_got, "contract")
     small = jnp.stack(
         [
             first_gain,
@@ -836,36 +878,30 @@
         ]
     )
     small = jnp.concatenate([small, thresholds_part.reshape(-1, width)], axis=0)
-    put(small, out_base, out_across, *project_got)
-    tick()
-
+    put(small, out_part)
+    tick()
+
+    project_sum.add()
+    mixing_sum.move()
+    mixing_sum.keep()
+    out_across = swap(at_now(out_part), "col", 2)
+    out_base = columns_base([active], full_contract, ids_contract, out_got, "contract")
     layer_out = (middle + (out_base + out_across.astype(f32) + biases[3])).astype(bf16)
-    projection_grad = weight_mine(
-        branch_full, ids_attend, [attended], project_got, "projection_grad"
-    )
-    if stepped:
-        far = swap(at_now(mixing_other[1]), "row", 1)
-        small = sum_rows(at_now(small))
-        put(far, small)
+    put(layer_out)
+    bit = 1
+    while bit < rows:
+        small = small + swap(at_now(small), "row", bit)
+        put(small)
         tick()
-
-        def mixing_mine(k, got):
-            parts = [got[:BLOCK], got[BLOCK:]]
-            return weight_rows(
-                first_full, mine[k : k + 2], mixed_grads, "mixing_grad_mine", parts, True
-            )
-
-        nearer = swap(at_now(mixing_other[0]), "row", 1)
-        terms = mixing_mine(2, at_now(far))
-        terms = [turn(terms[1], -3), turn(terms[0], -2)]
-        put(nearer, *terms)
-        tick()
-        own_term, step_term = mixing_mine(0, at_now(nearer))
-        terms += [turn(step_term, -1), own_term]
-        mixing_grad = sum(t.astype(f32) for t in terms)
-    else:
-        small = sum_rows(at_now(small))
-        mixing_grad = weight_mine(None, None, None, mixing_other, None)
+        bit *= 2
+        project_sum.add()
+        mixing_sum.add()
+        if mixing_sum.groups:
+            mixing_sum.move()
+    tick()
+    mixing_sum.add()
+    contract_grad, expand_grad = contract_sum.result, expand_sum.result
+    projection_grad, mixing_grad = project_sum.result, mixing_sum.result
     mixing_grad = jnp.stack(
         [mixing_grad[:, i * width : (i + 1) * width] for i in range(3)], axis=1
     )

time: 867 us -> 718 us (0.83)
  waiting for transfers between devices: 420 us -> 261 us
  other arithmetic: 38.1 us -> 52.9 us
    ppermute x6 -> x18, waiting for transfers between devices: 174 us -> 80.1 us  [turn(): lax.ppermute(x, 'row', [(i, (i + 2 * steps) % count) for i in range(count)])]
    ppermute x53 -> x60, waiting for transfers between devices: 245 us -> 181 us  [swap(): lax.ppermute(x, axis, [(i, i ^ bit) for i in range(lax.axis_size(axis))])]
    ppermute x6 -> x18, starting transfers between devices: 19.6 us -> 33.9 us  [turn(): lax.ppermute(x, 'row', [(i, (i + 2 * steps) % count) for i in range(count)])]
    convert_element_type x3 -> x12, other arithmetic: 7.38 us -> 17.7 us  [add(): self.carry = turn(total.astype(bf16), -1)]
    ppermute x53 -> x60, starting transfers between devices: 55 us -> 47.2 us  [swap(): lax.ppermute(x, axis, [(i, i ^ bit) for i in range(lax.axis_size(axis))])]
    pallas_call x30 -> x28, Pallas kernels: 243 us -> 238 us  [matmul_call(): pl.pallas_call(kernel, grid_spec=pltpu.PrefetchScalarGridSpec(num_scalar_...]
  transfers between devices with their start and end apart: 64 -> 79, of which waited for: 36 -> 44; matrix products, arithmetic and copies ran while one was open for 6% -> 8% of each run, Pallas kernels for 29% -> 35%
where the time goes in v4:
time: 718 us; the launch traced here: 712 us
  Pallas kernels  276 us (38%)
  waiting for transfers between devices  261 us (36%)
  starting transfers between devices  81.2 us (11%)
  other arithmetic  52.9 us (7%)
  local copies, waits for them, and re-layouts  25.5 us (4%)
  between operations  15.4 us (2%)
    pallas_call x28, Pallas kernels, matmul_call(): pl.pallas_call(kernel, grid_spec=pltpu.PrefetchScalarGridSpec(num_scalar_...  238 us
    ppermute x60, waiting for transfers between devices, swap(): lax.ppermute(x, axis, [(i, i ^ bit) for i in range(lax.axis_size(axis))])  181 us
    ppermute x18, waiting for transfers between devices, turn(): lax.ppermute(x, 'row', [(i, (i + 2 * steps) % count) for i in range(count)])  80.1 us
    ppermute x60, starting transfers between devices, swap(): lax.ppermute(x, axis, [(i, i ^ bit) for i in range(lax.axis_size(axis))])  47.2 us
    ppermute x18, starting transfers between devices, turn(): lax.ppermute(x, 'row', [(i, (i + 2 * steps) % count) for i in range(count)])  33.9 us
    pallas_call x1, Pallas kernels, attend_backward(): pl.pallas_call(partial(attend_back_kernel, rows=rows, scale=HD ** (-0.5))...  20.4 us
    convert_element_type x12, other arithmetic, add(): self.carry = turn(total.astype(bf16), -1)  17.7 us
    pallas_call x1, Pallas kernels, attend_forward(): pl.pallas_call(partial(attend_kernel, rows=rows, scale=HD ** (-0.5)), gri...  17.3 us
  transfers between devices with their start and end apart: 79, of which 44 were waited for; matrix products, arithmetic and copies ran while one was open for 8% of the time, Pallas kernels for 35%

profile of v4, /device:TPU:0, one launch (start us, length us, event | category | flops | bytes accessed | tf_op | source)
XLA Modules:
  0.0 712.0 jit_solution(8949315592082461791)
XLA Ops:
  11.7 2.6 collective-permute-start.1
  17.4 20.6 %collective-permute-done.1.refs_2_ = bf16[1024,512]{1,0:T(8,128)(2,1)S(1)} collective-permute-done((bf16[1024,512]{1,0:T(8,128)(2,1)S(1)}, bf16[1024,512]{1,0:T(8,128)(2,1)S(1)}, u32[]{:S(2)}, u32[]{:S(2)}) %collective-permute-start.1) | collective-permute-done | bytes 1048608 | tf_op jit(solution)/shard_map/ppermute | solution.py:429
  39.5 3.1 collective-permute-done.3.refs_2_
  45.8 21.0 %collective-permute-done.5.refs_6_ = bf16[256,2048]{1,0:T(8,128)(2,1)S(1)} collective-permute-done((bf16[256,2048]{1,0:T(8,128)(2,1)S(1)}, bf16[256,2048]{1,0:T(8,128)(2,1)S(1)}, u32[]{:S(2)}, u32[]{:S(2)}) %collective-permute-start.5) | collective-permute-done | bytes 1048608 | tf_op jit(solution)/shard_map/ppermute | solution.py:429
  72.4 2.9 collective-permute-done.10
  75.4 17.7 %collective-permute-done.11.refs_7_ = bf16[256,2048]{1,0:T(8,128)(2,1)S(1)} collective-permute-done((bf16[256,2048]{1,0:T(8,128)(2,1)S(1)}, bf16[256,2048]{1,0:T(8,128)(2,1)S(1)}, u32[]{:S(2)}, u32[]{:S(2)}) %collective-permute-start.11) | collective-permute-done | bytes 1048608 | tf_op jit(solution)/shard_map/ppermute | solution.py:429
  93.1 3.3 collective-permute-done.12.refs_4_
  100.9 21.7 %collective-permute-done.16.refs_2_ = bf16[256,2048]{1,0:T(8,128)(2,1)} collective-permute-done((bf16[256,2048]{1,0:T(8,128)(2,1)}, bf16[256,2048]{1,0:T(8,128)(2,1)}, u32[]{:S(2)}, u32[]{:S(2)}) %collective-permute-start.16) | collective-permute-done | bytes 1048608 | tf_op jit(solution)/shard_map/ppermute | solution.py:434
  123.5 5.5 cotangent_rows.1.a_ref.refs_0_
  129.6 7.2 %first_norm.1 = (bf16[1024,2048]{1,0:T(8,128)(2,1)}, f32[1024,1]{1,0:T(8,128)}, f32[1024,1]{1,0:T(8,128)}) custom-call(s32[8]{0:T(128)} %get-tuple-element.308.place_ref, bf16[1024,512]{1,0:T(8,128)(2,1)} %refs_0_.1, bf16[1024,512]{1,0:T(8,128)(2,1)} %copy-done.36, bf16[1024,512]{1,0:T(8,128)(2,1)} %copy-done.38, bf16[1024,512]{1,0:T(8,128)(2,1)} %copy-done.39, ...), custom_call_target="tpu_custom_call" | custom-call | flops 262144 | bytes 131456 | tf_op jit(solution)/shard_map/first_norm/pallas_call | solution.py:229
  138.2 6.5 collective-permute-done.15.refs_8_
  150.3 14.5 %mix.1 = (bf16[1024,1536]{1,0:T(8,128)(2,1)}, bf16[1024,2048]{1,0:T(8,128)(2,1)}, bf16[1024,2048]{1,0:T(8,128)(2,1)}) custom-call(bf16[1024,2048]{1,0:T(8,128)(2,1)} %get-tuple-element.275.refs_0_.a_ref, bf16[256,2048]{1,0:T(8,128)(2,1)} %copy-done.10, bf16[256,2048]{1,0:T(8,128)(2,1)} %copy-done.33, bf16[256,2048]{1,0:T(8,128)(2,1)} %copy-done.35, ...), custom_call_target="tpu_custom_call" | custom-call | flops 100663296 | bytes 376928 | tf_op jit(solution)/shard_map/mix/pallas_call | solution.py:229
  164.8 17.3 %attend_forward.1 = (bf16[1024,512]{1,0:T(8,128)(2,1)}, f32[4,2,1024]{2,1,0:T(2,128)}) custom-call(f32[8]{0:T(128)} %multiply_exponential_fusion.slope_ref, s32[1,1024,1]{2,1,0:T(8,128)} %copy.28.start_ref, bf16[1024,1536]{1,0:T(8,128)(2,1)} %get-tuple-element.168.q_ref.k_ref.v_ref, bf16[1024,1536]{1,0:T(8,128)(2,1)} %get-tuple-element.168.q_ref.k_ref.v_ref, ...), custom_call_target="tpu_custom_call" | custom-call | flops 67108864 | bytes 98304 | tf_op jit(solution)/shard_map/attend_forward/pallas_call | solution.py:79
  182.1 4.9 collective-permute-done.19.refs_4_
  187.9 4.6 project_sent.1
  197.8 4.1 project_part.1
  204.7 4.7 project_base.1
  209.4 18.0 %collective-permute-done.26 = bf16[1024,512]{1,0:T(8,128)(2,1)S(1)} collective-permute-done((bf16[1024,512]{1,0:T(8,128)(2,1)}, bf16[1024,512]{1,0:T(8,128)(2,1)S(1)}, u32[]{:S(2)}, u32[]{:S(2)}) %collective-permute-start.26) | collective-permute-done | bytes 1048608 | tf_op jit(solution)/shard_map/ppermute | solution.py:429
  227.4 2.2 fusion.19
  233.3 22.9 %collective-permute-done.29.refs_2_ = bf16[1024,512]{1,0:T(8,128)(2,1)S(1)} collective-permute-done((bf16[1024,512]{1,0:T(8,128)(2,1)S(1)}, bf16[1024,512]{1,0:T(8,128)(2,1)S(1)}, u32[]{:S(2)}, u32[]{:S(2)}) %collective-permute-start.29) | collective-permute-done | bytes 1048608 | tf_op jit(solution)/shard_map/ppermute | solution.py:429
  261.1 7.2 %second_norm.1 = (bf16[1024,2048]{1,0:T(8,128)(2,1)}, f32[1024,1]{1,0:T(8,128)}, f32[1024,1]{1,0:T(8,128)}) custom-call(s32[8]{0:T(128)} %get-tuple-element.308.place_ref, bf16[1024,512]{1,0:T(8,128)(2,1)} %copy-done.12, bf16[1024,512]{1,0:T(8,128)(2,1)} %copy-done.43, bf16[1024,512]{1,0:T(8,128)(2,1)} %copy-done.45, bf16[1024,512]{1,0:T(8,128)(2,1)} %copy-done.46, ...), custom_call_target="tpu_custom_call" | custom-call | flops 262144 | bytes 131456 | tf_op jit(solution)/shard_map/second_norm/pallas_call | solution.py:229
  268.3 18.2 %expand.1 = (bf16[1024,2048]{1,0:T(8,128)(2,1)}, f32[1024,2048]{1,0:T(8,128)}, bf16[1024,2048]{1,0:T(8,128)(2,1)}, bf16[1024,2048]{1,0:T(8,128)(2,1)}) custom-call(bf16[1024,2048]{1,0:T(8,128)(2,1)} %get-tuple-element.224.refs_0_.a_ref, bf16[256,2048]{1,0:T(8,128)(2,1)} %refs_1_.1, bf16[256,2048]{1,0:T(8,128)(2,1)} %collective-permute-done.16.refs_2_, ...), custom_call_target="tpu_custom_call" | custom-call | flops 134217728 | bytes 524416 | tf_op jit(solution)/shard_map/expand/pallas_call | solution.py:229
  286.4 11.1 %contract_grad_other.1 = (bf16[512,2048]{1,0:T(8,128)(2,1)}, bf16[256,2048]{1,0:T(8,128)(2,1)}, bf16[256,2048]{1,0:T(8,128)(2,1)}) custom-call(s32[4]{0:T(128)} %get-tuple-element.304.order_ref, bf16[1024,2048]{1,0:T(8,128)(2,1)} %cotangent_rows.1.a_ref.refs_0_, bf16[1024,2048]{1,0:T(8,128)(2,1)} %get-tuple-element.270.refs_0_), custom_call_target="tpu_custom_call" | custom-call | flops 67108864 | bytes 196608 | tf_op jit(solution)/shard_map/contract_grad_other/pallas_call | solution.py:229
  299.2 12.1 %contract_grad_mine.1 = (f32[256,2048]{1,0:T(8,128)}, f32[256,2048]{1,0:T(8,128)}, f32[256,2048]{1,0:T(8,128)}, f32[256,2048]{1,0:T(8,128)}) custom-call(s32[4]{0:T(128)} %get-tuple-element.303.order_ref, bf16[1024,2048]{1,0:T(8,128)(2,1)} %cotangent_rows.1.a_ref.refs_0_, bf16[1024,2048]{1,0:T(8,128)(2,1)} %get-tuple-element.270.refs_0_), custom_call_target="tpu_custom_call" | custom-call | flops 67108864 | bytes 262144 | tf_op jit(solution)/shard_map/contract_grad_mine/pallas_call | solution.py:229
  311.3 14.3 %contract_back.1 = (bf16[1024,2048]{1,0:T(8,128)(2,1)}, f32[1,2048]{1,0:T(1,128)}) custom-call(bf16[1024,2048]{1,0:T(8,128)(2,1)} %cotangent_rows.1.a_ref.refs_0_, bf16[2048,2048]{1,0:T(8,128)(2,1)} %all-gather.2.cloned.1.call-done.refs_1_.refs_2_, f32[1024,2048]{1,0:T(8,128)} %get-tuple-element.196.refs_2_), custom_call_target="tpu_custom_call" | custom-call | flops 134217728 | bytes 393344 | tf_op jit(solution)/shard_map/contract_back/pallas_call | solution.py:229
  325.6 9.2 %expand_back_sent.1 = (bf16[256,1024]{1,0:T(8,128)(2,1)}, bf16[256,1024]{1,0:T(8,128)(2,1)}, bf16[256,1024]{1,0:T(8,128)(2,1)}, bf16[256,1024]{1,0:T(8,128)(2,1)}) custom-call(s32[2,2]{1,0:T(2,128)} %bitcast.57, s32[1]{0:T(128)} %bitcast.2.side_ref, bf16[1024,2048]{1,0:T(8,128)(2,1)} %get-tuple-element.210.refs_0_, ...), custom_call_target="tpu_custom_call" | custom-call | flops 67108864 | bytes 229376 | tf_op jit(solution)/shard_map/expand_back_sent/pallas_call | solution.py:229
  335.8 9.8 %collective-permute-done.32 = bf16[512,2048]{1,0:T(8,128)(2,1)} collective-permute-done((bf16[512,2048]{1,0:T(8,128)(2,1)}, bf16[512,2048]{1,0:T(8,128)(2,1)}, u32[]{:S(2)}, u32[]{:S(2)}) %collective-permute-start.32) | collective-permute-done | bytes 2097184 | tf_op jit(solution)/shard_map/ppermute | solution.py:429
  345.5 2.8 fusion.20
  350.3 7.1 expand_back_part.1
  359.0 2.9 add_convert_fusion.6
  361.8 13.1 %collective-permute-start.38 = (bf16[256,2048]{1,0:T(8,128)(2,1)}, bf16[256,2048]{1,0:T(8,128)(2,1)}, u32[]{:S(2)}, u32[]{:S(2)}) collective-permute-start(bf16[256,2048]{1,0:T(8,128)(2,1)} %add_convert_fusion.6), channel_id=1, source_target_pairs={{0,24},{4,28},{8,0},{12,4},{16,8},{20,12},{24,16},{28,20},{1,25},{... | collective-permute-start | bytes 3145736 | tf_op jit(solution)/shard_map/ppermute | solution.py:434
  379.2 7.5 %expand_back_base.1 = f32[1024,512]{1,0:T(8,128)} custom-call(s32[2,1]{1,0:T(2,128)} %get-tuple-element.346.order_ref, s32[1]{0:T(128)} %bitcast.2.side_ref, bf16[1024,2048]{1,0:T(8,128)(2,1)} %get-tuple-element.210.refs_0_, bf16[1024,2048]{1,0:T(8,128)(2,1)} %get-tuple-element.203.refs_1_, bf16[1024,2048]{1,0:T(8,128)(2,1)} %get-tuple-element.204.refs_2_, ...), custom_call_target="tpu_custom_call" | custom-call | flops 33554432 | bytes 262144 | tf_op jit(solution)/shard_map/expand_back_base/pallas_call | solution.py:229
  386.7 11.0 %expand_grad_other.1 = (bf16[256,2048]{1,0:T(8,128)(2,1)}, bf16[256,2048]{1,0:T(8,128)(2,1)}, bf16[256,2048]{1,0:T(8,128)(2,1)}, bf16[256,2048]{1,0:T(8,128)(2,1)}) custom-call(s32[4]{0:T(128)} %get-tuple-element.305.order_ref, bf16[1024,2048]{1,0:T(8,128)(2,1)} %get-tuple-element.224.refs_0_.a_ref, bf16[1024,2048]{1,0:T(8,128)(2,1)} %get-tuple-element.210.refs_0_), custom_call_target="tpu_custom_call" | custom-call | flops 67108864 | bytes 196608 | tf_op jit(solution)/shard_map/expand_grad_other/pallas_call | solution.py:229
  402.1 2.7 add_convert_fusion.5
  412.2 12.3 %expand_grad_mine.1 = (f32[256,2048]{1,0:T(8,128)}, f32[256,2048]{1,0:T(8,128)}, f32[256,2048]{1,0:T(8,128)}, f32[256,2048]{1,0:T(8,128)}) custom-call(s32[4]{0:T(128)} %get-tuple-element.302.order_ref, bf16[1024,2048]{1,0:T(8,128)(2,1)} %get-tuple-element.224.refs_0_.a_ref, bf16[1024,2048]{1,0:T(8,128)(2,1)} %get-tuple-element.210.refs_0_), custom_call_target="tpu_custom_call" | custom-call | flops 67108864 | bytes 262144 | tf_op jit(solution)/shard_map/expand_grad_mine/pallas_call | solution.py:229
  424.5 5.6 collective-permute-done.44
  431.8 4.4 collective-permute-done.43.refs_2_
  439.2 5.5 branch_rows.1.a_ref.refs_0_
  444.7 5.7 projection_grad_other.1
  450.4 6.2 project_back.1.g_ref
  456.7 5.4 collective-permute-done.47
  463.6 2.9 add_convert_fusion.3
  470.3 20.4 %attend_backward.1 = (bf16[1024,512]{1,0:T(8,128)(2,1)}, bf16[1024,512]{1,0:T(8,128)(2,1)}, bf16[1024,512]{1,0:T(8,128)(2,1)}, f32[1,1,512]{2,1,0:T(1,128)}, f32[1,1,512]{2,1,0:T(1,128)}) custom-call(f32[8]{0:T(128)} %multiply_exponential_fusion.slope_ref, s32[1,1,1024]{2,1,0:T(1,128)} %bitcast.55, f32[4,2,1024]{2,1,0:T(2,128)} %get-tuple-element.235.log_ref, ...), custom_call_target="tpu_custom_call" | custom-call | flops 167772160 | bytes 114688 | tf_op jit(solution)/shard_map/attend_backward/pallas_call | solution.py:183
  493.3 7.7 %mix_back_sent.1 = (bf16[256,1024]{1,0:T(8,128)(2,1)}, bf16[256,1024]{1,0:T(8,128)(2,1)}, bf16[256,1024]{1,0:T(8,128)(2,1)}, bf16[256,1024]{1,0:T(8,128)(2,1)}) custom-call(s32[2,2]{1,0:T(2,128)} %bitcast.58, s32[1]{0:T(128)} %bitcast.2.side_ref, bf16[1024,512]{1,0:T(8,128)(2,1)} %get-tuple-element.254.refs_0_, ...), custom_call_target="tpu_custom_call" | custom-call | flops 50331648 | bytes 212992 | tf_op jit(solution)/shard_map/mix_back_sent/pallas_call | solution.py:229
  507.5 8.8 %mixing_grad_other.1 = (bf16[256,1536]{1,0:T(8,128)(2,1)}, bf16[256,1536]{1,0:T(8,128)(2,1)}, bf16[256,1536]{1,0:T(8,128)(2,1)}, bf16[256,1536]{1,0:T(8,128)(2,1)}) custom-call(s32[4]{0:T(128)} %get-tuple-element.305.order_ref, bf16[1024,2048]{1,0:T(8,128)(2,1)} %get-tuple-element.275.refs_0_.a_ref, bf16[1024,512]{1,0:T(8,128)(2,1)} %get-tuple-element.254.refs_0_, ...), custom_call_target="tpu_custom_call" | custom-call | flops 50331648 | bytes 163840 | tf_op jit(solution)/shard_map/mixing_grad_other/pallas_call | solution.py:229
  516.3 6.1 mix_back_part.1
  522.4 5.9 collective-permute-done.52
  530.2 9.6 %contract_sent.1 = bf16[1024,1024]{1,0:T(8,128)(2,1)} custom-call(s32[2,2]{1,0:T(2,128)} %bitcast.68, s32[1]{0:T(128)} %bitcast.2.side_ref, bf16[1024,2048]{1,0:T(8,128)(2,1)} %get-tuple-element.270.refs_0_, bf16[2048,2048]{1,0:T(8,128)(2,1)} %all-gather.2.cloned.1.call-done.refs_1_.refs_2_, bf16[2048,2048]{1,0:T(8,128)(2,1)} %all-gather.2.cloned.1.call-done.refs_1_.refs_2_), custom_call_target="tpu_custom_call" | custom-call | flops 67108864 | bytes 360448 | tf_op jit(solution)/shard_map/contract_sent/pallas_call | solution.py:229
  543.6 2.4 collective-permute-start.57
  547.7 6.6 mix_back_base.1
  554.3 11.2 %collective-permute-done.59 = bf16[1024,512]{1,0:T(8,128)(2,1)} collective-permute-done((bf16[1024,512]{1,0:T(8,128)(2,1)S(1)}, bf16[1024,512]{1,0:T(8,128)(2,1)}, u32[]{:S(2)}, u32[]{:S(2)}) %collective-permute-start.59) | collective-permute-done | bytes 1048608 | tf_op jit(solution)/shard_map/ppermute | solution.py:429
  565.5 3.5 convert_add_fusion.4
  578.2 2.7 fusion.5
  581.0 6.0 projection_grad_mine.1
  587.1 7.4 %contract_part.1 = bf16[1024,512]{1,0:T(8,128)(2,1)} custom-call(s32[2,1]{1,0:T(2,128)} %get-tuple-element.343.order_ref, s32[1]{0:T(128)} %bitcast.2.side_ref, bf16[1024,2048]{1,0:T(8,128)(2,1)} %get-tuple-element.270.refs_0_, bf16[2048,2048]{1,0:T(8,128)(2,1)} %all-gather.2.cloned.1.call-done.refs_1_.refs_2_, ...), custom_call_target="tpu_custom_call" | custom-call | flops 33554432 | bytes 376832 | tf_op jit(solution)/shard_map/contract_part/pallas_call | solution.py:229
  597.7 3.0 convert_add_fusion.2
  605.8 2.5 collective-permute-start.66
  608.3 7.6 %contract_base.1 = f32[1024,512]{1,0:T(8,128)} custom-call(s32[2,1]{1,0:T(2,128)} %get-tuple-element.344.order_ref, s32[1]{0:T(128)} %bitcast.2.side_ref, bf16[1024,2048]{1,0:T(8,128)(2,1)} %get-tuple-element.270.refs_0_, bf16[2048,2048]{1,0:T(8,128)(2,1)} %all-gather.2.cloned.1.call-done.refs_1_.refs_2_, ...), custom_call_target="tpu_custom_call" | custom-call | flops 33554432 | bytes 393216 | tf_op jit(solution)/shard_map/contract_base/pallas_call | solution.py:229
  615.9 10.1 %mixing_grad_mine.1 = (f32[256,1536]{1,0:T(8,128)}, f32[256,1536]{1,0:T(8,128)}, f32[256,1536]{1,0:T(8,128)}, f32[256,1536]{1,0:T(8,128)}) custom-call(s32[4]{0:T(128)} %get-tuple-element.302.order_ref, bf16[1024,2048]{1,0:T(8,128)(2,1)} %get-tuple-element.275.refs_0_.a_ref, bf16[1024,512]{1,0:T(8,128)(2,1)} %get-tuple-element.254.refs_0_, ...), custom_call_target="tpu_custom_call" | custom-call | flops 50331648 | bytes 212992 | tf_op jit(solution)/shard_map/mixing_grad_mine/pallas_call | solution.py:229
  635.8 18.3 %collective-permute-done.69 = bf16[256,512]{1,0:T(8,128)(2,1)S(1)} collective-permute-done((bf16[256,512]{1,0:T(8,128)(2,1)S(1)}, bf16[256,512]{1,0:T(8,128)(2,1)S(1)}, u32[]{:S(2)}, u32[]{:S(2)}) %collective-permute-start.69) | collective-permute-done | bytes 262176 | tf_op jit(solution)/shard_map/ppermute | solution.py:434
  662.9 17.5 %collective-permute-done.72 = f32[12,512]{1,0:T(8,128)S(1)} collective-permute-done((f32[12,512]{1,0:T(8,128)S(1)}, f32[12,512]{1,0:T(8,128)S(1)}, u32[]{:S(2)}, u32[]{:S(2)}) %collective-permute-start.72) | collective-permute-done | bytes 24608 | tf_op jit(solution)/shard_map/ppermute | solution.py:429
  680.8 3.1 collective-permute-start.77
  689.8 11.0 %collective-permute-done.77 = bf16[256,1536]{1,0:T(8,128)(2,1)S(1)} collective-permute-done((bf16[256,1536]{1,0:T(8,128)(2,1)S(1)}, bf16[256,1536]{1,0:T(8,128)(2,1)S(1)}, u32[]{:S(2)}, u32[]{:S(2)}) %collective-permute-start.77) | collective-permute-done | bytes 786464 | tf_op jit(solution)/shard_map/ppermute | solution.py:434
  700.8 2.2 collective-permute-done.76
  (367 shorter events, 140.6 us)
Async XLA Ops:
  7.2 304.1 %all-gather.2.cloned.1.call-start = ((), (), s32[]{:S(2)}) async-start(), calls=%async_computation | async-start | bytes 10485760 | tf_op jit(solution)/shard_map/all_gather | solution.py:471
  11.7 26.3 %collective-permute-start.1 = (bf16[1024,512]{1,0:T(8,128)(2,1)S(1)}, bf16[1024,512]{1,0:T(8,128)(2,1)S(1)}, u32[]{:S(2)}, u32[]{:S(2)}) collective-permute-start(bf16[1024,512]{1,0:T(8,128)(2,1)S(1)} %copy-done.1), channel_id=1, source_target_pairs={{0,2},{1,3},{2,0},{3,1},{4,6},{5,7},{6,4},{7,5},{8,10},{9,11},{10,... | collective-permute-start | bytes 3145736 | tf_op jit(solution)/shard_map/ppermute | solution.py:429
  14.3 25.2 %collective-permute-start.2 = (bf16[256,2048]{1,0:T(8,128)(2,1)S(1)}, bf16[256,2048]{1,0:T(8,128)(2,1)S(1)}, u32[]{:S(2)}, u32[]{:S(2)}) collective-permute-start(bf16[256,2048]{1,0:T(8,128)(2,1)S(1)} %pad_maximum_fusion.1.refs_1_), channel_id=1, source_target_pairs={{0,4},{4,0},{8,12},{12,8},{16,20},{20,16},{24,28},{28,24},{1,5},{5... | collective-permute-start | bytes 3145736 | tf_op jit(solution)/shard_map/ppermute | solution.py:429
  15.8 26.8 %collective-permute-start.3 = (bf16[256,2048]{1,0:T(8,128)(2,1)S(1)}, bf16[256,2048]{1,0:T(8,128)(2,1)S(1)}, u32[]{:S(2)}, u32[]{:S(2)}) collective-permute-start(bf16[256,2048]{1,0:T(8,128)(2,1)S(1)} %pad_maximum_fusion.1.refs_1_), channel_id=1, source_target_pairs={{0,8},{4,12},{8,16},{12,20},{16,24},{20,28},{24,0},{28,4},{1,9},{5... | collective-permute-start | bytes 3145736 | tf_op jit(solution)/shard_map/ppermute | solution.py:434
  42.6 24.2 %collective-permute-start.5 = (bf16[256,2048]{1,0:T(8,128)(2,1)S(1)}, bf16[256,2048]{1,0:T(8,128)(2,1)S(1)}, u32[]{:S(2)}, u32[]{:S(2)}) collective-permute-start(bf16[256,2048]{1,0:T(8,128)(2,1)S(1)} %collective-permute-done.3.refs_2_), channel_id=1, source_target_pairs={{0,4},{4,0},{8,12},{12,8},{16,20},{20,16},{24,28},{28,24},{1,5},{5... | collective-permute-start | bytes 3145736 | tf_op jit(solution)/shard_map/ppermute | solution.py:429
  43.1 25.7 %collective-permute-start.6 = (bf16[256,2048]{1,0:T(8,128)(2,1)S(1)}, bf16[256,2048]{1,0:T(8,128)(2,1)S(1)}, u32[]{:S(2)}, u32[]{:S(2)}) collective-permute-start(bf16[256,2048]{1,0:T(8,128)(2,1)S(1)} %collective-permute-done.3.refs_2_), channel_id=1, source_target_pairs={{0,8},{4,12},{8,16},{12,20},{16,24},{20,28},{24,0},{28,4},{1,9},{5... | collective-permute-start | bytes 3145736 | tf_op jit(solution)/shard_map/ppermute | solution.py:434
  43.1 25.7 %collective-permute-start.7 = (bf16[1024,512]{1,0:T(8,128)(2,1)S(1)}, bf16[1024,512]{1,0:T(8,128)(2,1)S(1)}, u32[]{:S(2)}, u32[]{:S(2)}) collective-permute-start(bf16[1024,512]{1,0:T(8,128)(2,1)S(1)} %copy-done.7), channel_id=1, source_target_pairs={{0,1},{1,0},{2,3},{3,2},{4,5},{5,4},{6,7},{7,6},{8,9},{9,8},{10,11... | collective-permute-start | bytes 3145736 | tf_op jit(solution)/shard_map/ppermute | solution.py:429
  43.6 25.2 %collective-permute-start.8 = (bf16[1024,512]{1,0:T(8,128)(2,1)S(1)}, bf16[1024,512]{1,0:T(8,128)(2,1)S(1)}, u32[]{:S(2)}, u32[]{:S(2)}) collective-permute-start(bf16[1024,512]{1,0:T(8,128)(2,1)S(1)} %copy-done.7), channel_id=1, source_target_pairs={{0,2},{1,3},{2,0},{3,1},{4,6},{5,7},{6,4},{7,5},{8,10},{9,11},{10,... | collective-permute-start | bytes 3145736 | tf_op jit(solution)/shard_map/ppermute | solution.py:429
  68.8 24.2 %collective-permute-start.11 = (bf16[256,2048]{1,0:T(8,128)(2,1)S(1)}, bf16[256,2048]{1,0:T(8,128)(2,1)S(1)}, u32[]{:S(2)}, u32[]{:S(2)}) collective-permute-start(bf16[256,2048]{1,0:T(8,128)(2,1)S(1)} %collective-permute-done.6.refs_3_), channel_id=1, source_target_pairs={{0,4},{4,0},{8,12},{12,8},{16,20},{20,16},{24,28},{28,24},{1,5},{5... | collective-permute-start | bytes 3145736 | tf_op jit(solution)/shard_map/ppermute | solution.py:429
  70.4 25.9 %collective-permute-start.12 = (bf16[256,2048]{1,0:T(8,128)(2,1)S(1)}, bf16[256,2048]{1,0:T(8,128)(2,1)}, u32[]{:S(2)}, u32[]{:S(2)}) collective-permute-start(bf16[256,2048]{1,0:T(8,128)(2,1)S(1)} %collective-permute-done.6.refs_3_), channel_id=1, source_target_pairs={{0,8},{4,12},{8,16},{12,20},{16,24},{20,28},{24,0},{28,4},{1,9},{5... | collective-permute-start | bytes 3145736 | tf_op jit(solution)/shard_map/ppermute | solution.py:434
  71.5 24.8 %collective-permute-start.13 = (bf16[1024,512]{1,0:T(8,128)(2,1)S(1)}, bf16[1024,512]{1,0:T(8,128)(2,1)S(1)}, u32[]{:S(2)}, u32[]{:S(2)}) collective-permute-start(bf16[1024,512]{1,0:T(8,128)(2,1)S(1)} %collective-permute-done.8.refs_2_), channel_id=1, source_target_pairs={{0,1},{1,0},{2,3},{3,2},{4,5},{5,4},{6,7},{7,6},{8,9},{9,8},{10,11... | collective-permute-start | bytes 3145736 | tf_op jit(solution)/shard_map/ppermute | solution.py:429
  97.3 25.2 %collective-permute-start.16 = (bf16[256,2048]{1,0:T(8,128)(2,1)}, bf16[256,2048]{1,0:T(8,128)(2,1)}, u32[]{:S(2)}, u32[]{:S(2)}) collective-permute-start(bf16[256,2048]{1,0:T(8,128)(2,1)} %refs_1_.1), channel_id=1, source_target_pairs={{0,8},{4,12},{8,16},{12,20},{16,24},{20,28},{24,0},{28,4},{1,9},{5... | collective-permute-start | bytes 3145736 | tf_op jit(solution)/shard_map/ppermute | solution.py:434
  98.7 38.2 %collective-permute-start.18 = (bf16[256,2048]{1,0:T(8,128)(2,1)}, bf16[256,2048]{1,0:T(8,128)(2,1)}, u32[]{:S(2)}, u32[]{:S(2)}) collective-permute-start(bf16[256,2048]{1,0:T(8,128)(2,1)} %param.21), channel_id=1, source_target_pairs={{0,4},{4,0},{8,12},{12,8},{16,20},{20,16},{24,28},{28,24},{1,5},{5... | collective-permute-start | bytes 3145736 | tf_op jit(solution)/shard_map/ppermute | solution.py:429
  99.4 45.3 %collective-permute-start.15 = (bf16[256,2048]{1,0:T(8,128)(2,1)}, bf16[256,2048]{1,0:T(8,128)(2,1)}, u32[]{:S(2)}, u32[]{:S(2)}) collective-permute-start(bf16[256,2048]{1,0:T(8,128)(2,1)} %collective-permute-done.12.refs_4_), channel_id=1, source_target_pairs={{0,4},{4,0},{8,12},{12,8},{16,20},{20,16},{24,28},{28,24},{1,5},{5... | collective-permute-start | bytes 3145736 | tf_op jit(solution)/shard_map/ppermute | solution.py:429
  122.5 24.3 %collective-permute-start.17 = (bf16[256,2048]{1,0:T(8,128)(2,1)}, bf16[256,2048]{1,0:T(8,128)(2,1)}, u32[]{:S(2)}, u32[]{:S(2)}) collective-permute-start(bf16[256,2048]{1,0:T(8,128)(2,1)} %collective-permute-done.16.refs_2_), channel_id=1, source_target_pairs={{0,8},{4,12},{8,16},{12,20},{16,24},{20,28},{24,0},{28,4},{1,9},{5... | collective-permute-start | bytes 3145736 | tf_op jit(solution)/shard_map/ppermute | solution.py:434
  146.9 40.2 %collective-permute-start.19 = (bf16[256,2048]{1,0:T(8,128)(2,1)}, bf16[256,2048]{1,0:T(8,128)(2,1)S(1)}, u32[]{:S(2)}, u32[]{:S(2)}) collective-permute-start(bf16[256,2048]{1,0:T(8,128)(2,1)} %collective-permute-done.17.refs_3_), channel_id=1, source_target_pairs={{0,8},{4,12},{8,16},{12,20},{16,24},{20,28},{24,0},{28,4},{1,9},{5... | collective-permute-start | bytes 3145736 | tf_op jit(solution)/shard_map/ppermute | solution.py:434
  146.9 40.1 %collective-permute-start.20 = (bf16[256,2048]{1,0:T(8,128)(2,1)}, bf16[256,2048]{1,0:T(8,128)(2,1)S(1)}, u32[]{:S(2)}, u32[]{:S(2)}) collective-permute-start(bf16[256,2048]{1,0:T(8,128)(2,1)} %refs_1_.1), channel_id=1, source_target_pairs={{0,4},{4,0},{8,12},{12,8},{16,20},{20,16},{24,28},{28,24},{1,5},{5... | collective-permute-start | bytes 3145736 | tf_op jit(solution)/shard_map/ppermute | solution.py:429
  187.1 15.5 %collective-permute-start.21 = (bf16[256,2048]{1,0:T(8,128)(2,1)}, bf16[256,2048]{1,0:T(8,128)(2,1)S(1)}, u32[]{:S(2)}, u32[]{:S(2)}) collective-permute-start(bf16[256,2048]{1,0:T(8,128)(2,1)} %collective-permute-done.16.refs_2_), channel_id=1, source_target_pairs={{0,4},{4,0},{8,12},{12,8},{16,20},{20,16},{24,28},{28,24},{1,5},{5... | collective-permute-start | bytes 3145736 | tf_op jit(solution)/shard_map/ppermute | solution.py:429
  202.6 24.8 %collective-permute-start.26 = (bf16[1024,512]{1,0:T(8,128)(2,1)}, bf16[1024,512]{1,0:T(8,128)(2,1)S(1)}, u32[]{:S(2)}, u32[]{:S(2)}) collective-permute-start(bf16[1024,512]{1,0:T(8,128)(2,1)} %project_part.1), channel_id=1, source_target_pairs={{0,2},{1,3},{2,0},{3,1},{4,6},{5,7},{6,4},{7,5},{8,10},{9,11},{10,... | collective-permute-start | bytes 3145736 | tf_op jit(solution)/shard_map/ppermute | solution.py:429
  203.0 26.6 %collective-permute-start.27 = (bf16[256,2048]{1,0:T(8,128)(2,1)}, bf16[256,2048]{1,0:T(8,128)(2,1)S(1)}, u32[]{:S(2)}, u32[]{:S(2)}) collective-permute-start(bf16[256,2048]{1,0:T(8,128)(2,1)} %collective-permute-done.17.refs_3_), channel_id=1, source_target_pairs={{0,4},{4,0},{8,12},{12,8},{16,20},{20,16},{24,28},{28,24},{1,5},{5... | collective-permute-start | bytes 3145736 | tf_op jit(solution)/shard_map/ppermute | solution.py:429
  230.6 25.6 %collective-permute-start.29 = (bf16[1024,512]{1,0:T(8,128)(2,1)S(1)}, bf16[1024,512]{1,0:T(8,128)(2,1)S(1)}, u32[]{:S(2)}, u32[]{:S(2)}) collective-permute-start(bf16[1024,512]{1,0:T(8,128)(2,1)S(1)} %get-tuple-element.183.refs_0_), channel_id=1, source_target_pairs={{0,2},{1,3},{2,0},{3,1},{4,6},{5,7},{6,4},{7,5},{8,10},{9,11},{10,... | collective-permute-start | bytes 3145736 | tf_op jit(solution)/shard_map/ppermute | solution.py:429
  230.9 25.4 %collective-permute-start.30 = (bf16[256,2048]{1,0:T(8,128)(2,1)S(1)}, bf16[256,2048]{1,0:T(8,128)(2,1)S(1)}, u32[]{:S(2)}, u32[]{:S(2)}) collective-permute-start(bf16[256,2048]{1,0:T(8,128)(2,1)S(1)} %copy-done.56), channel_id=1, source_target_pairs={{0,4},{4,0},{8,12},{12,8},{16,20},{20,16},{24,28},{28,24},{1,5},{5... | collective-permute-start | bytes 3145736 | tf_op jit(solution)/shard_map/ppermute | solution.py:429
  297.5 48.0 %collective-permute-start.32 = (bf16[512,2048]{1,0:T(8,128)(2,1)}, bf16[512,2048]{1,0:T(8,128)(2,1)}, u32[]{:S(2)}, u32[]{:S(2)}) collective-permute-start(bf16[512,2048]{1,0:T(8,128)(2,1)} %get-tuple-element.198), channel_id=1, source_target_pairs={{0,4},{4,0},{8,12},{12,8},{16,20},{20,16},{24,28},{28,24},{1,5},{5... | collective-permute-start | bytes 6291464 | tf_op jit(solution)/shard_map/ppermute | solution.py:429
  334.8 13.5 %collective-permute-start.33 = (bf16[256,1024]{1,0:T(8,128)(2,1)}, bf16[256,1024]{1,0:T(8,128)(2,1)S(1)}, u32[]{:S(2)}, u32[]{:S(2)}) collective-permute-start(bf16[256,1024]{1,0:T(8,128)(2,1)} %get-tuple-element.206), channel_id=1, source_target_pairs={{0,1},{1,0},{2,3},{3,2},{4,5},{5,4},{6,7},{7,6},{8,9},{9,8},{10,11... | collective-permute-start | bytes 1572872 | tf_op jit(solution)/shard_map/ppermute | solution.py:429
  334.8 13.5 %collective-permute-start.34 = (bf16[256,1024]{1,0:T(8,128)(2,1)}, bf16[256,1024]{1,0:T(8,128)(2,1)S(1)}, u32[]{:S(2)}, u32[]{:S(2)}) collective-permute-start(bf16[256,1024]{1,0:T(8,128)(2,1)} %get-tuple-element.207), channel_id=1, source_target_pairs={{0,1},{1,0},{2,3},{3,2},{4,5},{5,4},{6,7},{7,6},{8,9},{9,8},{10,11... | collective-permute-start | bytes 1572872 | tf_op jit(solution)/shard_map/ppermute | solution.py:429
  335.3 13.0 %collective-permute-start.35 = (bf16[256,1024]{1,0:T(8,128)(2,1)}, bf16[256,1024]{1,0:T(8,128)(2,1)S(1)}, u32[]{:S(2)}, u32[]{:S(2)}) collective-permute-start(bf16[256,1024]{1,0:T(8,128)(2,1)} %get-tuple-element.208), channel_id=1, source_target_pairs={{0,1},{1,0},{2,3},{3,2},{4,5},{5,4},{6,7},{7,6},{8,9},{9,8},{10,11... | collective-permute-start | bytes 1572872 | tf_op jit(solution)/shard_map/ppermute | solution.py:429
  335.4 13.0 %collective-permute-start.36 = (bf16[256,1024]{1,0:T(8,128)(2,1)}, bf16[256,1024]{1,0:T(8,128)(2,1)S(1)}, u32[]{:S(2)}, u32[]{:S(2)}) collective-permute-start(bf16[256,1024]{1,0:T(8,128)(2,1)} %get-tuple-element.209), channel_id=1, source_target_pairs={{0,1},{1,0},{2,3},{3,2},{4,5},{5,4},{6,7},{7,6},{8,9},{9,8},{10,11... | collective-permute-start | bytes 1572872 | tf_op jit(solution)/shard_map/ppermute | solution.py:429
  357.4 40.4 %collective-permute-start.37 = (bf16[1024,512]{1,0:T(8,128)(2,1)}, bf16[1024,512]{1,0:T(8,128)(2,1)}, u32[]{:S(2)}, u32[]{:S(2)}) collective-permute-start(bf16[1024,512]{1,0:T(8,128)(2,1)} %expand_back_part.1), channel_id=1, source_target_pairs={{0,2},{1,3},{2,0},{3,1},{4,6},{5,7},{6,4},{7,5},{8,10},{9,11},{10,... | collective-permute-start | bytes 3145736 | tf_op jit(solution)/shard_map/ppermute | solution.py:429
  361.8 37.5 %collective-permute-start.38 = (bf16[256,2048]{1,0:T(8,128)(2,1)}, bf16[256,2048]{1,0:T(8,128)(2,1)}, u32[]{:S(2)}, u32[]{:S(2)}) collective-permute-start(bf16[256,2048]{1,0:T(8,128)(2,1)} %add_convert_fusion.6), channel_id=1, source_target_pairs={{0,24},{4,28},{8,0},{12,4},{16,8},{20,12},{24,16},{28,20},{1,25},{... | collective-permute-start | bytes 3145736 | tf_op jit(solution)/shard_map/ppermute | solution.py:434
  374.9 24.4 %collective-permute-start.39 = (bf16[256,2048]{1,0:T(8,128)(2,1)}, bf16[256,2048]{1,0:T(8,128)(2,1)}, u32[]{:S(2)}, u32[]{:S(2)}) collective-permute-start(bf16[256,2048]{1,0:T(8,128)(2,1)} %get-tuple-element.213), channel_id=1, source_target_pairs={{0,4},{4,0},{8,12},{12,8},{16,20},{20,16},{24,28},{28,24},{1,5},{5... | collective-permute-start | bytes 3145736 | tf_op jit(solution)/shard_map/ppermute | solution.py:429
  401.7 6.7 collective-permute-start.41
  404.8 25.2 %collective-permute-start.44 = (bf16[256,2048]{1,0:T(8,128)(2,1)}, bf16[256,2048]{1,0:T(8,128)(2,1)S(1)}, u32[]{:S(2)}, u32[]{:S(2)}) collective-permute-start(bf16[256,2048]{1,0:T(8,128)(2,1)} %add_convert_fusion.5), channel_id=1, source_target_pairs={{0,24},{4,28},{8,0},{12,4},{16,8},{20,12},{24,16},{28,20},{1,25},{... | collective-permute-start | bytes 3145736 | tf_op jit(solution)/shard_map/ppermute | solution.py:434
  406.7 25.1 %collective-permute-start.45 = (bf16[256,2048]{1,0:T(8,128)(2,1)}, bf16[256,2048]{1,0:T(8,128)(2,1)}, u32[]{:S(2)}, u32[]{:S(2)}) collective-permute-start(bf16[256,2048]{1,0:T(8,128)(2,1)} %get-tuple-element.222), channel_id=1, source_target_pairs={{0,4},{4,0},{8,12},{12,8},{16,20},{20,16},{24,28},{28,24},{1,5},{5... | collective-permute-start | bytes 3145736 | tf_op jit(solution)/shard_map/ppermute | solution.py:429
  410.5 21.2 %collective-permute-start.42 = (bf16[1024,512]{1,0:T(8,128)(2,1)S(1)}, bf16[1024,512]{1,0:T(8,128)(2,1)}, u32[]{:S(2)}, u32[]{:S(2)}) collective-permute-start(bf16[1024,512]{1,0:T(8,128)(2,1)S(1)} %get-tuple-element.311.refs_0_), channel_id=1, source_target_pairs={{0,1},{1,0},{2,3},{3,2},{4,5},{5,4},{6,7},{7,6},{8,9},{9,8},{10,11... | collective-permute-start | bytes 3145736 | tf_op jit(solution)/shard_map/ppermute | solution.py:429
  410.5 25.7 %collective-permute-start.43 = (bf16[1024,512]{1,0:T(8,128)(2,1)S(1)}, bf16[1024,512]{1,0:T(8,128)(2,1)}, u32[]{:S(2)}, u32[]{:S(2)}) collective-permute-start(bf16[1024,512]{1,0:T(8,128)(2,1)S(1)} %get-tuple-element.311.refs_0_), channel_id=1, source_target_pairs={{0,2},{1,3},{2,0},{3,1},{4,6},{5,7},{6,4},{7,5},{8,10},{9,11},{10,... | collective-permute-start | bytes 3145736 | tf_op jit(solution)/shard_map/ppermute | solution.py:429
  436.2 25.9 %collective-permute-start.47 = (bf16[256,2048]{1,0:T(8,128)(2,1)}, bf16[256,2048]{1,0:T(8,128)(2,1)}, u32[]{:S(2)}, u32[]{:S(2)}) collective-permute-start(bf16[256,2048]{1,0:T(8,128)(2,1)} %get-tuple-element.231), channel_id=1, source_target_pairs={{0,4},{4,0},{8,12},{12,8},{16,20},{20,16},{24,28},{28,24},{1,5},{5... | collective-permute-start | bytes 3145736 | tf_op jit(solution)/shard_map/ppermute | solution.py:429
  438.3 25.3 %collective-permute-start.48 = (bf16[256,2048]{1,0:T(8,128)(2,1)S(1)}, bf16[256,2048]{1,0:T(8,128)(2,1)S(1)}, u32[]{:S(2)}, u32[]{:S(2)}) collective-permute-start(bf16[256,2048]{1,0:T(8,128)(2,1)S(1)} %add_convert_fusion.4), channel_id=1, source_target_pairs={{0,24},{4,28},{8,0},{12,4},{16,8},{20,12},{24,16},{28,20},{1,25},{... | collective-permute-start | bytes 3145736 | tf_op jit(solution)/shard_map/ppermute | solution.py:434
  466.5 24.7 %collective-permute-start.49 = (bf16[256,2048]{1,0:T(8,128)(2,1)}, bf16[256,2048]{1,0:T(8,128)(2,1)S(1)}, u32[]{:S(2)}, u32[]{:S(2)}) collective-permute-start(bf16[256,2048]{1,0:T(8,128)(2,1)} %add_convert_fusion.3), channel_id=1, source_target_pairs={{0,24},{4,28},{8,0},{12,4},{16,8},{20,12},{24,16},{28,20},{1,25},{... | collective-permute-start | bytes 3145736 | tf_op jit(solution)/shard_map/ppermute | solution.py:434
  468.6 24.7 %collective-permute-start.50 = (bf16[256,2048]{1,0:T(8,128)(2,1)}, bf16[256,2048]{1,0:T(8,128)(2,1)S(1)}, u32[]{:S(2)}, u32[]{:S(2)}) collective-permute-start(bf16[256,2048]{1,0:T(8,128)(2,1)} %get-tuple-element.234), channel_id=1, source_target_pairs={{0,4},{4,0},{8,12},{12,8},{16,20},{20,16},{24,28},{28,24},{1,5},{5... | collective-permute-start | bytes 3145736 | tf_op jit(solution)/shard_map/ppermute | solution.py:429
  502.5 25.9 %collective-permute-start.52 = (bf16[256,2048]{1,0:T(8,128)(2,1)}, bf16[256,2048]{1,0:T(8,128)(2,1)}, u32[]{:S(2)}, u32[]{:S(2)}) collective-permute-start(bf16[256,2048]{1,0:T(8,128)(2,1)} %add_convert_fusion.2), channel_id=1, source_target_pairs={{0,24},{4,28},{8,0},{12,4},{16,8},{20,12},{24,16},{28,20},{1,25},{... | collective-permute-start | bytes 3145736 | tf_op jit(solution)/shard_map/ppermute | solution.py:434
  504.3 25.8 %collective-permute-start.51 = (bf16[256,2048]{1,0:T(8,128)(2,1)}, bf16[256,2048]{1,0:T(8,128)(2,1)}, u32[]{:S(2)}, u32[]{:S(2)}) collective-permute-start(bf16[256,2048]{1,0:T(8,128)(2,1)} %get-tuple-element.238), channel_id=1, source_target_pairs={{0,4},{4,0},{8,12},{12,8},{16,20},{20,16},{24,28},{28,24},{1,5},{5... | collective-permute-start | bytes 3145736 | tf_op jit(solution)/shard_map/ppermute | solution.py:429
  506.3 10.0 %collective-permute-start.54 = (bf16[256,1024]{1,0:T(8,128)(2,1)}, bf16[256,1024]{1,0:T(8,128)(2,1)}, u32[]{:S(2)}, u32[]{:S(2)}) collective-permute-start(bf16[256,1024]{1,0:T(8,128)(2,1)} %get-tuple-element.249), channel_id=1, source_target_pairs={{0,1},{1,0},{2,3},{3,2},{4,5},{5,4},{6,7},{7,6},{8,9},{9,8},{10,11... | collective-permute-start | bytes 1572872 | tf_op jit(solution)/shard_map/ppermute | solution.py:429
  506.3 10.0 %collective-permute-start.55 = (bf16[256,1024]{1,0:T(8,128)(2,1)}, bf16[256,1024]{1,0:T(8,128)(2,1)}, u32[]{:S(2)}, u32[]{:S(2)}) collective-permute-start(bf16[256,1024]{1,0:T(8,128)(2,1)} %get-tuple-element.250), channel_id=1, source_target_pairs={{0,1},{1,0},{2,3},{3,2},{4,5},{5,4},{6,7},{7,6},{8,9},{9,8},{10,11... | collective-permute-start | bytes 1572872 | tf_op jit(solution)/shard_map/ppermute | solution.py:429
  506.8 9.5 %collective-permute-start.56 = (bf16[256,1024]{1,0:T(8,128)(2,1)}, bf16[256,1024]{1,0:T(8,128)(2,1)}, u32[]{:S(2)}, u32[]{:S(2)}) collective-permute-start(bf16[256,1024]{1,0:T(8,128)(2,1)} %get-tuple-element.251), channel_id=1, source_target_pairs={{0,1},{1,0},{2,3},{3,2},{4,5},{5,4},{6,7},{7,6},{8,9},{9,8},{10,11... | collective-permute-start | bytes 1572872 | tf_op jit(solution)/shard_map/ppermute | solution.py:429
  539.8 32.4 %collective-permute-start.60 = (bf16[1024,1024]{1,0:T(8,128)(2,1)}, bf16[1024,1024]{1,0:T(8,128)(2,1)}, u32[]{:S(2)}, u32[]{:S(2)}) collective-permute-start(bf16[1024,1024]{1,0:T(8,128)(2,1)} %contract_sent.1), channel_id=1, source_target_pairs={{0,1},{1,0},{2,3},{3,2},{4,5},{5,4},{6,7},{7,6},{8,9},{9,8},{10,11... | collective-permute-start | bytes 6291464 | tf_op jit(solution)/shard_map/ppermute | solution.py:429
  539.8 25.7 %collective-permute-start.59 = (bf16[1024,512]{1,0:T(8,128)(2,1)S(1)}, bf16[1024,512]{1,0:T(8,128)(2,1)}, u32[]{:S(2)}, u32[]{:S(2)}) collective-permute-start(bf16[1024,512]{1,0:T(8,128)(2,1)S(1)} %copy-done.44), channel_id=1, source_target_pairs={{0,2},{1,3},{2,0},{3,1},{4,6},{5,7},{6,4},{7,5},{8,10},{9,11},{10,... | collective-permute-start | bytes 3145736 | tf_op jit(solution)/shard_map/ppermute | solution.py:429
  543.6 25.5 %collective-permute-start.57 = (bf16[256,2048]{1,0:T(8,128)(2,1)S(1)}, bf16[256,2048]{1,0:T(8,128)(2,1)S(1)}, u32[]{:S(2)}, u32[]{:S(2)}) collective-permute-start(bf16[256,2048]{1,0:T(8,128)(2,1)S(1)} %add_convert_fusion.1), channel_id=1, source_target_pairs={{0,24},{4,28},{8,0},{12,4},{16,8},{20,12},{24,16},{28,20},{1,25},{... | collective-permute-start | bytes 3145736 | tf_op jit(solution)/shard_map/ppermute | solution.py:434
  546.0 25.2 %collective-permute-start.58 = (bf16[256,2048]{1,0:T(8,128)(2,1)}, bf16[256,2048]{1,0:T(8,128)(2,1)S(1)}, u32[]{:S(2)}, u32[]{:S(2)}) collective-permute-start(bf16[256,2048]{1,0:T(8,128)(2,1)} %get-tuple-element.253), channel_id=1, source_target_pairs={{0,4},{4,0},{8,12},{12,8},{16,20},{20,16},{24,28},{28,24},{1,5},{5... | collective-permute-start | bytes 3145736 | tf_op jit(solution)/shard_map/ppermute | solution.py:429
  572.1 24.4 %collective-permute-start.61 = (bf16[1024,512]{1,0:T(8,128)(2,1)}, bf16[1024,512]{1,0:T(8,128)(2,1)}, u32[]{:S(2)}, u32[]{:S(2)}) collective-permute-start(bf16[1024,512]{1,0:T(8,128)(2,1)} %projection_grad_other.1), channel_id=1, source_target_pairs={{0,4},{4,0},{8,12},{12,8},{16,20},{20,16},{24,28},{28,24},{1,5},{5... | collective-permute-start | bytes 3145736 | tf_op jit(solution)/shard_map/ppermute | solution.py:429
  596.5 29.5 %collective-permute-start.62 = (bf16[1024,512]{1,0:T(8,128)(2,1)}, bf16[1024,512]{1,0:T(8,128)(2,1)S(1)}, u32[]{:S(2)}, u32[]{:S(2)}) collective-permute-start(bf16[1024,512]{1,0:T(8,128)(2,1)} %contract_part.1), channel_id=1, source_target_pairs={{0,2},{1,3},{2,0},{3,1},{4,6},{5,7},{6,4},{7,5},{8,10},{9,11},{10,... | collective-permute-start | bytes 3145736 | tf_op jit(solution)/shard_map/ppermute | solution.py:429
  600.8 57.2 %collective-permute-start.63 = (f32[2,1024]{1,0:T(2,128)S(1)}, f32[2,1024]{1,0:T(2,128)S(1)}, u32[]{:S(2)}, u32[]{:S(2)}) collective-permute-start(f32[2,1024]{1,0:T(2,128)S(1)} %pad_maximum_fusion.5), channel_id=1, source_target_pairs={{0,1},{1,0},{2,3},{3,2},{4,5},{5,4},{6,7},{7,6},{8,9},{9,8},{10,11... | collective-permute-start | bytes 24584 | tf_op jit(solution)/shard_map/ppermute | solution.py:429
  600.9 25.2 %collective-permute-start.65 = (f32[12,512]{1,0:T(8,128)S(1)}, f32[12,512]{1,0:T(8,128)S(1)}, u32[]{:S(2)}, u32[]{:S(2)}) collective-permute-start(f32[12,512]{1,0:T(8,128)S(1)} %concatenate.27), channel_id=1, source_target_pairs={{0,4},{4,0},{8,12},{12,8},{16,20},{20,16},{24,28},{28,24},{1,5},{5... | collective-permute-start | bytes 73736 | tf_op jit(solution)/shard_map/ppermute | solution.py:429
  602.6 25.1 %collective-permute-start.67 = (bf16[256,1536]{1,0:T(8,128)(2,1)}, bf16[256,1536]{1,0:T(8,128)(2,1)}, u32[]{:S(2)}, u32[]{:S(2)}) collective-permute-start(bf16[256,1536]{1,0:T(8,128)(2,1)} %get-tuple-element.274), channel_id=1, source_target_pairs={{0,4},{4,0},{8,12},{12,8},{16,20},{20,16},{24,28},{28,24},{1,5},{5... | collective-permute-start | bytes 2359304 | tf_op jit(solution)/shard_map/ppermute | solution.py:429
  605.8 21.9 %collective-permute-start.66 = (bf16[256,512]{1,0:T(8,128)(2,1)}, bf16[256,512]{1,0:T(8,128)(2,1)}, u32[]{:S(2)}, u32[]{:S(2)}) collective-permute-start(bf16[256,512]{1,0:T(8,128)(2,1)} %add_convert_fusion.12), channel_id=1, source_target_pairs={{0,24},{4,28},{8,0},{12,4},{16,8},{20,12},{24,16},{28,20},{1,25},{... | collective-permute-start | bytes 786440 | tf_op jit(solution)/shard_map/ppermute | solution.py:434
  627.7 8.1 %collective-permute-start.68 = (f32[12,512]{1,0:T(8,128)S(1)}, f32[12,512]{1,0:T(8,128)S(1)}, u32[]{:S(2)}, u32[]{:S(2)}) collective-permute-start(f32[12,512]{1,0:T(8,128)S(1)} %add.356), channel_id=1, source_target_pairs={{0,8},{4,12},{8,0},{12,4},{16,24},{20,28},{24,16},{28,20},{1,9},{5... | collective-permute-start | bytes 73736 | tf_op jit(solution)/shard_map/ppermute | solution.py:429
  629.3 24.9 %collective-permute-start.70 = (bf16[256,1536]{1,0:T(8,128)(2,1)S(1)}, bf16[256,1536]{1,0:T(8,128)(2,1)S(1)}, u32[]{:S(2)}, u32[]{:S(2)}) collective-permute-start(bf16[256,1536]{1,0:T(8,128)(2,1)S(1)} %add_convert_fusion.9), channel_id=1, source_target_pairs={{0,24},{4,28},{8,0},{12,4},{16,8},{20,12},{24,16},{28,20},{1,25},{... | collective-permute-start | bytes 2359304 | tf_op jit(solution)/shard_map/ppermute | solution.py:434
  629.6 24.5 %collective-permute-start.71 = (bf16[256,1536]{1,0:T(8,128)(2,1)S(1)}, bf16[256,1536]{1,0:T(8,128)(2,1)S(1)}, u32[]{:S(2)}, u32[]{:S(2)}) collective-permute-start(bf16[256,1536]{1,0:T(8,128)(2,1)S(1)} %copy-done.79), channel_id=1, source_target_pairs={{0,4},{4,0},{8,12},{12,8},{16,20},{20,16},{24,28},{28,24},{1,5},{5... | collective-permute-start | bytes 2359304 | tf_op jit(solution)/shard_map/ppermute | solution.py:429
  632.5 21.7 %collective-permute-start.69 = (bf16[256,512]{1,0:T(8,128)(2,1)S(1)}, bf16[256,512]{1,0:T(8,128)(2,1)S(1)}, u32[]{:S(2)}, u32[]{:S(2)}) collective-permute-start(bf16[256,512]{1,0:T(8,128)(2,1)S(1)} %add_convert_fusion.11), channel_id=1, source_target_pairs={{0,24},{4,28},{8,0},{12,4},{16,8},{20,12},{24,16},{28,20},{1,25},{... | collective-permute-start | bytes 786440 | tf_op jit(solution)/shard_map/ppermute | solution.py:434
  654.5 25.9 %collective-permute-start.74 = (bf16[256,1536]{1,0:T(8,128)(2,1)S(1)}, bf16[256,1536]{1,0:T(8,128)(2,1)S(1)}, u32[]{:S(2)}, u32[]{:S(2)}) collective-permute-start(bf16[256,1536]{1,0:T(8,128)(2,1)S(1)} %add_convert_fusion.8), channel_id=1, source_target_pairs={{0,24},{4,28},{8,0},{12,4},{16,8},{20,12},{24,16},{28,20},{1,25},{... | collective-permute-start | bytes 2359304 | tf_op jit(solution)/shard_map/ppermute | solution.py:434
  656.5 24.0 %collective-permute-start.75 = (bf16[256,1536]{1,0:T(8,128)(2,1)S(1)}, bf16[256,1536]{1,0:T(8,128)(2,1)S(1)}, u32[]{:S(2)}, u32[]{:S(2)}) collective-permute-start(bf16[256,1536]{1,0:T(8,128)(2,1)S(1)} %copy-done.78), channel_id=1, source_target_pairs={{0,4},{4,0},{8,12},{12,8},{16,20},{20,16},{24,28},{28,24},{1,5},{5... | collective-permute-start | bytes 2359304 | tf_op jit(solution)/shard_map/ppermute | solution.py:429
  659.9 20.5 %collective-permute-start.73 = (bf16[256,512]{1,0:T(8,128)(2,1)S(1)}, bf16[256,512]{1,0:T(8,128)(2,1)S(1)}, u32[]{:S(2)}, u32[]{:S(2)}) collective-permute-start(bf16[256,512]{1,0:T(8,128)(2,1)S(1)} %add_convert_fusion.10), channel_id=1, source_target_pairs={{0,24},{4,28},{8,0},{12,4},{16,8},{20,12},{24,16},{28,20},{1,25},{... | collective-permute-start | bytes 786440 | tf_op jit(solution)/shard_map/ppermute | solution.py:434
  661.8 18.6 %collective-permute-start.72 = (f32[12,512]{1,0:T(8,128)S(1)}, f32[12,512]{1,0:T(8,128)S(1)}, u32[]{:S(2)}, u32[]{:S(2)}) collective-permute-start(f32[12,512]{1,0:T(8,128)S(1)} %add.358), channel_id=1, source_target_pairs={{0,16},{4,20},{8,24},{12,28},{16,0},{20,4},{24,8},{28,12},{1,17},{... | collective-permute-start | bytes 73736 | tf_op jit(solution)/shard_map/ppermute | solution.py:429
  680.8 20.1 %collective-permute-start.77 = (bf16[256,1536]{1,0:T(8,128)(2,1)S(1)}, bf16[256,1536]{1,0:T(8,128)(2,1)S(1)}, u32[]{:S(2)}, u32[]{:S(2)}) collective-permute-start(bf16[256,1536]{1,0:T(8,128)(2,1)S(1)} %add_convert_fusion.7), channel_id=1, source_target_pairs={{0,24},{4,28},{8,0},{12,4},{16,8},{20,12},{24,16},{28,20},{1,25},{... | collective-permute-start | bytes 2359304 | tf_op jit(solution)/shard_map/ppermute | solution.py:434
  683.9 19.2 %collective-permute-start.76 = (bf16[256,1536]{1,0:T(8,128)(2,1)S(1)}, bf16[256,1536]{1,0:T(8,128)(2,1)S(1)}, u32[]{:S(2)}, u32[]{:S(2)}) collective-permute-start(bf16[256,1536]{1,0:T(8,128)(2,1)S(1)} %copy-done.77), channel_id=1, source_target_pairs={{0,4},{4,0},{8,12},{12,8},{16,20},{20,16},{24,28},{28,24},{1,5},{5... | collective-permute-start | bytes 2359304 | tf_op jit(solution)/shard_map/ppermute | solution.py:429
  (95 other events, 1278.4 us)
Sparse Core Ops, SparseCore 0:
  147.0 158.7 all-gather.1

commit v5 on v4

--- a/solution.py
+++ b/solution.py
@@ -284,16 +284,16 @@
     return matmul_call(kernel, (steps,), ins, results, [], 2 * tokens * depth * width, name)
 
 
-def times_columns(xs, ws, order, side, dtype, name, first=0, added=(), block=0, chunks=1):
+def times_columns(xs, ws, order, side, dtype, name, first=0, added=(), block=0, chunks=None):
     tokens = xs[0].shape[0]
     count = order.shape[1]
     n_xs = len(xs)
     width = sum(x.shape[1] for x in xs)
-    rows = tokens // chunks
+    chunks = chunks or [tokens]
 
     def kernel(order_ref, side_ref, *refs):
         x_refs, w_refs = refs[:n_xs], refs[n_xs : n_xs + 2]
-        added_refs, out_refs = refs[n_xs + 2 : n_xs + 2 + len(added)], refs[-chunks:]
+        added_refs, out_refs = refs[n_xs + 2 : n_xs + 2 + len(added)], refs[-len(chunks) :]
         x = jnp.concatenate([r[...] for r in x_refs], axis=1)
         for i, w_ref in enumerate(w_refs):
             acc = lax.dot_general(x, w_ref[...], NT, preferred_element_type=f32)
@@ -301,8 +301,10 @@
             place = pl.ds(pl.multiple_of(place * BLOCK, BLOCK), BLOCK)
             if added:
                 acc = acc + jnp.concatenate([r[:, place] for r in added_refs]).astype(f32)
-            for c, out_ref in enumerate(out_refs):
-                out_ref[:, place] = acc[c * rows : (c + 1) * rows].astype(dtype)
+            at = 0
+            for out_ref, height in zip(out_refs, chunks):
+                out_ref[:, place] = acc[at : at + height].astype(dtype)
+                at += height
 
     def w_spec(i):
         return pl.BlockSpec((BLOCK, width), lambda n, order_ref, _: (order_ref[i, n], first // width))
@@ -317,13 +319,13 @@
         kernel,
         (count,),
         ins,
-        [((rows, 2 * BLOCK * count), dtype, pair(rows, 0))] * chunks,
+        [((height, 2 * BLOCK * count), dtype, pair(height, 0)) for height in chunks],
         [],
         4 * tokens * BLOCK * count * width,
         name,
         prefetch=(order, side),
     )
-    return done if chunks > 1 else done[0]
+    return done if len(chunks) > 1 else done[0]
 
 
 def weight_rows(a, order, gs, name, groups=None, dtype=bf16):
@@ -530,13 +532,14 @@
     def two(ws):
         return ws if len(ws) == 2 else [ws[0], ws[0]]
 
-    def columns_sent(xs, ws, ids, name, first=0, chunks=4):
+    def columns_sent(xs, ws, ids, name, first=0):
         order = columns_order(ids, ws)[:, :2]
         xs = [at_now(xs[0])] + xs[1:]
+        chunks = [3 * tokens_here // 8, 3 * tokens_here // 8, tokens_here // 4]
         sent = times_columns(
             xs, two(ws), order, sides, bf16, name + "_sent", first, chunks=chunks
         )
-        return [swap(v, "col", 1) for v in (sent if chunks > 1 else [sent])]
+        return [swap(v, "col", 1) for v in sent]
 
     def columns_part(xs, ws, ids, got, name, first=0):
         order = columns_order(ids, ws)[:, 3:]
@@ -552,7 +555,7 @@
             self.a, self.ids, self.gs, self.name = a, ids, gs, name
             self.left = rows // 2
             self.groups = groups or [[k] for k in reversed(range(self.left))]
-            self.got, self.carry, self.result = {}, None, None
+            self.got, self.kept, self.carry, self.result = {}, [], None, None
 
         def cut(self):
             if stepped:
@@ -571,18 +574,19 @@
                 mine = find(self.ids, 2 * back + side)
                 a = after(at_now(self.a), *first)
                 single = [[k] for k in range(rows // 2)]
-                self.kept = weight_rows(a, mine, self.gs, self.name + "_mine", single, f32)
+                self.kept = weight_rows(a, mine, self.gs, self.name + "_mine", single)
                 put(*self.kept)
 
-        def move(self):
+        def move(self, late=False):
             if stepped:
                 group = self.groups.pop(0)
                 got = swap(at_now(self.sent.pop(0)), "row", 1)
-                put(got)
+                if not late:
+                    put(got)
                 for j, k in enumerate(group):
-                    self.got[k] = got[j * BLOCK : (j + 1) * BLOCK]
-
-        def add(self):
+                    self.got[k] = (got, j * BLOCK)
+
+        def add(self, *first):
             if not stepped:
                 if self.result is None:
                     self.result = lax.psum_scatter(
@@ -590,7 +594,9 @@
                     )
                 return
             self.left -= 1
-            total = self.kept[self.left] + at_now(self.got[self.left]).astype(f32)
+            got, start = self.got[self.left]
+            got = after(at_now(got), *first)[start : start + BLOCK]
+            total = self.kept[self.left].astype(f32) + got.astype(f32)
             if self.carry is not None:
                 total = total + self.carry.astype(f32)
             if self.left == 0:
@@ -658,15 +664,19 @@
     put(first_full, cot_full)
     expand_own, expand_near = [expand], []
 
-    def expand_turn():
+    def expand_turn(start=None):
         if stepped:
-            expand_own.append(turn(at_now(expand_own[-1]), 1))
+            block = at_now(expand_own[2 if start is not None else -1])
+            if start is not None:
+                block = block[start : start + BLOCK // 2]
+            expand_own.append(turn(block, 1))
             put(expand_own[-1])
 
-    def expand_step(k):
+    def expand_step(*ks):
         if stepped:
-            expand_near.append(swap(at_now(expand_own[k]), "row", 1))
-            put(expand_near[k])
+            for k in ks:
+                expand_near.append(swap(at_now(expand_own[k]), "row", 1))
+                put(expand_near[k])
 
     expand_turn()
     expand_turn()
@@ -678,7 +688,7 @@
     def add_bias(acc, extra, out):
         out[0][...] = (acc + extra[0][...]).astype(bf16)
 
-    expand_turn()
+    expand_turn(0)
     expand_step(0)
     if stepped:
         full_contract = [gather_outer(at_now(contract_pair))]
@@ -704,15 +714,17 @@
     tick()
 
     expand_step(2)
+    expand_turn(BLOCK // 2)
     across = swap(at_now(part), "col", 2)
     base = columns_base([attended], full_attend, ids_attend, got, "project", mix_width)
     resid = tokens.astype(f32)
     middle = resid + (base + across.astype(f32) + biases[2])
     middle_low = middle.astype(bf16)
-    put(middle_low)
-    tick()
-
-    expand_step(3)
+    first_mean, first_scale = first_mean[:, 0], first_scale[:, 0]
+    put(middle_low, first_mean, first_scale)
+    tick()
+
+    expand_step(3, 4)
     middle_now = at_now(middle_low)
     middle_parts = [middle_low, swap(middle_now, "col", 1), swap(middle_now, "col", 2)]
     put(*middle_parts[1:])
@@ -740,7 +752,7 @@
         activate,
         "expand",
         tn=512,
-        joins=[range(rows // 2), range(rows // 2, rows)] if stepped else [],
+        joins=[range(len(expand_own)), range(len(expand_own), 2 * len(expand_own))] if stepped else [],
     )
     if stepped:
         full_expand = joined
@@ -756,10 +768,12 @@
         out[0][...] = grad
         out[1][...] = jnp.sum(grad.astype(f32), axis=0, keepdims=True)
 
-    contract_sum.move()
+    second_mean, second_scale = at_now(second_mean)[:, 0], at_now(second_scale)[:, 0]
+    put(second_mean, second_scale)
+    contract_sum.move(late=True)
     contract_sum.keep()
     hidden_grad, thresholds_part = times_rows(
-        at_now(cot_full),
+        after(at_now(cot_full), *contract_sum.kept[:1]),
         full_contract,
         [slope],
         [(hidden_shape, bf16), ((1, hidden_shape[1]), f32)],
@@ -787,14 +801,13 @@
         sums = sum_col_stats(
             jnp.stack([jnp.sum(scaled, axis=1), jnp.sum(scaled * centred, axis=1)])
         )
-        result = scale * (
+        result = scale[:, None] * (
             scaled - sums[0][:, None] / full - centred * (sums[1][:, None] / full)
         )
         return result, jnp.sum(upstream * centred, axis=0), jnp.sum(upstream, axis=0)
 
-    contract_sum.add()
     contract_sum.move()
-    second_centred = (middle - second_mean) * second_scale
+    second_centred = (middle - second_mean[:, None]) * second_scale[:, None]
     second_input, second_gain, second_shift = norm_back(
         at_now(second_back), second_centred, second_scale, gains[1]
     )
@@ -802,6 +815,7 @@
     middle_grad = cot_float + second_input
     branch_grad = middle_grad.astype(bf16)
     branch_parts = [branch_grad, swap(branch_grad, "col", 1), swap(branch_grad, "col", 2)]
+    contract_sum.add(branch_grad)
     expand_sum.keep(branch_grad)
     put(*branch_parts[1:])
     tick()
@@ -848,19 +862,19 @@
     tick()
 
     expand_sum.add()
-    expand_sum.move()
+    project_sum.move()
+    project_sum.keep()
     across = swap(at_now(part), "col", 2)
     base = columns_base(mixed_grads, full_attend, ids_attend, got, "mix_back")
-    out_got = columns_sent([active], full_contract, ids_contract, "contract", chunks=1)
     first_back = base + across.astype(f32)
-    put(first_back, *out_got)
-    tick()
-
-    expand_sum.add()
-    project_sum.move()
-    project_sum.keep()
-    out_part = columns_part([at_now(active)], full_contract, ids_contract, out_got, "contract")
-    first_centred = (resid - first_mean) * first_scale
+    put(first_back)
+    tick()
+
+    expand_sum.move()
+    for _ in range(rows // 2 - 1):
+        project_sum.add()
+    out_got = columns_sent([active], full_contract, ids_contract, "contract")
+    first_centred = (resid - first_mean[:, None]) * first_scale[:, None]
     first_input, first_gain, first_shift = norm_back(
         at_now(first_back), first_centred, first_scale, gains[0]
     )
@@ -878,27 +892,40 @@
         ]
     )
     small = jnp.concatenate([small, thresholds_part.reshape(-1, width)], axis=0)
-    put(small, out_part)
-    tick()
-
+    put(small, *out_got)
+    tick()
+
+    def small_step(bit):
+        return small + swap(at_now(small), "row", bit) if bit < rows else small
+
+    expand_sum.add()
     project_sum.add()
     mixing_sum.move()
     mixing_sum.keep()
+    out_part = columns_part([at_now(active)], full_contract, ids_contract, out_got, "contract")
+    small = small_step(1)
+    put(small, out_part)
+    tick()
+
+    mixing_sum.add()
+    mixing_sum.move()
     out_across = swap(at_now(out_part), "col", 2)
     out_base = columns_base([active], full_contract, ids_contract, out_got, "contract")
     layer_out = (middle + (out_base + out_across.astype(f32) + biases[3])).astype(bf16)
-    put(layer_out)
-    bit = 1
-    while bit < rows:
-        small = small + swap(at_now(small), "row", bit)
+    small = small_step(2)
+    put(small)
+    tick()
+
+    bit = 4
+    while bit < rows or mixing_sum.groups:
+        mixing_sum.add()
+        mixing_sum.groups and mixing_sum.move()
+        small = small_step(bit)
         put(small)
         tick()
         bit *= 2
-        project_sum.add()
-        mixing_sum.add()
-        if mixing_sum.groups:
-            mixing_sum.move()
-    tick()
+        if not stepped and bit >= rows:
+            break
     mixing_sum.add()
     contract_grad, expand_grad = contract_sum.result, expand_sum.result
     projection_grad, mixing_grad = project_sum.result, mixing_sum.result

time: 718 us -> 692 us (0.964)
  waiting for transfers between devices: 261 us -> 240 us
    ppermute x60, waiting for transfers between devices: 181 us -> 166 us  [swap(): lax.ppermute(x, axis, [(i, i ^ bit) for i in range(lax.axis_size(axis))])]
    ppermute x18 -> x19, starting transfers between devices: 33.9 us -> 41.6 us  [turn(): lax.ppermute(x, 'row', [(i, (i + 2 * steps) % count) for i in range(count)])]
    ppermute x18 -> x19, waiting for transfers between devices: 80.1 us -> 73.7 us  [turn(): lax.ppermute(x, 'row', [(i, (i + 2 * steps) % count) for i in range(count)])]
  transfers between devices with their start and end apart: 79 -> 80, of which waited for: 44 -> 43; matrix products, arithmetic and copies ran while one was open for 8% -> 9% of each run, Pallas kernels for 35% -> 39%
where the time goes in v5:
time: 692 us; the launch traced here: 686 us
  Pallas kernels  270 us (39%)
  waiting for transfers between devices  240 us (35%)
  starting transfers between devices  82.2 us (12%)
  other arithmetic  56.1 us (8%)
  local copies, waits for them, and re-layouts  22.7 us (3%)
  between operations  15.3 us (2%)
    pallas_call x28, Pallas kernels, matmul_call(): pl.pallas_call(kernel, grid_spec=pltpu.PrefetchScalarGridSpec(num_scalar_...  232 us
    ppermute x60, waiting for transfers between devices, swap(): lax.ppermute(x, axis, [(i, i ^ bit) for i in range(lax.axis_size(axis))])  166 us
    ppermute x19, waiting for transfers between devices, turn(): lax.ppermute(x, 'row', [(i, (i + 2 * steps) % count) for i in range(count)])  73.7 us
    ppermute x19, starting transfers between devices, turn(): lax.ppermute(x, 'row', [(i, (i + 2 * steps) % count) for i in range(count)])  41.6 us
    ppermute x60, starting transfers between devices, swap(): lax.ppermute(x, axis, [(i, i ^ bit) for i in range(lax.axis_size(axis))])  40.5 us
    convert_element_type x12, other arithmetic, add(): self.carry = turn(total.astype(bf16), -1)  21 us
    pallas_call x1, Pallas kernels, attend_backward(): pl.pallas_call(partial(attend_back_kernel, rows=rows, scale=HD ** (-0.5))...  20.3 us
    pallas_call x1, Pallas kernels, attend_forward(): pl.pallas_call(partial(attend_kernel, rows=rows, scale=HD ** (-0.5)), gri...  17.3 us
  transfers between devices with their start and end apart: 80, of which 43 were waited for; matrix products, arithmetic and copies ran while one was open for 9% of the time, Pallas kernels for 39%

profile of v5, /device:TPU:0, one launch (start us, length us, event | category | flops | bytes accessed | tf_op | source)
XLA Modules:
  0.0 686.1 jit_solution(5510907451311979513)
XLA Ops:
  17.4 20.6 %collective-permute-done.1.refs_2_ = bf16[1024,512]{1,0:T(8,128)(2,1)S(1)} collective-permute-done((bf16[1024,512]{1,0:T(8,128)(2,1)S(1)}, bf16[1024,512]{1,0:T(8,128)(2,1)S(1)}, u32[]{:S(2)}, u32[]{:S(2)}) %collective-permute-start.1) | collective-permute-done | bytes 1048608 | tf_op jit(solution)/shard_map/ppermute | solution.py:431
  39.5 3.1 collective-permute-done.3.refs_2_
  45.8 21.0 %collective-permute-done.5.refs_6_ = bf16[256,2048]{1,0:T(8,128)(2,1)S(1)} collective-permute-done((bf16[256,2048]{1,0:T(8,128)(2,1)S(1)}, bf16[256,2048]{1,0:T(8,128)(2,1)S(1)}, u32[]{:S(2)}, u32[]{:S(2)}) %collective-permute-start.5) | collective-permute-done | bytes 1048608 | tf_op jit(solution)/shard_map/ppermute | solution.py:431
  72.4 2.9 collective-permute-done.10
  75.4 17.7 %collective-permute-done.11.refs_7_ = bf16[256,2048]{1,0:T(8,128)(2,1)S(1)} collective-permute-done((bf16[256,2048]{1,0:T(8,128)(2,1)S(1)}, bf16[256,2048]{1,0:T(8,128)(2,1)S(1)}, u32[]{:S(2)}, u32[]{:S(2)}) %collective-permute-start.11) | collective-permute-done | bytes 1048608 | tf_op jit(solution)/shard_map/ppermute | solution.py:431
  93.1 3.3 collective-permute-done.12.refs_4_
  100.9 21.7 %collective-permute-done.16.refs_2_ = bf16[256,2048]{1,0:T(8,128)(2,1)} collective-permute-done((bf16[256,2048]{1,0:T(8,128)(2,1)}, bf16[256,2048]{1,0:T(8,128)(2,1)}, u32[]{:S(2)}, u32[]{:S(2)}) %collective-permute-start.16) | collective-permute-done | bytes 1048608 | tf_op jit(solution)/shard_map/ppermute | solution.py:436
  123.5 5.4 cotangent_rows.1.a_ref.refs_0_
  129.6 7.2 %first_norm.1 = (bf16[1024,2048]{1,0:T(8,128)(2,1)}, f32[1024,1]{1,0:T(8,128)}, f32[1024,1]{1,0:T(8,128)}) custom-call(s32[8]{0:T(128)} %get-tuple-element.314.place_ref, bf16[1024,512]{1,0:T(8,128)(2,1)} %refs_0_.1, bf16[1024,512]{1,0:T(8,128)(2,1)} %copy-done.26, bf16[1024,512]{1,0:T(8,128)(2,1)} %copy-done.27, bf16[1024,512]{1,0:T(8,128)(2,1)} %copy-done.28, ...), custom_call_target="tpu_custom_call" | custom-call | flops 262144 | bytes 131456 | tf_op jit(solution)/shard_map/first_norm/pallas_call | solution.py:229
  138.1 6.5 collective-permute-done.15.refs_8_
  151.6 14.2 %mix.1 = (bf16[1024,1536]{1,0:T(8,128)(2,1)}, bf16[1024,2048]{1,0:T(8,128)(2,1)}, bf16[1024,2048]{1,0:T(8,128)(2,1)}) custom-call(bf16[1024,2048]{1,0:T(8,128)(2,1)} %get-tuple-element.279.refs_0_.a_ref, bf16[256,2048]{1,0:T(8,128)(2,1)} %copy-done.10, bf16[256,2048]{1,0:T(8,128)(2,1)} %copy-done.21, bf16[256,2048]{1,0:T(8,128)(2,1)} %copy-done.24, ...), custom_call_target="tpu_custom_call" | custom-call | flops 100663296 | bytes 376928 | tf_op jit(solution)/shard_map/mix/pallas_call | solution.py:229
  165.9 17.3 %attend_forward.1 = (bf16[1024,512]{1,0:T(8,128)(2,1)}, f32[4,2,1024]{2,1,0:T(2,128)}) custom-call(f32[8]{0:T(128)} %multiply_exponential_fusion.slope_ref, s32[1,1024,1]{2,1,0:T(8,128)} %copy.28.start_ref, bf16[1024,1536]{1,0:T(8,128)(2,1)} %get-tuple-element.171.q_ref.k_ref.v_ref, bf16[1024,1536]{1,0:T(8,128)(2,1)} %get-tuple-element.171.q_ref.k_ref.v_ref, ...), custom_call_target="tpu_custom_call" | custom-call | flops 67108864 | bytes 98304 | tf_op jit(solution)/shard_map/attend_forward/pallas_call | solution.py:79
  186.2 4.7 project_sent.1
  192.3 3.1 collective-permute-done.24.refs_5_
  196.7 4.3 project_part.1
  201.0 3.9 collective-permute-done.21.refs_7_
  210.4 4.7 project_base.1
  215.1 11.3 %collective-permute-done.25 = bf16[1024,512]{1,0:T(8,128)(2,1)S(1)} collective-permute-done((bf16[1024,512]{1,0:T(8,128)(2,1)}, bf16[1024,512]{1,0:T(8,128)(2,1)S(1)}, u32[]{:S(2)}, u32[]{:S(2)}) %collective-permute-start.25) | collective-permute-done | bytes 1048608 | tf_op jit(solution)/shard_map/ppermute | solution.py:431
  229.8 5.3 collective-permute-done.27.refs_5_
  239.0 12.7 %collective-permute-done.30.refs_9_ = bf16[128,2048]{1,0:T(8,128)(2,1)S(1)} collective-permute-done((bf16[128,2048]{1,0:T(8,128)(2,1)S(1)}, bf16[128,2048]{1,0:T(8,128)(2,1)S(1)}, u32[]{:S(2)}, u32[]{:S(2)}) %collective-permute-start.30) | collective-permute-done | bytes 524320 | tf_op jit(solution)/shard_map/ppermute | solution.py:431
  251.8 10.5 %collective-permute-done.31.refs_10_ = bf16[128,2048]{1,0:T(8,128)(2,1)S(1)} collective-permute-done((bf16[128,2048]{1,0:T(8,128)(2,1)}, bf16[128,2048]{1,0:T(8,128)(2,1)S(1)}, u32[]{:S(2)}, u32[]{:S(2)}) %collective-permute-start.31) | collective-permute-done | bytes 524320 | tf_op jit(solution)/shard_map/ppermute | solution.py:431
  266.8 7.6 %second_norm.1 = (bf16[1024,2048]{1,0:T(8,128)(2,1)}, f32[1024,1]{1,0:T(8,128)}, f32[1024,1]{1,0:T(8,128)}) custom-call(s32[8]{0:T(128)} %get-tuple-element.314.place_ref, bf16[1024,512]{1,0:T(8,128)(2,1)} %copy-done.11, bf16[1024,512]{1,0:T(8,128)(2,1)} %copy-done.36, bf16[1024,512]{1,0:T(8,128)(2,1)} %copy-done.38, bf16[1024,512]{1,0:T(8,128)(2,1)} %copy-done.39, ...), custom_call_target="tpu_custom_call" | custom-call | flops 262144 | bytes 131456 | tf_op jit(solution)/shard_map/second_norm/pallas_call | solution.py:229
  274.4 18.2 %expand.1 = (bf16[1024,2048]{1,0:T(8,128)(2,1)}, f32[1024,2048]{1,0:T(8,128)}, bf16[1024,2048]{1,0:T(8,128)(2,1)}, bf16[1024,2048]{1,0:T(8,128)(2,1)}) custom-call(bf16[1024,2048]{1,0:T(8,128)(2,1)} %get-tuple-element.229.refs_0_.a_ref, bf16[256,2048]{1,0:T(8,128)(2,1)} %refs_1_.1, bf16[256,2048]{1,0:T(8,128)(2,1)} %collective-permute-done.16.refs_2_, ...), custom_call_target="tpu_custom_call" | custom-call | flops 134217728 | bytes 524416 | tf_op jit(solution)/shard_map/expand/pallas_call | solution.py:229
  292.6 10.7 %contract_grad_other.1 = (bf16[512,2048]{1,0:T(8,128)(2,1)}, bf16[256,2048]{1,0:T(8,128)(2,1)}, bf16[256,2048]{1,0:T(8,128)(2,1)}) custom-call(s32[4]{0:T(128)} %get-tuple-element.310.order_ref, bf16[1024,2048]{1,0:T(8,128)(2,1)} %cotangent_rows.1.a_ref.refs_0_, bf16[1024,2048]{1,0:T(8,128)(2,1)} %get-tuple-element.286.refs_0_), custom_call_target="tpu_custom_call" | custom-call | flops 67108864 | bytes 196608 | tf_op jit(solution)/shard_map/contract_grad_other/pallas_call | solution.py:229
  303.7 10.7 %contract_grad_mine.1 = (bf16[256,2048]{1,0:T(8,128)(2,1)}, bf16[256,2048]{1,0:T(8,128)(2,1)}, bf16[256,2048]{1,0:T(8,128)(2,1)}, bf16[256,2048]{1,0:T(8,128)(2,1)}) custom-call(s32[4]{0:T(128)} %get-tuple-element.309.order_ref, bf16[1024,2048]{1,0:T(8,128)(2,1)} %cotangent_rows.1.a_ref.refs_0_, bf16[1024,2048]{1,0:T(8,128)(2,1)} %get-tuple-element.286.refs_0_), custom_call_target="tpu_custom_call" | custom-call | flops 67108864 | bytes 196608 | tf_op jit(solution)/shard_map/contract_grad_mine/pallas_call | solution.py:229
  314.4 14.3 %contract_back.1 = (bf16[1024,2048]{1,0:T(8,128)(2,1)}, f32[1,2048]{1,0:T(1,128)}) custom-call(bf16[1024,2048]{1,0:T(8,128)(2,1)} %cotangent_rows.1.a_ref.refs_0_, bf16[2048,2048]{1,0:T(8,128)(2,1)} %all-gather.2.cloned.1.call-done.refs_1_.refs_2_, f32[1024,2048]{1,0:T(8,128)} %get-tuple-element.210.refs_2_), custom_call_target="tpu_custom_call" | custom-call | flops 134217728 | bytes 393344 | tf_op jit(solution)/shard_map/contract_back/pallas_call | solution.py:229
  328.7 9.3 %expand_back_sent.1 = (bf16[384,1024]{1,0:T(8,128)(2,1)}, bf16[384,1024]{1,0:T(8,128)(2,1)}, bf16[256,1024]{1,0:T(8,128)(2,1)}) custom-call(s32[2,2]{1,0:T(2,128)} %bitcast.57, s32[1]{0:T(128)} %bitcast.2.side_ref, bf16[1024,2048]{1,0:T(8,128)(2,1)} %get-tuple-element.225.refs_0_, bf16[1024,2048]{1,0:T(8,128)(2,1)} %get-tuple-element.212.refs_1_, ...), custom_call_target="tpu_custom_call" | custom-call | flops 67108864 | bytes 229376 | tf_op jit(solution)/shard_map/expand_back_sent/pallas_call | solution.py:229
  342.5 7.1 %expand_back_part.1 = bf16[1024,512]{1,0:T(8,128)(2,1)} custom-call(s32[2,1]{1,0:T(2,128)} %get-tuple-element.345.order_ref, s32[1]{0:T(128)} %bitcast.2.side_ref, bf16[1024,2048]{1,0:T(8,128)(2,1)} %get-tuple-element.225.refs_0_, bf16[1024,2048]{1,0:T(8,128)(2,1)} %get-tuple-element.212.refs_1_, bf16[1024,2048]{1,0:T(8,128)(2,1)} %get-tuple-element.213.refs_2_, ...), custom_call_target="tpu_custom_call" | custom-call | flops 33554432 | bytes 245760 | tf_op jit(solution)/shard_map/expand_back_part/pallas_call | solution.py:229
  353.2 16.4 %collective-permute-start.37 = (bf16[256,2048]{1,0:T(8,128)(2,1)S(1)}, bf16[256,2048]{1,0:T(8,128)(2,1)}, u32[]{:S(2)}, u32[]{:S(2)}) collective-permute-start(bf16[256,2048]{1,0:T(8,128)(2,1)S(1)} %add_convert_fusion.6), channel_id=1, source_target_pairs={{0,24},{4,28},{8,0},{12,4},{16,8},{20,12},{24,16},{28,20},{1,25},{... | collective-permute-start | bytes 3145736 | tf_op jit(solution)/shard_map/ppermute | solution.py:436
  369.9 7.5 %expand_back_base.1 = f32[1024,512]{1,0:T(8,128)} custom-call(s32[2,1]{1,0:T(2,128)} %get-tuple-element.346.order_ref, s32[1]{0:T(128)} %bitcast.2.side_ref, bf16[1024,2048]{1,0:T(8,128)(2,1)} %get-tuple-element.225.refs_0_, bf16[1024,2048]{1,0:T(8,128)(2,1)} %get-tuple-element.212.refs_1_, bf16[1024,2048]{1,0:T(8,128)(2,1)} %get-tuple-element.213.refs_2_, ...), custom_call_target="tpu_custom_call" | custom-call | flops 33554432 | bytes 262144 | tf_op jit(solution)/shard_map/expand_back_base/pallas_call | solution.py:229
  377.4 10.8 %expand_grad_other.1 = (bf16[256,2048]{1,0:T(8,128)(2,1)}, bf16[256,2048]{1,0:T(8,128)(2,1)}, bf16[256,2048]{1,0:T(8,128)(2,1)}, bf16[256,2048]{1,0:T(8,128)(2,1)}) custom-call(s32[4]{0:T(128)} %get-tuple-element.311.order_ref, bf16[1024,2048]{1,0:T(8,128)(2,1)} %get-tuple-element.229.refs_0_.a_ref, bf16[1024,2048]{1,0:T(8,128)(2,1)} %get-tuple-element.225.refs_0_), custom_call_target="tpu_custom_call" | custom-call | flops 67108864 | bytes 196608 | tf_op jit(solution)/shard_map/expand_grad_other/pallas_call | solution.py:229
  402.0 3.4 add_convert_fusion.5
  409.0 10.6 %expand_grad_mine.1 = (bf16[256,2048]{1,0:T(8,128)(2,1)}, bf16[256,2048]{1,0:T(8,128)(2,1)}, bf16[256,2048]{1,0:T(8,128)(2,1)}, bf16[256,2048]{1,0:T(8,128)(2,1)}) custom-call(s32[4]{0:T(128)} %get-tuple-element.308.order_ref, bf16[1024,2048]{1,0:T(8,128)(2,1)} %get-tuple-element.229.refs_0_.a_ref, bf16[1024,2048]{1,0:T(8,128)(2,1)} %get-tuple-element.225.refs_0_), custom_call_target="tpu_custom_call" | custom-call | flops 67108864 | bytes 196608 | tf_op jit(solution)/shard_map/expand_grad_mine/pallas_call | solution.py:229
  419.6 3.4 collective-permute-done.42
  423.1 6.7 collective-permute-done.43
  429.8 3.0 collective-permute-done.45.refs_2_
  433.6 3.4 add_convert_fusion.4
  437.8 5.5 branch_rows.1.a_ref.refs_0_
  443.3 5.6 projection_grad_other.1
  448.9 6.2 project_back.1.g_ref
  455.1 2.8 collective-permute-done.46
  457.9 4.9 collective-permute-done.47
  468.9 20.3 %attend_backward.1 = (bf16[1024,512]{1,0:T(8,128)(2,1)}, bf16[1024,512]{1,0:T(8,128)(2,1)}, bf16[1024,512]{1,0:T(8,128)(2,1)}, f32[1,1,512]{2,1,0:T(1,128)}, f32[1,1,512]{2,1,0:T(1,128)}) custom-call(f32[8]{0:T(128)} %multiply_exponential_fusion.slope_ref, s32[1,1,1024]{2,1,0:T(1,128)} %bitcast.55, f32[4,2,1024]{2,1,0:T(2,128)} %get-tuple-element.243.log_ref, ...), custom_call_target="tpu_custom_call" | custom-call | flops 167772160 | bytes 114688 | tf_op jit(solution)/shard_map/attend_backward/pallas_call | solution.py:183
  492.5 2.8 add_convert_fusion.2
  498.3 7.7 %mix_back_sent.1 = (bf16[384,1024]{1,0:T(8,128)(2,1)}, bf16[384,1024]{1,0:T(8,128)(2,1)}, bf16[256,1024]{1,0:T(8,128)(2,1)}) custom-call(s32[2,2]{1,0:T(2,128)} %bitcast.58, s32[1]{0:T(128)} %bitcast.2.side_ref, bf16[1024,512]{1,0:T(8,128)(2,1)} %get-tuple-element.266.refs_0_, bf16[1024,512]{1,0:T(8,128)(2,1)} %get-tuple-element.247.refs_1_, ...), custom_call_target="tpu_custom_call" | custom-call | flops 50331648 | bytes 212992 | tf_op jit(solution)/shard_map/mix_back_sent/pallas_call | solution.py:229
  506.5 8.8 %mixing_grad_other.1 = (bf16[256,1536]{1,0:T(8,128)(2,1)}, bf16[256,1536]{1,0:T(8,128)(2,1)}, bf16[256,1536]{1,0:T(8,128)(2,1)}, bf16[256,1536]{1,0:T(8,128)(2,1)}) custom-call(s32[4]{0:T(128)} %get-tuple-element.311.order_ref, bf16[1024,2048]{1,0:T(8,128)(2,1)} %get-tuple-element.279.refs_0_.a_ref, bf16[1024,512]{1,0:T(8,128)(2,1)} %get-tuple-element.266.refs_0_, ...), custom_call_target="tpu_custom_call" | custom-call | flops 50331648 | bytes 163840 | tf_op jit(solution)/shard_map/mixing_grad_other/pallas_call | solution.py:229
  517.3 6.1 mix_back_part.1
  528.8 5.7 projection_grad_mine.1
  534.4 6.6 mix_back_base.1
  541.0 8.2 %collective-permute-done.58 = bf16[1024,512]{1,0:T(8,128)(2,1)S(1)} collective-permute-done((bf16[1024,512]{1,0:T(8,128)(2,1)}, bf16[1024,512]{1,0:T(8,128)(2,1)S(1)}, u32[]{:S(2)}, u32[]{:S(2)}) %collective-permute-start.58) | collective-permute-done | bytes 1048608 | tf_op jit(solution)/shard_map/ppermute | solution.py:431
  549.2 3.2 convert_add_fusion.4
  556.5 4.8 collective-permute-done.60
  562.1 4.4 collective-permute-start.61
  567.2 9.4 %contract_sent.1 = (bf16[384,1024]{1,0:T(8,128)(2,1)}, bf16[384,1024]{1,0:T(8,128)(2,1)}, bf16[256,1024]{1,0:T(8,128)(2,1)}) custom-call(s32[2,2]{1,0:T(2,128)} %bitcast.68, s32[1]{0:T(128)} %bitcast.2.side_ref, bf16[1024,2048]{1,0:T(8,128)(2,1)} %get-tuple-element.286.refs_0_, bf16[2048,2048]{1,0:T(8,128)(2,1)} %all-gather.2.cloned.1.call-done.refs_1_.refs_2_, ...), custom_call_target="tpu_custom_call" | custom-call | flops 67108864 | bytes 360448 | tf_op jit(solution)/shard_map/contract_sent/pallas_call | solution.py:229
  584.4 5.5 collective-permute-done.62
  590.7 3.7 convert_add_fusion.2
  596.3 7.1 %contract_part.1 = bf16[1024,512]{1,0:T(8,128)(2,1)} custom-call(s32[2,1]{1,0:T(2,128)} %get-tuple-element.343.order_ref, s32[1]{0:T(128)} %bitcast.2.side_ref, bf16[1024,2048]{1,0:T(8,128)(2,1)} %get-tuple-element.286.refs_0_, bf16[2048,2048]{1,0:T(8,128)(2,1)} %all-gather.2.cloned.1.call-done.refs_1_.refs_2_, ...), custom_call_target="tpu_custom_call" | custom-call | flops 33554432 | bytes 376832 | tf_op jit(solution)/shard_map/contract_part/pallas_call | solution.py:229
  603.4 8.9 %mixing_grad_mine.1 = (bf16[256,1536]{1,0:T(8,128)(2,1)}, bf16[256,1536]{1,0:T(8,128)(2,1)}, bf16[256,1536]{1,0:T(8,128)(2,1)}, bf16[256,1536]{1,0:T(8,128)(2,1)}) custom-call(s32[4]{0:T(128)} %get-tuple-element.308.order_ref, bf16[1024,2048]{1,0:T(8,128)(2,1)} %get-tuple-element.279.refs_0_.a_ref, bf16[1024,512]{1,0:T(8,128)(2,1)} %get-tuple-element.266.refs_0_, ...), custom_call_target="tpu_custom_call" | custom-call | flops 50331648 | bytes 163840 | tf_op jit(solution)/shard_map/mixing_grad_mine/pallas_call | solution.py:229
  618.9 14.2 %collective-permute-done.71 = f32[12,512]{1,0:T(8,128)S(1)} collective-permute-done((f32[12,512]{1,0:T(8,128)S(1)}, f32[12,512]{1,0:T(8,128)S(1)}, u32[]{:S(2)}, u32[]{:S(2)}) %collective-permute-start.71) | collective-permute-done | bytes 24608 | tf_op jit(solution)/shard_map/ppermute | solution.py:431
  637.9 3.4 convert_add_fusion.3
  644.7 7.6 %contract_base.1 = f32[1024,512]{1,0:T(8,128)} custom-call(s32[2,1]{1,0:T(2,128)} %get-tuple-element.344.order_ref, s32[1]{0:T(128)} %bitcast.2.side_ref, bf16[1024,2048]{1,0:T(8,128)(2,1)} %get-tuple-element.286.refs_0_, bf16[2048,2048]{1,0:T(8,128)(2,1)} %all-gather.2.cloned.1.call-done.refs_1_.refs_2_, ...), custom_call_target="tpu_custom_call" | custom-call | flops 33554432 | bytes 393216 | tf_op jit(solution)/shard_map/contract_base/pallas_call | solution.py:229
  654.6 3.4 collective-permute-start.78
  660.5 3.0 collective-permute-done.68
  665.2 9.8 %collective-permute-done.78 = bf16[256,1536]{1,0:T(8,128)(2,1)S(1)} collective-permute-done((bf16[256,1536]{1,0:T(8,128)(2,1)S(1)}, bf16[256,1536]{1,0:T(8,128)(2,1)S(1)}, u32[]{:S(2)}, u32[]{:S(2)}) %collective-permute-start.78) | collective-permute-done | bytes 786464 | tf_op jit(solution)/shard_map/ppermute | solution.py:436
  (357 shorter events, 146.5 us)
Async XLA Ops:
  7.2 307.3 %all-gather.2.cloned.1.call-start = ((), (), s32[]{:S(2)}) async-start(), calls=%async_computation | async-start | bytes 10485760 | tf_op jit(solution)/shard_map/all_gather | solution.py:473
  11.7 26.3 %collective-permute-start.1 = (bf16[1024,512]{1,0:T(8,128)(2,1)S(1)}, bf16[1024,512]{1,0:T(8,128)(2,1)S(1)}, u32[]{:S(2)}, u32[]{:S(2)}) collective-permute-start(bf16[1024,512]{1,0:T(8,128)(2,1)S(1)} %copy-done.1), channel_id=1, source_target_pairs={{0,2},{1,3},{2,0},{3,1},{4,6},{5,7},{6,4},{7,5},{8,10},{9,11},{10,... | collective-permute-start | bytes 3145736 | tf_op jit(solution)/shard_map/ppermute | solution.py:431
  14.3 25.2 %collective-permute-start.2 = (bf16[256,2048]{1,0:T(8,128)(2,1)S(1)}, bf16[256,2048]{1,0:T(8,128)(2,1)S(1)}, u32[]{:S(2)}, u32[]{:S(2)}) collective-permute-start(bf16[256,2048]{1,0:T(8,128)(2,1)S(1)} %pad_maximum_fusion.1.refs_1_), channel_id=1, source_target_pairs={{0,4},{4,0},{8,12},{12,8},{16,20},{20,16},{24,28},{28,24},{1,5},{5... | collective-permute-start | bytes 3145736 | tf_op jit(solution)/shard_map/ppermute | solution.py:431
  15.8 26.8 %collective-permute-start.3 = (bf16[256,2048]{1,0:T(8,128)(2,1)S(1)}, bf16[256,2048]{1,0:T(8,128)(2,1)S(1)}, u32[]{:S(2)}, u32[]{:S(2)}) collective-permute-start(bf16[256,2048]{1,0:T(8,128)(2,1)S(1)} %pad_maximum_fusion.1.refs_1_), channel_id=1, source_target_pairs={{0,8},{4,12},{8,16},{12,20},{16,24},{20,28},{24,0},{28,4},{1,9},{5... | collective-permute-start | bytes 3145736 | tf_op jit(solution)/shard_map/ppermute | solution.py:436
  42.6 24.2 %collective-permute-start.5 = (bf16[256,2048]{1,0:T(8,128)(2,1)S(1)}, bf16[256,2048]{1,0:T(8,128)(2,1)S(1)}, u32[]{:S(2)}, u32[]{:S(2)}) collective-permute-start(bf16[256,2048]{1,0:T(8,128)(2,1)S(1)} %collective-permute-done.3.refs_2_), channel_id=1, source_target_pairs={{0,4},{4,0},{8,12},{12,8},{16,20},{20,16},{24,28},{28,24},{1,5},{5... | collective-permute-start | bytes 3145736 | tf_op jit(solution)/shard_map/ppermute | solution.py:431
  43.1 25.7 %collective-permute-start.6 = (bf16[256,2048]{1,0:T(8,128)(2,1)S(1)}, bf16[256,2048]{1,0:T(8,128)(2,1)S(1)}, u32[]{:S(2)}, u32[]{:S(2)}) collective-permute-start(bf16[256,2048]{1,0:T(8,128)(2,1)S(1)} %collective-permute-done.3.refs_2_), channel_id=1, source_target_pairs={{0,8},{4,12},{8,16},{12,20},{16,24},{20,28},{24,0},{28,4},{1,9},{5... | collective-permute-start | bytes 3145736 | tf_op jit(solution)/shard_map/ppermute | solution.py:436
  43.1 25.7 %collective-permute-start.7 = (bf16[1024,512]{1,0:T(8,128)(2,1)S(1)}, bf16[1024,512]{1,0:T(8,128)(2,1)S(1)}, u32[]{:S(2)}, u32[]{:S(2)}) collective-permute-start(bf16[1024,512]{1,0:T(8,128)(2,1)S(1)} %copy-done.7), channel_id=1, source_target_pairs={{0,1},{1,0},{2,3},{3,2},{4,5},{5,4},{6,7},{7,6},{8,9},{9,8},{10,11... | collective-permute-start | bytes 3145736 | tf_op jit(solution)/shard_map/ppermute | solution.py:431
  43.6 25.2 %collective-permute-start.8 = (bf16[1024,512]{1,0:T(8,128)(2,1)S(1)}, bf16[1024,512]{1,0:T(8,128)(2,1)S(1)}, u32[]{:S(2)}, u32[]{:S(2)}) collective-permute-start(bf16[1024,512]{1,0:T(8,128)(2,1)S(1)} %copy-done.7), channel_id=1, source_target_pairs={{0,2},{1,3},{2,0},{3,1},{4,6},{5,7},{6,4},{7,5},{8,10},{9,11},{10,... | collective-permute-start | bytes 3145736 | tf_op jit(solution)/shard_map/ppermute | solution.py:431
  68.8 24.2 %collective-permute-start.11 = (bf16[256,2048]{1,0:T(8,128)(2,1)S(1)}, bf16[256,2048]{1,0:T(8,128)(2,1)S(1)}, u32[]{:S(2)}, u32[]{:S(2)}) collective-permute-start(bf16[256,2048]{1,0:T(8,128)(2,1)S(1)} %collective-permute-done.6.refs_3_), channel_id=1, source_target_pairs={{0,4},{4,0},{8,12},{12,8},{16,20},{20,16},{24,28},{28,24},{1,5},{5... | collective-permute-start | bytes 3145736 | tf_op jit(solution)/shard_map/ppermute | solution.py:431
  70.4 25.9 %collective-permute-start.12 = (bf16[256,2048]{1,0:T(8,128)(2,1)S(1)}, bf16[256,2048]{1,0:T(8,128)(2,1)}, u32[]{:S(2)}, u32[]{:S(2)}) collective-permute-start(bf16[256,2048]{1,0:T(8,128)(2,1)S(1)} %collective-permute-done.6.refs_3_), channel_id=1, source_target_pairs={{0,8},{4,12},{8,16},{12,20},{16,24},{20,28},{24,0},{28,4},{1,9},{5... | collective-permute-start | bytes 3145736 | tf_op jit(solution)/shard_map/ppermute | solution.py:436
  71.5 24.8 %collective-permute-start.13 = (bf16[1024,512]{1,0:T(8,128)(2,1)S(1)}, bf16[1024,512]{1,0:T(8,128)(2,1)S(1)}, u32[]{:S(2)}, u32[]{:S(2)}) collective-permute-start(bf16[1024,512]{1,0:T(8,128)(2,1)S(1)} %collective-permute-done.8.refs_2_), channel_id=1, source_target_pairs={{0,1},{1,0},{2,3},{3,2},{4,5},{5,4},{6,7},{7,6},{8,9},{9,8},{10,11... | collective-permute-start | bytes 3145736 | tf_op jit(solution)/shard_map/ppermute | solution.py:431
  97.3 25.2 %collective-permute-start.16 = (bf16[256,2048]{1,0:T(8,128)(2,1)}, bf16[256,2048]{1,0:T(8,128)(2,1)}, u32[]{:S(2)}, u32[]{:S(2)}) collective-permute-start(bf16[256,2048]{1,0:T(8,128)(2,1)} %refs_1_.1), channel_id=1, source_target_pairs={{0,8},{4,12},{8,16},{12,20},{16,24},{20,28},{24,0},{28,4},{1,9},{5... | collective-permute-start | bytes 3145736 | tf_op jit(solution)/shard_map/ppermute | solution.py:436
  98.7 38.1 %collective-permute-start.18 = (bf16[256,2048]{1,0:T(8,128)(2,1)}, bf16[256,2048]{1,0:T(8,128)(2,1)}, u32[]{:S(2)}, u32[]{:S(2)}) collective-permute-start(bf16[256,2048]{1,0:T(8,128)(2,1)} %param.21), channel_id=1, source_target_pairs={{0,4},{4,0},{8,12},{12,8},{16,20},{20,16},{24,28},{28,24},{1,5},{5... | collective-permute-start | bytes 3145736 | tf_op jit(solution)/shard_map/ppermute | solution.py:431
  99.3 45.3 %collective-permute-start.15 = (bf16[256,2048]{1,0:T(8,128)(2,1)}, bf16[256,2048]{1,0:T(8,128)(2,1)}, u32[]{:S(2)}, u32[]{:S(2)}) collective-permute-start(bf16[256,2048]{1,0:T(8,128)(2,1)} %collective-permute-done.12.refs_4_), channel_id=1, source_target_pairs={{0,4},{4,0},{8,12},{12,8},{16,20},{20,16},{24,28},{28,24},{1,5},{5... | collective-permute-start | bytes 3145736 | tf_op jit(solution)/shard_map/ppermute | solution.py:431
  122.5 24.3 %collective-permute-start.17 = (bf16[256,2048]{1,0:T(8,128)(2,1)}, bf16[256,2048]{1,0:T(8,128)(2,1)}, u32[]{:S(2)}, u32[]{:S(2)}) collective-permute-start(bf16[256,2048]{1,0:T(8,128)(2,1)} %collective-permute-done.16.refs_2_), channel_id=1, source_target_pairs={{0,8},{4,12},{8,16},{12,20},{16,24},{20,28},{24,0},{28,4},{1,9},{5... | collective-permute-start | bytes 3145736 | tf_op jit(solution)/shard_map/ppermute | solution.py:436
  146.9 36.3 %collective-permute-start.20 = (bf16[256,2048]{1,0:T(8,128)(2,1)}, bf16[256,2048]{1,0:T(8,128)(2,1)S(1)}, u32[]{:S(2)}, u32[]{:S(2)}) collective-permute-start(bf16[256,2048]{1,0:T(8,128)(2,1)} %refs_1_.1), channel_id=1, source_target_pairs={{0,4},{4,0},{8,12},{12,8},{16,20},{20,16},{24,28},{28,24},{1,5},{5... | collective-permute-start | bytes 3145736 | tf_op jit(solution)/shard_map/ppermute | solution.py:431
  150.1 33.0 %collective-permute-start.19 = (bf16[128,2048]{1,0:T(8,128)(2,1)S(1)}, bf16[128,2048]{1,0:T(8,128)(2,1)S(1)}, u32[]{:S(2)}, u32[]{:S(2)}) collective-permute-start(bf16[128,2048]{1,0:T(8,128)(2,1)S(1)} %slice.116), channel_id=1, source_target_pairs={{0,8},{4,12},{8,16},{12,20},{16,24},{20,28},{24,0},{28,4},{1,9},{5... | collective-permute-start | bytes 1572872 | tf_op jit(solution)/shard_map/ppermute | solution.py:436
  184.0 20.9 %collective-permute-start.21 = (bf16[256,2048]{1,0:T(8,128)(2,1)}, bf16[256,2048]{1,0:T(8,128)(2,1)S(1)}, u32[]{:S(2)}, u32[]{:S(2)}) collective-permute-start(bf16[256,2048]{1,0:T(8,128)(2,1)} %collective-permute-done.16.refs_2_), channel_id=1, source_target_pairs={{0,4},{4,0},{8,12},{12,8},{16,20},{20,16},{24,28},{28,24},{1,5},{5... | collective-permute-start | bytes 3145736 | tf_op jit(solution)/shard_map/ppermute | solution.py:431
  204.8 21.5 %collective-permute-start.25 = (bf16[1024,512]{1,0:T(8,128)(2,1)}, bf16[1024,512]{1,0:T(8,128)(2,1)S(1)}, u32[]{:S(2)}, u32[]{:S(2)}) collective-permute-start(bf16[1024,512]{1,0:T(8,128)(2,1)} %project_part.1), channel_id=1, source_target_pairs={{0,2},{1,3},{2,0},{3,1},{4,6},{5,7},{6,4},{7,5},{8,10},{9,11},{10,... | collective-permute-start | bytes 3145736 | tf_op jit(solution)/shard_map/ppermute | solution.py:431
  204.9 30.2 %collective-permute-start.26 = (bf16[256,2048]{1,0:T(8,128)(2,1)}, bf16[256,2048]{1,0:T(8,128)(2,1)}, u32[]{:S(2)}, u32[]{:S(2)}) collective-permute-start(bf16[256,2048]{1,0:T(8,128)(2,1)} %collective-permute-done.17.refs_3_), channel_id=1, source_target_pairs={{0,4},{4,0},{8,12},{12,8},{16,20},{20,16},{24,28},{28,24},{1,5},{5... | collective-permute-start | bytes 3145736 | tf_op jit(solution)/shard_map/ppermute | solution.py:431
  209.2 25.9 %collective-permute-start.27 = (bf16[128,2048]{1,0:T(8,128)(2,1)}, bf16[128,2048]{1,0:T(8,128)(2,1)}, u32[]{:S(2)}, u32[]{:S(2)}) collective-permute-start(bf16[128,2048]{1,0:T(8,128)(2,1)} %slice.121), channel_id=1, source_target_pairs={{0,8},{4,12},{8,16},{12,20},{16,24},{20,28},{24,0},{28,4},{1,9},{5... | collective-permute-start | bytes 1572872 | tf_op jit(solution)/shard_map/ppermute | solution.py:436
  235.1 27.2 %collective-permute-start.28 = (bf16[1024,512]{1,0:T(8,128)(2,1)S(1)}, bf16[1024,512]{1,0:T(8,128)(2,1)S(1)}, u32[]{:S(2)}, u32[]{:S(2)}) collective-permute-start(bf16[1024,512]{1,0:T(8,128)(2,1)S(1)} %get-tuple-element.187.refs_0_), channel_id=1, source_target_pairs={{0,1},{1,0},{2,3},{3,2},{4,5},{5,4},{6,7},{7,6},{8,9},{9,8},{10,11... | collective-permute-start | bytes 3145736 | tf_op jit(solution)/shard_map/ppermute | solution.py:431
  235.1 28.0 %collective-permute-start.29 = (bf16[1024,512]{1,0:T(8,128)(2,1)S(1)}, bf16[1024,512]{1,0:T(8,128)(2,1)S(1)}, u32[]{:S(2)}, u32[]{:S(2)}) collective-permute-start(bf16[1024,512]{1,0:T(8,128)(2,1)S(1)} %get-tuple-element.187.refs_0_), channel_id=1, source_target_pairs={{0,2},{1,3},{2,0},{3,1},{4,6},{5,7},{6,4},{7,5},{8,10},{9,11},{10,... | collective-permute-start | bytes 3145736 | tf_op jit(solution)/shard_map/ppermute | solution.py:431
  237.0 14.8 %collective-permute-start.30 = (bf16[128,2048]{1,0:T(8,128)(2,1)S(1)}, bf16[128,2048]{1,0:T(8,128)(2,1)S(1)}, u32[]{:S(2)}, u32[]{:S(2)}) collective-permute-start(bf16[128,2048]{1,0:T(8,128)(2,1)S(1)} %copy-done.54), channel_id=1, source_target_pairs={{0,4},{4,0},{8,12},{12,8},{16,20},{20,16},{24,28},{28,24},{1,5},{5... | collective-permute-start | bytes 1572872 | tf_op jit(solution)/shard_map/ppermute | solution.py:431
  237.5 24.8 %collective-permute-start.31 = (bf16[128,2048]{1,0:T(8,128)(2,1)}, bf16[128,2048]{1,0:T(8,128)(2,1)S(1)}, u32[]{:S(2)}, u32[]{:S(2)}) collective-permute-start(bf16[128,2048]{1,0:T(8,128)(2,1)} %collective-permute-done.27.refs_5_), channel_id=1, source_target_pairs={{0,4},{4,0},{8,12},{12,8},{16,20},{20,16},{24,28},{28,24},{1,5},{5... | collective-permute-start | bytes 1572872 | tf_op jit(solution)/shard_map/ppermute | solution.py:431
  303.3 48.0 %collective-permute-start.33 = (bf16[512,2048]{1,0:T(8,128)(2,1)}, bf16[512,2048]{1,0:T(8,128)(2,1)}, u32[]{:S(2)}, u32[]{:S(2)}) collective-permute-start(bf16[512,2048]{1,0:T(8,128)(2,1)} %get-tuple-element.200), channel_id=1, source_target_pairs={{0,4},{4,0},{8,12},{12,8},{16,20},{20,16},{24,28},{28,24},{1,5},{5... | collective-permute-start | bytes 6291464 | tf_op jit(solution)/shard_map/ppermute | solution.py:431
  351.3 36.9 %collective-permute-start.39 = (bf16[1024,512]{1,0:T(8,128)(2,1)}, bf16[1024,512]{1,0:T(8,128)(2,1)S(1)}, u32[]{:S(2)}, u32[]{:S(2)}) collective-permute-start(bf16[1024,512]{1,0:T(8,128)(2,1)} %expand_back_part.1), channel_id=1, source_target_pairs={{0,2},{1,3},{2,0},{3,1},{4,6},{5,7},{6,4},{7,5},{8,10},{9,11},{10,... | collective-permute-start | bytes 3145736 | tf_op jit(solution)/shard_map/ppermute | solution.py:431
  353.2 38.0 %collective-permute-start.37 = (bf16[256,2048]{1,0:T(8,128)(2,1)S(1)}, bf16[256,2048]{1,0:T(8,128)(2,1)}, u32[]{:S(2)}, u32[]{:S(2)}) collective-permute-start(bf16[256,2048]{1,0:T(8,128)(2,1)S(1)} %add_convert_fusion.6), channel_id=1, source_target_pairs={{0,24},{4,28},{8,0},{12,4},{16,8},{20,12},{24,16},{28,20},{1,25},{... | collective-permute-start | bytes 3145736 | tf_op jit(solution)/shard_map/ppermute | solution.py:436
  369.6 24.1 %collective-permute-start.38 = (bf16[256,2048]{1,0:T(8,128)(2,1)}, bf16[256,2048]{1,0:T(8,128)(2,1)}, u32[]{:S(2)}, u32[]{:S(2)}) collective-permute-start(bf16[256,2048]{1,0:T(8,128)(2,1)} %get-tuple-element.219), channel_id=1, source_target_pairs={{0,4},{4,0},{8,12},{12,8},{16,20},{20,16},{24,28},{28,24},{1,5},{5... | collective-permute-start | bytes 3145736 | tf_op jit(solution)/shard_map/ppermute | solution.py:431
  397.9 25.2 %collective-permute-start.42 = (bf16[256,2048]{1,0:T(8,128)(2,1)}, bf16[256,2048]{1,0:T(8,128)(2,1)S(1)}, u32[]{:S(2)}, u32[]{:S(2)}) collective-permute-start(bf16[256,2048]{1,0:T(8,128)(2,1)} %get-tuple-element.231), channel_id=1, source_target_pairs={{0,4},{4,0},{8,12},{12,8},{16,20},{20,16},{24,28},{28,24},{1,5},{5... | collective-permute-start | bytes 3145736 | tf_op jit(solution)/shard_map/ppermute | solution.py:431
  405.4 24.4 %collective-permute-start.43 = (bf16[256,2048]{1,0:T(8,128)(2,1)}, bf16[256,2048]{1,0:T(8,128)(2,1)}, u32[]{:S(2)}, u32[]{:S(2)}) collective-permute-start(bf16[256,2048]{1,0:T(8,128)(2,1)} %add_convert_fusion.5), channel_id=1, source_target_pairs={{0,24},{4,28},{8,0},{12,4},{16,8},{20,12},{24,16},{28,20},{1,25},{... | collective-permute-start | bytes 3145736 | tf_op jit(solution)/shard_map/ppermute | solution.py:436
  407.3 22.5 %collective-permute-start.44 = (bf16[1024,512]{1,0:T(8,128)(2,1)S(1)}, bf16[1024,512]{1,0:T(8,128)(2,1)S(1)}, u32[]{:S(2)}, u32[]{:S(2)}) collective-permute-start(bf16[1024,512]{1,0:T(8,128)(2,1)S(1)} %get-tuple-element.317.refs_0_), channel_id=1, source_target_pairs={{0,1},{1,0},{2,3},{3,2},{4,5},{5,4},{6,7},{7,6},{8,9},{9,8},{10,11... | collective-permute-start | bytes 3145736 | tf_op jit(solution)/shard_map/ppermute | solution.py:431
  407.3 25.6 %collective-permute-start.45 = (bf16[1024,512]{1,0:T(8,128)(2,1)S(1)}, bf16[1024,512]{1,0:T(8,128)(2,1)S(1)}, u32[]{:S(2)}, u32[]{:S(2)}) collective-permute-start(bf16[1024,512]{1,0:T(8,128)(2,1)S(1)} %get-tuple-element.317.refs_0_), channel_id=1, source_target_pairs={{0,2},{1,3},{2,0},{3,1},{4,6},{5,7},{6,4},{7,5},{8,10},{9,11},{10,... | collective-permute-start | bytes 3145736 | tf_op jit(solution)/shard_map/ppermute | solution.py:431
  432.8 25.1 %collective-permute-start.46 = (bf16[256,2048]{1,0:T(8,128)(2,1)}, bf16[256,2048]{1,0:T(8,128)(2,1)}, u32[]{:S(2)}, u32[]{:S(2)}) collective-permute-start(bf16[256,2048]{1,0:T(8,128)(2,1)} %get-tuple-element.237), channel_id=1, source_target_pairs={{0,4},{4,0},{8,12},{12,8},{16,20},{20,16},{24,28},{28,24},{1,5},{5... | collective-permute-start | bytes 3145736 | tf_op jit(solution)/shard_map/ppermute | solution.py:431
  437.0 25.8 %collective-permute-start.47 = (bf16[256,2048]{1,0:T(8,128)(2,1)}, bf16[256,2048]{1,0:T(8,128)(2,1)S(1)}, u32[]{:S(2)}, u32[]{:S(2)}) collective-permute-start(bf16[256,2048]{1,0:T(8,128)(2,1)} %add_convert_fusion.4), channel_id=1, source_target_pairs={{0,24},{4,28},{8,0},{12,4},{16,8},{20,12},{24,16},{28,20},{1,25},{... | collective-permute-start | bytes 3145736 | tf_op jit(solution)/shard_map/ppermute | solution.py:436
  464.9 25.1 %collective-permute-start.49 = (bf16[256,2048]{1,0:T(8,128)(2,1)S(1)}, bf16[256,2048]{1,0:T(8,128)(2,1)S(1)}, u32[]{:S(2)}, u32[]{:S(2)}) collective-permute-start(bf16[256,2048]{1,0:T(8,128)(2,1)S(1)} %add_convert_fusion.3), channel_id=1, source_target_pairs={{0,24},{4,28},{8,0},{12,4},{16,8},{20,12},{24,16},{28,20},{1,25},{... | collective-permute-start | bytes 3145736 | tf_op jit(solution)/shard_map/ppermute | solution.py:436
  467.6 24.8 %collective-permute-start.50 = (bf16[256,2048]{1,0:T(8,128)(2,1)}, bf16[256,2048]{1,0:T(8,128)(2,1)}, u32[]{:S(2)}, u32[]{:S(2)}) collective-permute-start(bf16[256,2048]{1,0:T(8,128)(2,1)} %get-tuple-element.242), channel_id=1, source_target_pairs={{0,4},{4,0},{8,12},{12,8},{16,20},{20,16},{24,28},{28,24},{1,5},{5... | collective-permute-start | bytes 3145736 | tf_op jit(solution)/shard_map/ppermute | solution.py:431
  495.3 28.2 %collective-permute-start.52 = (bf16[256,2048]{1,0:T(8,128)(2,1)}, bf16[256,2048]{1,0:T(8,128)(2,1)S(1)}, u32[]{:S(2)}, u32[]{:S(2)}) collective-permute-start(bf16[256,2048]{1,0:T(8,128)(2,1)} %add_convert_fusion.2), channel_id=1, source_target_pairs={{0,24},{4,28},{8,0},{12,4},{16,8},{20,12},{24,16},{28,20},{1,25},{... | collective-permute-start | bytes 3145736 | tf_op jit(solution)/shard_map/ppermute | solution.py:436
  497.0 26.4 %collective-permute-start.51 = (bf16[256,2048]{1,0:T(8,128)(2,1)}, bf16[256,2048]{1,0:T(8,128)(2,1)}, u32[]{:S(2)}, u32[]{:S(2)}) collective-permute-start(bf16[256,2048]{1,0:T(8,128)(2,1)} %get-tuple-element.250), channel_id=1, source_target_pairs={{0,4},{4,0},{8,12},{12,8},{16,20},{20,16},{24,28},{28,24},{1,5},{5... | collective-permute-start | bytes 3145736 | tf_op jit(solution)/shard_map/ppermute | solution.py:431
  506.0 9.3 %collective-permute-start.53 = (bf16[384,1024]{1,0:T(8,128)(2,1)}, bf16[384,1024]{1,0:T(8,128)(2,1)S(1)}, u32[]{:S(2)}, u32[]{:S(2)}) collective-permute-start(bf16[384,1024]{1,0:T(8,128)(2,1)} %get-tuple-element.256), channel_id=1, source_target_pairs={{0,1},{1,0},{2,3},{3,2},{4,5},{5,4},{6,7},{7,6},{8,9},{9,8},{10,11... | collective-permute-start | bytes 2359304 | tf_op jit(solution)/shard_map/ppermute | solution.py:431
  506.0 9.4 %collective-permute-start.54 = (bf16[384,1024]{1,0:T(8,128)(2,1)}, bf16[384,1024]{1,0:T(8,128)(2,1)S(1)}, u32[]{:S(2)}, u32[]{:S(2)}) collective-permute-start(bf16[384,1024]{1,0:T(8,128)(2,1)} %get-tuple-element.257), channel_id=1, source_target_pairs={{0,1},{1,0},{2,3},{3,2},{4,5},{5,4},{6,7},{7,6},{8,9},{9,8},{10,11... | collective-permute-start | bytes 2359304 | tf_op jit(solution)/shard_map/ppermute | solution.py:431
  506.5 8.8 %collective-permute-start.55 = (bf16[256,1024]{1,0:T(8,128)(2,1)}, bf16[256,1024]{1,0:T(8,128)(2,1)S(1)}, u32[]{:S(2)}, u32[]{:S(2)}) collective-permute-start(bf16[256,1024]{1,0:T(8,128)(2,1)} %get-tuple-element.258), channel_id=1, source_target_pairs={{0,1},{1,0},{2,3},{3,2},{4,5},{5,4},{6,7},{7,6},{8,9},{9,8},{10,11... | collective-permute-start | bytes 1572872 | tf_op jit(solution)/shard_map/ppermute | solution.py:431
  523.4 25.8 %collective-permute-start.58 = (bf16[1024,512]{1,0:T(8,128)(2,1)}, bf16[1024,512]{1,0:T(8,128)(2,1)S(1)}, u32[]{:S(2)}, u32[]{:S(2)}) collective-permute-start(bf16[1024,512]{1,0:T(8,128)(2,1)} %mix_back_part.1), channel_id=1, source_target_pairs={{0,2},{1,3},{2,0},{3,1},{4,6},{5,7},{6,4},{7,5},{8,10},{9,11},{10,... | collective-permute-start | bytes 3145736 | tf_op jit(solution)/shard_map/ppermute | solution.py:431
  528.0 25.6 %collective-permute-start.56 = (bf16[256,2048]{1,0:T(8,128)(2,1)}, bf16[256,2048]{1,0:T(8,128)(2,1)}, u32[]{:S(2)}, u32[]{:S(2)}) collective-permute-start(bf16[256,2048]{1,0:T(8,128)(2,1)} %add_convert_fusion.1), channel_id=1, source_target_pairs={{0,24},{4,28},{8,0},{12,4},{16,8},{20,12},{24,16},{28,20},{1,25},{... | collective-permute-start | bytes 3145736 | tf_op jit(solution)/shard_map/ppermute | solution.py:436
  528.0 25.6 %collective-permute-start.57 = (bf16[1024,512]{1,0:T(8,128)(2,1)S(1)}, bf16[1024,512]{1,0:T(8,128)(2,1)S(1)}, u32[]{:S(2)}, u32[]{:S(2)}) collective-permute-start(bf16[1024,512]{1,0:T(8,128)(2,1)S(1)} %copy-done.31), channel_id=1, source_target_pairs={{0,4},{4,0},{8,12},{12,8},{16,20},{20,16},{24,28},{28,24},{1,5},{5... | collective-permute-start | bytes 3145736 | tf_op jit(solution)/shard_map/ppermute | solution.py:431
  553.7 7.6 %collective-permute-start.60 = (bf16[256,512]{1,0:T(8,128)(2,1)S(1)}, bf16[256,512]{1,0:T(8,128)(2,1)S(1)}, u32[]{:S(2)}, u32[]{:S(2)}) collective-permute-start(bf16[256,512]{1,0:T(8,128)(2,1)S(1)} %add_convert_fusion.12), channel_id=1, source_target_pairs={{0,24},{4,28},{8,0},{12,4},{16,8},{20,12},{24,16},{28,20},{1,25},{... | collective-permute-start | bytes 786440 | tf_op jit(solution)/shard_map/ppermute | solution.py:436
  555.8 34.1 %collective-permute-start.59 = (bf16[256,2048]{1,0:T(8,128)(2,1)}, bf16[256,2048]{1,0:T(8,128)(2,1)}, u32[]{:S(2)}, u32[]{:S(2)}) collective-permute-start(bf16[256,2048]{1,0:T(8,128)(2,1)} %get-tuple-element.268), channel_id=1, source_target_pairs={{0,4},{4,0},{8,12},{12,8},{16,20},{20,16},{24,28},{28,24},{1,5},{5... | collective-permute-start | bytes 3145736 | tf_op jit(solution)/shard_map/ppermute | solution.py:431
  562.1 17.0 %collective-permute-start.61 = (bf16[256,512]{1,0:T(8,128)(2,1)}, bf16[256,512]{1,0:T(8,128)(2,1)}, u32[]{:S(2)}, u32[]{:S(2)}) collective-permute-start(bf16[256,512]{1,0:T(8,128)(2,1)} %add_convert_fusion.11), channel_id=1, source_target_pairs={{0,24},{4,28},{8,0},{12,4},{16,8},{20,12},{24,16},{28,20},{1,25},{... | collective-permute-start | bytes 786440 | tf_op jit(solution)/shard_map/ppermute | solution.py:436
  576.6 13.3 %collective-permute-start.63 = (bf16[384,1024]{1,0:T(8,128)(2,1)}, bf16[384,1024]{1,0:T(8,128)(2,1)}, u32[]{:S(2)}, u32[]{:S(2)}) collective-permute-start(bf16[384,1024]{1,0:T(8,128)(2,1)} %get-tuple-element.275), channel_id=1, source_target_pairs={{0,1},{1,0},{2,3},{3,2},{4,5},{5,4},{6,7},{7,6},{8,9},{9,8},{10,11... | collective-permute-start | bytes 2359304 | tf_op jit(solution)/shard_map/ppermute | solution.py:431
  576.6 13.3 %collective-permute-start.64 = (bf16[384,1024]{1,0:T(8,128)(2,1)}, bf16[384,1024]{1,0:T(8,128)(2,1)}, u32[]{:S(2)}, u32[]{:S(2)}) collective-permute-start(bf16[384,1024]{1,0:T(8,128)(2,1)} %get-tuple-element.276), channel_id=1, source_target_pairs={{0,1},{1,0},{2,3},{3,2},{4,5},{5,4},{6,7},{7,6},{8,9},{9,8},{10,11... | collective-permute-start | bytes 2359304 | tf_op jit(solution)/shard_map/ppermute | solution.py:431
  581.0 8.9 %collective-permute-start.62 = (bf16[256,512]{1,0:T(8,128)(2,1)}, bf16[256,512]{1,0:T(8,128)(2,1)S(1)}, u32[]{:S(2)}, u32[]{:S(2)}) collective-permute-start(bf16[256,512]{1,0:T(8,128)(2,1)} %add_convert_fusion.10), channel_id=1, source_target_pairs={{0,24},{4,28},{8,0},{12,4},{16,8},{20,12},{24,16},{28,20},{1,25},{... | collective-permute-start | bytes 786440 | tf_op jit(solution)/shard_map/ppermute | solution.py:436
  583.9 11.9 %collective-permute-start.69 = (f32[2,1024]{1,0:T(2,128)S(1)}, f32[2,1024]{1,0:T(2,128)S(1)}, u32[]{:S(2)}, u32[]{:S(2)}) collective-permute-start(f32[2,1024]{1,0:T(2,128)S(1)} %pad_maximum_fusion.5), channel_id=1, source_target_pairs={{0,1},{1,0},{2,3},{3,2},{4,5},{5,4},{6,7},{7,6},{8,9},{9,8},{10,11... | collective-permute-start | bytes 24584 | tf_op jit(solution)/shard_map/ppermute | solution.py:431
  589.9 22.4 %collective-permute-start.66 = (bf16[256,1536]{1,0:T(8,128)(2,1)}, bf16[256,1536]{1,0:T(8,128)(2,1)}, u32[]{:S(2)}, u32[]{:S(2)}) collective-permute-start(bf16[256,1536]{1,0:T(8,128)(2,1)} %get-tuple-element.278), channel_id=1, source_target_pairs={{0,4},{4,0},{8,12},{12,8},{16,20},{20,16},{24,28},{28,24},{1,5},{5... | collective-permute-start | bytes 2359304 | tf_op jit(solution)/shard_map/ppermute | solution.py:431
  594.4 17.9 %collective-permute-start.67 = (f32[12,512]{1,0:T(8,128)S(1)}, f32[12,512]{1,0:T(8,128)S(1)}, u32[]{:S(2)}, u32[]{:S(2)}) collective-permute-start(f32[12,512]{1,0:T(8,128)S(1)} %concatenate.27), channel_id=1, source_target_pairs={{0,4},{4,0},{8,12},{12,8},{16,20},{20,16},{24,28},{28,24},{1,5},{5... | collective-permute-start | bytes 73736 | tf_op jit(solution)/shard_map/ppermute | solution.py:431
  595.7 21.1 %collective-permute-start.70 = (f32[2,1024]{1,0:T(2,128)S(1)}, f32[2,1024]{1,0:T(2,128)S(1)}, u32[]{:S(2)}, u32[]{:S(2)}) collective-permute-start(f32[2,1024]{1,0:T(2,128)S(1)} %fusion.17), channel_id=1, source_target_pairs={{0,2},{1,3},{2,0},{3,1},{4,6},{5,7},{6,4},{7,5},{8,10},{9,11},{10,... | collective-permute-start | bytes 24584 | tf_op jit(solution)/shard_map/ppermute | solution.py:431
  614.0 19.1 %collective-permute-start.72 = (bf16[256,1536]{1,0:T(8,128)(2,1)S(1)}, bf16[256,1536]{1,0:T(8,128)(2,1)S(1)}, u32[]{:S(2)}, u32[]{:S(2)}) collective-permute-start(bf16[256,1536]{1,0:T(8,128)(2,1)S(1)} %add_convert_fusion.9), channel_id=1, source_target_pairs={{0,24},{4,28},{8,0},{12,4},{16,8},{20,12},{24,16},{28,20},{1,25},{... | collective-permute-start | bytes 2359304 | tf_op jit(solution)/shard_map/ppermute | solution.py:436
  616.2 18.4 %collective-permute-start.73 = (bf16[256,1536]{1,0:T(8,128)(2,1)}, bf16[256,1536]{1,0:T(8,128)(2,1)S(1)}, u32[]{:S(2)}, u32[]{:S(2)}) collective-permute-start(bf16[256,1536]{1,0:T(8,128)(2,1)} %get-tuple-element.290), channel_id=1, source_target_pairs={{0,4},{4,0},{8,12},{12,8},{16,20},{20,16},{24,28},{28,24},{1,5},{5... | collective-permute-start | bytes 2359304 | tf_op jit(solution)/shard_map/ppermute | solution.py:431
  616.9 16.2 %collective-permute-start.71 = (f32[12,512]{1,0:T(8,128)S(1)}, f32[12,512]{1,0:T(8,128)S(1)}, u32[]{:S(2)}, u32[]{:S(2)}) collective-permute-start(f32[12,512]{1,0:T(8,128)S(1)} %add.353), channel_id=1, source_target_pairs={{0,8},{4,12},{8,0},{12,4},{16,24},{20,28},{24,16},{28,20},{1,9},{5... | collective-permute-start | bytes 73736 | tf_op jit(solution)/shard_map/ppermute | solution.py:431
  634.9 19.2 %collective-permute-start.75 = (bf16[256,1536]{1,0:T(8,128)(2,1)S(1)}, bf16[256,1536]{1,0:T(8,128)(2,1)S(1)}, u32[]{:S(2)}, u32[]{:S(2)}) collective-permute-start(bf16[256,1536]{1,0:T(8,128)(2,1)S(1)} %add_convert_fusion.8), channel_id=1, source_target_pairs={{0,24},{4,28},{8,0},{12,4},{16,8},{20,12},{24,16},{28,20},{1,25},{... | collective-permute-start | bytes 2359304 | tf_op jit(solution)/shard_map/ppermute | solution.py:436
  637.2 17.1 %collective-permute-start.76 = (bf16[256,1536]{1,0:T(8,128)(2,1)}, bf16[256,1536]{1,0:T(8,128)(2,1)S(1)}, u32[]{:S(2)}, u32[]{:S(2)}) collective-permute-start(bf16[256,1536]{1,0:T(8,128)(2,1)} %get-tuple-element.293), channel_id=1, source_target_pairs={{0,4},{4,0},{8,12},{12,8},{16,20},{20,16},{24,28},{28,24},{1,5},{5... | collective-permute-start | bytes 2359304 | tf_op jit(solution)/shard_map/ppermute | solution.py:431
  641.2 22.3 %collective-permute-start.68 = (bf16[1024,512]{1,0:T(8,128)(2,1)S(1)}, bf16[1024,512]{1,0:T(8,128)(2,1)S(1)}, u32[]{:S(2)}, u32[]{:S(2)}) collective-permute-start(bf16[1024,512]{1,0:T(8,128)(2,1)S(1)} %copy-done.47), channel_id=1, source_target_pairs={{0,2},{1,3},{2,0},{3,1},{4,6},{5,7},{6,4},{7,5},{8,10},{9,11},{10,... | collective-permute-start | bytes 3145736 | tf_op jit(solution)/shard_map/ppermute | solution.py:431
  642.8 11.3 %collective-permute-start.74 = (f32[12,512]{1,0:T(8,128)S(1)}, f32[12,512]{1,0:T(8,128)S(1)}, u32[]{:S(2)}, u32[]{:S(2)}) collective-permute-start(f32[12,512]{1,0:T(8,128)S(1)} %add.362), channel_id=1, source_target_pairs={{0,16},{4,20},{8,24},{12,28},{16,0},{20,4},{24,8},{28,12},{1,17},{... | collective-permute-start | bytes 73736 | tf_op jit(solution)/shard_map/ppermute | solution.py:431
  654.6 20.3 %collective-permute-start.78 = (bf16[256,1536]{1,0:T(8,128)(2,1)S(1)}, bf16[256,1536]{1,0:T(8,128)(2,1)S(1)}, u32[]{:S(2)}, u32[]{:S(2)}) collective-permute-start(bf16[256,1536]{1,0:T(8,128)(2,1)S(1)} %add_convert_fusion.7), channel_id=1, source_target_pairs={{0,24},{4,28},{8,0},{12,4},{16,8},{20,12},{24,16},{28,20},{1,25},{... | collective-permute-start | bytes 2359304 | tf_op jit(solution)/shard_map/ppermute | solution.py:436
  657.9 19.2 %collective-permute-start.77 = (bf16[256,1536]{1,0:T(8,128)(2,1)S(1)}, bf16[256,1536]{1,0:T(8,128)(2,1)S(1)}, u32[]{:S(2)}, u32[]{:S(2)}) collective-permute-start(bf16[256,1536]{1,0:T(8,128)(2,1)S(1)} %copy-done.73), channel_id=1, source_target_pairs={{0,4},{4,0},{8,12},{12,8},{16,20},{20,16},{24,28},{28,24},{1,5},{5... | collective-permute-start | bytes 2359304 | tf_op jit(solution)/shard_map/ppermute | solution.py:431
  (90 other events, 1193.7 us)
Sparse Core Ops, SparseCore 0:
  147.0 161.7 all-gather.1

commit v6 on v5

--- a/solution.py
+++ b/solution.py
@@ -101,7 +101,7 @@
             transcendentals=seqs * pairs * length * length // CHEAP,
         ),
         name="attend_forward",
-    )(slopes, starts[:, :, None], mixed, mixed, mixed)
+    )(slopes, starts, mixed, mixed, mixed)
 
 
 def attend_back_kernel(
@@ -208,7 +208,7 @@
             transcendentals=seqs * pairs * length * length // CHEAP,
         ),
         name="attend_backward",
-    )(slopes, starts[:, None, :], logs, mixed, mixed, mixed, grads)
+    )(slopes, starts, logs, mixed, mixed, mixed, grads)
 
 
 def resident(shape):
@@ -532,14 +532,18 @@
     def two(ws):
         return ws if len(ws) == 2 else [ws[0], ws[0]]
 
-    def columns_sent(xs, ws, ids, name, first=0):
+    def columns_sent(xs, ws, ids, name, first=0, whole=False):
         order = columns_order(ids, ws)[:, :2]
         xs = [at_now(xs[0])] + xs[1:]
         chunks = [3 * tokens_here // 8, 3 * tokens_here // 8, tokens_here // 4]
+        if whole:
+            chunks = [tokens_here]
         sent = times_columns(
             xs, two(ws), order, sides, bf16, name + "_sent", first, chunks=chunks
         )
-        return [swap(v, "col", 1) for v in sent]
+        if whole:
+            put(sent)
+        return [swap(v, "col", 1) for v in ([sent] if whole else sent)]
 
     def columns_part(xs, ws, ids, got, name, first=0):
         order = columns_order(ids, ws)[:, 3:]
@@ -556,6 +560,7 @@
             self.left = rows // 2
             self.groups = groups or [[k] for k in reversed(range(self.left))]
             self.got, self.kept, self.carry, self.result = {}, [], None, None
+            self.last = []
 
         def cut(self):
             if stepped:
@@ -577,10 +582,13 @@
                 self.kept = weight_rows(a, mine, self.gs, self.name + "_mine", single)
                 put(*self.kept)
 
-        def move(self, late=False):
+        def move(self, *first, late=False):
             if stepped:
+                if not self.groups:
+                    return
                 group = self.groups.pop(0)
-                got = swap(at_now(self.sent.pop(0)), "row", 1)
+                got = swap(after(at_now(self.sent.pop(0)), *first), "row", 1)
+                self.last = [got]
                 if not late:
                     put(got)
                 for j, k in enumerate(group):
@@ -608,6 +616,7 @@
     head_ids = (col * heads + jnp.arange(heads)).astype(f32)
     slopes = jnp.exp2(-8.0 * (head_ids + 1.0) / (heads * cols))
     starts = jnp.sum(segments[:, None, :] < segments[:, :, None], axis=2).astype(jnp.int32)
+    start_column, start_row = starts[:, :, None], starts[:, None, :]
     places_attend, places_expand = find(ids_attend, ours), find(ids_expand, ours)
     places_contract = find(ids_contract, ours)
     mix_width = 3 * width
@@ -651,7 +660,7 @@
     small_now = at_now(small)
     norms = [small, swap(small_now, "col", 1), swap(small_now, "col", 2)]
     cot_parts.append(swap(at_now(cot_parts[2]), "col", 1))
-    put(*norms[1:], cot_parts[3])
+    put(*norms[1:], cot_parts[3], start_column)
     tick()
 
     weight_step(3)
@@ -664,34 +673,27 @@
     put(first_full, cot_full)
     expand_own, expand_near = [expand], []
 
-    def expand_turn(start=None):
+    def expand_turn(*first):
         if stepped:
-            block = at_now(expand_own[2 if start is not None else -1])
-            if start is not None:
-                block = block[start : start + BLOCK // 2]
-            expand_own.append(turn(block, 1))
+            expand_own.append(turn(after(at_now(expand_own[-1]), *first), 1))
             put(expand_own[-1])
 
-    def expand_step(*ks):
+    def expand_step(k):
         if stepped:
-            for k in ks:
-                expand_near.append(swap(at_now(expand_own[k]), "row", 1))
-                put(expand_near[k])
+            expand_near.append(swap(at_now(expand_own[k]), "row", 1))
+            put(expand_near[k])
 
     expand_turn()
-    expand_turn()
+    tick()
+
+    def add_bias(acc, extra, out):
+        out[0][...] = (acc + extra[0][...]).astype(bf16)
+
+    expand_step(0)
     if stepped:
         contract_pair = jnp.concatenate([contract, swap(at_now(contract), "row", 1)], axis=0)
         put(contract_pair)
-    tick()
-
-    def add_bias(acc, extra, out):
-        out[0][...] = (acc + extra[0][...]).astype(bf16)
-
-    expand_turn(0)
-    expand_step(0)
-    if stepped:
-        full_contract = [gather_outer(at_now(contract_pair))]
+    expand_turn()
     mixed, *full_attend = times_rows(
         at_now(first_full),
         own + near,
@@ -703,10 +705,13 @@
         window=(0, mix_width),
         joins=[range(len(own)), range(len(own), len(own) + len(near))],
     )
-    attended, logs = attend_forward(mixed, starts, slopes, seqs)
+    expand_turn(mixed)
+    attended, logs = attend_forward(mixed, start_column, slopes, seqs)
     put(attended)
     tick()
 
+    if stepped:
+        full_contract = [gather_outer(at_now(contract_pair))]
     expand_step(1)
     got = columns_sent([attended], full_attend, ids_attend, "project", mix_width)
     part = columns_part([attended], full_attend, ids_attend, got, "project", mix_width)
@@ -714,7 +719,6 @@
     tick()
 
     expand_step(2)
-    expand_turn(BLOCK // 2)
     across = swap(at_now(part), "col", 2)
     base = columns_base([attended], full_attend, ids_attend, got, "project", mix_width)
     resid = tokens.astype(f32)
@@ -724,7 +728,7 @@
     put(middle_low, first_mean, first_scale)
     tick()
 
-    expand_step(3, 4)
+    expand_step(3)
     middle_now = at_now(middle_low)
     middle_parts = [middle_low, swap(middle_now, "col", 1), swap(middle_now, "col", 2)]
     put(*middle_parts[1:])
@@ -757,7 +761,7 @@
     if stepped:
         full_expand = joined
     contract_sum = WeightSum(
-        cot_full, ids_contract, [active], "contract_grad", [[3, 2], [1], [0]]
+        cot_full, ids_contract, [active], "contract_grad", [[3], [2, 1], [0]]
     )
     contract_sum.cut()
     put(active)
@@ -770,10 +774,14 @@
 
     second_mean, second_scale = at_now(second_mean)[:, 0], at_now(second_scale)[:, 0]
     put(second_mean, second_scale)
-    contract_sum.move(late=True)
+    contract_sum.move()
     contract_sum.keep()
+    tick()
+
+    contract_sum.add()
+    contract_sum.move()
     hidden_grad, thresholds_part = times_rows(
-        after(at_now(cot_full), *contract_sum.kept[:1]),
+        at_now(cot_full),
         full_contract,
         [slope],
         [(hidden_shape, bf16), ((1, hidden_shape[1]), f32)],
@@ -783,14 +791,14 @@
     )
     got = columns_sent([hidden_grad], full_expand, ids_expand, "expand_back")
     part = columns_part([hidden_grad], full_expand, ids_expand, got, "expand_back")
+    across = swap(part, "col", 2)
     put(part)
     tick()
 
     contract_sum.add()
     contract_sum.move()
-    across = swap(at_now(part), "col", 2)
     base = columns_base([hidden_grad], full_expand, ids_expand, got, "expand_back")
-    expand_sum = WeightSum(second_full, ids_expand, [hidden_grad], "expand_grad")
+    expand_sum = WeightSum(second_full, ids_expand, [hidden_grad], "expand_grad", [[3], [2, 1], [0]])
     expand_sum.cut()
     second_back = base + across.astype(f32)
     put(second_back)
@@ -806,7 +814,7 @@
         )
         return result, jnp.sum(upstream * centred, axis=0), jnp.sum(upstream, axis=0)
 
-    contract_sum.move()
+    expand_sum.move()
     second_centred = (middle - second_mean[:, None]) * second_scale[:, None]
     second_input, second_gain, second_shift = norm_back(
         at_now(second_back), second_centred, second_scale, gains[1]
@@ -817,6 +825,9 @@
     branch_parts = [branch_grad, swap(branch_grad, "col", 1), swap(branch_grad, "col", 2)]
     contract_sum.add(branch_grad)
     expand_sum.keep(branch_grad)
+    out_got = columns_sent(
+        [after(active, branch_grad)], full_contract, ids_contract, "contract", whole=True
+    )
     put(*branch_parts[1:])
     tick()
 
@@ -825,6 +836,7 @@
 
     contract_sum.add()
     expand_sum.move()
+    expand_sum.add()
     branch_parts.append(swap(at_now(branch_parts[2]), "col", 1))
     branch_full = lay_out(branch_parts, places_attend, "branch_rows")
     (attended_grad,) = times_rows(
@@ -837,43 +849,65 @@
         tn=width,
         window=(mix_width, width),
     )
-    project_sum = WeightSum(branch_full, ids_attend, [attended], "projection_grad", [[3, 2, 1, 0]])
-    project_sum.cut()
-    put(attended_grad)
-    tick()
-
-    expand_sum.add()
-    expand_sum.move()
+    if stepped:
+        project_other = weight_rows(
+            branch_full,
+            find(ids_attend, 2 * steps + 1 - side),
+            [attended],
+            "projection_grad_other",
+        )
+        put(project_other)
+    else:
+        project_sum = WeightSum(branch_full, ids_attend, [attended], "projection_grad", None)
+        project_sum.cut()
     query_back, key_back, value_back, query_sum, value_sum = attend_backward(
-        mixed, at_now(attended_grad), starts, logs, slopes, seqs
+        mixed, attended_grad, start_row, logs, slopes, seqs
     )
     mixed_grads = [query_back, key_back, value_back]
     put(query_back)
     tick()
 
-    contract_sum.add()
+    expand_sum.move()
+    if stepped:
+        project_got = swap(at_now(project_other), "row", 1)
+        put(project_got)
     expand_sum.add()
-    expand_sum.move()
     got = columns_sent(mixed_grads, full_attend, ids_attend, "mix_back")
-    mixing_sum = WeightSum(first_full, ids_attend, mixed_grads, "mixing_grad")
+    mixing_sum = WeightSum(
+        first_full, ids_attend, mixed_grads, "mixing_grad", [[3], [2], [1], [0]]
+    )
     mixing_sum.cut()
     part = columns_part(mixed_grads, full_attend, ids_attend, got, "mix_back")
-    put(part)
-    tick()
-
+    across = swap(part, "col", 2)
     expand_sum.add()
-    project_sum.move()
-    project_sum.keep()
-    across = swap(at_now(part), "col", 2)
     base = columns_base(mixed_grads, full_attend, ids_attend, got, "mix_back")
+    if stepped:
+        project_mine = weight_rows(
+            after(branch_full, part),
+            find(ids_attend, 2 * steps + side),
+            [attended],
+            "projection_grad_mine",
+        )
+        put(project_mine)
     first_back = base + across.astype(f32)
     put(first_back)
     tick()
 
-    expand_sum.move()
-    for _ in range(rows // 2 - 1):
+    if stepped:
+        total = at_now(project_mine).astype(f32) + project_got.astype(f32)
+        projection_grad = lax.psum_scatter(
+            total.astype(bf16),
+            "row",
+            scatter_dimension=0,
+            tiled=True,
+            axis_index_groups=outer_groups(),
+        ).astype(f32)
+    else:
         project_sum.add()
-    out_got = columns_sent([active], full_contract, ids_contract, "contract")
+        projection_grad = project_sum.result
+    expand_sum.add()
+    mixing_sum.move()
+    mixing_sum.keep()
     first_centred = (resid - first_mean[:, None]) * first_scale[:, None]
     first_input, first_gain, first_shift = norm_back(
         at_now(first_back), first_centred, first_scale, gains[0]
@@ -892,19 +926,17 @@
         ]
     )
     small = jnp.concatenate([small, thresholds_part.reshape(-1, width)], axis=0)
-    put(small, *out_got)
-    tick()
-
     def small_step(bit):
         return small + swap(at_now(small), "row", bit) if bit < rows else small
 
-    expand_sum.add()
-    project_sum.add()
+    put(small)
+    tick()
+
+    mixing_sum.add()
     mixing_sum.move()
-    mixing_sum.keep()
     out_part = columns_part([at_now(active)], full_contract, ids_contract, out_got, "contract")
-    small = small_step(1)
-    put(small, out_part)
+    small = small_step(2)
+    put(out_part, small)
     tick()
 
     mixing_sum.add()
@@ -912,23 +944,24 @@
     out_across = swap(at_now(out_part), "col", 2)
     out_base = columns_base([active], full_contract, ids_contract, out_got, "contract")
     layer_out = (middle + (out_base + out_across.astype(f32) + biases[3])).astype(bf16)
-    small = small_step(2)
-    put(small)
-    tick()
-
-    bit = 4
-    while bit < rows or mixing_sum.groups:
-        mixing_sum.add()
-        mixing_sum.groups and mixing_sum.move()
+    small = small_step(4)
+    put(small, projection_grad, out_base)
+    tick()
+
+    mixing_sum.add()
+    mixing_sum.move()
+    bit = 8
+    while bit < rows:
         small = small_step(bit)
         put(small)
         tick()
         bit *= 2
-        if not stepped and bit >= rows:
-            break
+    small = small_step(1)
+    put(small)
+    tick()
     mixing_sum.add()
     contract_grad, expand_grad = contract_sum.result, expand_sum.result
-    projection_grad, mixing_grad = project_sum.result, mixing_sum.result
+    mixing_grad = mixing_sum.result
     mixing_grad = jnp.stack(
         [mixing_grad[:, i * width : (i + 1) * width] for i in range(3)], axis=1
     )

time: 692 us -> 655 us (0.947)
  starting transfers between devices: 82.2 us -> 57 us
  waiting for transfers between devices: 240 us -> 224 us
    ppermute x19 -> x15, waiting for transfers between devices: 73.7 us -> 37.5 us  [turn(): lax.ppermute(x, 'row', [(i, (i + 2 * steps) % count) for i in range(count)])]
    ppermute x19 -> x15, starting transfers between devices: 41.6 us -> 14.7 us  [turn(): lax.ppermute(x, 'row', [(i, (i + 2 * steps) % count) for i in range(count)])]
    all_gather x1, waiting for transfers between devices: 0.01 us -> 10.6 us  [gather_outer(): lax.all_gather(w, 'row', axis=0, tiled=True, axis_index_groups=outer_grou...]
    ppermute x60 -> x56, waiting for transfers between devices: 166 us -> 176 us  [swap(): lax.ppermute(x, axis, [(i, i ^ bit) for i in range(lax.axis_size(axis))])]
    ppermute x60 -> x56, starting transfers between devices: 40.5 us -> 42 us  [swap(): lax.ppermute(x, axis, [(i, i ^ bit) for i in range(lax.axis_size(axis))])]
    convert_element_type x12 -> x9, other arithmetic: 21 us -> 21.9 us  [add(): self.carry = turn(total.astype(bf16), -1)]
  transfers between devices with their start and end apart: 80 -> 73, of which waited for: 43 -> 40; matrix products, arithmetic and copies ran while one was open for 9% -> 10% of each run, Pallas kernels for 39% -> 42%
where the time goes in v6:
time: 655 us; the launch traced here: 645 us
  Pallas kernels  269 us (41%)
  waiting for transfers between devices  224 us (34%)
  other arithmetic  62.7 us (10%)
  starting transfers between devices  57 us (9%)
  local copies, waits for them, and re-layouts  17.4 us (3%)
  between operations  15.2 us (2%)
    pallas_call x28, Pallas kernels, matmul_call(): pl.pallas_call(kernel, grid_spec=pltpu.PrefetchScalarGridSpec(num_scalar_...  232 us
    ppermute x56, waiting for transfers between devices, swap(): lax.ppermute(x, axis, [(i, i ^ bit) for i in range(lax.axis_size(axis))])  176 us
    ppermute x56, starting transfers between devices, swap(): lax.ppermute(x, axis, [(i, i ^ bit) for i in range(lax.axis_size(axis))])  42 us
    ppermute x15, waiting for transfers between devices, turn(): lax.ppermute(x, 'row', [(i, (i + 2 * steps) % count) for i in range(count)])  37.5 us
    convert_element_type x9, other arithmetic, add(): self.carry = turn(total.astype(bf16), -1)  21.9 us
    pallas_call x1, Pallas kernels, attend_backward(): pl.pallas_call(partial(attend_back_kernel, rows=rows, scale=HD ** (-0.5))...  20.3 us
    pallas_call x1, Pallas kernels, attend_forward(): pl.pallas_call(partial(attend_kernel, rows=rows, scale=HD ** (-0.5)), gri...  17.3 us
    ppermute x15, starting transfers between devices, turn(): lax.ppermute(x, 'row', [(i, (i + 2 * steps) % count) for i in range(count)])  14.7 us
  transfers between devices with their start and end apart: 73, of which 40 were waited for; matrix products, arithmetic and copies ran while one was open for 10% of the time, Pallas kernels for 42%

profile of v6, /device:TPU:0, one launch (start us, length us, event | category | flops | bytes accessed | tf_op | source)
XLA Modules:
  0.0 645.3 jit_solution(15120802156823470226)
XLA Ops:
  17.4 20.6 %collective-permute-done.1.refs_2_ = bf16[1024,512]{1,0:T(8,128)(2,1)S(1)} collective-permute-done((bf16[1024,512]{1,0:T(8,128)(2,1)S(1)}, bf16[1024,512]{1,0:T(8,128)(2,1)S(1)}, u32[]{:S(2)}, u32[]{:S(2)}) %collective-permute-start.1) | collective-permute-done | bytes 1048608 | tf_op jit(solution)/shard_map/ppermute | solution.py:431
  39.5 3.1 collective-permute-done.3.refs_2_
  45.3 23.0 %collective-permute-done.8.refs_2_ = bf16[1024,512]{1,0:T(8,128)(2,1)} collective-permute-done((bf16[1024,512]{1,0:T(8,128)(2,1)S(1)}, bf16[1024,512]{1,0:T(8,128)(2,1)}, u32[]{:S(2)}, u32[]{:S(2)}) %collective-permute-start.8) | collective-permute-done | bytes 1048608 | tf_op jit(solution)/shard_map/ppermute | solution.py:431
  76.7 18.2 %collective-permute-done.11.refs_7_ = bf16[256,2048]{1,0:T(8,128)(2,1)S(1)} collective-permute-done((bf16[256,2048]{1,0:T(8,128)(2,1)}, bf16[256,2048]{1,0:T(8,128)(2,1)S(1)}, u32[]{:S(2)}, u32[]{:S(2)}) %collective-permute-start.11) | collective-permute-done | bytes 1048608 | tf_op jit(solution)/shard_map/ppermute | solution.py:431
  94.9 3.1 collective-permute-done.12.refs_4_
  100.3 5.4 cotangent_rows.1.a_ref.refs_0_
  106.4 7.4 %first_norm.1 = (bf16[1024,2048]{1,0:T(8,128)(2,1)}, f32[1024,1]{1,0:T(8,128)}, f32[1024,1]{1,0:T(8,128)}) custom-call(s32[8]{0:T(128)} %get-tuple-element.286.place_ref, bf16[1024,512]{1,0:T(8,128)(2,1)} %refs_0_.1, bf16[1024,512]{1,0:T(8,128)(2,1)} %copy-done.28, bf16[1024,512]{1,0:T(8,128)(2,1)} %copy-done.29, bf16[1024,512]{1,0:T(8,128)(2,1)} %copy-done.31, ...), custom_call_target="tpu_custom_call" | custom-call | flops 262144 | bytes 131456 | tf_op jit(solution)/shard_map/first_norm/pallas_call | solution.py:229
  113.8 9.3 %collective-permute-done.16.refs_2_ = bf16[256,2048]{1,0:T(8,128)(2,1)} collective-permute-done((bf16[256,2048]{1,0:T(8,128)(2,1)}, bf16[256,2048]{1,0:T(8,128)(2,1)}, u32[]{:S(2)}, u32[]{:S(2)}) %collective-permute-start.16) | collective-permute-done | bytes 1048608 | tf_op jit(solution)/shard_map/ppermute | solution.py:436
  125.8 13.4 %mix.1 = (bf16[1024,1536]{1,0:T(8,128)(2,1)}, bf16[1024,2048]{1,0:T(8,128)(2,1)}, bf16[1024,2048]{1,0:T(8,128)(2,1)}) custom-call(bf16[1024,2048]{1,0:T(8,128)(2,1)} %get-tuple-element.244.refs_0_.a_ref, bf16[256,2048]{1,0:T(8,128)(2,1)} %copy-done.10, bf16[256,2048]{1,0:T(8,128)(2,1)} %copy-done.26, bf16[256,2048]{1,0:T(8,128)(2,1)} %collective-permute-done.6.refs_3_, ...), custom_call_target="tpu_custom_call" | custom-call | flops 100663296 | bytes 376928 | tf_op jit(solution)/shard_map/mix/pallas_call | solution.py:229
  139.2 7.9 %collective-permute-done.19.refs_3_ = bf16[256,2048]{1,0:T(8,128)(2,1)} collective-permute-done((bf16[256,2048]{1,0:T(8,128)(2,1)}, bf16[256,2048]{1,0:T(8,128)(2,1)}, u32[]{:S(2)}, u32[]{:S(2)}) %collective-permute-start.19) | collective-permute-done | bytes 1048608 | tf_op jit(solution)/shard_map/ppermute | solution.py:436
  148.8 17.3 %attend_forward.1 = (bf16[1024,512]{1,0:T(8,128)(2,1)}, f32[4,2,1024]{2,1,0:T(2,128)}) custom-call(f32[8]{0:T(128)} %multiply_exponential_fusion.slope_ref, s32[1,1024,1]{2,1,0:T(8,128)} %copy.28.start_ref, bf16[1024,1536]{1,0:T(8,128)(2,1)} %get-tuple-element.154.q_ref.k_ref.v_ref, bf16[1024,1536]{1,0:T(8,128)(2,1)} %get-tuple-element.154.q_ref.k_ref.v_ref, ...), custom_call_target="tpu_custom_call" | custom-call | flops 67108864 | bytes 98304 | tf_op jit(solution)/shard_map/attend_forward/pallas_call | solution.py:79
  173.3 4.7 project_sent.1
  179.3 3.2 collective-permute-done.24.refs_5_
  183.7 4.1 project_part.1
  187.8 4.0 collective-permute-done.21.refs_6_
  199.2 4.7 project_base.1
  203.9 9.4 %collective-permute-done.25 = bf16[1024,512]{1,0:T(8,128)(2,1)S(1)} collective-permute-done((bf16[1024,512]{1,0:T(8,128)(2,1)}, bf16[1024,512]{1,0:T(8,128)(2,1)S(1)}, u32[]{:S(2)}, u32[]{:S(2)}) %collective-permute-start.25) | collective-permute-done | bytes 1048608 | tf_op jit(solution)/shard_map/ppermute | solution.py:431
  218.8 18.2 %collective-permute-done.29.refs_8_ = bf16[256,2048]{1,0:T(8,128)(2,1)S(1)} collective-permute-done((bf16[256,2048]{1,0:T(8,128)(2,1)}, bf16[256,2048]{1,0:T(8,128)(2,1)S(1)}, u32[]{:S(2)}, u32[]{:S(2)}) %collective-permute-start.29) | collective-permute-done | bytes 1048608 | tf_op jit(solution)/shard_map/ppermute | solution.py:431
  237.0 5.7 collective-permute-done.28.refs_2_
  246.3 7.2 %second_norm.1 = (bf16[1024,2048]{1,0:T(8,128)(2,1)}, f32[1024,1]{1,0:T(8,128)}, f32[1024,1]{1,0:T(8,128)}) custom-call(s32[8]{0:T(128)} %get-tuple-element.286.place_ref, bf16[1024,512]{1,0:T(8,128)(2,1)} %copy-done.11, bf16[1024,512]{1,0:T(8,128)(2,1)} %copy-done.33, bf16[1024,512]{1,0:T(8,128)(2,1)} %copy-done.34, bf16[1024,512]{1,0:T(8,128)(2,1)} %copy-done.36, ...), custom_call_target="tpu_custom_call" | custom-call | flops 262144 | bytes 131456 | tf_op jit(solution)/shard_map/second_norm/pallas_call | solution.py:229
  253.5 18.3 %expand.1 = (bf16[1024,2048]{1,0:T(8,128)(2,1)}, f32[1024,2048]{1,0:T(8,128)}, bf16[1024,2048]{1,0:T(8,128)(2,1)}, bf16[1024,2048]{1,0:T(8,128)(2,1)}) custom-call(bf16[1024,2048]{1,0:T(8,128)(2,1)} %get-tuple-element.217.refs_0_.a_ref, bf16[256,2048]{1,0:T(8,128)(2,1)} %refs_1_.1, bf16[256,2048]{1,0:T(8,128)(2,1)} %collective-permute-done.16.refs_2_, ...), custom_call_target="tpu_custom_call" | custom-call | flops 134217728 | bytes 524416 | tf_op jit(solution)/shard_map/expand/pallas_call | solution.py:229
  271.8 10.7 %contract_grad_other.1 = (bf16[256,2048]{1,0:T(8,128)(2,1)}, bf16[512,2048]{1,0:T(8,128)(2,1)}, bf16[256,2048]{1,0:T(8,128)(2,1)}) custom-call(s32[4]{0:T(128)} %get-tuple-element.280.order_ref, bf16[1024,2048]{1,0:T(8,128)(2,1)} %cotangent_rows.1.a_ref.refs_0_, bf16[1024,2048]{1,0:T(8,128)(2,1)} %get-tuple-element.258.refs_0_), custom_call_target="tpu_custom_call" | custom-call | flops 67108864 | bytes 196608 | tf_op jit(solution)/shard_map/contract_grad_other/pallas_call | solution.py:229
  286.6 10.7 %contract_grad_mine.1 = (bf16[256,2048]{1,0:T(8,128)(2,1)}, bf16[256,2048]{1,0:T(8,128)(2,1)}, bf16[256,2048]{1,0:T(8,128)(2,1)}, bf16[256,2048]{1,0:T(8,128)(2,1)}) custom-call(s32[4]{0:T(128)} %get-tuple-element.281.order_ref, bf16[1024,2048]{1,0:T(8,128)(2,1)} %cotangent_rows.1.a_ref.refs_0_, bf16[1024,2048]{1,0:T(8,128)(2,1)} %get-tuple-element.258.refs_0_), custom_call_target="tpu_custom_call" | custom-call | flops 67108864 | bytes 196608 | tf_op jit(solution)/shard_map/contract_grad_mine/pallas_call | solution.py:229
  297.3 10.6 %collective-permute-done.31 = bf16[256,2048]{1,0:T(8,128)(2,1)} collective-permute-done((bf16[256,2048]{1,0:T(8,128)(2,1)}, bf16[256,2048]{1,0:T(8,128)(2,1)}, u32[]{:S(2)}, u32[]{:S(2)}) %collective-permute-start.31) | collective-permute-done | bytes 1048608 | tf_op jit(solution)/shard_map/ppermute | solution.py:431
  309.6 2.9 add_convert_fusion.7
  315.1 10.6 %all-gather.2.cloned.1.call-done.refs_1_.refs_2_ = bf16[2048,2048]{1,0:T(8,128)(2,1)} async-done(((bf16[512,2048]{1,0:T(8,128)(2,1)}), bf16[2048,2048]{1,0:T(8,128)(2,1)}) %all-gather.2.cloned.1.call-update) | async-done | bytes 8388624 | tf_op jit(solution)/shard_map/all_gather | solution.py:473
  325.7 14.3 %contract_back.1 = (bf16[1024,2048]{1,0:T(8,128)(2,1)}, f32[1,2048]{1,0:T(1,128)}) custom-call(bf16[1024,2048]{1,0:T(8,128)(2,1)} %cotangent_rows.1.a_ref.refs_0_, bf16[2048,2048]{1,0:T(8,128)(2,1)} %all-gather.2.cloned.1.call-done.refs_1_.refs_2_, f32[1024,2048]{1,0:T(8,128)} %get-tuple-element.197.refs_2_), custom_call_target="tpu_custom_call" | custom-call | flops 134217728 | bytes 393344 | tf_op jit(solution)/shard_map/contract_back/pallas_call | solution.py:229
  340.0 9.3 %expand_back_sent.1 = (bf16[384,1024]{1,0:T(8,128)(2,1)}, bf16[384,1024]{1,0:T(8,128)(2,1)}, bf16[256,1024]{1,0:T(8,128)(2,1)}) custom-call(s32[2,2]{1,0:T(2,128)} %bitcast.57, s32[1]{0:T(128)} %bitcast.2.side_ref, bf16[1024,2048]{1,0:T(8,128)(2,1)} %get-tuple-element.211.refs_0_, bf16[1024,2048]{1,0:T(8,128)(2,1)} %get-tuple-element.199.refs_1_, ...), custom_call_target="tpu_custom_call" | custom-call | flops 67108864 | bytes 229376 | tf_op jit(solution)/shard_map/expand_back_sent/pallas_call | solution.py:229
  349.8 3.8 collective-permute-done.36.refs_5_
  355.6 7.1 %expand_back_part.1 = bf16[1024,512]{1,0:T(8,128)(2,1)} custom-call(s32[2,1]{1,0:T(2,128)} %get-tuple-element.317.order_ref, s32[1]{0:T(128)} %bitcast.2.side_ref, bf16[1024,2048]{1,0:T(8,128)(2,1)} %get-tuple-element.211.refs_0_, bf16[1024,2048]{1,0:T(8,128)(2,1)} %get-tuple-element.199.refs_1_, bf16[1024,2048]{1,0:T(8,128)(2,1)} %get-tuple-element.200.refs_2_, ...), custom_call_target="tpu_custom_call" | custom-call | flops 33554432 | bytes 245760 | tf_op jit(solution)/shard_map/expand_back_part/pallas_call | solution.py:229
  365.7 3.1 add_convert_fusion.6
  368.9 7.5 %expand_back_base.1 = f32[1024,512]{1,0:T(8,128)} custom-call(s32[2,1]{1,0:T(2,128)} %get-tuple-element.318.order_ref, s32[1]{0:T(128)} %bitcast.2.side_ref, bf16[1024,2048]{1,0:T(8,128)(2,1)} %get-tuple-element.211.refs_0_, bf16[1024,2048]{1,0:T(8,128)(2,1)} %get-tuple-element.199.refs_1_, bf16[1024,2048]{1,0:T(8,128)(2,1)} %get-tuple-element.200.refs_2_, ...), custom_call_target="tpu_custom_call" | custom-call | flops 33554432 | bytes 262144 | tf_op jit(solution)/shard_map/expand_back_base/pallas_call | solution.py:229
  376.4 10.8 %expand_grad_other.1 = (bf16[256,2048]{1,0:T(8,128)(2,1)}, bf16[512,2048]{1,0:T(8,128)(2,1)}, bf16[256,2048]{1,0:T(8,128)(2,1)}) custom-call(s32[4]{0:T(128)} %get-tuple-element.279.order_ref, bf16[1024,2048]{1,0:T(8,128)(2,1)} %get-tuple-element.217.refs_0_.a_ref, bf16[1024,2048]{1,0:T(8,128)(2,1)} %get-tuple-element.211.refs_0_), custom_call_target="tpu_custom_call" | custom-call | flops 67108864 | bytes 196608 | tf_op jit(solution)/shard_map/expand_grad_other/pallas_call | solution.py:229
  389.3 4.6 collective-permute-done.37
  402.3 3.1 add_convert_fusion.5
  408.8 10.7 %expand_grad_mine.1 = (bf16[256,2048]{1,0:T(8,128)(2,1)}, bf16[256,2048]{1,0:T(8,128)(2,1)}, bf16[256,2048]{1,0:T(8,128)(2,1)}, bf16[256,2048]{1,0:T(8,128)(2,1)}) custom-call(s32[4]{0:T(128)} %get-tuple-element.282.order_ref, bf16[1024,2048]{1,0:T(8,128)(2,1)} %get-tuple-element.217.refs_0_.a_ref, bf16[1024,2048]{1,0:T(8,128)(2,1)} %get-tuple-element.211.refs_0_), custom_call_target="tpu_custom_call" | custom-call | flops 67108864 | bytes 196608 | tf_op jit(solution)/shard_map/expand_grad_mine/pallas_call | solution.py:229
  419.5 9.5 %contract_sent.1 = bf16[1024,1024]{1,0:T(8,128)(2,1)} custom-call(s32[2,2]{1,0:T(2,128)} %bitcast.68, s32[1]{0:T(128)} %bitcast.2.side_ref, bf16[1024,2048]{1,0:T(8,128)(2,1)} %get-tuple-element.258.refs_0_, bf16[2048,2048]{1,0:T(8,128)(2,1)} %all-gather.2.cloned.1.call-done.refs_1_.refs_2_, bf16[2048,2048]{1,0:T(8,128)(2,1)} %all-gather.2.cloned.1.call-done.refs_1_.refs_2_), custom_call_target="tpu_custom_call" | custom-call | flops 67108864 | bytes 360448 | tf_op jit(solution)/shard_map/contract_sent/pallas_call | solution.py:229
  429.9 3.6 collective-permute-done.45.refs_2_
  436.9 5.6 branch_rows.1.a_ref.refs_0_
  442.5 5.5 projection_grad_other.1
  448.0 6.1 project_back.1.g_ref
  454.1 20.3 %attend_backward.1 = (bf16[1024,512]{1,0:T(8,128)(2,1)}, bf16[1024,512]{1,0:T(8,128)(2,1)}, bf16[1024,512]{1,0:T(8,128)(2,1)}, f32[1,1,512]{2,1,0:T(1,128)}, f32[1,1,512]{2,1,0:T(1,128)}) custom-call(f32[8]{0:T(128)} %multiply_exponential_fusion.slope_ref, s32[1,1,1024]{2,1,0:T(1,128)} %bitcast.55, f32[4,2,1024]{2,1,0:T(2,128)} %get-tuple-element.227.log_ref, ...), custom_call_target="tpu_custom_call" | custom-call | flops 167772160 | bytes 114688 | tf_op jit(solution)/shard_map/attend_backward/pallas_call | solution.py:183
  474.5 6.5 %collective-permute-done.46 = bf16[512,2048]{1,0:T(8,128)(2,1)S(1)} collective-permute-done((bf16[512,2048]{1,0:T(8,128)(2,1)}, bf16[512,2048]{1,0:T(8,128)(2,1)S(1)}, u32[]{:S(2)}, u32[]{:S(2)}) %collective-permute-start.46) | collective-permute-done | bytes 2097184 | tf_op jit(solution)/shard_map/ppermute | solution.py:431
  481.0 2.8 add_convert_fusion.3
  484.0 7.7 %mix_back_sent.1 = (bf16[384,1024]{1,0:T(8,128)(2,1)}, bf16[384,1024]{1,0:T(8,128)(2,1)}, bf16[256,1024]{1,0:T(8,128)(2,1)}) custom-call(s32[2,2]{1,0:T(2,128)} %bitcast.58, s32[1]{0:T(128)} %bitcast.2.side_ref, bf16[1024,512]{1,0:T(8,128)(2,1)} %get-tuple-element.239.refs_0_, bf16[1024,512]{1,0:T(8,128)(2,1)} %get-tuple-element.233.refs_1_, ...), custom_call_target="tpu_custom_call" | custom-call | flops 50331648 | bytes 212992 | tf_op jit(solution)/shard_map/mix_back_sent/pallas_call | solution.py:229
  492.7 3.4 collective-permute-done.55.refs_7_
  498.2 6.1 mix_back_part.1
  504.9 3.3 collective-permute-done.51
  508.2 3.1 add_convert_fusion.2
  515.3 8.8 %mixing_grad_other.1 = (bf16[256,1536]{1,0:T(8,128)(2,1)}, bf16[256,1536]{1,0:T(8,128)(2,1)}, bf16[256,1536]{1,0:T(8,128)(2,1)}, bf16[256,1536]{1,0:T(8,128)(2,1)}) custom-call(s32[4]{0:T(128)} %get-tuple-element.279.order_ref, bf16[1024,2048]{1,0:T(8,128)(2,1)} %get-tuple-element.244.refs_0_.a_ref, bf16[1024,512]{1,0:T(8,128)(2,1)} %get-tuple-element.239.refs_0_, ...), custom_call_target="tpu_custom_call" | custom-call | flops 50331648 | bytes 163840 | tf_op jit(solution)/shard_map/mixing_grad_other/pallas_call | solution.py:229
  524.1 5.5 projection_grad_mine.1
  529.6 6.6 %mix_back_base.1 = f32[1024,512]{1,0:T(8,128)} custom-call(s32[2,1]{1,0:T(2,128)} %get-tuple-element.318.order_ref, s32[1]{0:T(128)} %bitcast.2.side_ref, bf16[1024,512]{1,0:T(8,128)(2,1)} %get-tuple-element.239.refs_0_, bf16[1024,512]{1,0:T(8,128)(2,1)} %get-tuple-element.233.refs_1_, bf16[1024,512]{1,0:T(8,128)(2,1)} %get-tuple-element.234.refs_2_, ...), custom_call_target="tpu_custom_call" | custom-call | flops 25165824 | bytes 245760 | tf_op jit(solution)/shard_map/mix_back_base/pallas_call | solution.py:229
  536.1 3.6 convert_add_fusion.4
  541.0 3.1 convert_add_fusion.2
  546.5 2.7 fusion.5
  549.4 9.0 %mixing_grad_mine.1 = (bf16[256,1536]{1,0:T(8,128)(2,1)}, bf16[256,1536]{1,0:T(8,128)(2,1)}, bf16[256,1536]{1,0:T(8,128)(2,1)}, bf16[256,1536]{1,0:T(8,128)(2,1)}) custom-call(s32[4]{0:T(128)} %get-tuple-element.282.order_ref, bf16[1024,2048]{1,0:T(8,128)(2,1)} %get-tuple-element.244.refs_0_.a_ref, bf16[1024,512]{1,0:T(8,128)(2,1)} %get-tuple-element.239.refs_0_, ...), custom_call_target="tpu_custom_call" | custom-call | flops 50331648 | bytes 163840 | tf_op jit(solution)/shard_map/mixing_grad_mine/pallas_call | solution.py:229
  563.5 3.4 convert_add_fusion.3
  569.3 7.4 %contract_part.1 = bf16[1024,512]{1,0:T(8,128)(2,1)} custom-call(s32[2,1]{1,0:T(2,128)} %get-tuple-element.315.order_ref, s32[1]{0:T(128)} %bitcast.2.side_ref, bf16[1024,2048]{1,0:T(8,128)(2,1)} %get-tuple-element.258.refs_0_, bf16[2048,2048]{1,0:T(8,128)(2,1)} %all-gather.2.cloned.1.call-done.refs_1_.refs_2_, ...), custom_call_target="tpu_custom_call" | custom-call | flops 33554432 | bytes 376832 | tf_op jit(solution)/shard_map/contract_part/pallas_call | solution.py:229
  576.7 11.2 %collective-permute-done.61 = f32[12,512]{1,0:T(8,128)S(1)} collective-permute-done((f32[12,512]{1,0:T(8,128)S(1)}, f32[12,512]{1,0:T(8,128)S(1)}, u32[]{:S(2)}, u32[]{:S(2)}) %collective-permute-start.61) | collective-permute-done | bytes 24608 | tf_op jit(solution)/shard_map/ppermute | solution.py:431
  596.5 7.7 %contract_base.1 = f32[1024,512]{1,0:T(8,128)} custom-call(s32[2,1]{1,0:T(2,128)} %get-tuple-element.316.order_ref, s32[1]{0:T(128)} %bitcast.2.side_ref, bf16[1024,2048]{1,0:T(8,128)(2,1)} %get-tuple-element.258.refs_0_, bf16[2048,2048]{1,0:T(8,128)(2,1)} %all-gather.2.cloned.1.call-done.refs_1_.refs_2_, ...), custom_call_target="tpu_custom_call" | custom-call | flops 33554432 | bytes 393216 | tf_op jit(solution)/shard_map/contract_base/pallas_call | solution.py:229
  604.2 6.8 %collective-permute-done.65 = f32[12,512]{1,0:T(8,128)S(1)} collective-permute-done((f32[12,512]{1,0:T(8,128)S(1)}, f32[12,512]{1,0:T(8,128)S(1)}, u32[]{:S(2)}, u32[]{:S(2)}) %collective-permute-start.65) | collective-permute-done | bytes 24608 | tf_op jit(solution)/shard_map/ppermute | solution.py:431
  616.7 3.2 collective-permute-start.70
  619.9 11.2 %collective-permute-done.68 = f32[12,512]{1,0:T(8,128)S(1)} collective-permute-done((f32[12,512]{1,0:T(8,128)S(1)}, f32[12,512]{1,0:T(8,128)S(1)}, u32[]{:S(2)}, u32[]{:S(2)}) %collective-permute-start.68) | collective-permute-done | bytes 24608 | tf_op jit(solution)/shard_map/ppermute | solution.py:431
  633.0 2.9 add_convert_fusion.1
  (311 shorter events, 125.6 us)
Async XLA Ops:
  7.2 318.5 %all-gather.2.cloned.1.call-start = ((), (), s32[]{:S(2)}) async-start(), calls=%async_computation.1 | async-start | bytes 10485760 | tf_op jit(solution)/shard_map/all_gather | solution.py:473
  11.2 6.2 collective-permute-start
  11.7 26.3 %collective-permute-start.1 = (bf16[1024,512]{1,0:T(8,128)(2,1)S(1)}, bf16[1024,512]{1,0:T(8,128)(2,1)S(1)}, u32[]{:S(2)}, u32[]{:S(2)}) collective-permute-start(bf16[1024,512]{1,0:T(8,128)(2,1)S(1)} %copy-done.1), channel_id=1, source_target_pairs={{0,2},{1,3},{2,0},{3,1},{4,6},{5,7},{6,4},{7,5},{8,10},{9,11},{10,... | collective-permute-start | bytes 3145736 | tf_op jit(solution)/shard_map/ppermute | solution.py:431
  14.3 25.2 %collective-permute-start.2 = (bf16[256,2048]{1,0:T(8,128)(2,1)S(1)}, bf16[256,2048]{1,0:T(8,128)(2,1)S(1)}, u32[]{:S(2)}, u32[]{:S(2)}) collective-permute-start(bf16[256,2048]{1,0:T(8,128)(2,1)S(1)} %pad_maximum_fusion.1.refs_1_), channel_id=1, source_target_pairs={{0,4},{4,0},{8,12},{12,8},{16,20},{20,16},{24,28},{28,24},{1,5},{5... | collective-permute-start | bytes 3145736 | tf_op jit(solution)/shard_map/ppermute | solution.py:431
  15.8 26.8 %collective-permute-start.3 = (bf16[256,2048]{1,0:T(8,128)(2,1)S(1)}, bf16[256,2048]{1,0:T(8,128)(2,1)S(1)}, u32[]{:S(2)}, u32[]{:S(2)}) collective-permute-start(bf16[256,2048]{1,0:T(8,128)(2,1)S(1)} %pad_maximum_fusion.1.refs_1_), channel_id=1, source_target_pairs={{0,8},{4,12},{8,16},{12,20},{16,24},{20,28},{24,0},{28,4},{1,9},{5... | collective-permute-start | bytes 3145736 | tf_op jit(solution)/shard_map/ppermute | solution.py:436
  42.6 25.7 %collective-permute-start.8 = (bf16[1024,512]{1,0:T(8,128)(2,1)S(1)}, bf16[1024,512]{1,0:T(8,128)(2,1)}, u32[]{:S(2)}, u32[]{:S(2)}) collective-permute-start(bf16[1024,512]{1,0:T(8,128)(2,1)S(1)} %copy-done.7), channel_id=1, source_target_pairs={{0,2},{1,3},{2,0},{3,1},{4,6},{5,7},{6,4},{7,5},{8,10},{9,11},{10,... | collective-permute-start | bytes 3145736 | tf_op jit(solution)/shard_map/ppermute | solution.py:431
  43.2 25.2 %collective-permute-start.5 = (bf16[256,2048]{1,0:T(8,128)(2,1)S(1)}, bf16[256,2048]{1,0:T(8,128)(2,1)S(1)}, u32[]{:S(2)}, u32[]{:S(2)}) collective-permute-start(bf16[256,2048]{1,0:T(8,128)(2,1)S(1)} %collective-permute-done.3.refs_2_), channel_id=1, source_target_pairs={{0,4},{4,0},{8,12},{12,8},{16,20},{20,16},{24,28},{28,24},{1,5},{5... | collective-permute-start | bytes 3145736 | tf_op jit(solution)/shard_map/ppermute | solution.py:431
  43.7 26.8 %collective-permute-start.6 = (bf16[256,2048]{1,0:T(8,128)(2,1)S(1)}, bf16[256,2048]{1,0:T(8,128)(2,1)}, u32[]{:S(2)}, u32[]{:S(2)}) collective-permute-start(bf16[256,2048]{1,0:T(8,128)(2,1)S(1)} %collective-permute-done.3.refs_2_), channel_id=1, source_target_pairs={{0,8},{4,12},{8,16},{12,20},{16,24},{20,28},{24,0},{28,4},{1,9},{5... | collective-permute-start | bytes 3145736 | tf_op jit(solution)/shard_map/ppermute | solution.py:436
  43.7 26.9 %collective-permute-start.4 = (bf16[1024,512]{1,0:T(8,128)(2,1)S(1)}, bf16[1024,512]{1,0:T(8,128)(2,1)S(1)}, u32[]{:S(2)}, u32[]{:S(2)}) collective-permute-start(bf16[1024,512]{1,0:T(8,128)(2,1)S(1)} %collective-permute-done.1.refs_2_), channel_id=1, source_target_pairs={{0,1},{1,0},{2,3},{3,2},{4,5},{5,4},{6,7},{7,6},{8,9},{9,8},{10,11... | collective-permute-start | bytes 3145736 | tf_op jit(solution)/shard_map/ppermute | solution.py:431
  70.6 24.4 %collective-permute-start.11 = (bf16[256,2048]{1,0:T(8,128)(2,1)}, bf16[256,2048]{1,0:T(8,128)(2,1)S(1)}, u32[]{:S(2)}, u32[]{:S(2)}) collective-permute-start(bf16[256,2048]{1,0:T(8,128)(2,1)} %collective-permute-done.6.refs_3_), channel_id=1, source_target_pairs={{0,4},{4,0},{8,12},{12,8},{16,20},{20,16},{24,28},{28,24},{1,5},{5... | collective-permute-start | bytes 3145736 | tf_op jit(solution)/shard_map/ppermute | solution.py:431
  72.2 25.9 %collective-permute-start.12 = (bf16[256,2048]{1,0:T(8,128)(2,1)}, bf16[256,2048]{1,0:T(8,128)(2,1)}, u32[]{:S(2)}, u32[]{:S(2)}) collective-permute-start(bf16[256,2048]{1,0:T(8,128)(2,1)} %collective-permute-done.6.refs_3_), channel_id=1, source_target_pairs={{0,8},{4,12},{8,16},{12,20},{16,24},{20,28},{24,0},{28,4},{1,9},{5... | collective-permute-start | bytes 3145736 | tf_op jit(solution)/shard_map/ppermute | solution.py:436
  72.2 25.9 %collective-permute-start.13 = (bf16[1024,512]{1,0:T(8,128)(2,1)}, bf16[1024,512]{1,0:T(8,128)(2,1)}, u32[]{:S(2)}, u32[]{:S(2)}) collective-permute-start(bf16[1024,512]{1,0:T(8,128)(2,1)} %collective-permute-done.8.refs_2_), channel_id=1, source_target_pairs={{0,1},{1,0},{2,3},{3,2},{4,5},{5,4},{6,7},{7,6},{8,9},{9,8},{10,11... | collective-permute-start | bytes 3145736 | tf_op jit(solution)/shard_map/ppermute | solution.py:431
  98.1 25.0 %collective-permute-start.16 = (bf16[256,2048]{1,0:T(8,128)(2,1)}, bf16[256,2048]{1,0:T(8,128)(2,1)}, u32[]{:S(2)}, u32[]{:S(2)}) collective-permute-start(bf16[256,2048]{1,0:T(8,128)(2,1)} %refs_1_.1), channel_id=1, source_target_pairs={{0,8},{4,12},{8,16},{12,20},{16,24},{20,28},{24,0},{28,4},{1,9},{5... | collective-permute-start | bytes 3145736 | tf_op jit(solution)/shard_map/ppermute | solution.py:436
  98.1 25.0 %collective-permute-start.15 = (bf16[256,2048]{1,0:T(8,128)(2,1)}, bf16[256,2048]{1,0:T(8,128)(2,1)}, u32[]{:S(2)}, u32[]{:S(2)}) collective-permute-start(bf16[256,2048]{1,0:T(8,128)(2,1)} %collective-permute-done.12.refs_4_), channel_id=1, source_target_pairs={{0,4},{4,0},{8,12},{12,8},{16,20},{20,16},{24,28},{28,24},{1,5},{5... | collective-permute-start | bytes 3145736 | tf_op jit(solution)/shard_map/ppermute | solution.py:431
  99.5 6.2 collective-permute-start.14
  123.1 24.1 %collective-permute-start.19 = (bf16[256,2048]{1,0:T(8,128)(2,1)}, bf16[256,2048]{1,0:T(8,128)(2,1)}, u32[]{:S(2)}, u32[]{:S(2)}) collective-permute-start(bf16[256,2048]{1,0:T(8,128)(2,1)} %collective-permute-done.16.refs_2_), channel_id=1, source_target_pairs={{0,8},{4,12},{8,16},{12,20},{16,24},{20,28},{24,0},{28,4},{1,9},{5... | collective-permute-start | bytes 3145736 | tf_op jit(solution)/shard_map/ppermute | solution.py:436
  123.1 43.0 %collective-permute-start.18 = (bf16[256,2048]{1,0:T(8,128)(2,1)S(1)}, bf16[256,2048]{1,0:T(8,128)(2,1)}, u32[]{:S(2)}, u32[]{:S(2)}) collective-permute-start(bf16[256,2048]{1,0:T(8,128)(2,1)S(1)} %copy-done.37), channel_id=1, source_target_pairs={{0,4},{4,0},{8,12},{12,8},{16,20},{20,16},{24,28},{28,24},{1,5},{5... | collective-permute-start | bytes 3145736 | tf_op jit(solution)/shard_map/ppermute | solution.py:431
  125.3 42.4 %collective-permute-start.17 = (bf16[256,2048]{1,0:T(8,128)(2,1)}, bf16[256,2048]{1,0:T(8,128)(2,1)}, u32[]{:S(2)}, u32[]{:S(2)}) collective-permute-start(bf16[256,2048]{1,0:T(8,128)(2,1)} %refs_1_.1), channel_id=1, source_target_pairs={{0,4},{4,0},{8,12},{12,8},{16,20},{20,16},{24,28},{28,24},{1,5},{5... | collective-permute-start | bytes 3145736 | tf_op jit(solution)/shard_map/ppermute | solution.py:431
  147.2 23.1 %collective-permute-start.20 = (bf16[256,2048]{1,0:T(8,128)(2,1)}, bf16[256,2048]{1,0:T(8,128)(2,1)}, u32[]{:S(2)}, u32[]{:S(2)}) collective-permute-start(bf16[256,2048]{1,0:T(8,128)(2,1)} %collective-permute-done.19.refs_3_), channel_id=1, source_target_pairs={{0,8},{4,12},{8,16},{12,20},{16,24},{20,28},{24,0},{28,4},{1,9},{5... | collective-permute-start | bytes 3145736 | tf_op jit(solution)/shard_map/ppermute | solution.py:436
  170.3 440.7 %reduce-scatter.2.cloned.1.call-start = ((), (), s32[]{:S(2)}) async-start(), calls=%async_computation.2 | async-start | bytes 1310720 | tf_op jit(solution)/shard_map/reduce_scatter | solution.py:898
  170.6 21.2 %collective-permute-start.21 = (bf16[256,2048]{1,0:T(8,128)(2,1)}, bf16[256,2048]{1,0:T(8,128)(2,1)S(1)}, u32[]{:S(2)}, u32[]{:S(2)}) collective-permute-start(bf16[256,2048]{1,0:T(8,128)(2,1)} %collective-permute-done.16.refs_2_), channel_id=1, source_target_pairs={{0,4},{4,0},{8,12},{12,8},{16,20},{20,16},{24,28},{28,24},{1,5},{5... | collective-permute-start | bytes 3145736 | tf_op jit(solution)/shard_map/ppermute | solution.py:431
  178.0 4.4 collective-permute-start.22
  178.0 4.4 collective-permute-start.23
  178.6 3.9 collective-permute-start.24
  191.8 21.5 %collective-permute-start.25 = (bf16[1024,512]{1,0:T(8,128)(2,1)}, bf16[1024,512]{1,0:T(8,128)(2,1)S(1)}, u32[]{:S(2)}, u32[]{:S(2)}) collective-permute-start(bf16[1024,512]{1,0:T(8,128)(2,1)} %project_part.1), channel_id=1, source_target_pairs={{0,2},{1,3},{2,0},{3,1},{4,6},{5,7},{6,4},{7,5},{8,10},{9,11},{10,... | collective-permute-start | bytes 3145736 | tf_op jit(solution)/shard_map/ppermute | solution.py:431
  194.3 22.4 %collective-permute-start.26 = (bf16[256,2048]{1,0:T(8,128)(2,1)}, bf16[256,2048]{1,0:T(8,128)(2,1)}, u32[]{:S(2)}, u32[]{:S(2)}) collective-permute-start(bf16[256,2048]{1,0:T(8,128)(2,1)} %collective-permute-done.19.refs_3_), channel_id=1, source_target_pairs={{0,4},{4,0},{8,12},{12,8},{16,20},{20,16},{24,28},{28,24},{1,5},{5... | collective-permute-start | bytes 3145736 | tf_op jit(solution)/shard_map/ppermute | solution.py:431
  216.6 20.3 %collective-permute-start.29 = (bf16[256,2048]{1,0:T(8,128)(2,1)}, bf16[256,2048]{1,0:T(8,128)(2,1)S(1)}, u32[]{:S(2)}, u32[]{:S(2)}) collective-permute-start(bf16[256,2048]{1,0:T(8,128)(2,1)} %collective-permute-done.20.refs_4_), channel_id=1, source_target_pairs={{0,4},{4,0},{8,12},{12,8},{16,20},{20,16},{24,28},{28,24},{1,5},{5... | collective-permute-start | bytes 3145736 | tf_op jit(solution)/shard_map/ppermute | solution.py:431
  216.9 20.0 %collective-permute-start.27 = (bf16[1024,512]{1,0:T(8,128)(2,1)S(1)}, bf16[1024,512]{1,0:T(8,128)(2,1)S(1)}, u32[]{:S(2)}, u32[]{:S(2)}) collective-permute-start(bf16[1024,512]{1,0:T(8,128)(2,1)S(1)} %get-tuple-element.173.refs_0_), channel_id=1, source_target_pairs={{0,1},{1,0},{2,3},{3,2},{4,5},{5,4},{6,7},{7,6},{8,9},{9,8},{10,11... | collective-permute-start | bytes 3145736 | tf_op jit(solution)/shard_map/ppermute | solution.py:431
  217.0 25.7 %collective-permute-start.28 = (bf16[1024,512]{1,0:T(8,128)(2,1)S(1)}, bf16[1024,512]{1,0:T(8,128)(2,1)S(1)}, u32[]{:S(2)}, u32[]{:S(2)}) collective-permute-start(bf16[1024,512]{1,0:T(8,128)(2,1)S(1)} %get-tuple-element.173.refs_0_), channel_id=1, source_target_pairs={{0,2},{1,3},{2,0},{3,1},{4,6},{5,7},{6,4},{7,5},{8,10},{9,11},{10,... | collective-permute-start | bytes 3145736 | tf_op jit(solution)/shard_map/ppermute | solution.py:431
  282.4 25.5 %collective-permute-start.31 = (bf16[256,2048]{1,0:T(8,128)(2,1)}, bf16[256,2048]{1,0:T(8,128)(2,1)}, u32[]{:S(2)}, u32[]{:S(2)}) collective-permute-start(bf16[256,2048]{1,0:T(8,128)(2,1)} %get-tuple-element.185), channel_id=1, source_target_pairs={{0,4},{4,0},{8,12},{12,8},{16,20},{20,16},{24,28},{28,24},{1,5},{5... | collective-permute-start | bytes 3145736 | tf_op jit(solution)/shard_map/ppermute | solution.py:431
  307.9 56.2 %collective-permute-start.33 = (bf16[512,2048]{1,0:T(8,128)(2,1)}, bf16[512,2048]{1,0:T(8,128)(2,1)}, u32[]{:S(2)}, u32[]{:S(2)}) collective-permute-start(bf16[512,2048]{1,0:T(8,128)(2,1)} %get-tuple-element.194), channel_id=1, source_target_pairs={{0,4},{4,0},{8,12},{12,8},{16,20},{20,16},{24,28},{28,24},{1,5},{5... | collective-permute-start | bytes 6291464 | tf_op jit(solution)/shard_map/ppermute | solution.py:431
  312.5 51.6 %collective-permute-start.32 = (bf16[256,2048]{1,0:T(8,128)(2,1)}, bf16[256,2048]{1,0:T(8,128)(2,1)}, u32[]{:S(2)}, u32[]{:S(2)}) collective-permute-start(bf16[256,2048]{1,0:T(8,128)(2,1)} %add_convert_fusion.7), channel_id=1, source_target_pairs={{0,24},{4,28},{8,0},{12,4},{16,8},{20,12},{24,16},{28,20},{1,25},{... | collective-permute-start | bytes 3145736 | tf_op jit(solution)/shard_map/ppermute | solution.py:436
  349.2 4.4 collective-permute-start.34
  349.3 4.3 collective-permute-start.35
  362.6 25.4 %collective-permute-start.39 = (bf16[1024,512]{1,0:T(8,128)(2,1)}, bf16[1024,512]{1,0:T(8,128)(2,1)S(1)}, u32[]{:S(2)}, u32[]{:S(2)}) collective-permute-start(bf16[1024,512]{1,0:T(8,128)(2,1)} %expand_back_part.1), channel_id=1, source_target_pairs={{0,2},{1,3},{2,0},{3,1},{4,6},{5,7},{6,4},{7,5},{8,10},{9,11},{10,... | collective-permute-start | bytes 3145736 | tf_op jit(solution)/shard_map/ppermute | solution.py:431
  364.1 25.2 %collective-permute-start.38 = (bf16[256,2048]{1,0:T(8,128)(2,1)}, bf16[256,2048]{1,0:T(8,128)(2,1)S(1)}, u32[]{:S(2)}, u32[]{:S(2)}) collective-permute-start(bf16[256,2048]{1,0:T(8,128)(2,1)} %get-tuple-element.210), channel_id=1, source_target_pairs={{0,4},{4,0},{8,12},{12,8},{16,20},{20,16},{24,28},{28,24},{1,5},{5... | collective-permute-start | bytes 3145736 | tf_op jit(solution)/shard_map/ppermute | solution.py:431
  368.8 25.0 %collective-permute-start.37 = (bf16[256,2048]{1,0:T(8,128)(2,1)}, bf16[256,2048]{1,0:T(8,128)(2,1)}, u32[]{:S(2)}, u32[]{:S(2)}) collective-permute-start(bf16[256,2048]{1,0:T(8,128)(2,1)} %add_convert_fusion.6), channel_id=1, source_target_pairs={{0,24},{4,28},{8,0},{12,4},{16,8},{20,12},{24,16},{28,20},{1,25},{... | collective-permute-start | bytes 3145736 | tf_op jit(solution)/shard_map/ppermute | solution.py:436
  396.8 32.1 %collective-permute-start.40 = (bf16[256,2048]{1,0:T(8,128)(2,1)}, bf16[256,2048]{1,0:T(8,128)(2,1)}, u32[]{:S(2)}, u32[]{:S(2)}) collective-permute-start(bf16[256,2048]{1,0:T(8,128)(2,1)} %get-tuple-element.212), channel_id=1, source_target_pairs={{0,4},{4,0},{8,12},{12,8},{16,20},{20,16},{24,28},{28,24},{1,5},{5... | collective-permute-start | bytes 3145736 | tf_op jit(solution)/shard_map/ppermute | solution.py:431
  405.3 24.6 %collective-permute-start.43 = (bf16[256,2048]{1,0:T(8,128)(2,1)}, bf16[256,2048]{1,0:T(8,128)(2,1)}, u32[]{:S(2)}, u32[]{:S(2)}) collective-permute-start(bf16[256,2048]{1,0:T(8,128)(2,1)} %add_convert_fusion.5), channel_id=1, source_target_pairs={{0,24},{4,28},{8,0},{12,4},{16,8},{20,12},{24,16},{28,20},{1,25},{... | collective-permute-start | bytes 3145736 | tf_op jit(solution)/shard_map/ppermute | solution.py:436
  407.6 22.3 %collective-permute-start.44 = (bf16[1024,512]{1,0:T(8,128)(2,1)}, bf16[1024,512]{1,0:T(8,128)(2,1)}, u32[]{:S(2)}, u32[]{:S(2)}) collective-permute-start(bf16[1024,512]{1,0:T(8,128)(2,1)} %get-tuple-element.289.refs_0_), channel_id=1, source_target_pairs={{0,1},{1,0},{2,3},{3,2},{4,5},{5,4},{6,7},{7,6},{8,9},{9,8},{10,11... | collective-permute-start | bytes 3145736 | tf_op jit(solution)/shard_map/ppermute | solution.py:431
  407.6 25.9 %collective-permute-start.45 = (bf16[1024,512]{1,0:T(8,128)(2,1)}, bf16[1024,512]{1,0:T(8,128)(2,1)}, u32[]{:S(2)}, u32[]{:S(2)}) collective-permute-start(bf16[1024,512]{1,0:T(8,128)(2,1)} %get-tuple-element.289.refs_0_), channel_id=1, source_target_pairs={{0,2},{1,3},{2,0},{3,1},{4,6},{5,7},{6,4},{7,5},{8,10},{9,11},{10,... | collective-permute-start | bytes 3145736 | tf_op jit(solution)/shard_map/ppermute | solution.py:431
  433.5 47.5 %collective-permute-start.46 = (bf16[512,2048]{1,0:T(8,128)(2,1)}, bf16[512,2048]{1,0:T(8,128)(2,1)S(1)}, u32[]{:S(2)}, u32[]{:S(2)}) collective-permute-start(bf16[512,2048]{1,0:T(8,128)(2,1)} %get-tuple-element.224), channel_id=1, source_target_pairs={{0,4},{4,0},{8,12},{12,8},{16,20},{20,16},{24,28},{28,24},{1,5},{5... | collective-permute-start | bytes 6291464 | tf_op jit(solution)/shard_map/ppermute | solution.py:431
  435.6 38.9 %collective-permute-start.47 = (bf16[256,2048]{1,0:T(8,128)(2,1)S(1)}, bf16[256,2048]{1,0:T(8,128)(2,1)}, u32[]{:S(2)}, u32[]{:S(2)}) collective-permute-start(bf16[256,2048]{1,0:T(8,128)(2,1)S(1)} %add_convert_fusion.4), channel_id=1, source_target_pairs={{0,24},{4,28},{8,0},{12,4},{16,8},{20,12},{24,16},{28,20},{1,25},{... | collective-permute-start | bytes 3145736 | tf_op jit(solution)/shard_map/ppermute | solution.py:436
  483.8 24.4 %collective-permute-start.51 = (bf16[256,2048]{1,0:T(8,128)(2,1)}, bf16[256,2048]{1,0:T(8,128)(2,1)}, u32[]{:S(2)}, u32[]{:S(2)}) collective-permute-start(bf16[256,2048]{1,0:T(8,128)(2,1)} %add_convert_fusion.3), channel_id=1, source_target_pairs={{0,24},{4,28},{8,0},{12,4},{16,8},{20,12},{24,16},{28,20},{1,25},{... | collective-permute-start | bytes 3145736 | tf_op jit(solution)/shard_map/ppermute | solution.py:436
  491.7 4.8 collective-permute-start.53
  491.7 4.8 collective-permute-start.54
  492.2 47.5 %collective-permute-start.50 = (bf16[1024,512]{1,0:T(8,128)(2,1)}, bf16[1024,512]{1,0:T(8,128)(2,1)}, u32[]{:S(2)}, u32[]{:S(2)}) collective-permute-start(bf16[1024,512]{1,0:T(8,128)(2,1)} %projection_grad_other.1), channel_id=1, source_target_pairs={{0,4},{4,0},{8,12},{12,8},{16,20},{20,16},{24,28},{28,24},{1,5},{5... | collective-permute-start | bytes 3145736 | tf_op jit(solution)/shard_map/ppermute | solution.py:431
  496.0 44.5 %collective-permute-start.49 = (bf16[256,2048]{1,0:T(8,128)(2,1)}, bf16[256,2048]{1,0:T(8,128)(2,1)}, u32[]{:S(2)}, u32[]{:S(2)}) collective-permute-start(bf16[256,2048]{1,0:T(8,128)(2,1)} %get-tuple-element.229), channel_id=1, source_target_pairs={{0,4},{4,0},{8,12},{12,8},{16,20},{20,16},{24,28},{28,24},{1,5},{5... | collective-permute-start | bytes 3145736 | tf_op jit(solution)/shard_map/ppermute | solution.py:431
  504.3 31.8 %collective-permute-start.56 = (bf16[1024,512]{1,0:T(8,128)(2,1)}, bf16[1024,512]{1,0:T(8,128)(2,1)}, u32[]{:S(2)}, u32[]{:S(2)}) collective-permute-start(bf16[1024,512]{1,0:T(8,128)(2,1)} %mix_back_part.1), channel_id=1, source_target_pairs={{0,2},{1,3},{2,0},{3,1},{4,6},{5,7},{6,4},{7,5},{8,10},{9,11},{10,... | collective-permute-start | bytes 3145736 | tf_op jit(solution)/shard_map/ppermute | solution.py:431
  511.2 29.3 %collective-permute-start.52 = (bf16[256,2048]{1,0:T(8,128)(2,1)}, bf16[256,2048]{1,0:T(8,128)(2,1)}, u32[]{:S(2)}, u32[]{:S(2)}) collective-permute-start(bf16[256,2048]{1,0:T(8,128)(2,1)} %add_convert_fusion.2), channel_id=1, source_target_pairs={{0,24},{4,28},{8,0},{12,4},{16,8},{20,12},{24,16},{28,20},{1,25},{... | collective-permute-start | bytes 3145736 | tf_op jit(solution)/shard_map/ppermute | solution.py:436
  515.2 54.1 %collective-permute-start.60 = (bf16[1024,1024]{1,0:T(8,128)(2,1)}, bf16[1024,1024]{1,0:T(8,128)(2,1)}, u32[]{:S(2)}, u32[]{:S(2)}) collective-permute-start(bf16[1024,1024]{1,0:T(8,128)(2,1)} %contract_sent.1), channel_id=1, source_target_pairs={{0,1},{1,0},{2,3},{3,2},{4,5},{5,4},{6,7},{7,6},{8,9},{9,8},{10,11... | collective-permute-start | bytes 6291464 | tf_op jit(solution)/shard_map/ppermute | solution.py:431
  540.5 19.6 %collective-permute-start.57 = (bf16[256,1536]{1,0:T(8,128)(2,1)}, bf16[256,1536]{1,0:T(8,128)(2,1)}, u32[]{:S(2)}, u32[]{:S(2)}) collective-permute-start(bf16[256,1536]{1,0:T(8,128)(2,1)} %get-tuple-element.246), channel_id=1, source_target_pairs={{0,4},{4,0},{8,12},{12,8},{16,20},{20,16},{24,28},{28,24},{1,5},{5... | collective-permute-start | bytes 2359304 | tf_op jit(solution)/shard_map/ppermute | solution.py:431
  549.3 19.4 %collective-permute-start.63 = (f32[2,1024]{1,0:T(2,128)S(1)}, f32[2,1024]{1,0:T(2,128)S(1)}, u32[]{:S(2)}, u32[]{:S(2)}) collective-permute-start(f32[2,1024]{1,0:T(2,128)S(1)} %pad_maximum_fusion.5), channel_id=1, source_target_pairs={{0,1},{1,0},{2,3},{3,2},{4,5},{5,4},{6,7},{7,6},{8,9},{9,8},{10,11... | collective-permute-start | bytes 24584 | tf_op jit(solution)/shard_map/ppermute | solution.py:431
  560.1 27.8 %collective-permute-start.59 = (bf16[256,1536]{1,0:T(8,128)(2,1)}, bf16[256,1536]{1,0:T(8,128)(2,1)S(1)}, u32[]{:S(2)}, u32[]{:S(2)}) collective-permute-start(bf16[256,1536]{1,0:T(8,128)(2,1)} %get-tuple-element.255), channel_id=1, source_target_pairs={{0,4},{4,0},{8,12},{12,8},{16,20},{20,16},{24,28},{28,24},{1,5},{5... | collective-permute-start | bytes 2359304 | tf_op jit(solution)/shard_map/ppermute | solution.py:431
  563.0 24.9 %collective-permute-start.58 = (bf16[256,1536]{1,0:T(8,128)(2,1)}, bf16[256,1536]{1,0:T(8,128)(2,1)S(1)}, u32[]{:S(2)}, u32[]{:S(2)}) collective-permute-start(bf16[256,1536]{1,0:T(8,128)(2,1)} %add_convert_fusion.10), channel_id=1, source_target_pairs={{0,24},{4,28},{8,0},{12,4},{16,8},{20,12},{24,16},{28,20},{1,25},{... | collective-permute-start | bytes 2359304 | tf_op jit(solution)/shard_map/ppermute | solution.py:436
  566.9 21.0 %collective-permute-start.61 = (f32[12,512]{1,0:T(8,128)S(1)}, f32[12,512]{1,0:T(8,128)S(1)}, u32[]{:S(2)}, u32[]{:S(2)}) collective-permute-start(f32[12,512]{1,0:T(8,128)S(1)} %concatenate.27), channel_id=1, source_target_pairs={{0,8},{4,12},{8,0},{12,4},{16,24},{20,28},{24,16},{28,20},{1,9},{5... | collective-permute-start | bytes 73736 | tf_op jit(solution)/shard_map/ppermute | solution.py:431
  568.7 23.9 %collective-permute-start.64 = (f32[2,1024]{1,0:T(2,128)S(1)}, f32[2,1024]{1,0:T(2,128)S(1)}, u32[]{:S(2)}, u32[]{:S(2)}) collective-permute-start(f32[2,1024]{1,0:T(2,128)S(1)} %fusion.18), channel_id=1, source_target_pairs={{0,2},{1,3},{2,0},{3,1},{4,6},{5,7},{6,4},{7,5},{8,10},{9,11},{10,... | collective-permute-start | bytes 24584 | tf_op jit(solution)/shard_map/ppermute | solution.py:431
  587.9 25.1 %collective-permute-start.67 = (bf16[256,1536]{1,0:T(8,128)(2,1)}, bf16[256,1536]{1,0:T(8,128)(2,1)}, u32[]{:S(2)}, u32[]{:S(2)}) collective-permute-start(bf16[256,1536]{1,0:T(8,128)(2,1)} %get-tuple-element.262), channel_id=1, source_target_pairs={{0,4},{4,0},{8,12},{12,8},{16,20},{20,16},{24,28},{28,24},{1,5},{5... | collective-permute-start | bytes 2359304 | tf_op jit(solution)/shard_map/ppermute | solution.py:431
  590.6 22.4 %collective-permute-start.66 = (bf16[256,1536]{1,0:T(8,128)(2,1)}, bf16[256,1536]{1,0:T(8,128)(2,1)}, u32[]{:S(2)}, u32[]{:S(2)}) collective-permute-start(bf16[256,1536]{1,0:T(8,128)(2,1)} %add_convert_fusion.9), channel_id=1, source_target_pairs={{0,24},{4,28},{8,0},{12,4},{16,8},{20,12},{24,16},{28,20},{1,25},{... | collective-permute-start | bytes 2359304 | tf_op jit(solution)/shard_map/ppermute | solution.py:436
  592.6 18.4 %collective-permute-start.65 = (f32[12,512]{1,0:T(8,128)S(1)}, f32[12,512]{1,0:T(8,128)S(1)}, u32[]{:S(2)}, u32[]{:S(2)}) collective-permute-start(f32[12,512]{1,0:T(8,128)S(1)} %add.341), channel_id=1, source_target_pairs={{0,16},{4,20},{8,24},{12,28},{16,0},{20,4},{24,8},{28,12},{1,17},{... | collective-permute-start | bytes 73736 | tf_op jit(solution)/shard_map/ppermute | solution.py:431
  593.1 39.9 %collective-permute-start.62 = (bf16[1024,512]{1,0:T(8,128)(2,1)}, bf16[1024,512]{1,0:T(8,128)(2,1)}, u32[]{:S(2)}, u32[]{:S(2)}) collective-permute-start(bf16[1024,512]{1,0:T(8,128)(2,1)} %contract_part.1), channel_id=1, source_target_pairs={{0,2},{1,3},{2,0},{3,1},{4,6},{5,7},{6,4},{7,5},{8,10},{9,11},{10,... | collective-permute-start | bytes 3145736 | tf_op jit(solution)/shard_map/ppermute | solution.py:431
  613.0 22.9 %collective-permute-start.69 = (bf16[256,1536]{1,0:T(8,128)(2,1)}, bf16[256,1536]{1,0:T(8,128)(2,1)S(1)}, u32[]{:S(2)}, u32[]{:S(2)}) collective-permute-start(bf16[256,1536]{1,0:T(8,128)(2,1)} %get-tuple-element.265), channel_id=1, source_target_pairs={{0,4},{4,0},{8,12},{12,8},{16,20},{20,16},{24,28},{28,24},{1,5},{5... | collective-permute-start | bytes 2359304 | tf_op jit(solution)/shard_map/ppermute | solution.py:431
  614.0 17.2 %collective-permute-start.68 = (f32[12,512]{1,0:T(8,128)S(1)}, f32[12,512]{1,0:T(8,128)S(1)}, u32[]{:S(2)}, u32[]{:S(2)}) collective-permute-start(f32[12,512]{1,0:T(8,128)S(1)} %add.350), channel_id=1, source_target_pairs={{0,4},{4,0},{8,12},{12,8},{16,20},{20,16},{24,28},{28,24},{1,5},{5... | collective-permute-start | bytes 73736 | tf_op jit(solution)/shard_map/ppermute | solution.py:431
  616.7 19.7 %collective-permute-start.70 = (bf16[256,1536]{1,0:T(8,128)(2,1)S(1)}, bf16[256,1536]{1,0:T(8,128)(2,1)S(1)}, u32[]{:S(2)}, u32[]{:S(2)}) collective-permute-start(bf16[256,1536]{1,0:T(8,128)(2,1)S(1)} %add_convert_fusion.8), channel_id=1, source_target_pairs={{0,24},{4,28},{8,0},{12,4},{16,8},{20,12},{24,16},{28,20},{1,25},{... | collective-permute-start | bytes 2359304 | tf_op jit(solution)/shard_map/ppermute | solution.py:436
  (68 other events, 1061.5 us)
Sparse Core Ops, SparseCore 0:
  170.5 155.1 all-gather.1
  546.7 30.6 reduce-scatter.1

commit v7 on v6

--- a/solution.py
+++ b/solution.py
@@ -17,7 +17,7 @@
 far = -1e33
 NT = (((1,), (1,)), ((), ()))
 TN = (((0,), (0,)), ((), ()))
-VMEM_LIMIT = 56 << 20
+VMEM_LIMIT = 40 << 20
 CHEAP = 64
 f32 = jnp.float32
 bf16 = jnp.bfloat16
@@ -244,8 +244,10 @@
     )(*prefetch, *[a for a, _ in ins])
 
 
-def times_rows(x, ws, extras, outs, finish, name, tn, window=None, joins=()):
+def times_rows(x, ws, extras, outs, finish, name, tn, window=None, joins=(), skip=0):
     tokens, depth = x.shape
+    picks = [w[1] if isinstance(w, tuple) else None for w in ws]
+    ws = [w[0] if isinstance(w, tuple) else w for w in ws]
     first, width = window or (0, ws[0].shape[1])
     first, tiles = first // tn, width // tn
     n_ws, n_ex, n_out = len(ws), len(extras), len(outs)
@@ -269,14 +271,17 @@
         else:
             pl.when(pl.program_id(0) < tiles)(multiply)
 
-    def spec(rows):
-        return pl.BlockSpec((rows, tn), lambda n: (0, jnp.minimum(n, tiles - 1)))
-
-    def tile(rows):
+    def spec(rows, skipped=0):
+        return pl.BlockSpec((rows, tn), lambda n: (0, jnp.minimum(n, tiles - 1) + skipped))
+
+    def tile(rows, pick=None):
+        if pick is not None:
+            return pl.BlockSpec((BLOCK, tn), lambda n: (pick, n + first))
         return pl.BlockSpec((rows, tn), lambda n: (0, n + first))
 
-    ins = [(x, resident(x.shape))] + [(w, tile(w.shape[0])) for w in ws]
-    ins += [(e, spec(e.shape[0])) for e in extras]
+    ins = [(x, resident(x.shape))]
+    ins += [(w, tile(w.shape[0], pick)) for w, pick in zip(ws, picks)]
+    ins += [(e, spec(e.shape[0], skip // tn)) for e in extras]
     results = [(s, t, spec(s[0])) for s, t in outs]
     for places in joins:
         rows = sum(ws[i].shape[0] for i in places)
@@ -284,19 +289,22 @@
     return matmul_call(kernel, (steps,), ins, results, [], 2 * tokens * depth * width, name)
 
 
-def times_columns(xs, ws, order, side, dtype, name, first=0, added=(), block=0, chunks=None):
+def times_columns(xs, ws, order, side, dtype, name, added=(), block=0, chunks=None):
     tokens = xs[0].shape[0]
     count = order.shape[1]
     n_xs = len(xs)
     width = sum(x.shape[1] for x in xs)
     chunks = chunks or [tokens]
+    n_ws = len(ws[0])
 
     def kernel(order_ref, side_ref, *refs):
-        x_refs, w_refs = refs[:n_xs], refs[n_xs : n_xs + 2]
-        added_refs, out_refs = refs[n_xs + 2 : n_xs + 2 + len(added)], refs[-len(chunks) :]
+        x_refs, w_refs = refs[:n_xs], refs[n_xs : n_xs + 2 * n_ws]
+        after_ws = n_xs + 2 * n_ws
+        added_refs, out_refs = refs[after_ws : after_ws + len(added)], refs[-len(chunks) :]
         x = jnp.concatenate([r[...] for r in x_refs], axis=1)
-        for i, w_ref in enumerate(w_refs):
-            acc = lax.dot_general(x, w_ref[...], NT, preferred_element_type=f32)
+        for i in range(2):
+            w = jnp.concatenate([r[...] for r in w_refs[i * n_ws : (i + 1) * n_ws]], axis=1)
+            acc = lax.dot_general(x, w, NT, preferred_element_type=f32)
             place = side_ref[0] if i == 0 else 1 - side_ref[0]
             place = pl.ds(pl.multiple_of(place * BLOCK, BLOCK), BLOCK)
             if added:
@@ -306,14 +314,16 @@
                 out_ref[:, place] = acc[at : at + height].astype(dtype)
                 at += height
 
-    def w_spec(i):
-        return pl.BlockSpec((BLOCK, width), lambda n, order_ref, _: (order_ref[i, n], first // width))
+    def w_spec(i, over, start, columns):
+        return pl.BlockSpec(
+            (BLOCK, columns), lambda n, order_ref, _: (order_ref[i, n] // over, start // columns)
+        )
 
     def pair(height, start):
         return pl.BlockSpec((height, 2 * BLOCK), lambda n, *_: (0, start + n))
 
     ins = [(x, resident(x.shape)) for x in xs]
-    ins += [(w, w_spec(i)) for i, w in enumerate(ws)]
+    ins += [(w, w_spec(i, *rest)) for i, part in enumerate(ws) for w, *rest in part]
     ins += [(b, pair(b.shape[0], block)) for b in added]
     done = matmul_call(
         kernel,
@@ -527,10 +537,14 @@
     def columns_order(ids, ws):
         want = jnp.stack([2 * away + side, 2 * away + 1 - side]).reshape(-1)
         order = find(ids, want).reshape(2, -1)
-        return order if len(ws) == 1 else order % (blocks // 2)
-
-    def two(ws):
-        return ws if len(ws) == 2 else [ws[0], ws[0]]
+        return order if len(ws) != 2 else order % (blocks // 2)
+
+    def two(xs, ws, first):
+        columns = sum(x.shape[1] for x in xs)
+        if len(ws) <= 2:
+            return [[(w, 1, first, columns)] for w in (ws if len(ws) == 2 else [ws[0], ws[0]])]
+        half = columns // 2
+        return [[(w, 2, 0, half), (ws[2], 1, 0, half)] for w in ws[:2]]
 
     def columns_sent(xs, ws, ids, name, first=0, whole=False):
         order = columns_order(ids, ws)[:, :2]
@@ -539,7 +553,7 @@
         if whole:
             chunks = [tokens_here]
         sent = times_columns(
-            xs, two(ws), order, sides, bf16, name + "_sent", first, chunks=chunks
+            xs, two(xs, ws, first), order, sides, bf16, name + "_sent", chunks=chunks
         )
         if whole:
             put(sent)
@@ -547,12 +561,12 @@
 
     def columns_part(xs, ws, ids, got, name, first=0):
         order = columns_order(ids, ws)[:, 3:]
-        return times_columns(xs, two(ws), order, sides, bf16, name + "_part", first, got, 1)
+        return times_columns(xs, two(xs, ws, first), order, sides, bf16, name + "_part", got, 1)
 
     def columns_base(xs, ws, ids, got, name, first=0):
         order = columns_order(ids, ws)[:, 2:3]
         xs = [at_now(xs[0])] + xs[1:]
-        return times_columns(xs, two(ws), order, sides, f32, name + "_base", first, got, 0)
+        return times_columns(xs, two(xs, ws, first), order, sides, f32, name + "_base", got, 0)
 
     class WeightSum:
         def __init__(self, a, ids, gs, name, groups=None):
@@ -691,7 +705,11 @@
 
     expand_step(0)
     if stepped:
-        contract_pair = jnp.concatenate([contract, swap(at_now(contract), "row", 1)], axis=0)
+        half = contract.shape[1] // 2
+        contract_late = contract[:, half:]
+        contract_pair = jnp.concatenate(
+            [contract_late, swap(at_now(contract_late), "row", 1)], axis=0
+        )
         put(contract_pair)
     expand_turn()
     mixed, *full_attend = times_rows(
@@ -711,7 +729,8 @@
     tick()
 
     if stepped:
-        full_contract = [gather_outer(at_now(contract_pair))]
+        contract_mine = gather_outer(at_now(contract[:, :half]))
+        contract_rest = gather_outer(at_now(contract_pair))
     expand_step(1)
     got = columns_sent([attended], full_attend, ids_attend, "project", mix_width)
     part = columns_part([attended], full_attend, ids_attend, got, "project", mix_width)
@@ -732,14 +751,18 @@
     middle_now = at_now(middle_low)
     middle_parts = [middle_low, swap(middle_now, "col", 1), swap(middle_now, "col", 2)]
     put(*middle_parts[1:])
-    tick()
+    if stepped:
+        put(contract_mine)
+    tick()
+
+    if stepped:
+        contract_near = swap(at_now(contract_mine), "row", 1)
+        full_contract = [contract_mine, contract_near, contract_rest]
 
     middle_parts.append(swap(at_now(middle_parts[2]), "col", 1))
     second_full, second_mean, second_scale = normalize(
         middle_parts, norms[1:2], norms[3:4], places_expand, "second_norm"
     )
-    put(second_full)
-    tick()
 
     def activate(acc, extra, out):
         hidden = acc + extra[0][...]
@@ -749,7 +772,7 @@
 
     hidden_shape = (tokens_here, expand.shape[1])
     active, slope, *joined = times_rows(
-        at_now(second_full),
+        second_full,
         expand_own + expand_near if stepped else full_expand,
         [thresholds[None]],
         [(hidden_shape, bf16), (hidden_shape, f32)],
@@ -761,10 +784,13 @@
     if stepped:
         full_expand = joined
     contract_sum = WeightSum(
-        cot_full, ids_contract, [active], "contract_grad", [[3], [2, 1], [0]]
+        cot_full, ids_contract, [active], "contract_grad", [[3, 2], [1], [0]]
     )
     contract_sum.cut()
+    contract_sum.keep(active)
     put(active)
+    if stepped:
+        put(contract_near)
     tick()
 
     def back_activate(acc, extra, out):
@@ -775,30 +801,39 @@
     second_mean, second_scale = at_now(second_mean)[:, 0], at_now(second_scale)[:, 0]
     put(second_mean, second_scale)
     contract_sum.move()
-    contract_sum.keep()
+
+    def contract_back(rows_of, name, skip, width, *first):
+        return times_rows(
+            after(at_now(cot_full), *first),
+            rows_of,
+            [slope],
+            [((tokens_here, width), bf16), ((1, width), f32)],
+            back_activate,
+            name,
+            tn=512,
+            skip=skip,
+        )
+
+    if stepped:
+        pairs = [(w, k) for k in range(rows // 2) for w in full_contract[:2]]
+        early, early_sum = contract_back(pairs, "contract_back_early", 0, half)
+        late, late_sum = contract_back([contract_rest], "contract_back_late", half, half, early)
+        hidden_grads, thresholds_part = [early, late], jnp.concatenate([early_sum, late_sum], axis=1)
+    else:
+        hidden_grad, thresholds_part = contract_back(
+            full_contract, "contract_back", 0, hidden_shape[1]
+        )
+        hidden_grads = [hidden_grad]
+    got = columns_sent(hidden_grads, full_expand, ids_expand, "expand_back")
+    part = columns_part(hidden_grads, full_expand, ids_expand, got, "expand_back")
+    across = swap(part, "col", 2)
+    put(part)
     tick()
 
     contract_sum.add()
     contract_sum.move()
-    hidden_grad, thresholds_part = times_rows(
-        at_now(cot_full),
-        full_contract,
-        [slope],
-        [(hidden_shape, bf16), ((1, hidden_shape[1]), f32)],
-        back_activate,
-        "contract_back",
-        tn=512,
-    )
-    got = columns_sent([hidden_grad], full_expand, ids_expand, "expand_back")
-    part = columns_part([hidden_grad], full_expand, ids_expand, got, "expand_back")
-    across = swap(part, "col", 2)
-    put(part)
-    tick()
-
-    contract_sum.add()
-    contract_sum.move()
-    base = columns_base([hidden_grad], full_expand, ids_expand, got, "expand_back")
-    expand_sum = WeightSum(second_full, ids_expand, [hidden_grad], "expand_grad", [[3], [2, 1], [0]])
+    base = columns_base(hidden_grads, full_expand, ids_expand, got, "expand_back")
+    expand_sum = WeightSum(second_full, ids_expand, hidden_grads, "expand_grad", [[3], [2, 1], [0]])
     expand_sum.cut()
     second_back = base + across.astype(f32)
     put(second_back)
@@ -814,6 +849,7 @@
         )
         return result, jnp.sum(upstream * centred, axis=0), jnp.sum(upstream, axis=0)
 
+    contract_sum.move()
     expand_sum.move()
     second_centred = (middle - second_mean[:, None]) * second_scale[:, None]
     second_input, second_gain, second_shift = norm_back(
@@ -836,7 +872,6 @@
 
     contract_sum.add()
     expand_sum.move()
-    expand_sum.add()
     branch_parts.append(swap(at_now(branch_parts[2]), "col", 1))
     branch_full = lay_out(branch_parts, places_attend, "branch_rows")
     (attended_grad,) = times_rows(
@@ -849,17 +884,11 @@
         tn=width,
         window=(mix_width, width),
     )
-    if stepped:
-        project_other = weight_rows(
-            branch_full,
-            find(ids_attend, 2 * steps + 1 - side),
-            [attended],
-            "projection_grad_other",
-        )
-        put(project_other)
-    else:
-        project_sum = WeightSum(branch_full, ids_attend, [attended], "projection_grad", None)
-        project_sum.cut()
+    project_sum = WeightSum(
+        branch_full, ids_attend, [attended], "projection_grad", [[3, 2, 1, 0]]
+    )
+    project_sum.cut()
+    expand_sum.add(attended_grad)
     query_back, key_back, value_back, query_sum, value_sum = attend_backward(
         mixed, attended_grad, start_row, logs, slopes, seqs
     )
@@ -867,47 +896,31 @@
     put(query_back)
     tick()
 
-    expand_sum.move()
-    if stepped:
-        project_got = swap(at_now(project_other), "row", 1)
-        put(project_got)
+    contract_sum.add()
+    project_sum.move()
+    mixing_sum = WeightSum(
+        first_full, ids_attend, mixed_grads, "mixing_grad", [[3, 2], [1, 0]]
+    )
+    mixing_sum.cut()
+    mixed_grads = [after(query_back, mixing_sum.sent[0]), key_back, value_back]
+    mixing_sum.move(*project_sum.last)
     expand_sum.add()
     got = columns_sent(mixed_grads, full_attend, ids_attend, "mix_back")
-    mixing_sum = WeightSum(
-        first_full, ids_attend, mixed_grads, "mixing_grad", [[3], [2], [1], [0]]
-    )
-    mixing_sum.cut()
     part = columns_part(mixed_grads, full_attend, ids_attend, got, "mix_back")
     across = swap(part, "col", 2)
     expand_sum.add()
     base = columns_base(mixed_grads, full_attend, ids_attend, got, "mix_back")
-    if stepped:
-        project_mine = weight_rows(
-            after(branch_full, part),
-            find(ids_attend, 2 * steps + side),
-            [attended],
-            "projection_grad_mine",
-        )
-        put(project_mine)
+    project_sum.keep(part)
+    mixing_sum.keep(part)
     first_back = base + across.astype(f32)
     put(first_back)
     tick()
 
-    if stepped:
-        total = at_now(project_mine).astype(f32) + project_got.astype(f32)
-        projection_grad = lax.psum_scatter(
-            total.astype(bf16),
-            "row",
-            scatter_dimension=0,
-            tiled=True,
-            axis_index_groups=outer_groups(),
-        ).astype(f32)
-    else:
-        project_sum.add()
-        projection_grad = project_sum.result
-    expand_sum.add()
+    project_sum.add()
     mixing_sum.move()
-    mixing_sum.keep()
+    mixing_sum.add()
+    mixing_sum.add()
+    out_part = columns_part([at_now(active)], full_contract, ids_contract, out_got, "contract")
     first_centred = (resid - first_mean[:, None]) * first_scale[:, None]
     first_input, first_gain, first_shift = norm_back(
         at_now(first_back), first_centred, first_scale, gains[0]
@@ -926,42 +939,29 @@
         ]
     )
     small = jnp.concatenate([small, thresholds_part.reshape(-1, width)], axis=0)
-    def small_step(bit):
-        return small + swap(at_now(small), "row", bit) if bit < rows else small
-
-    put(small)
-    tick()
-
+    bits = [1 << i for i in range(1, rows.bit_length() - 1)] + [1]
+    put(small, out_part)
+    tick()
+
+    expand_sum.move()
     mixing_sum.add()
-    mixing_sum.move()
-    out_part = columns_part([at_now(active)], full_contract, ids_contract, out_got, "contract")
-    small = small_step(2)
-    put(out_part, small)
-    tick()
-
-    mixing_sum.add()
-    mixing_sum.move()
+    project_sum.add()
+    project_sum.add()
+    small = at_now(small)
+    for bit in bits[:-1]:
+        small = small + swap(small, "row", bit)
     out_across = swap(at_now(out_part), "col", 2)
     out_base = columns_base([active], full_contract, ids_contract, out_got, "contract")
     layer_out = (middle + (out_base + out_across.astype(f32) + biases[3])).astype(bf16)
-    small = small_step(4)
-    put(small, projection_grad, out_base)
-    tick()
-
-    mixing_sum.add()
-    mixing_sum.move()
-    bit = 8
-    while bit < rows:
-        small = small_step(bit)
-        put(small)
-        tick()
-        bit *= 2
-    small = small_step(1)
-    put(small)
-    tick()
+    put(small, out_base)
+    tick()
+
+    small = small + swap(at_now(small), "row", bits[-1])
+    expand_sum.add()
+    project_sum.add()
     mixing_sum.add()
     contract_grad, expand_grad = contract_sum.result, expand_sum.result
-    mixing_grad = mixing_sum.result
+    projection_grad, mixing_grad = project_sum.result, mixing_sum.result
     mixing_grad = jnp.stack(
         [mixing_grad[:, i * width : (i + 1) * width] for i in range(3)], axis=1
     )

time: 655 us -> 650 us (level)
  Pallas kernels: 269 us -> 200 us
  local copies, waits for them, and re-layouts: 17.4 us -> 78.3 us
  starting transfers between devices: 57 us -> 66.5 us
    pallas_call x28 -> x29, Pallas kernels: 232 us -> 165 us  [matmul_call(): pl.pallas_call(kernel, grid_spec=pltpu.PrefetchScalarGridSpec(num_scalar_...]
    unnamed x122 -> x267, local copies, waits for them, and re-layouts: 9.86 us -> 73.7 us
    ppermute x15 -> x18, waiting for transfers between devices: 37.5 us -> 91.3 us  [turn(): lax.ppermute(x, 'row', [(i, (i + 2 * steps) % count) for i in range(count)])]
    ppermute x56 -> x55, waiting for transfers between devices: 176 us -> 128 us  [swap(): lax.ppermute(x, axis, [(i, i ^ bit) for i in range(lax.axis_size(axis))])]
    ppermute x15 -> x18, starting transfers between devices: 14.7 us -> 30.4 us  [turn(): lax.ppermute(x, 'row', [(i, (i + 2 * steps) % count) for i in range(count)])]
    all_gather x1 -> x2, waiting for transfers between devices: 10.6 us -> 0.01 us  [gather_outer(): lax.all_gather(w, 'row', axis=0, tiled=True, axis_index_groups=outer_grou...]
    ppermute x56 -> x55, starting transfers between devices: 42 us -> 35.8 us  [swap(): lax.ppermute(x, axis, [(i, i ^ bit) for i in range(lax.axis_size(axis))])]
    convert_element_type x9 -> x12, other arithmetic: 21.9 us -> 25.7 us  [add(): self.carry = turn(total.astype(bf16), -1)]
  transfers between devices with their start and end apart: 73 -> 75, of which waited for: 40 -> 36; matrix products, arithmetic and copies ran while one was open for 10% -> 10% of each run, Pallas kernels for 42% -> 31%
where the time goes in v7:
time: 650 us; the launch traced here: 641 us
  waiting for transfers between devices  220 us (34%)
  Pallas kernels  200 us (31%)
  local copies, waits for them, and re-layouts  78.3 us (12%)
  starting transfers between devices  66.5 us (10%)
  other arithmetic  60.8 us (9%)
  between operations  15.9 us (2%)
    pallas_call x29, Pallas kernels, matmul_call(): pl.pallas_call(kernel, grid_spec=pltpu.PrefetchScalarGridSpec(num_scalar_...  165 us
    ppermute x55, waiting for transfers between devices, swap(): lax.ppermute(x, axis, [(i, i ^ bit) for i in range(lax.axis_size(axis))])  128 us
    ppermute x18, waiting for transfers between devices, turn(): lax.ppermute(x, 'row', [(i, (i + 2 * steps) % count) for i in range(count)])  91.3 us
    unnamed x267, local copies, waits for them, and re-layouts  73.7 us
    ppermute x55, starting transfers between devices, swap(): lax.ppermute(x, axis, [(i, i ^ bit) for i in range(lax.axis_size(axis))])  35.8 us
    ppermute x18, starting transfers between devices, turn(): lax.ppermute(x, 'row', [(i, (i + 2 * steps) % count) for i in range(count)])  30.4 us
    convert_element_type x12, other arithmetic, add(): self.carry = turn(total.astype(bf16), -1)  25.7 us
    pallas_call x1, Pallas kernels, attend_backward(): pl.pallas_call(partial(attend_back_kernel, rows=rows, scale=HD ** (-0.5))...  19.2 us
  transfers between devices with their start and end apart: 75, of which 36 were waited for; matrix products, arithmetic and copies ran while one was open for 10% of the time, Pallas kernels for 31%

profile of v7, /device:TPU:0, one launch (start us, length us, event | category | flops | bytes accessed | tf_op | source)
XLA Modules:
  0.0 640.9 jit_solution(1139805917659599296)
XLA Ops:
  11.2 3.0 collective-permute-start.1
  18.2 19.1 %collective-permute-done.1.refs_2_ = bf16[1024,512]{1,0:T(8,128)(2,1)S(1)} collective-permute-done((bf16[1024,512]{1,0:T(8,128)(2,1)S(1)}, bf16[1024,512]{1,0:T(8,128)(2,1)S(1)}, u32[]{:S(2)}, u32[]{:S(2)}) %collective-permute-start.1) | collective-permute-done | bytes 1048608 | tf_op jit(solution)/shard_map/ppermute | solution.py:441
  38.3 3.3 collective-permute-done.3.refs_2_
  49.8 19.5 %collective-permute-done.6.refs_3_ = bf16[256,2048]{1,0:T(8,128)(2,1)S(1)} collective-permute-done((bf16[256,2048]{1,0:T(8,128)(2,1)S(1)}, bf16[256,2048]{1,0:T(8,128)(2,1)S(1)}, u32[]{:S(2)}, u32[]{:S(2)}) %collective-permute-start.6) | collective-permute-done | bytes 1048608 | tf_op jit(solution)/shard_map/ppermute | solution.py:446
  77.4 2.9 collective-permute-done.10
  80.3 20.2 %collective-permute-done.12.refs_4_ = bf16[256,2048]{1,0:T(8,128)(2,1)} collective-permute-done((bf16[256,2048]{1,0:T(8,128)(2,1)S(1)}, bf16[256,2048]{1,0:T(8,128)(2,1)}, u32[]{:S(2)}, u32[]{:S(2)}) %collective-permute-start.12) | collective-permute-done | bytes 1048608 | tf_op jit(solution)/shard_map/ppermute | solution.py:446
  102.7 3.3 cotangent_rows.1.a_ref.refs_0_
  108.2 4.1 first_norm.1
  114.3 10.4 %collective-permute-done.15.refs_8_ = bf16[256,2048]{1,0:T(8,128)(2,1)} collective-permute-done((bf16[256,2048]{1,0:T(8,128)(2,1)}, bf16[256,2048]{1,0:T(8,128)(2,1)}, u32[]{:S(2)}, u32[]{:S(2)}) %collective-permute-start.15) | collective-permute-done | bytes 1048608 | tf_op jit(solution)/shard_map/ppermute | solution.py:441
  128.4 12.5 %mix.1 = (bf16[1024,1536]{1,0:T(8,128)(2,1)S(1)}, bf16[1024,2048]{1,0:T(8,128)(2,1)}, bf16[1024,2048]{1,0:T(8,128)(2,1)}) custom-call(bf16[1024,2048]{1,0:T(8,128)(2,1)} %copy-done.34, bf16[256,2048]{1,0:T(8,128)(2,1)S(1)} %copy-done.56, bf16[256,2048]{1,0:T(8,128)(2,1)S(1)} %copy-done.70, bf16[256,2048]{1,0:T(8,128)(2,1)S(1)} %copy-done.74, ...), custom_call_target="tpu_custom_call" | custom-call | flops 100663296 | bytes 376928 | tf_op jit(solution)/shard_map/mix/pallas_call | solution.py:229
  140.9 10.6 %collective-permute-done.19.refs_3_ = bf16[256,2048]{1,0:T(8,128)(2,1)} collective-permute-done((bf16[256,2048]{1,0:T(8,128)(2,1)}, bf16[256,2048]{1,0:T(8,128)(2,1)}, u32[]{:S(2)}, u32[]{:S(2)}) %collective-permute-start.19) | collective-permute-done | bytes 1048608 | tf_op jit(solution)/shard_map/ppermute | solution.py:446
  156.2 15.7 %attend_forward.1 = (bf16[1024,512]{1,0:T(8,128)(2,1)S(1)}, f32[4,2,1024]{2,1,0:T(2,128)S(1)}) custom-call(f32[8]{0:T(128)S(1)} %multiply_exponential_fusion.slope_ref, s32[1,1024,1]{2,1,0:T(8,128)S(1)} %copy-done.63, bf16[1024,1536]{1,0:T(8,128)(2,1)S(1)} %get-tuple-element.163.q_ref.k_ref.v_ref, ...), custom_call_target="tpu_custom_call" | custom-call | flops 67108864 | bytes 98304 | tf_op jit(solution)/shard_map/attend_forward/pallas_call | solution.py:79
  181.9 3.1 project_sent.1
  185.6 3.8 collective-permute-done.24.refs_5_
  207.4 14.3 %collective-permute-done.25 = bf16[1024,512]{1,0:T(8,128)(2,1)} collective-permute-done((bf16[1024,512]{1,0:T(8,128)(2,1)}, bf16[1024,512]{1,0:T(8,128)(2,1)}, u32[]{:S(2)}, u32[]{:S(2)}) %collective-permute-start.25) | collective-permute-done | bytes 1048608 | tf_op jit(solution)/shard_map/ppermute | solution.py:441
  221.7 3.1 fusion.19
  225.7 22.1 %collective-permute-done.28.refs_2_ = bf16[1024,512]{1,0:T(8,128)(2,1)S(1)} collective-permute-done((bf16[1024,512]{1,0:T(8,128)(2,1)S(1)}, bf16[1024,512]{1,0:T(8,128)(2,1)S(1)}, u32[]{:S(2)}, u32[]{:S(2)}) %collective-permute-start.28) | collective-permute-done | bytes 1048608 | tf_op jit(solution)/shard_map/ppermute | solution.py:441
  257.5 4.1 second_norm.1
  265.3 18.0 %expand.1 = (bf16[1024,2048]{1,0:T(8,128)(2,1)S(1)}, f32[1024,2048]{1,0:T(8,128)}, bf16[1024,2048]{1,0:T(8,128)(2,1)}, bf16[1024,2048]{1,0:T(8,128)(2,1)}) custom-call(bf16[1024,2048]{1,0:T(8,128)(2,1)} %copy-done.37, bf16[256,2048]{1,0:T(8,128)(2,1)} %refs_1_.1, bf16[256,2048]{1,0:T(8,128)(2,1)} %collective-permute-done.16.refs_2_, ...), custom_call_target="tpu_custom_call" | custom-call | flops 134217728 | bytes 524416 | tf_op jit(solution)/shard_map/expand/pallas_call | solution.py:229
  283.3 8.1 %contract_grad_other.1 = (bf16[512,2048]{1,0:T(8,128)(2,1)}, bf16[256,2048]{1,0:T(8,128)(2,1)S(1)}, bf16[256,2048]{1,0:T(8,128)(2,1)}) custom-call(s32[4]{0:T(128)S(1)} %get-tuple-element.297.order_ref, bf16[1024,2048]{1,0:T(8,128)(2,1)S(1)} %copy-done.13, bf16[1024,2048]{1,0:T(8,128)(2,1)S(1)} %get-tuple-element.277.refs_0_), custom_call_target="tpu_custom_call" | custom-call | flops 67108864 | bytes 196608 | tf_op jit(solution)/shard_map/contract_grad_other/pallas_call | solution.py:229
  292.3 6.4 %contract_grad_mine.1 = (bf16[256,2048]{1,0:T(8,128)(2,1)S(1)}, bf16[256,2048]{1,0:T(8,128)(2,1)S(1)}, bf16[256,2048]{1,0:T(8,128)(2,1)S(1)}, bf16[256,2048]{1,0:T(8,128)(2,1)S(1)}) custom-call(s32[4]{0:T(128)S(1)} %get-tuple-element.298.order_ref, bf16[1024,2048]{1,0:T(8,128)(2,1)S(1)} %copy-done.13, bf16[1024,2048]{1,0:T(8,128)(2,1)S(1)} %get-tuple-element.277.refs_0_), custom_call_target="tpu_custom_call" | custom-call | flops 67108864 | bytes 196608 | tf_op jit(solution)/shard_map/contract_grad_mine/pallas_call | solution.py:229
  300.4 6.9 %contract_back_early.1 = (bf16[1024,1024]{1,0:T(8,128)(2,1)S(1)}, f32[1,1024]{1,0:T(1,128)S(1)}) custom-call(bf16[1024,2048]{1,0:T(8,128)(2,1)S(1)} %copy-done.13, bf16[1024,1024]{1,0:T(8,128)(2,1)S(1)} %copy-done.18, bf16[1024,1024]{1,0:T(8,128)(2,1)S(1)} %collective-permute-done.31.refs_2_.refs_4_.refs_6_.refs_8_.refs_3_, ...), custom_call_target="tpu_custom_call" | custom-call | flops 67108864 | bytes 491584 | tf_op jit(solution)/shard_map/contract_back_early/pallas_call | solution.py:229
  313.1 7.5 %contract_back_late.1 = (bf16[1024,1024]{1,0:T(8,128)(2,1)S(1)}, f32[1,1024]{1,0:T(1,128)S(1)}) custom-call(bf16[1024,2048]{1,0:T(8,128)(2,1)S(1)} %copy-done.14, bf16[2048,1024]{1,0:T(8,128)(2,1)S(1)} %copy-done.9, f32[1024,2048]{1,0:T(8,128)} %get-tuple-element.201.refs_9_.refs_2_), custom_call_target="tpu_custom_call" | custom-call | flops 67108864 | bytes 294976 | tf_op jit(solution)/shard_map/contract_back_late/pallas_call | solution.py:229
  320.6 7.6 %expand_back_sent.1 = (bf16[384,1024]{1,0:T(8,128)(2,1)}, bf16[384,1024]{1,0:T(8,128)(2,1)}, bf16[256,1024]{1,0:T(8,128)(2,1)}) custom-call(s32[2,2]{1,0:T(2,128)S(1)} %bitcast.44, s32[1]{0:T(128)} %bitcast.2.side_ref, bf16[1024,1024]{1,0:T(8,128)(2,1)S(1)} %copy-done.26, bf16[1024,1024]{1,0:T(8,128)(2,1)S(1)} %get-tuple-element.208.refs_1_, ...), custom_call_target="tpu_custom_call" | custom-call | flops 67108864 | bytes 229376 | tf_op jit(solution)/shard_map/expand_back_sent/pallas_call | solution.py:229
  338.1 4.5 expand_back_part.1
  344.1 2.8 collective-permute-done.32
  349.5 3.6 collective-permute-start.37
  353.6 4.8 expand_back_base.1
  358.4 8.3 %expand_grad_other.1 = (bf16[256,2048]{1,0:T(8,128)(2,1)}, bf16[512,2048]{1,0:T(8,128)(2,1)}, bf16[256,2048]{1,0:T(8,128)(2,1)S(1)}) custom-call(s32[4]{0:T(128)S(1)} %get-tuple-element.296.order_ref, bf16[1024,2048]{1,0:T(8,128)(2,1)S(1)} %copy-done.38, bf16[1024,1024]{1,0:T(8,128)(2,1)S(1)} %copy-done.27, bf16[1024,1024]{1,0:T(8,128)(2,1)S(1)} %copy-done.30), custom_call_target="tpu_custom_call" | custom-call | flops 67108864 | bytes 196608 | tf_op jit(solution)/shard_map/expand_grad_other/pallas_call | solution.py:229
  369.6 5.6 collective-permute-done.37
  385.6 3.1 add_convert_fusion.5
  398.0 6.4 %expand_grad_mine.1 = (bf16[256,2048]{1,0:T(8,128)(2,1)S(1)}, bf16[256,2048]{1,0:T(8,128)(2,1)S(1)}, bf16[256,2048]{1,0:T(8,128)(2,1)S(1)}, bf16[256,2048]{1,0:T(8,128)(2,1)S(1)}) custom-call(s32[4]{0:T(128)S(1)} %get-tuple-element.299.order_ref, bf16[1024,2048]{1,0:T(8,128)(2,1)S(1)} %copy-done.39, bf16[1024,1024]{1,0:T(8,128)(2,1)S(1)} %copy-done.28, ...), custom_call_target="tpu_custom_call" | custom-call | flops 67108864 | bytes 196608 | tf_op jit(solution)/shard_map/expand_grad_mine/pallas_call | solution.py:229
  404.5 7.7 %contract_sent.1 = bf16[1024,1024]{1,0:T(8,128)(2,1)S(1)} custom-call(s32[2,2]{1,0:T(2,128)S(1)} %bitcast.46, s32[1]{0:T(128)} %bitcast.2.side_ref, bf16[1024,2048]{1,0:T(8,128)(2,1)S(1)} %copy-done.16, bf16[1024,1024]{1,0:T(8,128)(2,1)S(1)} %copy-done.18, bf16[2048,1024]{1,0:T(8,128)(2,1)} %all-gather.5.cloned.1.call-done.refs_1_.refs_2_.refs_4_, ...), custom_call_target="tpu_custom_call" | custom-call | flops 67108864 | bytes 294912 | tf_op jit(solution)/shard_map/contract_sent/pallas_call | solution.py:229
  412.2 16.7 %collective-permute-done.44 = bf16[256,2048]{1,0:T(8,128)(2,1)} collective-permute-done((bf16[256,2048]{1,0:T(8,128)(2,1)}, bf16[256,2048]{1,0:T(8,128)(2,1)}, u32[]{:S(2)}, u32[]{:S(2)}) %collective-permute-start.44) | collective-permute-done | bytes 1048608 | tf_op jit(solution)/shard_map/ppermute | solution.py:441
  429.3 3.1 add_convert_fusion.4
  434.7 4.3 branch_rows.1.a_ref.refs_0_
  441.5 2.6 add_convert_fusion.3
  446.4 3.1 projection_grad_other.1
  449.5 19.2 %attend_backward.1 = (bf16[1024,512]{1,0:T(8,128)(2,1)S(1)}, bf16[1024,512]{1,0:T(8,128)(2,1)S(1)}, bf16[1024,512]{1,0:T(8,128)(2,1)S(1)}, f32[1,1,512]{2,1,0:T(1,128)S(1)}, f32[1,1,512]{2,1,0:T(1,128)S(1)}) custom-call(f32[8]{0:T(128)S(1)} %multiply_exponential_fusion.slope_ref, s32[1,1,1024]{2,1,0:T(1,128)S(1)} %bitcast.42, ...), custom_call_target="tpu_custom_call" | custom-call | flops 167772160 | bytes 114688 | tf_op jit(solution)/shard_map/attend_backward/pallas_call | solution.py:183
  468.8 8.5 %collective-permute-done.48 = bf16[512,2048]{1,0:T(8,128)(2,1)} collective-permute-done((bf16[512,2048]{1,0:T(8,128)(2,1)}, bf16[512,2048]{1,0:T(8,128)(2,1)}, u32[]{:S(2)}, u32[]{:S(2)}) %collective-permute-start.48) | collective-permute-done | bytes 2097184 | tf_op jit(solution)/shard_map/ppermute | solution.py:441
  477.3 3.1 collective-permute-done.49
  482.2 3.1 add_convert_fusion.2
  485.2 4.1 collective-permute-start.55
  489.3 6.9 %mixing_grad_other.1 = (bf16[512,1536]{1,0:T(8,128)(2,1)}, bf16[512,1536]{1,0:T(8,128)(2,1)}) custom-call(s32[4]{0:T(128)S(1)} %get-tuple-element.296.order_ref, bf16[1024,2048]{1,0:T(8,128)(2,1)S(1)} %copy-done.35, bf16[1024,512]{1,0:T(8,128)(2,1)S(1)} %get-tuple-element.249.refs_0_, bf16[1024,512]{1,0:T(8,128)(2,1)S(1)} %get-tuple-element.245.refs_1_, ...), custom_call_target="tpu_custom_call" | custom-call | flops 50331648 | bytes 163840 | tf_op jit(solution)/shard_map/mixing_grad_other/pallas_call | solution.py:229
  496.2 4.7 mix_back_sent.1
  501.6 3.6 collective-permute-done.52.refs_7_
  505.3 4.6 mix_back_part.1
  511.3 3.1 add_convert_fusion.1
  514.4 4.3 collective-permute-start.56
  521.2 3.1 projection_grad_mine.1
  531.5 4.0 mix_back_base.1
  535.5 5.3 mixing_grad_mine.1
  543.0 3.9 collective-permute-done.54
  553.5 15.2 %collective-permute-done.60 = bf16[256,1536]{1,0:T(8,128)(2,1)S(1)} collective-permute-done((bf16[256,1536]{1,0:T(8,128)(2,1)S(1)}, bf16[256,1536]{1,0:T(8,128)(2,1)S(1)}, u32[]{:S(2)}, u32[]{:S(2)}) %collective-permute-start.60) | collective-permute-done | bytes 786464 | tf_op jit(solution)/shard_map/ppermute | solution.py:446
  572.9 3.4 convert_add_fusion.2
  580.1 4.8 contract_part.1
  584.9 4.3 collective-permute-done.61
  591.6 2.7 collective-permute-start.70
  597.4 3.7 collective-permute-done.70
  601.2 4.4 collective-permute-start.71
  609.4 4.6 contract_base.1
  614.0 5.4 collective-permute-done.67
  619.4 3.0 collective-permute-done.71
  625.7 3.2 convert_add_fusion.3
  (462 shorter events, 182.6 us)
Async XLA Ops:
  7.2 244.7 %all-gather.3.cloned.1.call-start = ((), (), s32[]{:S(2)}) async-start(), calls=%async_computation | async-start | bytes 2621440 | tf_op jit(solution)/shard_map/all_gather | solution.py:483
  11.2 26.2 %collective-permute-start.1 = (bf16[1024,512]{1,0:T(8,128)(2,1)S(1)}, bf16[1024,512]{1,0:T(8,128)(2,1)S(1)}, u32[]{:S(2)}, u32[]{:S(2)}) collective-permute-start(bf16[1024,512]{1,0:T(8,128)(2,1)S(1)} %copy-done.50), channel_id=1, source_target_pairs={{0,2},{1,3},{2,0},{3,1},{4,6},{5,7},{6,4},{7,5},{8,10},{9,11},{10,... | collective-permute-start | bytes 3145736 | tf_op jit(solution)/shard_map/ppermute | solution.py:441
  14.2 23.2 %collective-permute-start = (bf16[1024,512]{1,0:T(8,128)(2,1)S(1)}, bf16[1024,512]{1,0:T(8,128)(2,1)S(1)}, u32[]{:S(2)}, u32[]{:S(2)}) collective-permute-start(bf16[1024,512]{1,0:T(8,128)(2,1)S(1)} %copy-done.50), channel_id=1, source_target_pairs={{0,1},{1,0},{2,3},{3,2},{4,5},{5,4},{6,7},{7,6},{8,9},{9,8},{10,11... | collective-permute-start | bytes 3145736 | tf_op jit(solution)/shard_map/ppermute | solution.py:441
  14.2 27.4 %collective-permute-start.3 = (bf16[256,2048]{1,0:T(8,128)(2,1)S(1)}, bf16[256,2048]{1,0:T(8,128)(2,1)S(1)}, u32[]{:S(2)}, u32[]{:S(2)}) collective-permute-start(bf16[256,2048]{1,0:T(8,128)(2,1)S(1)} %pad_maximum_fusion.1.refs_1_), channel_id=1, source_target_pairs={{0,8},{4,12},{8,16},{12,20},{16,24},{20,28},{24,0},{28,4},{1,9},{5... | collective-permute-start | bytes 3145736 | tf_op jit(solution)/shard_map/ppermute | solution.py:446
  15.8 25.9 %collective-permute-start.2 = (bf16[256,2048]{1,0:T(8,128)(2,1)S(1)}, bf16[256,2048]{1,0:T(8,128)(2,1)S(1)}, u32[]{:S(2)}, u32[]{:S(2)}) collective-permute-start(bf16[256,2048]{1,0:T(8,128)(2,1)S(1)} %pad_maximum_fusion.1.refs_1_), channel_id=1, source_target_pairs={{0,4},{4,0},{8,12},{12,8},{16,20},{20,16},{24,28},{28,24},{1,5},{5... | collective-permute-start | bytes 3145736 | tf_op jit(solution)/shard_map/ppermute | solution.py:441
  42.6 26.7 %collective-permute-start.6 = (bf16[256,2048]{1,0:T(8,128)(2,1)S(1)}, bf16[256,2048]{1,0:T(8,128)(2,1)S(1)}, u32[]{:S(2)}, u32[]{:S(2)}) collective-permute-start(bf16[256,2048]{1,0:T(8,128)(2,1)S(1)} %collective-permute-done.3.refs_2_), channel_id=1, source_target_pairs={{0,8},{4,12},{8,16},{12,20},{16,24},{20,28},{24,0},{28,4},{1,9},{5... | collective-permute-start | bytes 3145736 | tf_op jit(solution)/shard_map/ppermute | solution.py:446
  43.6 25.7 %collective-permute-start.5 = (bf16[256,2048]{1,0:T(8,128)(2,1)S(1)}, bf16[256,2048]{1,0:T(8,128)(2,1)S(1)}, u32[]{:S(2)}, u32[]{:S(2)}) collective-permute-start(bf16[256,2048]{1,0:T(8,128)(2,1)S(1)} %collective-permute-done.3.refs_2_), channel_id=1, source_target_pairs={{0,4},{4,0},{8,12},{12,8},{16,20},{20,16},{24,28},{28,24},{1,5},{5... | collective-permute-start | bytes 3145736 | tf_op jit(solution)/shard_map/ppermute | solution.py:441
  47.1 25.7 %collective-permute-start.8 = (bf16[1024,512]{1,0:T(8,128)(2,1)S(1)}, bf16[1024,512]{1,0:T(8,128)(2,1)}, u32[]{:S(2)}, u32[]{:S(2)}) collective-permute-start(bf16[1024,512]{1,0:T(8,128)(2,1)S(1)} %copy-done.53), channel_id=1, source_target_pairs={{0,2},{1,3},{2,0},{3,1},{4,6},{5,7},{6,4},{7,5},{8,10},{9,11},{10,... | collective-permute-start | bytes 3145736 | tf_op jit(solution)/shard_map/ppermute | solution.py:441
  47.6 25.1 %collective-permute-start.7 = (bf16[1024,512]{1,0:T(8,128)(2,1)S(1)}, bf16[1024,512]{1,0:T(8,128)(2,1)S(1)}, u32[]{:S(2)}, u32[]{:S(2)}) collective-permute-start(bf16[1024,512]{1,0:T(8,128)(2,1)S(1)} %copy-done.53), channel_id=1, source_target_pairs={{0,1},{1,0},{2,3},{3,2},{4,5},{5,4},{6,7},{7,6},{8,9},{9,8},{10,11... | collective-permute-start | bytes 3145736 | tf_op jit(solution)/shard_map/ppermute | solution.py:441
  73.8 26.7 %collective-permute-start.12 = (bf16[256,2048]{1,0:T(8,128)(2,1)S(1)}, bf16[256,2048]{1,0:T(8,128)(2,1)}, u32[]{:S(2)}, u32[]{:S(2)}) collective-permute-start(bf16[256,2048]{1,0:T(8,128)(2,1)S(1)} %collective-permute-done.6.refs_3_), channel_id=1, source_target_pairs={{0,8},{4,12},{8,16},{12,20},{16,24},{20,28},{24,0},{28,4},{1,9},{5... | collective-permute-start | bytes 3145736 | tf_op jit(solution)/shard_map/ppermute | solution.py:446
  75.4 25.1 %collective-permute-start.11 = (bf16[256,2048]{1,0:T(8,128)(2,1)S(1)}, bf16[256,2048]{1,0:T(8,128)(2,1)}, u32[]{:S(2)}, u32[]{:S(2)}) collective-permute-start(bf16[256,2048]{1,0:T(8,128)(2,1)S(1)} %collective-permute-done.6.refs_3_), channel_id=1, source_target_pairs={{0,4},{4,0},{8,12},{12,8},{16,20},{20,16},{24,28},{28,24},{1,5},{5... | collective-permute-start | bytes 3145736 | tf_op jit(solution)/shard_map/ppermute | solution.py:441
  75.9 24.6 %collective-permute-start.13 = (bf16[1024,512]{1,0:T(8,128)(2,1)}, bf16[1024,512]{1,0:T(8,128)(2,1)}, u32[]{:S(2)}, u32[]{:S(2)}) collective-permute-start(bf16[1024,512]{1,0:T(8,128)(2,1)} %collective-permute-done.8.refs_2_), channel_id=1, source_target_pairs={{0,1},{1,0},{2,3},{3,2},{4,5},{5,4},{6,7},{7,6},{8,9},{9,8},{10,11... | collective-permute-start | bytes 3145736 | tf_op jit(solution)/shard_map/ppermute | solution.py:441
  100.5 24.2 %collective-permute-start.15 = (bf16[256,2048]{1,0:T(8,128)(2,1)}, bf16[256,2048]{1,0:T(8,128)(2,1)}, u32[]{:S(2)}, u32[]{:S(2)}) collective-permute-start(bf16[256,2048]{1,0:T(8,128)(2,1)} %collective-permute-done.12.refs_4_), channel_id=1, source_target_pairs={{0,4},{4,0},{8,12},{12,8},{16,20},{20,16},{24,28},{28,24},{1,5},{5... | collective-permute-start | bytes 3145736 | tf_op jit(solution)/shard_map/ppermute | solution.py:441
  101.0 25.7 %collective-permute-start.16 = (bf16[256,2048]{1,0:T(8,128)(2,1)}, bf16[256,2048]{1,0:T(8,128)(2,1)}, u32[]{:S(2)}, u32[]{:S(2)}) collective-permute-start(bf16[256,2048]{1,0:T(8,128)(2,1)} %refs_1_.1), channel_id=1, source_target_pairs={{0,8},{4,12},{8,16},{12,20},{16,24},{20,28},{24,0},{28,4},{1,9},{5... | collective-permute-start | bytes 3145736 | tf_op jit(solution)/shard_map/ppermute | solution.py:446
  101.3 6.8 %collective-permute-start.14 = (f32[4,512]{1,0:T(4,128)S(1)}, f32[4,512]{1,0:T(4,128)S(1)}, u32[]{:S(2)}, u32[]{:S(2)}) collective-permute-start(f32[4,512]{1,0:T(4,128)S(1)} %collective-permute-done.10), channel_id=1, source_target_pairs={{0,1},{1,0},{2,3},{3,2},{4,5},{5,4},{6,7},{7,6},{8,9},{9,8},{10,11... | collective-permute-start | bytes 24584 | tf_op jit(solution)/shard_map/ppermute | solution.py:441
  126.7 24.8 %collective-permute-start.19 = (bf16[256,2048]{1,0:T(8,128)(2,1)}, bf16[256,2048]{1,0:T(8,128)(2,1)}, u32[]{:S(2)}, u32[]{:S(2)}) collective-permute-start(bf16[256,2048]{1,0:T(8,128)(2,1)} %collective-permute-done.16.refs_2_), channel_id=1, source_target_pairs={{0,8},{4,12},{8,16},{12,20},{16,24},{20,28},{24,0},{28,4},{1,9},{5... | collective-permute-start | bytes 3145736 | tf_op jit(solution)/shard_map/ppermute | solution.py:446
  126.8 48.4 %collective-permute-start.17 = (bf16[256,2048]{1,0:T(8,128)(2,1)}, bf16[256,2048]{1,0:T(8,128)(2,1)}, u32[]{:S(2)}, u32[]{:S(2)}) collective-permute-start(bf16[256,2048]{1,0:T(8,128)(2,1)} %refs_1_.1), channel_id=1, source_target_pairs={{0,4},{4,0},{8,12},{12,8},{16,20},{20,16},{24,28},{28,24},{1,5},{5... | collective-permute-start | bytes 3145736 | tf_op jit(solution)/shard_map/ppermute | solution.py:441
  151.5 23.9 %collective-permute-start.20 = (bf16[256,2048]{1,0:T(8,128)(2,1)}, bf16[256,2048]{1,0:T(8,128)(2,1)}, u32[]{:S(2)}, u32[]{:S(2)}) collective-permute-start(bf16[256,2048]{1,0:T(8,128)(2,1)} %collective-permute-done.19.refs_3_), channel_id=1, source_target_pairs={{0,8},{4,12},{8,16},{12,20},{16,24},{20,28},{24,0},{28,4},{1,9},{5... | collective-permute-start | bytes 3145736 | tf_op jit(solution)/shard_map/ppermute | solution.py:446
  152.6 20.3 %collective-permute-start.18 = (bf16[256,1024]{1,0:T(8,128)(2,1)}, bf16[256,1024]{1,0:T(8,128)(2,1)}, u32[]{:S(2)}, u32[]{:S(2)}) collective-permute-start(bf16[256,1024]{1,0:T(8,128)(2,1)} %get-tuple-element.166), channel_id=1, source_target_pairs={{0,4},{4,0},{8,12},{12,8},{16,20},{20,16},{24,28},{28,24},{1,5},{5... | collective-permute-start | bytes 1572872 | tf_op jit(solution)/shard_map/ppermute | solution.py:441
  175.5 133.2 %all-gather.5.cloned.1.call-start = ((), (), s32[]{:S(2)}) async-start(), calls=%async_computation.1 | async-start | bytes 5242880 | tf_op jit(solution)/shard_map/all_gather | solution.py:483
  175.7 21.7 %collective-permute-start.21 = (bf16[256,2048]{1,0:T(8,128)(2,1)}, bf16[256,2048]{1,0:T(8,128)(2,1)}, u32[]{:S(2)}, u32[]{:S(2)}) collective-permute-start(bf16[256,2048]{1,0:T(8,128)(2,1)} %collective-permute-done.16.refs_2_), channel_id=1, source_target_pairs={{0,4},{4,0},{8,12},{12,8},{16,20},{20,16},{24,28},{28,24},{1,5},{5... | collective-permute-start | bytes 3145736 | tf_op jit(solution)/shard_map/ppermute | solution.py:441
  185.0 4.4 collective-permute-start.22
  185.0 4.4 collective-permute-start.23
  197.4 24.3 %collective-permute-start.25 = (bf16[1024,512]{1,0:T(8,128)(2,1)}, bf16[1024,512]{1,0:T(8,128)(2,1)}, u32[]{:S(2)}, u32[]{:S(2)}) collective-permute-start(bf16[1024,512]{1,0:T(8,128)(2,1)} %project_part.1), channel_id=1, source_target_pairs={{0,2},{1,3},{2,0},{3,1},{4,6},{5,7},{6,4},{7,5},{8,10},{9,11},{10,... | collective-permute-start | bytes 3145736 | tf_op jit(solution)/shard_map/ppermute | solution.py:441
  197.9 26.8 %collective-permute-start.26 = (bf16[256,2048]{1,0:T(8,128)(2,1)}, bf16[256,2048]{1,0:T(8,128)(2,1)}, u32[]{:S(2)}, u32[]{:S(2)}) collective-permute-start(bf16[256,2048]{1,0:T(8,128)(2,1)} %collective-permute-done.19.refs_3_), channel_id=1, source_target_pairs={{0,4},{4,0},{8,12},{12,8},{16,20},{20,16},{24,28},{28,24},{1,5},{5... | collective-permute-start | bytes 3145736 | tf_op jit(solution)/shard_map/ppermute | solution.py:441
  224.8 23.1 %collective-permute-start.28 = (bf16[1024,512]{1,0:T(8,128)(2,1)S(1)}, bf16[1024,512]{1,0:T(8,128)(2,1)S(1)}, u32[]{:S(2)}, u32[]{:S(2)}) collective-permute-start(bf16[1024,512]{1,0:T(8,128)(2,1)S(1)} %get-tuple-element.182.refs_0_), channel_id=1, source_target_pairs={{0,2},{1,3},{2,0},{3,1},{4,6},{5,7},{6,4},{7,5},{8,10},{9,11},{10,... | collective-permute-start | bytes 3145736 | tf_op jit(solution)/shard_map/ppermute | solution.py:441
  225.1 22.7 %collective-permute-start.27 = (bf16[1024,512]{1,0:T(8,128)(2,1)S(1)}, bf16[1024,512]{1,0:T(8,128)(2,1)S(1)}, u32[]{:S(2)}, u32[]{:S(2)}) collective-permute-start(bf16[1024,512]{1,0:T(8,128)(2,1)S(1)} %get-tuple-element.182.refs_0_), channel_id=1, source_target_pairs={{0,1},{1,0},{2,3},{3,2},{4,5},{5,4},{6,7},{7,6},{8,9},{9,8},{10,11... | collective-permute-start | bytes 3145736 | tf_op jit(solution)/shard_map/ppermute | solution.py:441
  225.1 25.8 %collective-permute-start.29 = (bf16[256,2048]{1,0:T(8,128)(2,1)}, bf16[256,2048]{1,0:T(8,128)(2,1)S(1)}, u32[]{:S(2)}, u32[]{:S(2)}) collective-permute-start(bf16[256,2048]{1,0:T(8,128)(2,1)} %collective-permute-done.20.refs_4_), channel_id=1, source_target_pairs={{0,4},{4,0},{8,12},{12,8},{16,20},{20,16},{24,28},{28,24},{1,5},{5... | collective-permute-start | bytes 3145736 | tf_op jit(solution)/shard_map/ppermute | solution.py:441
  251.9 47.6 %collective-permute-start.31 = (bf16[1024,1024]{1,0:T(8,128)(2,1)}, bf16[1024,1024]{1,0:T(8,128)(2,1)S(1)}, u32[]{:S(2)}, u32[]{:S(2)}) collective-permute-start(bf16[1024,1024]{1,0:T(8,128)(2,1)} %all-gather.3.cloned.1.call-done.refs_1_.refs_3_.refs_5_.refs_7_), channel_id=1, source_target_pairs={{0,4},{4,0},{8,12},{12,8},{16,20},{20,16},{24,28},{28,24},{1,5},{5... | collective-permute-start | bytes 6291464 | tf_op jit(solution)/shard_map/ppermute | solution.py:441
  299.5 47.4 %collective-permute-start.32 = (bf16[512,2048]{1,0:T(8,128)(2,1)}, bf16[512,2048]{1,0:T(8,128)(2,1)}, u32[]{:S(2)}, u32[]{:S(2)}) collective-permute-start(bf16[512,2048]{1,0:T(8,128)(2,1)} %get-tuple-element.205), channel_id=1, source_target_pairs={{0,4},{4,0},{8,12},{12,8},{16,20},{20,16},{24,28},{28,24},{1,5},{5... | collective-permute-start | bytes 6291464 | tf_op jit(solution)/shard_map/ppermute | solution.py:441
  328.2 4.5 collective-permute-start.33
  328.4 4.4 collective-permute-start.34
  342.6 25.4 %collective-permute-start.36 = (bf16[1024,512]{1,0:T(8,128)(2,1)S(1)}, bf16[1024,512]{1,0:T(8,128)(2,1)}, u32[]{:S(2)}, u32[]{:S(2)}) collective-permute-start(bf16[1024,512]{1,0:T(8,128)(2,1)S(1)} %expand_back_part.1), channel_id=1, source_target_pairs={{0,2},{1,3},{2,0},{3,1},{4,6},{5,7},{6,4},{7,5},{8,10},{9,11},{10,... | collective-permute-start | bytes 3145736 | tf_op jit(solution)/shard_map/ppermute | solution.py:441
  349.5 25.7 %collective-permute-start.37 = (bf16[256,2048]{1,0:T(8,128)(2,1)}, bf16[256,2048]{1,0:T(8,128)(2,1)}, u32[]{:S(2)}, u32[]{:S(2)}) collective-permute-start(bf16[256,2048]{1,0:T(8,128)(2,1)} %add_convert_fusion.6), channel_id=1, source_target_pairs={{0,24},{4,28},{8,0},{12,4},{16,8},{20,12},{24,16},{28,20},{1,25},{... | collective-permute-start | bytes 3145736 | tf_op jit(solution)/shard_map/ppermute | solution.py:446
  353.1 24.1 %collective-permute-start.38 = (bf16[256,2048]{1,0:T(8,128)(2,1)S(1)}, bf16[256,2048]{1,0:T(8,128)(2,1)}, u32[]{:S(2)}, u32[]{:S(2)}) collective-permute-start(bf16[256,2048]{1,0:T(8,128)(2,1)S(1)} %copy-done.117), channel_id=1, source_target_pairs={{0,4},{4,0},{8,12},{12,8},{16,20},{20,16},{24,28},{28,24},{1,5},{5... | collective-permute-start | bytes 3145736 | tf_op jit(solution)/shard_map/ppermute | solution.py:441
  381.1 31.0 %collective-permute-start.43 = (bf16[256,2048]{1,0:T(8,128)(2,1)}, bf16[256,2048]{1,0:T(8,128)(2,1)}, u32[]{:S(2)}, u32[]{:S(2)}) collective-permute-start(bf16[256,2048]{1,0:T(8,128)(2,1)} %get-tuple-element.223), channel_id=1, source_target_pairs={{0,4},{4,0},{8,12},{12,8},{16,20},{20,16},{24,28},{28,24},{1,5},{5... | collective-permute-start | bytes 3145736 | tf_op jit(solution)/shard_map/ppermute | solution.py:441
  381.4 47.5 %collective-permute-start.44 = (bf16[256,2048]{1,0:T(8,128)(2,1)}, bf16[256,2048]{1,0:T(8,128)(2,1)}, u32[]{:S(2)}, u32[]{:S(2)}) collective-permute-start(bf16[256,2048]{1,0:T(8,128)(2,1)} %get-tuple-element.224), channel_id=1, source_target_pairs={{0,4},{4,0},{8,12},{12,8},{16,20},{20,16},{24,28},{28,24},{1,5},{5... | collective-permute-start | bytes 3145736 | tf_op jit(solution)/shard_map/ppermute | solution.py:441
  388.6 40.2 %collective-permute-start.45 = (bf16[256,2048]{1,0:T(8,128)(2,1)}, bf16[256,2048]{1,0:T(8,128)(2,1)}, u32[]{:S(2)}, u32[]{:S(2)}) collective-permute-start(bf16[256,2048]{1,0:T(8,128)(2,1)} %add_convert_fusion.5), channel_id=1, source_target_pairs={{0,24},{4,28},{8,0},{12,4},{16,8},{20,12},{24,16},{28,20},{1,25},{... | collective-permute-start | bytes 3145736 | tf_op jit(solution)/shard_map/ppermute | solution.py:446
  390.9 37.9 %collective-permute-start.42 = (bf16[1024,512]{1,0:T(8,128)(2,1)}, bf16[1024,512]{1,0:T(8,128)(2,1)}, u32[]{:S(2)}, u32[]{:S(2)}) collective-permute-start(bf16[1024,512]{1,0:T(8,128)(2,1)} %get-tuple-element.305.refs_0_), channel_id=1, source_target_pairs={{0,2},{1,3},{2,0},{3,1},{4,6},{5,7},{6,4},{7,5},{8,10},{9,11},{10,... | collective-permute-start | bytes 3145736 | tf_op jit(solution)/shard_map/ppermute | solution.py:441
  392.5 36.4 %collective-permute-start.41 = (bf16[1024,512]{1,0:T(8,128)(2,1)}, bf16[1024,512]{1,0:T(8,128)(2,1)}, u32[]{:S(2)}, u32[]{:S(2)}) collective-permute-start(bf16[1024,512]{1,0:T(8,128)(2,1)} %get-tuple-element.305.refs_0_), channel_id=1, source_target_pairs={{0,1},{1,0},{2,3},{3,2},{4,5},{5,4},{6,7},{7,6},{8,9},{9,8},{10,11... | collective-permute-start | bytes 3145736 | tf_op jit(solution)/shard_map/ppermute | solution.py:441
  428.9 5.8 collective-permute-start.46
  429.0 48.4 %collective-permute-start.48 = (bf16[512,2048]{1,0:T(8,128)(2,1)}, bf16[512,2048]{1,0:T(8,128)(2,1)}, u32[]{:S(2)}, u32[]{:S(2)}) collective-permute-start(bf16[512,2048]{1,0:T(8,128)(2,1)} %get-tuple-element.237), channel_id=1, source_target_pairs={{0,4},{4,0},{8,12},{12,8},{16,20},{20,16},{24,28},{28,24},{1,5},{5... | collective-permute-start | bytes 6291464 | tf_op jit(solution)/shard_map/ppermute | solution.py:441
  432.4 36.4 %collective-permute-start.47 = (bf16[256,2048]{1,0:T(8,128)(2,1)}, bf16[256,2048]{1,0:T(8,128)(2,1)}, u32[]{:S(2)}, u32[]{:S(2)}) collective-permute-start(bf16[256,2048]{1,0:T(8,128)(2,1)} %add_convert_fusion.4), channel_id=1, source_target_pairs={{0,24},{4,28},{8,0},{12,4},{16,8},{20,12},{24,16},{28,20},{1,25},{... | collective-permute-start | bytes 3145736 | tf_op jit(solution)/shard_map/ppermute | solution.py:446
  444.1 36.4 %collective-permute-start.49 = (bf16[256,2048]{1,0:T(8,128)(2,1)}, bf16[256,2048]{1,0:T(8,128)(2,1)}, u32[]{:S(2)}, u32[]{:S(2)}) collective-permute-start(bf16[256,2048]{1,0:T(8,128)(2,1)} %add_convert_fusion.3), channel_id=1, source_target_pairs={{0,24},{4,28},{8,0},{12,4},{16,8},{20,12},{24,16},{28,20},{1,25},{... | collective-permute-start | bytes 3145736 | tf_op jit(solution)/shard_map/ppermute | solution.py:446
  480.4 30.0 %collective-permute-start.53 = (bf16[1024,512]{1,0:T(8,128)(2,1)S(1)}, bf16[1024,512]{1,0:T(8,128)(2,1)S(1)}, u32[]{:S(2)}, u32[]{:S(2)}) collective-permute-start(bf16[1024,512]{1,0:T(8,128)(2,1)S(1)} %projection_grad_other.1), channel_id=1, source_target_pairs={{0,4},{4,0},{8,12},{12,8},{16,20},{20,16},{24,28},{28,24},{1,5},{5... | collective-permute-start | bytes 3145736 | tf_op jit(solution)/shard_map/ppermute | solution.py:441
  485.2 26.0 %collective-permute-start.55 = (bf16[256,2048]{1,0:T(8,128)(2,1)}, bf16[256,2048]{1,0:T(8,128)(2,1)}, u32[]{:S(2)}, u32[]{:S(2)}) collective-permute-start(bf16[256,2048]{1,0:T(8,128)(2,1)} %add_convert_fusion.2), channel_id=1, source_target_pairs={{0,24},{4,28},{8,0},{12,4},{16,8},{20,12},{24,16},{28,20},{1,25},{... | collective-permute-start | bytes 3145736 | tf_op jit(solution)/shard_map/ppermute | solution.py:446
  501.0 4.2 collective-permute-start.50
  509.9 30.9 %collective-permute-start.57 = (bf16[1024,512]{1,0:T(8,128)(2,1)}, bf16[1024,512]{1,0:T(8,128)(2,1)}, u32[]{:S(2)}, u32[]{:S(2)}) collective-permute-start(bf16[1024,512]{1,0:T(8,128)(2,1)} %mix_back_part.1), channel_id=1, source_target_pairs={{0,2},{1,3},{2,0},{3,1},{4,6},{5,7},{6,4},{7,5},{8,10},{9,11},{10,... | collective-permute-start | bytes 3145736 | tf_op jit(solution)/shard_map/ppermute | solution.py:441
  510.4 36.5 %collective-permute-start.54 = (bf16[512,1536]{1,0:T(8,128)(2,1)}, bf16[512,1536]{1,0:T(8,128)(2,1)}, u32[]{:S(2)}, u32[]{:S(2)}) collective-permute-start(bf16[512,1536]{1,0:T(8,128)(2,1)} %get-tuple-element.258), channel_id=1, source_target_pairs={{0,4},{4,0},{8,12},{12,8},{16,20},{20,16},{24,28},{28,24},{1,5},{5... | collective-permute-start | bytes 4718600 | tf_op jit(solution)/shard_map/ppermute | solution.py:441
  514.4 28.6 %collective-permute-start.56 = (bf16[256,2048]{1,0:T(8,128)(2,1)}, bf16[256,2048]{1,0:T(8,128)(2,1)}, u32[]{:S(2)}, u32[]{:S(2)}) collective-permute-start(bf16[256,2048]{1,0:T(8,128)(2,1)} %add_convert_fusion.1), channel_id=1, source_target_pairs={{0,24},{4,28},{8,0},{12,4},{16,8},{20,12},{24,16},{28,20},{1,25},{... | collective-permute-start | bytes 3145736 | tf_op jit(solution)/shard_map/ppermute | solution.py:446
  518.8 57.5 %collective-permute-start.62 = (bf16[1024,1024]{1,0:T(8,128)(2,1)}, bf16[1024,1024]{1,0:T(8,128)(2,1)}, u32[]{:S(2)}, u32[]{:S(2)}) collective-permute-start(bf16[1024,1024]{1,0:T(8,128)(2,1)} %copy-done.64), channel_id=1, source_target_pairs={{0,1},{1,0},{2,3},{3,2},{4,5},{5,4},{6,7},{7,6},{8,9},{9,8},{10,11... | collective-permute-start | bytes 6291464 | tf_op jit(solution)/shard_map/ppermute | solution.py:441
  548.2 20.5 %collective-permute-start.60 = (bf16[256,1536]{1,0:T(8,128)(2,1)S(1)}, bf16[256,1536]{1,0:T(8,128)(2,1)S(1)}, u32[]{:S(2)}, u32[]{:S(2)}) collective-permute-start(bf16[256,1536]{1,0:T(8,128)(2,1)S(1)} %add_convert_fusion.9), channel_id=1, source_target_pairs={{0,24},{4,28},{8,0},{12,4},{16,8},{20,12},{24,16},{28,20},{1,25},{... | collective-permute-start | bytes 2359304 | tf_op jit(solution)/shard_map/ppermute | solution.py:446
  551.5 33.5 %collective-permute-start.58 = (bf16[256,512]{1,0:T(8,128)(2,1)}, bf16[256,512]{1,0:T(8,128)(2,1)}, u32[]{:S(2)}, u32[]{:S(2)}) collective-permute-start(bf16[256,512]{1,0:T(8,128)(2,1)} %add_convert_fusion.12), channel_id=1, source_target_pairs={{0,24},{4,28},{8,0},{12,4},{16,8},{20,12},{24,16},{28,20},{1,25},{... | collective-permute-start | bytes 786440 | tf_op jit(solution)/shard_map/ppermute | solution.py:446
  551.5 37.8 %collective-permute-start.59 = (bf16[512,1536]{1,0:T(8,128)(2,1)}, bf16[512,1536]{1,0:T(8,128)(2,1)}, u32[]{:S(2)}, u32[]{:S(2)}) collective-permute-start(bf16[512,1536]{1,0:T(8,128)(2,1)} %get-tuple-element.269), channel_id=1, source_target_pairs={{0,4},{4,0},{8,12},{12,8},{16,20},{20,16},{24,28},{28,24},{1,5},{5... | collective-permute-start | bytes 4718600 | tf_op jit(solution)/shard_map/ppermute | solution.py:441
  551.9 33.0 %collective-permute-start.65 = (f32[2,1024]{1,0:T(2,128)S(1)}, f32[2,1024]{1,0:T(2,128)S(1)}, u32[]{:S(2)}, u32[]{:S(2)}) collective-permute-start(f32[2,1024]{1,0:T(2,128)S(1)} %fusion.17), channel_id=1, source_target_pairs={{0,2},{1,3},{2,0},{3,1},{4,6},{5,7},{6,4},{7,5},{8,10},{9,11},{10,... | collective-permute-start | bytes 24584 | tf_op jit(solution)/shard_map/ppermute | solution.py:441
  571.1 18.2 %collective-permute-start.61 = (bf16[256,1536]{1,0:T(8,128)(2,1)}, bf16[256,1536]{1,0:T(8,128)(2,1)}, u32[]{:S(2)}, u32[]{:S(2)}) collective-permute-start(bf16[256,1536]{1,0:T(8,128)(2,1)} %add_convert_fusion.8), channel_id=1, source_target_pairs={{0,24},{4,28},{8,0},{12,4},{16,8},{20,12},{24,16},{28,20},{1,25},{... | collective-permute-start | bytes 2359304 | tf_op jit(solution)/shard_map/ppermute | solution.py:446
  589.3 7.8 %collective-permute-start.66 = (f32[12,512]{1,0:T(8,128)S(1)}, f32[12,512]{1,0:T(8,128)S(1)}, u32[]{:S(2)}, u32[]{:S(2)}) collective-permute-start(f32[12,512]{1,0:T(8,128)S(1)} %concatenate.31), channel_id=1, source_target_pairs={{0,8},{4,12},{8,0},{12,4},{16,24},{20,28},{24,16},{28,20},{1,9},{5... | collective-permute-start | bytes 73736 | tf_op jit(solution)/shard_map/ppermute | solution.py:441
  591.6 9.5 %collective-permute-start.70 = (bf16[256,512]{1,0:T(8,128)(2,1)S(1)}, bf16[256,512]{1,0:T(8,128)(2,1)S(1)}, u32[]{:S(2)}, u32[]{:S(2)}) collective-permute-start(bf16[256,512]{1,0:T(8,128)(2,1)S(1)} %add_convert_fusion.11), channel_id=1, source_target_pairs={{0,24},{4,28},{8,0},{12,4},{16,8},{20,12},{24,16},{28,20},{1,25},{... | collective-permute-start | bytes 786440 | tf_op jit(solution)/shard_map/ppermute | solution.py:446
  594.3 28.1 %collective-permute-start.68 = (bf16[256,2048]{1,0:T(8,128)(2,1)S(1)}, bf16[256,2048]{1,0:T(8,128)(2,1)S(1)}, u32[]{:S(2)}, u32[]{:S(2)}) collective-permute-start(bf16[256,2048]{1,0:T(8,128)(2,1)S(1)} %copy-done.115), channel_id=1, source_target_pairs={{0,4},{4,0},{8,12},{12,8},{16,20},{20,16},{24,28},{28,24},{1,5},{5... | collective-permute-start | bytes 3145736 | tf_op jit(solution)/shard_map/ppermute | solution.py:441
  596.4 26.0 %collective-permute-start.69 = (bf16[256,1536]{1,0:T(8,128)(2,1)S(1)}, bf16[256,1536]{1,0:T(8,128)(2,1)S(1)}, u32[]{:S(2)}, u32[]{:S(2)}) collective-permute-start(bf16[256,1536]{1,0:T(8,128)(2,1)S(1)} %add_convert_fusion.7), channel_id=1, source_target_pairs={{0,24},{4,28},{8,0},{12,4},{16,8},{20,12},{24,16},{28,20},{1,25},{... | collective-permute-start | bytes 2359304 | tf_op jit(solution)/shard_map/ppermute | solution.py:446
  597.1 22.3 %collective-permute-start.67 = (f32[12,512]{1,0:T(8,128)S(1)}, f32[12,512]{1,0:T(8,128)S(1)}, u32[]{:S(2)}, u32[]{:S(2)}) collective-permute-start(f32[12,512]{1,0:T(8,128)S(1)} %add.360), channel_id=1, source_target_pairs={{0,16},{4,20},{8,24},{12,28},{16,0},{20,4},{24,8},{28,12},{1,17},{... | collective-permute-start | bytes 73736 | tf_op jit(solution)/shard_map/ppermute | solution.py:441
  601.2 21.2 %collective-permute-start.71 = (bf16[256,512]{1,0:T(8,128)(2,1)S(1)}, bf16[256,512]{1,0:T(8,128)(2,1)S(1)}, u32[]{:S(2)}, u32[]{:S(2)}) collective-permute-start(bf16[256,512]{1,0:T(8,128)(2,1)S(1)} %add_convert_fusion.10), channel_id=1, source_target_pairs={{0,24},{4,28},{8,0},{12,4},{16,8},{20,12},{24,16},{28,20},{1,25},{... | collective-permute-start | bytes 786440 | tf_op jit(solution)/shard_map/ppermute | solution.py:446
  607.8 21.1 %collective-permute-start.63 = (bf16[1024,512]{1,0:T(8,128)(2,1)S(1)}, bf16[1024,512]{1,0:T(8,128)(2,1)S(1)}, u32[]{:S(2)}, u32[]{:S(2)}) collective-permute-start(bf16[1024,512]{1,0:T(8,128)(2,1)S(1)} %contract_part.1), channel_id=1, source_target_pairs={{0,2},{1,3},{2,0},{3,1},{4,6},{5,7},{6,4},{7,5},{8,10},{9,11},{10,... | collective-permute-start | bytes 3145736 | tf_op jit(solution)/shard_map/ppermute | solution.py:441
  622.4 9.3 %collective-permute-start.72 = (f32[12,512]{1,0:T(8,128)S(1)}, f32[12,512]{1,0:T(8,128)S(1)}, u32[]{:S(2)}, u32[]{:S(2)}) collective-permute-start(f32[12,512]{1,0:T(8,128)S(1)} %add.361), channel_id=1, source_target_pairs={{0,4},{4,0},{8,12},{12,8},{16,20},{20,16},{24,28},{28,24},{1,5},{5... | collective-permute-start | bytes 73736 | tf_op jit(solution)/shard_map/ppermute | solution.py:441
  (143 other events, 1338.5 us)
Sparse Core Ops, SparseCore 0:
  175.6 45.2 all-gather.2
  223.0 79.5 all-gather.4

commit v8 on v6

--- a/solution.py
+++ b/solution.py
@@ -17,7 +17,7 @@
 far = -1e33
 NT = (((1,), (1,)), ((), ()))
 TN = (((0,), (0,)), ((), ()))
-VMEM_LIMIT = 56 << 20
+VMEM_LIMIT = 26 << 20
 CHEAP = 64
 f32 = jnp.float32
 bf16 = jnp.bfloat16

time: 655 us -> 645 us (0.985)
  Pallas kernels: 269 us -> 181 us
  local copies, waits for them, and re-layouts: 17.4 us -> 91.3 us
  waiting for transfers between devices: 224 us -> 235 us
  other arithmetic: 62.7 us -> 54 us
    pallas_call x28, Pallas kernels: 232 us -> 146 us  [matmul_call(): pl.pallas_call(kernel, grid_spec=pltpu.PrefetchScalarGridSpec(num_scalar_...]
    unnamed x122 -> x262, local copies, waits for them, and re-layouts: 9.86 us -> 85 us
    ppermute x56, waiting for transfers between devices: 176 us -> 186 us  [swap(): lax.ppermute(x, axis, [(i, i ^ bit) for i in range(lax.axis_size(axis))])]
    convert_element_type x9, other arithmetic: 21.9 us -> 15.3 us  [add(): self.carry = turn(total.astype(bf16), -1)]
  transfers between devices with their start and end apart: 73 -> 73, of which waited for: 40 -> 39; matrix products, arithmetic and copies ran while one was open for 10% -> 9% of each run, Pallas kernels for 42% -> 29%
where the time goes in v8:
time: 645 us; the launch traced here: 636 us
  waiting for transfers between devices  235 us (36%)
  Pallas kernels  181 us (28%)
  local copies, waits for them, and re-layouts  91.3 us (14%)
  starting transfers between devices  58 us (9%)
  other arithmetic  54 us (8%)
  between operations  15.8 us (2%)
    ppermute x56, waiting for transfers between devices, swap(): lax.ppermute(x, axis, [(i, i ^ bit) for i in range(lax.axis_size(axis))])  186 us
    pallas_call x28, Pallas kernels, matmul_call(): pl.pallas_call(kernel, grid_spec=pltpu.PrefetchScalarGridSpec(num_scalar_...  146 us
    unnamed x262, local copies, waits for them, and re-layouts  85 us
    ppermute x15, waiting for transfers between devices, turn(): lax.ppermute(x, 'row', [(i, (i + 2 * steps) % count) for i in range(count)])  37.9 us
    ppermute x56, starting transfers between devices, swap(): lax.ppermute(x, axis, [(i, i ^ bit) for i in range(lax.axis_size(axis))])  36.6 us
    ppermute x15, starting transfers between devices, turn(): lax.ppermute(x, 'row', [(i, (i + 2 * steps) % count) for i in range(count)])  21.1 us
    pallas_call x1, Pallas kernels, attend_backward(): pl.pallas_call(partial(attend_back_kernel, rows=rows, scale=HD ** (-0.5))...  19.3 us
    pallas_call x1, Pallas kernels, attend_forward(): pl.pallas_call(partial(attend_kernel, rows=rows, scale=HD ** (-0.5)), gri...  15.7 us
  transfers between devices with their start and end apart: 73, of which 39 were waited for; matrix products, arithmetic and copies ran while one was open for 9% of the time, Pallas kernels for 29%

profile of v8, /device:TPU:0, one launch (start us, length us, event | category | flops | bytes accessed | tf_op | source)
XLA Modules:
  0.0 635.7 jit_solution(15543280919785838359)
XLA Ops:
  19.3 18.7 %collective-permute-done.1.refs_2_ = bf16[1024,512]{1,0:T(8,128)(2,1)S(1)} collective-permute-done((bf16[1024,512]{1,0:T(8,128)(2,1)S(1)}, bf16[1024,512]{1,0:T(8,128)(2,1)S(1)}, u32[]{:S(2)}, u32[]{:S(2)}) %collective-permute-start.1) | collective-permute-done | bytes 1048608 | tf_op jit(solution)/shard_map/ppermute | solution.py:431
  47.2 21.1 %collective-permute-done.8.refs_2_ = bf16[1024,512]{1,0:T(8,128)(2,1)} collective-permute-done((bf16[1024,512]{1,0:T(8,128)(2,1)S(1)}, bf16[1024,512]{1,0:T(8,128)(2,1)}, u32[]{:S(2)}, u32[]{:S(2)}) %collective-permute-start.8) | collective-permute-done | bytes 1048608 | tf_op jit(solution)/shard_map/ppermute | solution.py:431
  78.4 17.2 %collective-permute-done.11.refs_7_ = bf16[256,2048]{1,0:T(8,128)(2,1)S(1)} collective-permute-done((bf16[256,2048]{1,0:T(8,128)(2,1)S(1)}, bf16[256,2048]{1,0:T(8,128)(2,1)S(1)}, u32[]{:S(2)}, u32[]{:S(2)}) %collective-permute-start.11) | collective-permute-done | bytes 1048608 | tf_op jit(solution)/shard_map/ppermute | solution.py:431
  104.4 3.2 cotangent_rows.1.a_ref.refs_0_
  109.8 4.1 first_norm.1
  113.9 10.9 %collective-permute-done.16.refs_2_ = bf16[256,2048]{1,0:T(8,128)(2,1)} collective-permute-done((bf16[256,2048]{1,0:T(8,128)(2,1)}, bf16[256,2048]{1,0:T(8,128)(2,1)}, u32[]{:S(2)}, u32[]{:S(2)}) %collective-permute-start.16) | collective-permute-done | bytes 1048608 | tf_op jit(solution)/shard_map/ppermute | solution.py:436
  127.0 9.9 %mix.1 = (bf16[1024,1536]{1,0:T(8,128)(2,1)S(1)}, bf16[1024,2048]{1,0:T(8,128)(2,1)S(1)}, bf16[1024,2048]{1,0:T(8,128)(2,1)S(1)}) custom-call(bf16[1024,2048]{1,0:T(8,128)(2,1)S(1)} %get-tuple-element.244.refs_0_.a_ref, bf16[256,2048]{1,0:T(8,128)(2,1)S(1)} %copy-done.58, bf16[256,2048]{1,0:T(8,128)(2,1)S(1)} %copy-done.80, ...), custom_call_target="tpu_custom_call" | custom-call | flops 100663296 | bytes 376928 | tf_op jit(solution)/shard_map/mix/pallas_call | solution.py:229
  140.9 8.1 %collective-permute-done.19.refs_3_ = bf16[256,2048]{1,0:T(8,128)(2,1)} collective-permute-done((bf16[256,2048]{1,0:T(8,128)(2,1)}, bf16[256,2048]{1,0:T(8,128)(2,1)}, u32[]{:S(2)}, u32[]{:S(2)}) %collective-permute-start.19) | collective-permute-done | bytes 1048608 | tf_op jit(solution)/shard_map/ppermute | solution.py:436
  152.3 15.7 %attend_forward.1 = (bf16[1024,512]{1,0:T(8,128)(2,1)S(1)}, f32[4,2,1024]{2,1,0:T(2,128)S(1)}) custom-call(f32[8]{0:T(128)S(1)} %multiply_exponential_fusion.slope_ref, s32[1,1024,1]{2,1,0:T(8,128)S(1)} %copy-done.72, bf16[1024,1536]{1,0:T(8,128)(2,1)S(1)} %get-tuple-element.154.q_ref.k_ref.v_ref, ...), custom_call_target="tpu_custom_call" | custom-call | flops 67108864 | bytes 98304 | tf_op jit(solution)/shard_map/attend_forward/pallas_call | solution.py:79
  182.0 3.5 collective-permute-done.24.refs_5_
  187.9 6.2 collective-permute-done.21.refs_6_
  209.3 4.1 collective-permute-done.25
  213.5 3.1 fusion.20
  219.5 18.5 %collective-permute-done.29.refs_8_ = bf16[256,2048]{1,0:T(8,128)(2,1)S(1)} collective-permute-done((bf16[256,2048]{1,0:T(8,128)(2,1)}, bf16[256,2048]{1,0:T(8,128)(2,1)S(1)}, u32[]{:S(2)}, u32[]{:S(2)}) %collective-permute-start.29) | collective-permute-done | bytes 1048608 | tf_op jit(solution)/shard_map/ppermute | solution.py:431
  237.9 5.6 collective-permute-done.28.refs_2_
  246.2 4.1 second_norm.1
  251.9 17.8 %expand.1 = (bf16[1024,2048]{1,0:T(8,128)(2,1)S(1)}, f32[1024,2048]{1,0:T(8,128)}, bf16[1024,2048]{1,0:T(8,128)(2,1)S(1)}, bf16[1024,2048]{1,0:T(8,128)(2,1)S(1)}) custom-call(bf16[1024,2048]{1,0:T(8,128)(2,1)S(1)} %get-tuple-element.217.refs_0_.a_ref, bf16[256,2048]{1,0:T(8,128)(2,1)} %refs_1_.1, bf16[256,2048]{1,0:T(8,128)(2,1)} %collective-permute-done.16.refs_2_, ...), custom_call_target="tpu_custom_call" | custom-call | flops 134217728 | bytes 524416 | tf_op jit(solution)/shard_map/expand/pallas_call | solution.py:229
  271.8 8.1 %contract_grad_other.1 = (bf16[256,2048]{1,0:T(8,128)(2,1)}, bf16[512,2048]{1,0:T(8,128)(2,1)}, bf16[256,2048]{1,0:T(8,128)(2,1)S(1)}) custom-call(s32[4]{0:T(128)S(1)} %get-tuple-element.280.order_ref, bf16[1024,2048]{1,0:T(8,128)(2,1)S(1)} %copy-done.20, bf16[1024,2048]{1,0:T(8,128)(2,1)S(1)} %get-tuple-element.258.refs_0_), custom_call_target="tpu_custom_call" | custom-call | flops 67108864 | bytes 196608 | tf_op jit(solution)/shard_map/contract_grad_other/pallas_call | solution.py:229
  289.4 6.4 %contract_grad_mine.1 = (bf16[256,2048]{1,0:T(8,128)(2,1)S(1)}, bf16[256,2048]{1,0:T(8,128)(2,1)S(1)}, bf16[256,2048]{1,0:T(8,128)(2,1)S(1)}, bf16[256,2048]{1,0:T(8,128)(2,1)S(1)}) custom-call(s32[4]{0:T(128)S(1)} %get-tuple-element.281.order_ref, bf16[1024,2048]{1,0:T(8,128)(2,1)S(1)} %copy-done.21, bf16[1024,2048]{1,0:T(8,128)(2,1)S(1)} %copy-done.16), custom_call_target="tpu_custom_call" | custom-call | flops 67108864 | bytes 196608 | tf_op jit(solution)/shard_map/contract_grad_mine/pallas_call | solution.py:229
  296.8 9.6 %collective-permute-done.31 = bf16[256,2048]{1,0:T(8,128)(2,1)} collective-permute-done((bf16[256,2048]{1,0:T(8,128)(2,1)}, bf16[256,2048]{1,0:T(8,128)(2,1)}, u32[]{:S(2)}, u32[]{:S(2)}) %collective-permute-start.31) | collective-permute-done | bytes 1048608 | tf_op jit(solution)/shard_map/ppermute | solution.py:431
  308.0 2.6 add_convert_fusion.7
  310.6 5.5 collective-permute-start.32
  316.1 11.1 %all-gather.2.cloned.1.call-done.refs_1_.refs_2_ = bf16[2048,2048]{1,0:T(8,128)(2,1)} async-done(((bf16[512,2048]{1,0:T(8,128)(2,1)}), bf16[2048,2048]{1,0:T(8,128)(2,1)}) %all-gather.2.cloned.1.call-update) | async-done | bytes 8388624 | tf_op jit(solution)/shard_map/all_gather | solution.py:473
  327.2 3.4 copy-done
  332.8 3.4 copy-done.51
  336.1 10.9 %contract_back.1 = (bf16[1024,2048]{1,0:T(8,128)(2,1)S(1)}, f32[1,2048]{1,0:T(1,128)S(1)}) custom-call(bf16[1024,2048]{1,0:T(8,128)(2,1)S(1)} %copy-done.22, bf16[2048,2048]{1,0:T(8,128)(2,1)S(1)} %copy-done, f32[1024,2048]{1,0:T(8,128)S(1)} %copy-done.51), custom_call_target="tpu_custom_call" | custom-call | flops 134217728 | bytes 393344 | tf_op jit(solution)/shard_map/contract_back/pallas_call | solution.py:229
  347.1 5.5 expand_back_sent.1
  353.3 3.6 collective-permute-done.36.refs_5_
  356.9 3.0 expand_back_part.1
  365.7 3.0 expand_back_base.1
  368.8 7.8 %expand_grad_other.1 = (bf16[256,2048]{1,0:T(8,128)(2,1)}, bf16[512,2048]{1,0:T(8,128)(2,1)S(1)}, bf16[256,2048]{1,0:T(8,128)(2,1)}) custom-call(s32[4]{0:T(128)S(1)} %get-tuple-element.279.order_ref, bf16[1024,2048]{1,0:T(8,128)(2,1)S(1)} %copy-done.33, bf16[1024,2048]{1,0:T(8,128)(2,1)S(1)} %get-tuple-element.211.refs_0_), custom_call_target="tpu_custom_call" | custom-call | flops 67108864 | bytes 196608 | tf_op jit(solution)/shard_map/expand_grad_other/pallas_call | solution.py:229
  376.5 8.6 %collective-permute-done.39 = bf16[1024,512]{1,0:T(8,128)(2,1)S(1)} collective-permute-done((bf16[1024,512]{1,0:T(8,128)(2,1)S(1)}, bf16[1024,512]{1,0:T(8,128)(2,1)S(1)}, u32[]{:S(2)}, u32[]{:S(2)}) %collective-permute-start.39) | collective-permute-done | bytes 1048608 | tf_op jit(solution)/shard_map/ppermute | solution.py:431
  386.5 3.5 collective-permute-done.37
  398.3 2.7 add_convert_fusion.5
  408.1 6.4 %expand_grad_mine.1 = (bf16[256,2048]{1,0:T(8,128)(2,1)S(1)}, bf16[256,2048]{1,0:T(8,128)(2,1)S(1)}, bf16[256,2048]{1,0:T(8,128)(2,1)S(1)}, bf16[256,2048]{1,0:T(8,128)(2,1)S(1)}) custom-call(s32[4]{0:T(128)S(1)} %get-tuple-element.282.order_ref, bf16[1024,2048]{1,0:T(8,128)(2,1)S(1)} %copy-done.34, bf16[1024,2048]{1,0:T(8,128)(2,1)S(1)} %copy-done.14), custom_call_target="tpu_custom_call" | custom-call | flops 67108864 | bytes 196608 | tf_op jit(solution)/shard_map/expand_grad_mine/pallas_call | solution.py:229
  415.6 3.4 copy-done.1
  419.0 5.6 contract_sent.1
  425.4 3.7 collective-permute-done.45.refs_2_
  432.5 3.6 branch_rows.1.a_ref.refs_0_
  436.1 3.6 projection_grad_other.1
  442.5 19.3 %attend_backward.1 = (bf16[1024,512]{1,0:T(8,128)(2,1)S(1)}, bf16[1024,512]{1,0:T(8,128)(2,1)S(1)}, bf16[1024,512]{1,0:T(8,128)(2,1)S(1)}, f32[1,1,512]{2,1,0:T(1,128)S(1)}, f32[1,1,512]{2,1,0:T(1,128)S(1)}) custom-call(f32[8]{0:T(128)S(1)} %multiply_exponential_fusion.slope_ref, s32[1,1,1024]{2,1,0:T(1,128)S(1)} %bitcast.42, ...), custom_call_target="tpu_custom_call" | custom-call | flops 167772160 | bytes 114688 | tf_op jit(solution)/shard_map/attend_backward/pallas_call | solution.py:183
  461.8 14.6 %collective-permute-done.46 = bf16[512,2048]{1,0:T(8,128)(2,1)S(1)} collective-permute-done((bf16[512,2048]{1,0:T(8,128)(2,1)S(1)}, bf16[512,2048]{1,0:T(8,128)(2,1)S(1)}, u32[]{:S(2)}, u32[]{:S(2)}) %collective-permute-start.46) | collective-permute-done | bytes 2097184 | tf_op jit(solution)/shard_map/ppermute | solution.py:431
  477.9 4.7 mix_back_sent.1
  483.6 3.3 collective-permute-done.55.refs_7_
  487.2 3.4 mix_back_part.1
  492.7 8.2 %collective-permute-done.51 = bf16[256,2048]{1,0:T(8,128)(2,1)S(1)} collective-permute-done((bf16[256,2048]{1,0:T(8,128)(2,1)S(1)}, bf16[256,2048]{1,0:T(8,128)(2,1)S(1)}, u32[]{:S(2)}, u32[]{:S(2)}) %collective-permute-start.51) | collective-permute-done | bytes 1048608 | tf_op jit(solution)/shard_map/ppermute | solution.py:436
  502.4 3.0 collective-permute-start.52
  510.4 6.4 %mixing_grad_other.1 = (bf16[256,1536]{1,0:T(8,128)(2,1)}, bf16[256,1536]{1,0:T(8,128)(2,1)S(1)}, bf16[256,1536]{1,0:T(8,128)(2,1)}, bf16[256,1536]{1,0:T(8,128)(2,1)S(1)}) custom-call(s32[4]{0:T(128)S(1)} %get-tuple-element.279.order_ref, bf16[1024,2048]{1,0:T(8,128)(2,1)S(1)} %copy-done.30, bf16[1024,512]{1,0:T(8,128)(2,1)S(1)} %copy-done.41, ...), custom_call_target="tpu_custom_call" | custom-call | flops 50331648 | bytes 163840 | tf_op jit(solution)/shard_map/mixing_grad_other/pallas_call | solution.py:229
  517.7 2.8 projection_grad_mine.1
  525.3 3.1 convert_add_fusion.4
  528.4 3.2 collective-permute-done.49
  531.9 3.1 convert_add_fusion.2
  537.5 3.1 fusion.5
  543.2 5.3 mixing_grad_mine.1
  548.5 2.6 collective-permute-done.57
  553.0 3.6 convert_add_fusion.3
  558.9 3.4 copy-done.2
  562.3 5.2 contract_part.1
  567.6 10.5 %collective-permute-done.61 = f32[12,512]{1,0:T(8,128)S(1)} collective-permute-done((f32[12,512]{1,0:T(8,128)S(1)}, f32[12,512]{1,0:T(8,128)S(1)}, u32[]{:S(2)}, u32[]{:S(2)}) %collective-permute-start.61) | collective-permute-done | bytes 24608 | tf_op jit(solution)/shard_map/ppermute | solution.py:431
  587.0 4.3 contract_base.1
  592.6 8.8 %collective-permute-done.65 = f32[12,512]{1,0:T(8,128)S(1)} collective-permute-done((f32[12,512]{1,0:T(8,128)S(1)}, f32[12,512]{1,0:T(8,128)S(1)}, u32[]{:S(2)}, u32[]{:S(2)}) %collective-permute-start.65) | collective-permute-done | bytes 24608 | tf_op jit(solution)/shard_map/ppermute | solution.py:431
  607.2 3.1 collective-permute-start.70
  610.2 11.3 %collective-permute-done.68 = f32[12,512]{1,0:T(8,128)S(1)} collective-permute-done((f32[12,512]{1,0:T(8,128)S(1)}, f32[12,512]{1,0:T(8,128)S(1)}, u32[]{:S(2)}, u32[]{:S(2)}) %collective-permute-start.68) | collective-permute-done | bytes 24608 | tf_op jit(solution)/shard_map/ppermute | solution.py:431
  623.4 2.9 add_convert_fusion.1
  (451 shorter events, 183.9 us)
Async XLA Ops:
  7.2 320.0 %all-gather.2.cloned.1.call-start = ((), (), s32[]{:S(2)}) async-start(), calls=%async_computation.1 | async-start | bytes 10485760 | tf_op jit(solution)/shard_map/all_gather | solution.py:473
  11.2 7.2 %collective-permute-start = (bf16[1024,512]{1,0:T(8,128)(2,1)S(1)}, bf16[1024,512]{1,0:T(8,128)(2,1)S(1)}, u32[]{:S(2)}, u32[]{:S(2)}) collective-permute-start(bf16[1024,512]{1,0:T(8,128)(2,1)S(1)} %copy-done.47), channel_id=1, source_target_pairs={{0,1},{1,0},{2,3},{3,2},{4,5},{5,4},{6,7},{7,6},{8,9},{9,8},{10,11... | collective-permute-start | bytes 3145736 | tf_op jit(solution)/shard_map/ppermute | solution.py:431
  11.7 26.3 %collective-permute-start.1 = (bf16[1024,512]{1,0:T(8,128)(2,1)S(1)}, bf16[1024,512]{1,0:T(8,128)(2,1)S(1)}, u32[]{:S(2)}, u32[]{:S(2)}) collective-permute-start(bf16[1024,512]{1,0:T(8,128)(2,1)S(1)} %copy-done.47), channel_id=1, source_target_pairs={{0,2},{1,3},{2,0},{3,1},{4,6},{5,7},{6,4},{7,5},{8,10},{9,11},{10,... | collective-permute-start | bytes 3145736 | tf_op jit(solution)/shard_map/ppermute | solution.py:431
  14.3 25.2 %collective-permute-start.2 = (bf16[256,2048]{1,0:T(8,128)(2,1)S(1)}, bf16[256,2048]{1,0:T(8,128)(2,1)S(1)}, u32[]{:S(2)}, u32[]{:S(2)}) collective-permute-start(bf16[256,2048]{1,0:T(8,128)(2,1)S(1)} %pad_maximum_fusion.1.refs_1_), channel_id=1, source_target_pairs={{0,4},{4,0},{8,12},{12,8},{16,20},{20,16},{24,28},{28,24},{1,5},{5... | collective-permute-start | bytes 3145736 | tf_op jit(solution)/shard_map/ppermute | solution.py:431
  15.8 26.8 %collective-permute-start.3 = (bf16[256,2048]{1,0:T(8,128)(2,1)S(1)}, bf16[256,2048]{1,0:T(8,128)(2,1)S(1)}, u32[]{:S(2)}, u32[]{:S(2)}) collective-permute-start(bf16[256,2048]{1,0:T(8,128)(2,1)S(1)} %pad_maximum_fusion.1.refs_1_), channel_id=1, source_target_pairs={{0,8},{4,12},{8,16},{12,20},{16,24},{20,28},{24,0},{28,4},{1,9},{5... | collective-permute-start | bytes 3145736 | tf_op jit(solution)/shard_map/ppermute | solution.py:436
  42.6 25.7 %collective-permute-start.8 = (bf16[1024,512]{1,0:T(8,128)(2,1)S(1)}, bf16[1024,512]{1,0:T(8,128)(2,1)}, u32[]{:S(2)}, u32[]{:S(2)}) collective-permute-start(bf16[1024,512]{1,0:T(8,128)(2,1)S(1)} %copy-done.54), channel_id=1, source_target_pairs={{0,2},{1,3},{2,0},{3,1},{4,6},{5,7},{6,4},{7,5},{8,10},{9,11},{10,... | collective-permute-start | bytes 3145736 | tf_op jit(solution)/shard_map/ppermute | solution.py:431
  43.1 25.3 %collective-permute-start.5 = (bf16[256,2048]{1,0:T(8,128)(2,1)S(1)}, bf16[256,2048]{1,0:T(8,128)(2,1)S(1)}, u32[]{:S(2)}, u32[]{:S(2)}) collective-permute-start(bf16[256,2048]{1,0:T(8,128)(2,1)S(1)} %collective-permute-done.3.refs_2_), channel_id=1, source_target_pairs={{0,4},{4,0},{8,12},{12,8},{16,20},{20,16},{24,28},{28,24},{1,5},{5... | collective-permute-start | bytes 3145736 | tf_op jit(solution)/shard_map/ppermute | solution.py:431
  43.6 26.8 %collective-permute-start.6 = (bf16[256,2048]{1,0:T(8,128)(2,1)S(1)}, bf16[256,2048]{1,0:T(8,128)(2,1)S(1)}, u32[]{:S(2)}, u32[]{:S(2)}) collective-permute-start(bf16[256,2048]{1,0:T(8,128)(2,1)S(1)} %collective-permute-done.3.refs_2_), channel_id=1, source_target_pairs={{0,8},{4,12},{8,16},{12,20},{16,24},{20,28},{24,0},{28,4},{1,9},{5... | collective-permute-start | bytes 3145736 | tf_op jit(solution)/shard_map/ppermute | solution.py:436
  45.2 25.3 %collective-permute-start.4 = (bf16[1024,512]{1,0:T(8,128)(2,1)S(1)}, bf16[1024,512]{1,0:T(8,128)(2,1)S(1)}, u32[]{:S(2)}, u32[]{:S(2)}) collective-permute-start(bf16[1024,512]{1,0:T(8,128)(2,1)S(1)} %collective-permute-done.1.refs_2_), channel_id=1, source_target_pairs={{0,1},{1,0},{2,3},{3,2},{4,5},{5,4},{6,7},{7,6},{8,9},{9,8},{10,11... | collective-permute-start | bytes 3145736 | tf_op jit(solution)/shard_map/ppermute | solution.py:431
  71.4 24.2 %collective-permute-start.11 = (bf16[256,2048]{1,0:T(8,128)(2,1)S(1)}, bf16[256,2048]{1,0:T(8,128)(2,1)S(1)}, u32[]{:S(2)}, u32[]{:S(2)}) collective-permute-start(bf16[256,2048]{1,0:T(8,128)(2,1)S(1)} %collective-permute-done.6.refs_3_), channel_id=1, source_target_pairs={{0,4},{4,0},{8,12},{12,8},{16,20},{20,16},{24,28},{28,24},{1,5},{5... | collective-permute-start | bytes 3145736 | tf_op jit(solution)/shard_map/ppermute | solution.py:431
  72.9 25.8 %collective-permute-start.12 = (bf16[256,2048]{1,0:T(8,128)(2,1)S(1)}, bf16[256,2048]{1,0:T(8,128)(2,1)}, u32[]{:S(2)}, u32[]{:S(2)}) collective-permute-start(bf16[256,2048]{1,0:T(8,128)(2,1)S(1)} %collective-permute-done.6.refs_3_), channel_id=1, source_target_pairs={{0,8},{4,12},{8,16},{12,20},{16,24},{20,28},{24,0},{28,4},{1,9},{5... | collective-permute-start | bytes 3145736 | tf_op jit(solution)/shard_map/ppermute | solution.py:436
  73.9 24.8 %collective-permute-start.13 = (bf16[1024,512]{1,0:T(8,128)(2,1)}, bf16[1024,512]{1,0:T(8,128)(2,1)S(1)}, u32[]{:S(2)}, u32[]{:S(2)}) collective-permute-start(bf16[1024,512]{1,0:T(8,128)(2,1)} %collective-permute-done.8.refs_2_), channel_id=1, source_target_pairs={{0,1},{1,0},{2,3},{3,2},{4,5},{5,4},{6,7},{7,6},{8,9},{9,8},{10,11... | collective-permute-start | bytes 3145736 | tf_op jit(solution)/shard_map/ppermute | solution.py:431
  74.6 3.7 collective-permute-start.10
  99.7 25.1 %collective-permute-start.16 = (bf16[256,2048]{1,0:T(8,128)(2,1)}, bf16[256,2048]{1,0:T(8,128)(2,1)}, u32[]{:S(2)}, u32[]{:S(2)}) collective-permute-start(bf16[256,2048]{1,0:T(8,128)(2,1)} %refs_1_.1), channel_id=1, source_target_pairs={{0,8},{4,12},{8,16},{12,20},{16,24},{20,28},{24,0},{28,4},{1,9},{5... | collective-permute-start | bytes 3145736 | tf_op jit(solution)/shard_map/ppermute | solution.py:436
  99.7 25.1 %collective-permute-start.15 = (bf16[256,2048]{1,0:T(8,128)(2,1)}, bf16[256,2048]{1,0:T(8,128)(2,1)}, u32[]{:S(2)}, u32[]{:S(2)}) collective-permute-start(bf16[256,2048]{1,0:T(8,128)(2,1)} %collective-permute-done.12.refs_4_), channel_id=1, source_target_pairs={{0,4},{4,0},{8,12},{12,8},{16,20},{20,16},{24,28},{28,24},{1,5},{5... | collective-permute-start | bytes 3145736 | tf_op jit(solution)/shard_map/ppermute | solution.py:431
  100.5 9.2 %collective-permute-start.14 = (f32[4,512]{1,0:T(4,128)S(1)}, f32[4,512]{1,0:T(4,128)S(1)}, u32[]{:S(2)}, u32[]{:S(2)}) collective-permute-start(f32[4,512]{1,0:T(4,128)S(1)} %collective-permute-done.10), channel_id=1, source_target_pairs={{0,1},{1,0},{2,3},{3,2},{4,5},{5,4},{6,7},{7,6},{8,9},{9,8},{10,11... | collective-permute-start | bytes 24584 | tf_op jit(solution)/shard_map/ppermute | solution.py:431
  124.8 24.1 %collective-permute-start.19 = (bf16[256,2048]{1,0:T(8,128)(2,1)}, bf16[256,2048]{1,0:T(8,128)(2,1)}, u32[]{:S(2)}, u32[]{:S(2)}) collective-permute-start(bf16[256,2048]{1,0:T(8,128)(2,1)} %collective-permute-done.16.refs_2_), channel_id=1, source_target_pairs={{0,8},{4,12},{8,16},{12,20},{16,24},{20,28},{24,0},{28,4},{1,9},{5... | collective-permute-start | bytes 3145736 | tf_op jit(solution)/shard_map/ppermute | solution.py:436
  124.8 44.2 %collective-permute-start.18 = (bf16[256,2048]{1,0:T(8,128)(2,1)}, bf16[256,2048]{1,0:T(8,128)(2,1)}, u32[]{:S(2)}, u32[]{:S(2)}) collective-permute-start(bf16[256,2048]{1,0:T(8,128)(2,1)} %param.21), channel_id=1, source_target_pairs={{0,4},{4,0},{8,12},{12,8},{16,20},{20,16},{24,28},{28,24},{1,5},{5... | collective-permute-start | bytes 3145736 | tf_op jit(solution)/shard_map/ppermute | solution.py:431
  125.4 45.9 %collective-permute-start.17 = (bf16[256,2048]{1,0:T(8,128)(2,1)}, bf16[256,2048]{1,0:T(8,128)(2,1)}, u32[]{:S(2)}, u32[]{:S(2)}) collective-permute-start(bf16[256,2048]{1,0:T(8,128)(2,1)} %refs_1_.1), channel_id=1, source_target_pairs={{0,4},{4,0},{8,12},{12,8},{16,20},{20,16},{24,28},{28,24},{1,5},{5... | collective-permute-start | bytes 3145736 | tf_op jit(solution)/shard_map/ppermute | solution.py:431
  148.9 23.2 %collective-permute-start.20 = (bf16[256,2048]{1,0:T(8,128)(2,1)}, bf16[256,2048]{1,0:T(8,128)(2,1)}, u32[]{:S(2)}, u32[]{:S(2)}) collective-permute-start(bf16[256,2048]{1,0:T(8,128)(2,1)} %collective-permute-done.19.refs_3_), channel_id=1, source_target_pairs={{0,8},{4,12},{8,16},{12,20},{16,24},{20,28},{24,0},{28,4},{1,9},{5... | collective-permute-start | bytes 3145736 | tf_op jit(solution)/shard_map/ppermute | solution.py:436
  172.2 429.3 %reduce-scatter.2.cloned.1.call-start = ((), (), s32[]{:S(2)}) async-start(), calls=%async_computation.2 | async-start | bytes 1310720 | tf_op jit(solution)/shard_map/reduce_scatter | solution.py:898
  172.4 21.6 %collective-permute-start.21 = (bf16[256,2048]{1,0:T(8,128)(2,1)}, bf16[256,2048]{1,0:T(8,128)(2,1)}, u32[]{:S(2)}, u32[]{:S(2)}) collective-permute-start(bf16[256,2048]{1,0:T(8,128)(2,1)} %collective-permute-done.16.refs_2_), channel_id=1, source_target_pairs={{0,4},{4,0},{8,12},{12,8},{16,20},{20,16},{24,28},{28,24},{1,5},{5... | collective-permute-start | bytes 3145736 | tf_op jit(solution)/shard_map/ppermute | solution.py:431
  181.3 4.2 collective-permute-start.22
  181.3 4.2 collective-permute-start.23
  194.0 19.4 %collective-permute-start.25 = (bf16[1024,512]{1,0:T(8,128)(2,1)}, bf16[1024,512]{1,0:T(8,128)(2,1)}, u32[]{:S(2)}, u32[]{:S(2)}) collective-permute-start(bf16[1024,512]{1,0:T(8,128)(2,1)} %project_part.1), channel_id=1, source_target_pairs={{0,2},{1,3},{2,0},{3,1},{4,6},{5,7},{6,4},{7,5},{8,10},{9,11},{10,... | collective-permute-start | bytes 3145736 | tf_op jit(solution)/shard_map/ppermute | solution.py:431
  196.4 20.9 %collective-permute-start.26 = (bf16[256,2048]{1,0:T(8,128)(2,1)}, bf16[256,2048]{1,0:T(8,128)(2,1)}, u32[]{:S(2)}, u32[]{:S(2)}) collective-permute-start(bf16[256,2048]{1,0:T(8,128)(2,1)} %collective-permute-done.19.refs_3_), channel_id=1, source_target_pairs={{0,4},{4,0},{8,12},{12,8},{16,20},{20,16},{24,28},{28,24},{1,5},{5... | collective-permute-start | bytes 3145736 | tf_op jit(solution)/shard_map/ppermute | solution.py:431
  217.3 20.6 %collective-permute-start.29 = (bf16[256,2048]{1,0:T(8,128)(2,1)}, bf16[256,2048]{1,0:T(8,128)(2,1)S(1)}, u32[]{:S(2)}, u32[]{:S(2)}) collective-permute-start(bf16[256,2048]{1,0:T(8,128)(2,1)} %collective-permute-done.20.refs_4_), channel_id=1, source_target_pairs={{0,4},{4,0},{8,12},{12,8},{16,20},{20,16},{24,28},{28,24},{1,5},{5... | collective-permute-start | bytes 3145736 | tf_op jit(solution)/shard_map/ppermute | solution.py:431
  218.0 20.0 %collective-permute-start.27 = (bf16[1024,512]{1,0:T(8,128)(2,1)S(1)}, bf16[1024,512]{1,0:T(8,128)(2,1)S(1)}, u32[]{:S(2)}, u32[]{:S(2)}) collective-permute-start(bf16[1024,512]{1,0:T(8,128)(2,1)S(1)} %get-tuple-element.173.refs_0_), channel_id=1, source_target_pairs={{0,1},{1,0},{2,3},{3,2},{4,5},{5,4},{6,7},{7,6},{8,9},{9,8},{10,11... | collective-permute-start | bytes 3145736 | tf_op jit(solution)/shard_map/ppermute | solution.py:431
  218.0 25.6 %collective-permute-start.28 = (bf16[1024,512]{1,0:T(8,128)(2,1)S(1)}, bf16[1024,512]{1,0:T(8,128)(2,1)S(1)}, u32[]{:S(2)}, u32[]{:S(2)}) collective-permute-start(bf16[1024,512]{1,0:T(8,128)(2,1)S(1)} %get-tuple-element.173.refs_0_), channel_id=1, source_target_pairs={{0,2},{1,3},{2,0},{3,1},{4,6},{5,7},{6,4},{7,5},{8,10},{9,11},{10,... | collective-permute-start | bytes 3145736 | tf_op jit(solution)/shard_map/ppermute | solution.py:431
  280.9 25.5 %collective-permute-start.31 = (bf16[256,2048]{1,0:T(8,128)(2,1)}, bf16[256,2048]{1,0:T(8,128)(2,1)}, u32[]{:S(2)}, u32[]{:S(2)}) collective-permute-start(bf16[256,2048]{1,0:T(8,128)(2,1)} %get-tuple-element.185), channel_id=1, source_target_pairs={{0,4},{4,0},{8,12},{12,8},{16,20},{20,16},{24,28},{28,24},{1,5},{5... | collective-permute-start | bytes 3145736 | tf_op jit(solution)/shard_map/ppermute | solution.py:431
  306.4 55.0 %collective-permute-start.33 = (bf16[512,2048]{1,0:T(8,128)(2,1)}, bf16[512,2048]{1,0:T(8,128)(2,1)}, u32[]{:S(2)}, u32[]{:S(2)}) collective-permute-start(bf16[512,2048]{1,0:T(8,128)(2,1)} %get-tuple-element.194), channel_id=1, source_target_pairs={{0,4},{4,0},{8,12},{12,8},{16,20},{20,16},{24,28},{28,24},{1,5},{5... | collective-permute-start | bytes 6291464 | tf_op jit(solution)/shard_map/ppermute | solution.py:431
  310.6 50.8 %collective-permute-start.32 = (bf16[256,2048]{1,0:T(8,128)(2,1)}, bf16[256,2048]{1,0:T(8,128)(2,1)}, u32[]{:S(2)}, u32[]{:S(2)}) collective-permute-start(bf16[256,2048]{1,0:T(8,128)(2,1)} %add_convert_fusion.7), channel_id=1, source_target_pairs={{0,24},{4,28},{8,0},{12,4},{16,8},{20,12},{24,16},{28,20},{1,25},{... | collective-permute-start | bytes 3145736 | tf_op jit(solution)/shard_map/ppermute | solution.py:436
  352.7 4.2 collective-permute-start.34
  352.8 4.1 collective-permute-start.35
  359.9 25.3 %collective-permute-start.39 = (bf16[1024,512]{1,0:T(8,128)(2,1)S(1)}, bf16[1024,512]{1,0:T(8,128)(2,1)S(1)}, u32[]{:S(2)}, u32[]{:S(2)}) collective-permute-start(bf16[1024,512]{1,0:T(8,128)(2,1)S(1)} %expand_back_part.1), channel_id=1, source_target_pairs={{0,2},{1,3},{2,0},{3,1},{4,6},{5,7},{6,4},{7,5},{8,10},{9,11},{10,... | collective-permute-start | bytes 3145736 | tf_op jit(solution)/shard_map/ppermute | solution.py:431
  361.5 25.0 %collective-permute-start.38 = (bf16[256,2048]{1,0:T(8,128)(2,1)S(1)}, bf16[256,2048]{1,0:T(8,128)(2,1)S(1)}, u32[]{:S(2)}, u32[]{:S(2)}) collective-permute-start(bf16[256,2048]{1,0:T(8,128)(2,1)S(1)} %copy-done.113), channel_id=1, source_target_pairs={{0,4},{4,0},{8,12},{12,8},{16,20},{20,16},{24,28},{28,24},{1,5},{5... | collective-permute-start | bytes 3145736 | tf_op jit(solution)/shard_map/ppermute | solution.py:431
  365.0 24.9 %collective-permute-start.37 = (bf16[256,2048]{1,0:T(8,128)(2,1)S(1)}, bf16[256,2048]{1,0:T(8,128)(2,1)S(1)}, u32[]{:S(2)}, u32[]{:S(2)}) collective-permute-start(bf16[256,2048]{1,0:T(8,128)(2,1)S(1)} %add_convert_fusion.6), channel_id=1, source_target_pairs={{0,24},{4,28},{8,0},{12,4},{16,8},{20,12},{24,16},{28,20},{1,25},{... | collective-permute-start | bytes 3145736 | tf_op jit(solution)/shard_map/ppermute | solution.py:436
  392.9 31.7 %collective-permute-start.40 = (bf16[256,2048]{1,0:T(8,128)(2,1)}, bf16[256,2048]{1,0:T(8,128)(2,1)}, u32[]{:S(2)}, u32[]{:S(2)}) collective-permute-start(bf16[256,2048]{1,0:T(8,128)(2,1)} %get-tuple-element.212), channel_id=1, source_target_pairs={{0,4},{4,0},{8,12},{12,8},{16,20},{20,16},{24,28},{28,24},{1,5},{5... | collective-permute-start | bytes 3145736 | tf_op jit(solution)/shard_map/ppermute | solution.py:431
  401.0 24.4 %collective-permute-start.43 = (bf16[256,2048]{1,0:T(8,128)(2,1)}, bf16[256,2048]{1,0:T(8,128)(2,1)}, u32[]{:S(2)}, u32[]{:S(2)}) collective-permute-start(bf16[256,2048]{1,0:T(8,128)(2,1)} %add_convert_fusion.5), channel_id=1, source_target_pairs={{0,24},{4,28},{8,0},{12,4},{16,8},{20,12},{24,16},{28,20},{1,25},{... | collective-permute-start | bytes 3145736 | tf_op jit(solution)/shard_map/ppermute | solution.py:436
  403.2 22.2 %collective-permute-start.44 = (bf16[1024,512]{1,0:T(8,128)(2,1)}, bf16[1024,512]{1,0:T(8,128)(2,1)}, u32[]{:S(2)}, u32[]{:S(2)}) collective-permute-start(bf16[1024,512]{1,0:T(8,128)(2,1)} %get-tuple-element.289.refs_0_), channel_id=1, source_target_pairs={{0,1},{1,0},{2,3},{3,2},{4,5},{5,4},{6,7},{7,6},{8,9},{9,8},{10,11... | collective-permute-start | bytes 3145736 | tf_op jit(solution)/shard_map/ppermute | solution.py:431
  403.3 25.9 %collective-permute-start.45 = (bf16[1024,512]{1,0:T(8,128)(2,1)}, bf16[1024,512]{1,0:T(8,128)(2,1)}, u32[]{:S(2)}, u32[]{:S(2)}) collective-permute-start(bf16[1024,512]{1,0:T(8,128)(2,1)} %get-tuple-element.289.refs_0_), channel_id=1, source_target_pairs={{0,2},{1,3},{2,0},{3,1},{4,6},{5,7},{6,4},{7,5},{8,10},{9,11},{10,... | collective-permute-start | bytes 3145736 | tf_op jit(solution)/shard_map/ppermute | solution.py:431
  429.1 47.3 %collective-permute-start.46 = (bf16[512,2048]{1,0:T(8,128)(2,1)S(1)}, bf16[512,2048]{1,0:T(8,128)(2,1)S(1)}, u32[]{:S(2)}, u32[]{:S(2)}) collective-permute-start(bf16[512,2048]{1,0:T(8,128)(2,1)S(1)} %copy-done.111), channel_id=1, source_target_pairs={{0,4},{4,0},{8,12},{12,8},{16,20},{20,16},{24,28},{28,24},{1,5},{5... | collective-permute-start | bytes 6291464 | tf_op jit(solution)/shard_map/ppermute | solution.py:431
  431.3 30.5 %collective-permute-start.47 = (bf16[256,2048]{1,0:T(8,128)(2,1)S(1)}, bf16[256,2048]{1,0:T(8,128)(2,1)S(1)}, u32[]{:S(2)}, u32[]{:S(2)}) collective-permute-start(bf16[256,2048]{1,0:T(8,128)(2,1)S(1)} %add_convert_fusion.4), channel_id=1, source_target_pairs={{0,24},{4,28},{8,0},{12,4},{16,8},{20,12},{24,16},{28,20},{1,25},{... | collective-permute-start | bytes 3145736 | tf_op jit(solution)/shard_map/ppermute | solution.py:436
  477.0 24.0 %collective-permute-start.51 = (bf16[256,2048]{1,0:T(8,128)(2,1)S(1)}, bf16[256,2048]{1,0:T(8,128)(2,1)S(1)}, u32[]{:S(2)}, u32[]{:S(2)}) collective-permute-start(bf16[256,2048]{1,0:T(8,128)(2,1)S(1)} %add_convert_fusion.3), channel_id=1, source_target_pairs={{0,24},{4,28},{8,0},{12,4},{16,8},{20,12},{24,16},{28,20},{1,25},{... | collective-permute-start | bytes 3145736 | tf_op jit(solution)/shard_map/ppermute | solution.py:436
  482.7 4.5 collective-permute-start.53
  482.7 4.5 collective-permute-start.54
  483.3 45.0 %collective-permute-start.50 = (bf16[1024,512]{1,0:T(8,128)(2,1)}, bf16[1024,512]{1,0:T(8,128)(2,1)}, u32[]{:S(2)}, u32[]{:S(2)}) collective-permute-start(bf16[1024,512]{1,0:T(8,128)(2,1)} %projection_grad_other.1), channel_id=1, source_target_pairs={{0,4},{4,0},{8,12},{12,8},{16,20},{20,16},{24,28},{28,24},{1,5},{5... | collective-permute-start | bytes 3145736 | tf_op jit(solution)/shard_map/ppermute | solution.py:431
  486.9 44.7 %collective-permute-start.49 = (bf16[256,2048]{1,0:T(8,128)(2,1)}, bf16[256,2048]{1,0:T(8,128)(2,1)}, u32[]{:S(2)}, u32[]{:S(2)}) collective-permute-start(bf16[256,2048]{1,0:T(8,128)(2,1)} %get-tuple-element.229), channel_id=1, source_target_pairs={{0,4},{4,0},{8,12},{12,8},{16,20},{20,16},{24,28},{28,24},{1,5},{5... | collective-permute-start | bytes 3145736 | tf_op jit(solution)/shard_map/ppermute | solution.py:431
  492.4 32.9 %collective-permute-start.56 = (bf16[1024,512]{1,0:T(8,128)(2,1)}, bf16[1024,512]{1,0:T(8,128)(2,1)}, u32[]{:S(2)}, u32[]{:S(2)}) collective-permute-start(bf16[1024,512]{1,0:T(8,128)(2,1)} %mix_back_part.1), channel_id=1, source_target_pairs={{0,2},{1,3},{2,0},{3,1},{4,6},{5,7},{6,4},{7,5},{8,10},{9,11},{10,... | collective-permute-start | bytes 3145736 | tf_op jit(solution)/shard_map/ppermute | solution.py:431
  502.4 29.2 %collective-permute-start.52 = (bf16[256,2048]{1,0:T(8,128)(2,1)}, bf16[256,2048]{1,0:T(8,128)(2,1)}, u32[]{:S(2)}, u32[]{:S(2)}) collective-permute-start(bf16[256,2048]{1,0:T(8,128)(2,1)} %add_convert_fusion.2), channel_id=1, source_target_pairs={{0,24},{4,28},{8,0},{12,4},{16,8},{20,12},{24,16},{28,20},{1,25},{... | collective-permute-start | bytes 3145736 | tf_op jit(solution)/shard_map/ppermute | solution.py:436
  506.7 52.2 %collective-permute-start.60 = (bf16[1024,1024]{1,0:T(8,128)(2,1)}, bf16[1024,1024]{1,0:T(8,128)(2,1)}, u32[]{:S(2)}, u32[]{:S(2)}) collective-permute-start(bf16[1024,1024]{1,0:T(8,128)(2,1)} %copy-done.67), channel_id=1, source_target_pairs={{0,1},{1,0},{2,3},{3,2},{4,5},{5,4},{6,7},{7,6},{8,9},{9,8},{10,11... | collective-permute-start | bytes 6291464 | tf_op jit(solution)/shard_map/ppermute | solution.py:431
  531.6 19.4 %collective-permute-start.57 = (bf16[256,1536]{1,0:T(8,128)(2,1)}, bf16[256,1536]{1,0:T(8,128)(2,1)}, u32[]{:S(2)}, u32[]{:S(2)}) collective-permute-start(bf16[256,1536]{1,0:T(8,128)(2,1)} %get-tuple-element.246), channel_id=1, source_target_pairs={{0,4},{4,0},{8,12},{12,8},{16,20},{20,16},{24,28},{28,24},{1,5},{5... | collective-permute-start | bytes 2359304 | tf_op jit(solution)/shard_map/ppermute | solution.py:431
  540.7 18.0 %collective-permute-start.63 = (f32[2,1024]{1,0:T(2,128)S(1)}, f32[2,1024]{1,0:T(2,128)S(1)}, u32[]{:S(2)}, u32[]{:S(2)}) collective-permute-start(f32[2,1024]{1,0:T(2,128)S(1)} %pad_maximum_fusion.5), channel_id=1, source_target_pairs={{0,1},{1,0},{2,3},{3,2},{4,5},{5,4},{6,7},{7,6},{8,9},{9,8},{10,11... | collective-permute-start | bytes 24584 | tf_op jit(solution)/shard_map/ppermute | solution.py:431
  551.1 27.0 %collective-permute-start.59 = (bf16[256,1536]{1,0:T(8,128)(2,1)S(1)}, bf16[256,1536]{1,0:T(8,128)(2,1)S(1)}, u32[]{:S(2)}, u32[]{:S(2)}) collective-permute-start(bf16[256,1536]{1,0:T(8,128)(2,1)S(1)} %copy-done.116), channel_id=1, source_target_pairs={{0,4},{4,0},{8,12},{12,8},{16,20},{20,16},{24,28},{28,24},{1,5},{5... | collective-permute-start | bytes 2359304 | tf_op jit(solution)/shard_map/ppermute | solution.py:431
  552.7 25.4 %collective-permute-start.58 = (bf16[256,1536]{1,0:T(8,128)(2,1)S(1)}, bf16[256,1536]{1,0:T(8,128)(2,1)S(1)}, u32[]{:S(2)}, u32[]{:S(2)}) collective-permute-start(bf16[256,1536]{1,0:T(8,128)(2,1)S(1)} %add_convert_fusion.10), channel_id=1, source_target_pairs={{0,24},{4,28},{8,0},{12,4},{16,8},{20,12},{24,16},{28,20},{1,25},{... | collective-permute-start | bytes 2359304 | tf_op jit(solution)/shard_map/ppermute | solution.py:436
  556.6 21.4 %collective-permute-start.61 = (f32[12,512]{1,0:T(8,128)S(1)}, f32[12,512]{1,0:T(8,128)S(1)}, u32[]{:S(2)}, u32[]{:S(2)}) collective-permute-start(f32[12,512]{1,0:T(8,128)S(1)} %concatenate.27), channel_id=1, source_target_pairs={{0,8},{4,12},{8,0},{12,4},{16,24},{20,28},{24,16},{28,20},{1,9},{5... | collective-permute-start | bytes 73736 | tf_op jit(solution)/shard_map/ppermute | solution.py:431
  558.7 24.4 %collective-permute-start.64 = (f32[2,1024]{1,0:T(2,128)S(1)}, f32[2,1024]{1,0:T(2,128)S(1)}, u32[]{:S(2)}, u32[]{:S(2)}) collective-permute-start(f32[2,1024]{1,0:T(2,128)S(1)} %fusion.18), channel_id=1, source_target_pairs={{0,2},{1,3},{2,0},{3,1},{4,6},{5,7},{6,4},{7,5},{8,10},{9,11},{10,... | collective-permute-start | bytes 24584 | tf_op jit(solution)/shard_map/ppermute | solution.py:431
  578.1 25.4 %collective-permute-start.67 = (bf16[256,1536]{1,0:T(8,128)(2,1)}, bf16[256,1536]{1,0:T(8,128)(2,1)}, u32[]{:S(2)}, u32[]{:S(2)}) collective-permute-start(bf16[256,1536]{1,0:T(8,128)(2,1)} %get-tuple-element.262), channel_id=1, source_target_pairs={{0,4},{4,0},{8,12},{12,8},{16,20},{20,16},{24,28},{28,24},{1,5},{5... | collective-permute-start | bytes 2359304 | tf_op jit(solution)/shard_map/ppermute | solution.py:431
  580.8 22.7 %collective-permute-start.66 = (bf16[256,1536]{1,0:T(8,128)(2,1)}, bf16[256,1536]{1,0:T(8,128)(2,1)}, u32[]{:S(2)}, u32[]{:S(2)}) collective-permute-start(bf16[256,1536]{1,0:T(8,128)(2,1)} %add_convert_fusion.9), channel_id=1, source_target_pairs={{0,24},{4,28},{8,0},{12,4},{16,8},{20,12},{24,16},{28,20},{1,25},{... | collective-permute-start | bytes 2359304 | tf_op jit(solution)/shard_map/ppermute | solution.py:436
  583.1 18.4 %collective-permute-start.65 = (f32[12,512]{1,0:T(8,128)S(1)}, f32[12,512]{1,0:T(8,128)S(1)}, u32[]{:S(2)}, u32[]{:S(2)}) collective-permute-start(f32[12,512]{1,0:T(8,128)S(1)} %add.341), channel_id=1, source_target_pairs={{0,16},{4,20},{8,24},{12,28},{16,0},{20,4},{24,8},{28,12},{1,17},{... | collective-permute-start | bytes 73736 | tf_op jit(solution)/shard_map/ppermute | solution.py:431
  583.6 39.7 %collective-permute-start.62 = (bf16[1024,512]{1,0:T(8,128)(2,1)}, bf16[1024,512]{1,0:T(8,128)(2,1)}, u32[]{:S(2)}, u32[]{:S(2)}) collective-permute-start(bf16[1024,512]{1,0:T(8,128)(2,1)} %contract_part.1), channel_id=1, source_target_pairs={{0,2},{1,3},{2,0},{3,1},{4,6},{5,7},{6,4},{7,5},{8,10},{9,11},{10,... | collective-permute-start | bytes 3145736 | tf_op jit(solution)/shard_map/ppermute | solution.py:431
  603.5 22.8 %collective-permute-start.69 = (bf16[256,1536]{1,0:T(8,128)(2,1)}, bf16[256,1536]{1,0:T(8,128)(2,1)S(1)}, u32[]{:S(2)}, u32[]{:S(2)}) collective-permute-start(bf16[256,1536]{1,0:T(8,128)(2,1)} %copy-done.114), channel_id=1, source_target_pairs={{0,4},{4,0},{8,12},{12,8},{16,20},{20,16},{24,28},{28,24},{1,5},{5... | collective-permute-start | bytes 2359304 | tf_op jit(solution)/shard_map/ppermute | solution.py:431
  604.1 17.5 %collective-permute-start.68 = (f32[12,512]{1,0:T(8,128)S(1)}, f32[12,512]{1,0:T(8,128)S(1)}, u32[]{:S(2)}, u32[]{:S(2)}) collective-permute-start(f32[12,512]{1,0:T(8,128)S(1)} %add.350), channel_id=1, source_target_pairs={{0,4},{4,0},{8,12},{12,8},{16,20},{20,16},{24,28},{28,24},{1,5},{5... | collective-permute-start | bytes 73736 | tf_op jit(solution)/shard_map/ppermute | solution.py:431
  607.2 19.5 %collective-permute-start.70 = (bf16[256,1536]{1,0:T(8,128)(2,1)S(1)}, bf16[256,1536]{1,0:T(8,128)(2,1)S(1)}, u32[]{:S(2)}, u32[]{:S(2)}) collective-permute-start(bf16[256,1536]{1,0:T(8,128)(2,1)S(1)} %add_convert_fusion.8), channel_id=1, source_target_pairs={{0,24},{4,28},{8,0},{12,4},{16,8},{20,12},{24,16},{28,20},{1,25},{... | collective-permute-start | bytes 2359304 | tf_op jit(solution)/shard_map/ppermute | solution.py:436
  (138 other events, 1181.5 us)
Sparse Core Ops, SparseCore 0:
  172.3 154.8 all-gather.1
  537.6 32.0 reduce-scatter.1

commit v9 on v8

--- a/solution.py
+++ b/solution.py
@@ -644,7 +644,7 @@
                 put(own[k + 1])
 
     weight_step(0)
-    tokens_now = at_now(tokens)
+    tokens_now = tokens
     token_parts = [tokens, swap(tokens_now, "col", 1), swap(tokens_now, "col", 2)]
     put(*token_parts[1:])
     tick()
@@ -823,7 +823,7 @@
     middle_grad = cot_float + second_input
     branch_grad = middle_grad.astype(bf16)
     branch_parts = [branch_grad, swap(branch_grad, "col", 1), swap(branch_grad, "col", 2)]
-    contract_sum.add(branch_grad)
+    contract_sum.add()
     expand_sum.keep(branch_grad)
     out_got = columns_sent(
         [after(active, branch_grad)], full_contract, ids_contract, "contract", whole=True

time: 645 us -> 643 us (level)
  transfers between devices with their start and end apart: 73 -> 73, of which waited for: 39 -> 37; matrix products, arithmetic and copies ran while one was open for 9% -> 9% of each run, Pallas kernels for 29% -> 29%
where the time goes in v9:
time: 643 us; the launch traced here: 634 us
  waiting for transfers between devices  230 us (36%)
  Pallas kernels  181 us (28%)
  local copies, waits for them, and re-layouts  91.3 us (14%)
  starting transfers between devices  61.1 us (10%)
  other arithmetic  54.2 us (8%)
  between operations  15.8 us (2%)
    ppermute x56, waiting for transfers between devices, swap(): lax.ppermute(x, axis, [(i, i ^ bit) for i in range(lax.axis_size(axis))])  184 us
    pallas_call x28, Pallas kernels, matmul_call(): pl.pallas_call(kernel, grid_spec=pltpu.PrefetchScalarGridSpec(num_scalar_...  146 us
    unnamed x262, local copies, waits for them, and re-layouts  85 us
    ppermute x56, starting transfers between devices, swap(): lax.ppermute(x, axis, [(i, i ^ bit) for i in range(lax.axis_size(axis))])  42.4 us
    ppermute x15, waiting for transfers between devices, turn(): lax.ppermute(x, 'row', [(i, (i + 2 * steps) % count) for i in range(count)])  35.4 us
    pallas_call x1, Pallas kernels, attend_backward(): pl.pallas_call(partial(attend_back_kernel, rows=rows, scale=HD ** (-0.5))...  19.3 us
    ppermute x15, starting transfers between devices, turn(): lax.ppermute(x, 'row', [(i, (i + 2 * steps) % count) for i in range(count)])  18.4 us
    pallas_call x1, Pallas kernels, attend_forward(): pl.pallas_call(partial(attend_kernel, rows=rows, scale=HD ** (-0.5)), gri...  15.7 us
  transfers between devices with their start and end apart: 73, of which 37 were waited for; matrix products, arithmetic and copies ran while one was open for 9% of the time, Pallas kernels for 29%

profile of v9, /device:TPU:0, one launch (start us, length us, event | category | flops | bytes accessed | tf_op | source)
XLA Modules:
  0.0 633.7 jit_solution(14687961868064492219)
XLA Ops:
  11.2 3.0 collective-permute-start.2
  18.2 19.1 %collective-permute-done.2.refs_5_ = bf16[256,2048]{1,0:T(8,128)(2,1)S(1)} collective-permute-done((bf16[256,2048]{1,0:T(8,128)(2,1)S(1)}, bf16[256,2048]{1,0:T(8,128)(2,1)S(1)}, u32[]{:S(2)}, u32[]{:S(2)}) %collective-permute-start.2) | collective-permute-done | bytes 1048608 | tf_op jit(solution)/shard_map/ppermute | solution.py:431
  48.9 19.1 %collective-permute-done.8.refs_2_ = bf16[1024,512]{1,0:T(8,128)(2,1)} collective-permute-done((bf16[1024,512]{1,0:T(8,128)(2,1)S(1)}, bf16[1024,512]{1,0:T(8,128)(2,1)}, u32[]{:S(2)}, u32[]{:S(2)}) %collective-permute-start.8) | collective-permute-done | bytes 1048608 | tf_op jit(solution)/shard_map/ppermute | solution.py:431
  76.2 2.9 collective-permute-done.10
  79.0 17.2 %collective-permute-done.11.refs_7_ = bf16[256,2048]{1,0:T(8,128)(2,1)S(1)} collective-permute-done((bf16[256,2048]{1,0:T(8,128)(2,1)S(1)}, bf16[256,2048]{1,0:T(8,128)(2,1)S(1)}, u32[]{:S(2)}, u32[]{:S(2)}) %collective-permute-start.11) | collective-permute-done | bytes 1048608 | tf_op jit(solution)/shard_map/ppermute | solution.py:431
  105.1 3.2 cotangent_rows.1.a_ref.refs_0_
  110.5 4.1 first_norm.1
  114.6 10.9 %collective-permute-done.16.refs_2_ = bf16[256,2048]{1,0:T(8,128)(2,1)} collective-permute-done((bf16[256,2048]{1,0:T(8,128)(2,1)}, bf16[256,2048]{1,0:T(8,128)(2,1)}, u32[]{:S(2)}, u32[]{:S(2)}) %collective-permute-start.16) | collective-permute-done | bytes 1048608 | tf_op jit(solution)/shard_map/ppermute | solution.py:436
  127.7 9.9 %mix.1 = (bf16[1024,1536]{1,0:T(8,128)(2,1)S(1)}, bf16[1024,2048]{1,0:T(8,128)(2,1)S(1)}, bf16[1024,2048]{1,0:T(8,128)(2,1)S(1)}) custom-call(bf16[1024,2048]{1,0:T(8,128)(2,1)S(1)} %get-tuple-element.240.refs_0_.a_ref, bf16[256,2048]{1,0:T(8,128)(2,1)S(1)} %copy-done.58, bf16[256,2048]{1,0:T(8,128)(2,1)S(1)} %copy-done.78, ...), custom_call_target="tpu_custom_call" | custom-call | flops 100663296 | bytes 376928 | tf_op jit(solution)/shard_map/mix/pallas_call | solution.py:229
  141.6 8.1 %collective-permute-done.19.refs_3_ = bf16[256,2048]{1,0:T(8,128)(2,1)} collective-permute-done((bf16[256,2048]{1,0:T(8,128)(2,1)}, bf16[256,2048]{1,0:T(8,128)(2,1)}, u32[]{:S(2)}, u32[]{:S(2)}) %collective-permute-start.19) | collective-permute-done | bytes 1048608 | tf_op jit(solution)/shard_map/ppermute | solution.py:436
  153.0 15.7 %attend_forward.1 = (bf16[1024,512]{1,0:T(8,128)(2,1)S(1)}, f32[4,2,1024]{2,1,0:T(2,128)S(1)}) custom-call(f32[8]{0:T(128)S(1)} %multiply_exponential_fusion.slope_ref, s32[1,1024,1]{2,1,0:T(8,128)S(1)} %copy-done.72, bf16[1024,1536]{1,0:T(8,128)(2,1)S(1)} %get-tuple-element.151.q_ref.k_ref.v_ref, ...), custom_call_target="tpu_custom_call" | custom-call | flops 67108864 | bytes 98304 | tf_op jit(solution)/shard_map/attend_forward/pallas_call | solution.py:79
  182.7 3.5 collective-permute-done.24.refs_5_
  188.6 7.1 %collective-permute-done.21.refs_6_ = bf16[256,2048]{1,0:T(8,128)(2,1)} collective-permute-done((bf16[256,2048]{1,0:T(8,128)(2,1)}, bf16[256,2048]{1,0:T(8,128)(2,1)}, u32[]{:S(2)}, u32[]{:S(2)}) %collective-permute-start.21) | collective-permute-done | bytes 1048608 | tf_op jit(solution)/shard_map/ppermute | solution.py:431
  208.6 5.6 collective-permute-done.25
  214.2 3.1 fusion.20
  219.2 19.4 %collective-permute-done.29.refs_8_ = bf16[256,2048]{1,0:T(8,128)(2,1)S(1)} collective-permute-done((bf16[256,2048]{1,0:T(8,128)(2,1)}, bf16[256,2048]{1,0:T(8,128)(2,1)S(1)}, u32[]{:S(2)}, u32[]{:S(2)}) %collective-permute-start.29) | collective-permute-done | bytes 1048608 | tf_op jit(solution)/shard_map/ppermute | solution.py:431
  238.6 5.7 collective-permute-done.28.refs_2_
  247.0 4.1 second_norm.1
  252.7 17.8 %expand.1 = (bf16[1024,2048]{1,0:T(8,128)(2,1)S(1)}, f32[1024,2048]{1,0:T(8,128)}, bf16[1024,2048]{1,0:T(8,128)(2,1)S(1)}, bf16[1024,2048]{1,0:T(8,128)(2,1)S(1)}) custom-call(bf16[1024,2048]{1,0:T(8,128)(2,1)S(1)} %get-tuple-element.213.refs_0_.a_ref, bf16[256,2048]{1,0:T(8,128)(2,1)} %refs_1_.1, bf16[256,2048]{1,0:T(8,128)(2,1)} %collective-permute-done.16.refs_2_, ...), custom_call_target="tpu_custom_call" | custom-call | flops 134217728 | bytes 524416 | tf_op jit(solution)/shard_map/expand/pallas_call | solution.py:229
  272.6 8.1 %contract_grad_other.1 = (bf16[256,2048]{1,0:T(8,128)(2,1)}, bf16[512,2048]{1,0:T(8,128)(2,1)}, bf16[256,2048]{1,0:T(8,128)(2,1)S(1)}) custom-call(s32[4]{0:T(128)S(1)} %get-tuple-element.276.order_ref, bf16[1024,2048]{1,0:T(8,128)(2,1)S(1)} %copy-done.20, bf16[1024,2048]{1,0:T(8,128)(2,1)S(1)} %get-tuple-element.254.refs_0_), custom_call_target="tpu_custom_call" | custom-call | flops 67108864 | bytes 196608 | tf_op jit(solution)/shard_map/contract_grad_other/pallas_call | solution.py:229
  290.2 6.4 %contract_grad_mine.1 = (bf16[256,2048]{1,0:T(8,128)(2,1)S(1)}, bf16[256,2048]{1,0:T(8,128)(2,1)S(1)}, bf16[256,2048]{1,0:T(8,128)(2,1)S(1)}, bf16[256,2048]{1,0:T(8,128)(2,1)S(1)}) custom-call(s32[4]{0:T(128)S(1)} %get-tuple-element.277.order_ref, bf16[1024,2048]{1,0:T(8,128)(2,1)S(1)} %copy-done.21, bf16[1024,2048]{1,0:T(8,128)(2,1)S(1)} %copy-done.16), custom_call_target="tpu_custom_call" | custom-call | flops 67108864 | bytes 196608 | tf_op jit(solution)/shard_map/contract_grad_mine/pallas_call | solution.py:229
  297.7 9.5 %collective-permute-done.31 = bf16[256,2048]{1,0:T(8,128)(2,1)} collective-permute-done((bf16[256,2048]{1,0:T(8,128)(2,1)}, bf16[256,2048]{1,0:T(8,128)(2,1)}, u32[]{:S(2)}, u32[]{:S(2)}) %collective-permute-start.31) | collective-permute-done | bytes 1048608 | tf_op jit(solution)/shard_map/ppermute | solution.py:431
  308.8 2.6 add_convert_fusion.7
  311.4 4.6 collective-permute-start.32
  316.0 10.9 %all-gather.2.cloned.1.call-done.refs_1_.refs_2_ = bf16[2048,2048]{1,0:T(8,128)(2,1)} async-done(((bf16[512,2048]{1,0:T(8,128)(2,1)}), bf16[2048,2048]{1,0:T(8,128)(2,1)}) %all-gather.2.cloned.1.call-update) | async-done | bytes 8388624 | tf_op jit(solution)/shard_map/all_gather | solution.py:473
  326.9 3.4 copy-done
  332.5 3.4 copy-done.51
  335.9 10.9 %contract_back.1 = (bf16[1024,2048]{1,0:T(8,128)(2,1)S(1)}, f32[1,2048]{1,0:T(1,128)S(1)}) custom-call(bf16[1024,2048]{1,0:T(8,128)(2,1)S(1)} %copy-done.22, bf16[2048,2048]{1,0:T(8,128)(2,1)S(1)} %copy-done, f32[1024,2048]{1,0:T(8,128)S(1)} %copy-done.51), custom_call_target="tpu_custom_call" | custom-call | flops 134217728 | bytes 393344 | tf_op jit(solution)/shard_map/contract_back/pallas_call | solution.py:229
  346.9 5.5 expand_back_sent.1
  353.1 3.6 collective-permute-done.36.refs_5_
  356.7 3.0 expand_back_part.1
  364.9 3.1 expand_back_base.1
  368.0 7.8 %expand_grad_other.1 = (bf16[256,2048]{1,0:T(8,128)(2,1)}, bf16[512,2048]{1,0:T(8,128)(2,1)S(1)}, bf16[256,2048]{1,0:T(8,128)(2,1)}) custom-call(s32[4]{0:T(128)S(1)} %get-tuple-element.275.order_ref, bf16[1024,2048]{1,0:T(8,128)(2,1)S(1)} %copy-done.33, bf16[1024,2048]{1,0:T(8,128)(2,1)S(1)} %get-tuple-element.208.refs_0_), custom_call_target="tpu_custom_call" | custom-call | flops 67108864 | bytes 196608 | tf_op jit(solution)/shard_map/expand_grad_other/pallas_call | solution.py:229
  375.8 9.2 %collective-permute-done.39 = bf16[1024,512]{1,0:T(8,128)(2,1)S(1)} collective-permute-done((bf16[1024,512]{1,0:T(8,128)(2,1)S(1)}, bf16[1024,512]{1,0:T(8,128)(2,1)S(1)}, u32[]{:S(2)}, u32[]{:S(2)}) %collective-permute-start.39) | collective-permute-done | bytes 1048608 | tf_op jit(solution)/shard_map/ppermute | solution.py:431
  386.2 3.3 collective-permute-done.37
  392.5 2.7 add_convert_fusion.5
  406.3 6.4 %expand_grad_mine.1 = (bf16[256,2048]{1,0:T(8,128)(2,1)S(1)}, bf16[256,2048]{1,0:T(8,128)(2,1)S(1)}, bf16[256,2048]{1,0:T(8,128)(2,1)S(1)}, bf16[256,2048]{1,0:T(8,128)(2,1)S(1)}) custom-call(s32[4]{0:T(128)S(1)} %get-tuple-element.278.order_ref, bf16[1024,2048]{1,0:T(8,128)(2,1)S(1)} %copy-done.34, bf16[1024,2048]{1,0:T(8,128)(2,1)S(1)} %copy-done.14), custom_call_target="tpu_custom_call" | custom-call | flops 67108864 | bytes 196608 | tf_op jit(solution)/shard_map/expand_grad_mine/pallas_call | solution.py:229
  413.8 3.4 copy-done.1
  417.2 5.6 contract_sent.1
  422.8 3.5 collective-permute-done.45.refs_2_
  430.6 3.6 branch_rows.1.a_ref.refs_0_
  434.2 3.6 projection_grad_other.1
  440.6 19.3 %attend_backward.1 = (bf16[1024,512]{1,0:T(8,128)(2,1)S(1)}, bf16[1024,512]{1,0:T(8,128)(2,1)S(1)}, bf16[1024,512]{1,0:T(8,128)(2,1)S(1)}, f32[1,1,512]{2,1,0:T(1,128)S(1)}, f32[1,1,512]{2,1,0:T(1,128)S(1)}) custom-call(f32[8]{0:T(128)S(1)} %multiply_exponential_fusion.slope_ref, s32[1,1,1024]{2,1,0:T(1,128)S(1)} %bitcast.42, ...), custom_call_target="tpu_custom_call" | custom-call | flops 167772160 | bytes 114688 | tf_op jit(solution)/shard_map/attend_backward/pallas_call | solution.py:183
  459.9 13.6 %collective-permute-done.46 = bf16[512,2048]{1,0:T(8,128)(2,1)S(1)} collective-permute-done((bf16[512,2048]{1,0:T(8,128)(2,1)S(1)}, bf16[512,2048]{1,0:T(8,128)(2,1)S(1)}, u32[]{:S(2)}, u32[]{:S(2)}) %collective-permute-start.46) | collective-permute-done | bytes 2097184 | tf_op jit(solution)/shard_map/ppermute | solution.py:431
  474.4 4.7 mix_back_sent.1
  484.9 3.4 mix_back_part.1
  491.7 6.5 %collective-permute-done.51 = bf16[256,2048]{1,0:T(8,128)(2,1)S(1)} collective-permute-done((bf16[256,2048]{1,0:T(8,128)(2,1)S(1)}, bf16[256,2048]{1,0:T(8,128)(2,1)S(1)}, u32[]{:S(2)}, u32[]{:S(2)}) %collective-permute-start.51) | collective-permute-done | bytes 1048608 | tf_op jit(solution)/shard_map/ppermute | solution.py:436
  506.9 6.4 %mixing_grad_other.1 = (bf16[256,1536]{1,0:T(8,128)(2,1)}, bf16[256,1536]{1,0:T(8,128)(2,1)S(1)}, bf16[256,1536]{1,0:T(8,128)(2,1)}, bf16[256,1536]{1,0:T(8,128)(2,1)S(1)}) custom-call(s32[4]{0:T(128)S(1)} %get-tuple-element.275.order_ref, bf16[1024,2048]{1,0:T(8,128)(2,1)S(1)} %copy-done.30, bf16[1024,512]{1,0:T(8,128)(2,1)S(1)} %copy-done.41, ...), custom_call_target="tpu_custom_call" | custom-call | flops 50331648 | bytes 163840 | tf_op jit(solution)/shard_map/mixing_grad_other/pallas_call | solution.py:229
  514.2 2.8 projection_grad_mine.1
  519.2 2.5 mix_back_base.1
  521.8 3.1 convert_add_fusion.4
  524.8 3.3 collective-permute-done.49
  529.6 3.1 convert_add_fusion.2
  535.2 3.1 fusion.5
  540.9 5.3 mixing_grad_mine.1
  551.0 3.7 convert_add_fusion.3
  558.3 3.4 copy-done.2
  561.7 5.2 contract_part.1
  566.9 9.4 %collective-permute-done.61 = f32[12,512]{1,0:T(8,128)S(1)} collective-permute-done((f32[12,512]{1,0:T(8,128)S(1)}, f32[12,512]{1,0:T(8,128)S(1)}, u32[]{:S(2)}, u32[]{:S(2)}) %collective-permute-start.61) | collective-permute-done | bytes 24608 | tf_op jit(solution)/shard_map/ppermute | solution.py:431
  585.0 4.3 contract_base.1
  590.6 8.9 %collective-permute-done.65 = f32[12,512]{1,0:T(8,128)S(1)} collective-permute-done((f32[12,512]{1,0:T(8,128)S(1)}, f32[12,512]{1,0:T(8,128)S(1)}, u32[]{:S(2)}, u32[]{:S(2)}) %collective-permute-start.65) | collective-permute-done | bytes 24608 | tf_op jit(solution)/shard_map/ppermute | solution.py:431
  605.2 3.2 collective-permute-start.70
  608.4 11.3 %collective-permute-done.68 = f32[12,512]{1,0:T(8,128)S(1)} collective-permute-done((f32[12,512]{1,0:T(8,128)S(1)}, f32[12,512]{1,0:T(8,128)S(1)}, u32[]{:S(2)}, u32[]{:S(2)}) %collective-permute-start.68) | collective-permute-done | bytes 24608 | tf_op jit(solution)/shard_map/ppermute | solution.py:431
  621.5 2.9 add_convert_fusion.1
  (451 shorter events, 185.0 us)
Async XLA Ops:
  7.2 319.8 %all-gather.2.cloned.1.call-start = ((), (), s32[]{:S(2)}) async-start(), calls=%async_computation.1 | async-start | bytes 10485760 | tf_op jit(solution)/shard_map/all_gather | solution.py:473
  11.2 26.2 %collective-permute-start.2 = (bf16[256,2048]{1,0:T(8,128)(2,1)S(1)}, bf16[256,2048]{1,0:T(8,128)(2,1)S(1)}, u32[]{:S(2)}, u32[]{:S(2)}) collective-permute-start(bf16[256,2048]{1,0:T(8,128)(2,1)S(1)} %pad_maximum_fusion.1.refs_1_), channel_id=1, source_target_pairs={{0,4},{4,0},{8,12},{12,8},{16,20},{20,16},{24,28},{28,24},{1,5},{5... | collective-permute-start | bytes 3145736 | tf_op jit(solution)/shard_map/ppermute | solution.py:431
  14.2 26.5 %collective-permute-start.3 = (bf16[256,2048]{1,0:T(8,128)(2,1)S(1)}, bf16[256,2048]{1,0:T(8,128)(2,1)S(1)}, u32[]{:S(2)}, u32[]{:S(2)}) collective-permute-start(bf16[256,2048]{1,0:T(8,128)(2,1)S(1)} %pad_maximum_fusion.1.refs_1_), channel_id=1, source_target_pairs={{0,8},{4,12},{8,16},{12,20},{16,24},{20,28},{24,0},{28,4},{1,9},{5... | collective-permute-start | bytes 3145736 | tf_op jit(solution)/shard_map/ppermute | solution.py:436
  16.8 23.9 %collective-permute-start = (bf16[1024,512]{1,0:T(8,128)(2,1)S(1)}, bf16[1024,512]{1,0:T(8,128)(2,1)S(1)}, u32[]{:S(2)}, u32[]{:S(2)}) collective-permute-start(bf16[1024,512]{1,0:T(8,128)(2,1)S(1)} %copy-done.47), channel_id=1, source_target_pairs={{0,1},{1,0},{2,3},{3,2},{4,5},{5,4},{6,7},{7,6},{8,9},{9,8},{10,11... | collective-permute-start | bytes 3145736 | tf_op jit(solution)/shard_map/ppermute | solution.py:431
  16.8 25.6 %collective-permute-start.1 = (bf16[1024,512]{1,0:T(8,128)(2,1)S(1)}, bf16[1024,512]{1,0:T(8,128)(2,1)S(1)}, u32[]{:S(2)}, u32[]{:S(2)}) collective-permute-start(bf16[1024,512]{1,0:T(8,128)(2,1)S(1)} %copy-done.47), channel_id=1, source_target_pairs={{0,2},{1,3},{2,0},{3,1},{4,6},{5,7},{6,4},{7,5},{8,10},{9,11},{10,... | collective-permute-start | bytes 3145736 | tf_op jit(solution)/shard_map/ppermute | solution.py:431
  42.3 5.5 collective-permute-start.7
  42.3 25.7 %collective-permute-start.8 = (bf16[1024,512]{1,0:T(8,128)(2,1)S(1)}, bf16[1024,512]{1,0:T(8,128)(2,1)}, u32[]{:S(2)}, u32[]{:S(2)}) collective-permute-start(bf16[1024,512]{1,0:T(8,128)(2,1)S(1)} %copy-done.54), channel_id=1, source_target_pairs={{0,2},{1,3},{2,0},{3,1},{4,6},{5,7},{6,4},{7,5},{8,10},{9,11},{10,... | collective-permute-start | bytes 3145736 | tf_op jit(solution)/shard_map/ppermute | solution.py:431
  43.8 25.3 %collective-permute-start.5 = (bf16[256,2048]{1,0:T(8,128)(2,1)S(1)}, bf16[256,2048]{1,0:T(8,128)(2,1)S(1)}, u32[]{:S(2)}, u32[]{:S(2)}) collective-permute-start(bf16[256,2048]{1,0:T(8,128)(2,1)S(1)} %collective-permute-done.3.refs_2_), channel_id=1, source_target_pairs={{0,4},{4,0},{8,12},{12,8},{16,20},{20,16},{24,28},{28,24},{1,5},{5... | collective-permute-start | bytes 3145736 | tf_op jit(solution)/shard_map/ppermute | solution.py:431
  44.3 26.8 %collective-permute-start.6 = (bf16[256,2048]{1,0:T(8,128)(2,1)S(1)}, bf16[256,2048]{1,0:T(8,128)(2,1)S(1)}, u32[]{:S(2)}, u32[]{:S(2)}) collective-permute-start(bf16[256,2048]{1,0:T(8,128)(2,1)S(1)} %collective-permute-done.3.refs_2_), channel_id=1, source_target_pairs={{0,8},{4,12},{8,16},{12,20},{16,24},{20,28},{24,0},{28,4},{1,9},{5... | collective-permute-start | bytes 3145736 | tf_op jit(solution)/shard_map/ppermute | solution.py:436
  46.9 24.3 %collective-permute-start.4 = (bf16[1024,512]{1,0:T(8,128)(2,1)S(1)}, bf16[1024,512]{1,0:T(8,128)(2,1)S(1)}, u32[]{:S(2)}, u32[]{:S(2)}) collective-permute-start(bf16[1024,512]{1,0:T(8,128)(2,1)S(1)} %collective-permute-done.1.refs_2_), channel_id=1, source_target_pairs={{0,1},{1,0},{2,3},{3,2},{4,5},{5,4},{6,7},{7,6},{8,9},{9,8},{10,11... | collective-permute-start | bytes 3145736 | tf_op jit(solution)/shard_map/ppermute | solution.py:431
  72.1 24.2 %collective-permute-start.11 = (bf16[256,2048]{1,0:T(8,128)(2,1)S(1)}, bf16[256,2048]{1,0:T(8,128)(2,1)S(1)}, u32[]{:S(2)}, u32[]{:S(2)}) collective-permute-start(bf16[256,2048]{1,0:T(8,128)(2,1)S(1)} %collective-permute-done.6.refs_3_), channel_id=1, source_target_pairs={{0,4},{4,0},{8,12},{12,8},{16,20},{20,16},{24,28},{28,24},{1,5},{5... | collective-permute-start | bytes 3145736 | tf_op jit(solution)/shard_map/ppermute | solution.py:431
  73.6 25.8 %collective-permute-start.12 = (bf16[256,2048]{1,0:T(8,128)(2,1)S(1)}, bf16[256,2048]{1,0:T(8,128)(2,1)}, u32[]{:S(2)}, u32[]{:S(2)}) collective-permute-start(bf16[256,2048]{1,0:T(8,128)(2,1)S(1)} %collective-permute-done.6.refs_3_), channel_id=1, source_target_pairs={{0,8},{4,12},{8,16},{12,20},{16,24},{20,28},{24,0},{28,4},{1,9},{5... | collective-permute-start | bytes 3145736 | tf_op jit(solution)/shard_map/ppermute | solution.py:436
  74.6 24.8 %collective-permute-start.13 = (bf16[1024,512]{1,0:T(8,128)(2,1)}, bf16[1024,512]{1,0:T(8,128)(2,1)S(1)}, u32[]{:S(2)}, u32[]{:S(2)}) collective-permute-start(bf16[1024,512]{1,0:T(8,128)(2,1)} %collective-permute-done.8.refs_2_), channel_id=1, source_target_pairs={{0,1},{1,0},{2,3},{3,2},{4,5},{5,4},{6,7},{7,6},{8,9},{9,8},{10,11... | collective-permute-start | bytes 3145736 | tf_op jit(solution)/shard_map/ppermute | solution.py:431
  100.4 25.1 %collective-permute-start.16 = (bf16[256,2048]{1,0:T(8,128)(2,1)}, bf16[256,2048]{1,0:T(8,128)(2,1)}, u32[]{:S(2)}, u32[]{:S(2)}) collective-permute-start(bf16[256,2048]{1,0:T(8,128)(2,1)} %refs_1_.1), channel_id=1, source_target_pairs={{0,8},{4,12},{8,16},{12,20},{16,24},{20,28},{24,0},{28,4},{1,9},{5... | collective-permute-start | bytes 3145736 | tf_op jit(solution)/shard_map/ppermute | solution.py:436
  100.4 25.1 %collective-permute-start.15 = (bf16[256,2048]{1,0:T(8,128)(2,1)}, bf16[256,2048]{1,0:T(8,128)(2,1)}, u32[]{:S(2)}, u32[]{:S(2)}) collective-permute-start(bf16[256,2048]{1,0:T(8,128)(2,1)} %collective-permute-done.12.refs_4_), channel_id=1, source_target_pairs={{0,4},{4,0},{8,12},{12,8},{16,20},{20,16},{24,28},{28,24},{1,5},{5... | collective-permute-start | bytes 3145736 | tf_op jit(solution)/shard_map/ppermute | solution.py:431
  101.2 9.2 %collective-permute-start.14 = (f32[4,512]{1,0:T(4,128)S(1)}, f32[4,512]{1,0:T(4,128)S(1)}, u32[]{:S(2)}, u32[]{:S(2)}) collective-permute-start(f32[4,512]{1,0:T(4,128)S(1)} %collective-permute-done.10), channel_id=1, source_target_pairs={{0,1},{1,0},{2,3},{3,2},{4,5},{5,4},{6,7},{7,6},{8,9},{9,8},{10,11... | collective-permute-start | bytes 24584 | tf_op jit(solution)/shard_map/ppermute | solution.py:431
  125.5 24.1 %collective-permute-start.19 = (bf16[256,2048]{1,0:T(8,128)(2,1)}, bf16[256,2048]{1,0:T(8,128)(2,1)}, u32[]{:S(2)}, u32[]{:S(2)}) collective-permute-start(bf16[256,2048]{1,0:T(8,128)(2,1)} %collective-permute-done.16.refs_2_), channel_id=1, source_target_pairs={{0,8},{4,12},{8,16},{12,20},{16,24},{20,28},{24,0},{28,4},{1,9},{5... | collective-permute-start | bytes 3145736 | tf_op jit(solution)/shard_map/ppermute | solution.py:436
  125.5 44.2 %collective-permute-start.18 = (bf16[256,2048]{1,0:T(8,128)(2,1)}, bf16[256,2048]{1,0:T(8,128)(2,1)}, u32[]{:S(2)}, u32[]{:S(2)}) collective-permute-start(bf16[256,2048]{1,0:T(8,128)(2,1)} %param.21), channel_id=1, source_target_pairs={{0,4},{4,0},{8,12},{12,8},{16,20},{20,16},{24,28},{28,24},{1,5},{5... | collective-permute-start | bytes 3145736 | tf_op jit(solution)/shard_map/ppermute | solution.py:431
  126.1 45.9 %collective-permute-start.17 = (bf16[256,2048]{1,0:T(8,128)(2,1)}, bf16[256,2048]{1,0:T(8,128)(2,1)}, u32[]{:S(2)}, u32[]{:S(2)}) collective-permute-start(bf16[256,2048]{1,0:T(8,128)(2,1)} %refs_1_.1), channel_id=1, source_target_pairs={{0,4},{4,0},{8,12},{12,8},{16,20},{20,16},{24,28},{28,24},{1,5},{5... | collective-permute-start | bytes 3145736 | tf_op jit(solution)/shard_map/ppermute | solution.py:431
  149.6 23.2 %collective-permute-start.20 = (bf16[256,2048]{1,0:T(8,128)(2,1)}, bf16[256,2048]{1,0:T(8,128)(2,1)}, u32[]{:S(2)}, u32[]{:S(2)}) collective-permute-start(bf16[256,2048]{1,0:T(8,128)(2,1)} %collective-permute-done.19.refs_3_), channel_id=1, source_target_pairs={{0,8},{4,12},{8,16},{12,20},{16,24},{20,28},{24,0},{28,4},{1,9},{5... | collective-permute-start | bytes 3145736 | tf_op jit(solution)/shard_map/ppermute | solution.py:436
  172.9 426.7 %reduce-scatter.2.cloned.1.call-start = ((), (), s32[]{:S(2)}) async-start(), calls=%async_computation.2 | async-start | bytes 1310720 | tf_op jit(solution)/shard_map/reduce_scatter | solution.py:898
  173.1 22.6 %collective-permute-start.21 = (bf16[256,2048]{1,0:T(8,128)(2,1)}, bf16[256,2048]{1,0:T(8,128)(2,1)}, u32[]{:S(2)}, u32[]{:S(2)}) collective-permute-start(bf16[256,2048]{1,0:T(8,128)(2,1)} %collective-permute-done.16.refs_2_), channel_id=1, source_target_pairs={{0,4},{4,0},{8,12},{12,8},{16,20},{20,16},{24,28},{28,24},{1,5},{5... | collective-permute-start | bytes 3145736 | tf_op jit(solution)/shard_map/ppermute | solution.py:431
  182.0 4.2 collective-permute-start.22
  182.1 4.2 collective-permute-start.23
  195.7 18.5 %collective-permute-start.25 = (bf16[1024,512]{1,0:T(8,128)(2,1)}, bf16[1024,512]{1,0:T(8,128)(2,1)}, u32[]{:S(2)}, u32[]{:S(2)}) collective-permute-start(bf16[1024,512]{1,0:T(8,128)(2,1)} %project_part.1), channel_id=1, source_target_pairs={{0,2},{1,3},{2,0},{3,1},{4,6},{5,7},{6,4},{7,5},{8,10},{9,11},{10,... | collective-permute-start | bytes 3145736 | tf_op jit(solution)/shard_map/ppermute | solution.py:431
  195.7 22.7 %collective-permute-start.26 = (bf16[256,2048]{1,0:T(8,128)(2,1)}, bf16[256,2048]{1,0:T(8,128)(2,1)}, u32[]{:S(2)}, u32[]{:S(2)}) collective-permute-start(bf16[256,2048]{1,0:T(8,128)(2,1)} %collective-permute-done.19.refs_3_), channel_id=1, source_target_pairs={{0,4},{4,0},{8,12},{12,8},{16,20},{20,16},{24,28},{28,24},{1,5},{5... | collective-permute-start | bytes 3145736 | tf_op jit(solution)/shard_map/ppermute | solution.py:431
  218.4 20.2 %collective-permute-start.29 = (bf16[256,2048]{1,0:T(8,128)(2,1)}, bf16[256,2048]{1,0:T(8,128)(2,1)S(1)}, u32[]{:S(2)}, u32[]{:S(2)}) collective-permute-start(bf16[256,2048]{1,0:T(8,128)(2,1)} %collective-permute-done.20.refs_4_), channel_id=1, source_target_pairs={{0,4},{4,0},{8,12},{12,8},{16,20},{20,16},{24,28},{28,24},{1,5},{5... | collective-permute-start | bytes 3145736 | tf_op jit(solution)/shard_map/ppermute | solution.py:431
  218.8 19.9 %collective-permute-start.27 = (bf16[1024,512]{1,0:T(8,128)(2,1)S(1)}, bf16[1024,512]{1,0:T(8,128)(2,1)S(1)}, u32[]{:S(2)}, u32[]{:S(2)}) collective-permute-start(bf16[1024,512]{1,0:T(8,128)(2,1)S(1)} %get-tuple-element.170.refs_0_), channel_id=1, source_target_pairs={{0,1},{1,0},{2,3},{3,2},{4,5},{5,4},{6,7},{7,6},{8,9},{9,8},{10,11... | collective-permute-start | bytes 3145736 | tf_op jit(solution)/shard_map/ppermute | solution.py:431
  218.8 25.6 %collective-permute-start.28 = (bf16[1024,512]{1,0:T(8,128)(2,1)S(1)}, bf16[1024,512]{1,0:T(8,128)(2,1)S(1)}, u32[]{:S(2)}, u32[]{:S(2)}) collective-permute-start(bf16[1024,512]{1,0:T(8,128)(2,1)S(1)} %get-tuple-element.170.refs_0_), channel_id=1, source_target_pairs={{0,2},{1,3},{2,0},{3,1},{4,6},{5,7},{6,4},{7,5},{8,10},{9,11},{10,... | collective-permute-start | bytes 3145736 | tf_op jit(solution)/shard_map/ppermute | solution.py:431
  281.7 25.5 %collective-permute-start.31 = (bf16[256,2048]{1,0:T(8,128)(2,1)}, bf16[256,2048]{1,0:T(8,128)(2,1)}, u32[]{:S(2)}, u32[]{:S(2)}) collective-permute-start(bf16[256,2048]{1,0:T(8,128)(2,1)} %get-tuple-element.182), channel_id=1, source_target_pairs={{0,4},{4,0},{8,12},{12,8},{16,20},{20,16},{24,28},{28,24},{1,5},{5... | collective-permute-start | bytes 3145736 | tf_op jit(solution)/shard_map/ppermute | solution.py:431
  307.2 54.0 %collective-permute-start.33 = (bf16[512,2048]{1,0:T(8,128)(2,1)}, bf16[512,2048]{1,0:T(8,128)(2,1)}, u32[]{:S(2)}, u32[]{:S(2)}) collective-permute-start(bf16[512,2048]{1,0:T(8,128)(2,1)} %get-tuple-element.191), channel_id=1, source_target_pairs={{0,4},{4,0},{8,12},{12,8},{16,20},{20,16},{24,28},{28,24},{1,5},{5... | collective-permute-start | bytes 6291464 | tf_op jit(solution)/shard_map/ppermute | solution.py:431
  311.4 49.8 %collective-permute-start.32 = (bf16[256,2048]{1,0:T(8,128)(2,1)}, bf16[256,2048]{1,0:T(8,128)(2,1)}, u32[]{:S(2)}, u32[]{:S(2)}) collective-permute-start(bf16[256,2048]{1,0:T(8,128)(2,1)} %add_convert_fusion.7), channel_id=1, source_target_pairs={{0,24},{4,28},{8,0},{12,4},{16,8},{20,12},{24,16},{28,20},{1,25},{... | collective-permute-start | bytes 3145736 | tf_op jit(solution)/shard_map/ppermute | solution.py:436
  352.4 4.2 collective-permute-start.34
  359.7 25.3 %collective-permute-start.39 = (bf16[1024,512]{1,0:T(8,128)(2,1)S(1)}, bf16[1024,512]{1,0:T(8,128)(2,1)S(1)}, u32[]{:S(2)}, u32[]{:S(2)}) collective-permute-start(bf16[1024,512]{1,0:T(8,128)(2,1)S(1)} %expand_back_part.1), channel_id=1, source_target_pairs={{0,2},{1,3},{2,0},{3,1},{4,6},{5,7},{6,4},{7,5},{8,10},{9,11},{10,... | collective-permute-start | bytes 3145736 | tf_op jit(solution)/shard_map/ppermute | solution.py:431
  361.2 25.0 %collective-permute-start.38 = (bf16[256,2048]{1,0:T(8,128)(2,1)S(1)}, bf16[256,2048]{1,0:T(8,128)(2,1)S(1)}, u32[]{:S(2)}, u32[]{:S(2)}) collective-permute-start(bf16[256,2048]{1,0:T(8,128)(2,1)S(1)} %copy-done.113), channel_id=1, source_target_pairs={{0,4},{4,0},{8,12},{12,8},{16,20},{20,16},{24,28},{28,24},{1,5},{5... | collective-permute-start | bytes 3145736 | tf_op jit(solution)/shard_map/ppermute | solution.py:431
  364.8 24.7 %collective-permute-start.37 = (bf16[256,2048]{1,0:T(8,128)(2,1)S(1)}, bf16[256,2048]{1,0:T(8,128)(2,1)S(1)}, u32[]{:S(2)}, u32[]{:S(2)}) collective-permute-start(bf16[256,2048]{1,0:T(8,128)(2,1)S(1)} %add_convert_fusion.6), channel_id=1, source_target_pairs={{0,24},{4,28},{8,0},{12,4},{16,8},{20,12},{24,16},{28,20},{1,25},{... | collective-permute-start | bytes 3145736 | tf_op jit(solution)/shard_map/ppermute | solution.py:436
  391.9 6.2 collective-permute-start.43
  395.3 27.5 %collective-permute-start.41 = (bf16[256,2048]{1,0:T(8,128)(2,1)}, bf16[256,2048]{1,0:T(8,128)(2,1)}, u32[]{:S(2)}, u32[]{:S(2)}) collective-permute-start(bf16[256,2048]{1,0:T(8,128)(2,1)} %add_convert_fusion.5), channel_id=1, source_target_pairs={{0,24},{4,28},{8,0},{12,4},{16,8},{20,12},{24,16},{28,20},{1,25},{... | collective-permute-start | bytes 3145736 | tf_op jit(solution)/shard_map/ppermute | solution.py:436
  397.5 25.3 %collective-permute-start.40 = (bf16[256,2048]{1,0:T(8,128)(2,1)}, bf16[256,2048]{1,0:T(8,128)(2,1)}, u32[]{:S(2)}, u32[]{:S(2)}) collective-permute-start(bf16[256,2048]{1,0:T(8,128)(2,1)} %get-tuple-element.209), channel_id=1, source_target_pairs={{0,4},{4,0},{8,12},{12,8},{16,20},{20,16},{24,28},{28,24},{1,5},{5... | collective-permute-start | bytes 3145736 | tf_op jit(solution)/shard_map/ppermute | solution.py:431
  400.4 22.4 %collective-permute-start.44 = (bf16[1024,512]{1,0:T(8,128)(2,1)}, bf16[1024,512]{1,0:T(8,128)(2,1)}, u32[]{:S(2)}, u32[]{:S(2)}) collective-permute-start(bf16[1024,512]{1,0:T(8,128)(2,1)} %get-tuple-element.285.refs_0_), channel_id=1, source_target_pairs={{0,1},{1,0},{2,3},{3,2},{4,5},{5,4},{6,7},{7,6},{8,9},{9,8},{10,11... | collective-permute-start | bytes 3145736 | tf_op jit(solution)/shard_map/ppermute | solution.py:431
  400.4 25.9 %collective-permute-start.45 = (bf16[1024,512]{1,0:T(8,128)(2,1)}, bf16[1024,512]{1,0:T(8,128)(2,1)}, u32[]{:S(2)}, u32[]{:S(2)}) collective-permute-start(bf16[1024,512]{1,0:T(8,128)(2,1)} %get-tuple-element.285.refs_0_), channel_id=1, source_target_pairs={{0,2},{1,3},{2,0},{3,1},{4,6},{5,7},{6,4},{7,5},{8,10},{9,11},{10,... | collective-permute-start | bytes 3145736 | tf_op jit(solution)/shard_map/ppermute | solution.py:431
  426.3 47.3 %collective-permute-start.46 = (bf16[512,2048]{1,0:T(8,128)(2,1)S(1)}, bf16[512,2048]{1,0:T(8,128)(2,1)S(1)}, u32[]{:S(2)}, u32[]{:S(2)}) collective-permute-start(bf16[512,2048]{1,0:T(8,128)(2,1)S(1)} %copy-done.111), channel_id=1, source_target_pairs={{0,4},{4,0},{8,12},{12,8},{16,20},{20,16},{24,28},{28,24},{1,5},{5... | collective-permute-start | bytes 6291464 | tf_op jit(solution)/shard_map/ppermute | solution.py:431
  429.4 30.5 %collective-permute-start.47 = (bf16[256,2048]{1,0:T(8,128)(2,1)S(1)}, bf16[256,2048]{1,0:T(8,128)(2,1)S(1)}, u32[]{:S(2)}, u32[]{:S(2)}) collective-permute-start(bf16[256,2048]{1,0:T(8,128)(2,1)S(1)} %add_convert_fusion.4), channel_id=1, source_target_pairs={{0,24},{4,28},{8,0},{12,4},{16,8},{20,12},{24,16},{28,20},{1,25},{... | collective-permute-start | bytes 3145736 | tf_op jit(solution)/shard_map/ppermute | solution.py:436
  474.1 24.2 %collective-permute-start.51 = (bf16[256,2048]{1,0:T(8,128)(2,1)S(1)}, bf16[256,2048]{1,0:T(8,128)(2,1)S(1)}, u32[]{:S(2)}, u32[]{:S(2)}) collective-permute-start(bf16[256,2048]{1,0:T(8,128)(2,1)S(1)} %add_convert_fusion.3), channel_id=1, source_target_pairs={{0,24},{4,28},{8,0},{12,4},{16,8},{20,12},{24,16},{28,20},{1,25},{... | collective-permute-start | bytes 3145736 | tf_op jit(solution)/shard_map/ppermute | solution.py:436
  479.2 5.8 collective-permute-start.53
  479.2 5.7 collective-permute-start.54
  479.8 45.0 %collective-permute-start.50 = (bf16[1024,512]{1,0:T(8,128)(2,1)}, bf16[1024,512]{1,0:T(8,128)(2,1)}, u32[]{:S(2)}, u32[]{:S(2)}) collective-permute-start(bf16[1024,512]{1,0:T(8,128)(2,1)} %projection_grad_other.1), channel_id=1, source_target_pairs={{0,4},{4,0},{8,12},{12,8},{16,20},{20,16},{24,28},{28,24},{1,5},{5... | collective-permute-start | bytes 3145736 | tf_op jit(solution)/shard_map/ppermute | solution.py:431
  483.4 44.7 %collective-permute-start.49 = (bf16[256,2048]{1,0:T(8,128)(2,1)}, bf16[256,2048]{1,0:T(8,128)(2,1)}, u32[]{:S(2)}, u32[]{:S(2)}) collective-permute-start(bf16[256,2048]{1,0:T(8,128)(2,1)} %get-tuple-element.225), channel_id=1, source_target_pairs={{0,4},{4,0},{8,12},{12,8},{16,20},{20,16},{24,28},{28,24},{1,5},{5... | collective-permute-start | bytes 3145736 | tf_op jit(solution)/shard_map/ppermute | solution.py:431
  490.1 31.7 %collective-permute-start.56 = (bf16[1024,512]{1,0:T(8,128)(2,1)}, bf16[1024,512]{1,0:T(8,128)(2,1)}, u32[]{:S(2)}, u32[]{:S(2)}) collective-permute-start(bf16[1024,512]{1,0:T(8,128)(2,1)} %mix_back_part.1), channel_id=1, source_target_pairs={{0,2},{1,3},{2,0},{3,1},{4,6},{5,7},{6,4},{7,5},{8,10},{9,11},{10,... | collective-permute-start | bytes 3145736 | tf_op jit(solution)/shard_map/ppermute | solution.py:431
  499.8 28.3 %collective-permute-start.52 = (bf16[256,2048]{1,0:T(8,128)(2,1)}, bf16[256,2048]{1,0:T(8,128)(2,1)}, u32[]{:S(2)}, u32[]{:S(2)}) collective-permute-start(bf16[256,2048]{1,0:T(8,128)(2,1)} %add_convert_fusion.2), channel_id=1, source_target_pairs={{0,24},{4,28},{8,0},{12,4},{16,8},{20,12},{24,16},{28,20},{1,25},{... | collective-permute-start | bytes 3145736 | tf_op jit(solution)/shard_map/ppermute | solution.py:436
  503.1 55.1 %collective-permute-start.60 = (bf16[1024,1024]{1,0:T(8,128)(2,1)}, bf16[1024,1024]{1,0:T(8,128)(2,1)}, u32[]{:S(2)}, u32[]{:S(2)}) collective-permute-start(bf16[1024,1024]{1,0:T(8,128)(2,1)} %copy-done.67), channel_id=1, source_target_pairs={{0,1},{1,0},{2,3},{3,2},{4,5},{5,4},{6,7},{7,6},{8,9},{9,8},{10,11... | collective-permute-start | bytes 6291464 | tf_op jit(solution)/shard_map/ppermute | solution.py:431
  528.1 19.4 %collective-permute-start.57 = (bf16[256,1536]{1,0:T(8,128)(2,1)}, bf16[256,1536]{1,0:T(8,128)(2,1)}, u32[]{:S(2)}, u32[]{:S(2)}) collective-permute-start(bf16[256,1536]{1,0:T(8,128)(2,1)} %get-tuple-element.242), channel_id=1, source_target_pairs={{0,4},{4,0},{8,12},{12,8},{16,20},{20,16},{24,28},{28,24},{1,5},{5... | collective-permute-start | bytes 2359304 | tf_op jit(solution)/shard_map/ppermute | solution.py:431
  538.4 18.0 %collective-permute-start.63 = (f32[2,1024]{1,0:T(2,128)S(1)}, f32[2,1024]{1,0:T(2,128)S(1)}, u32[]{:S(2)}, u32[]{:S(2)}) collective-permute-start(f32[2,1024]{1,0:T(2,128)S(1)} %pad_maximum_fusion.5), channel_id=1, source_target_pairs={{0,1},{1,0},{2,3},{3,2},{4,5},{5,4},{6,7},{7,6},{8,9},{9,8},{10,11... | collective-permute-start | bytes 24584 | tf_op jit(solution)/shard_map/ppermute | solution.py:431
  547.5 28.8 %collective-permute-start.59 = (bf16[256,1536]{1,0:T(8,128)(2,1)S(1)}, bf16[256,1536]{1,0:T(8,128)(2,1)S(1)}, u32[]{:S(2)}, u32[]{:S(2)}) collective-permute-start(bf16[256,1536]{1,0:T(8,128)(2,1)S(1)} %copy-done.116), channel_id=1, source_target_pairs={{0,4},{4,0},{8,12},{12,8},{16,20},{20,16},{24,28},{28,24},{1,5},{5... | collective-permute-start | bytes 2359304 | tf_op jit(solution)/shard_map/ppermute | solution.py:431
  550.4 25.9 %collective-permute-start.58 = (bf16[256,1536]{1,0:T(8,128)(2,1)S(1)}, bf16[256,1536]{1,0:T(8,128)(2,1)S(1)}, u32[]{:S(2)}, u32[]{:S(2)}) collective-permute-start(bf16[256,1536]{1,0:T(8,128)(2,1)S(1)} %add_convert_fusion.10), channel_id=1, source_target_pairs={{0,24},{4,28},{8,0},{12,4},{16,8},{20,12},{24,16},{28,20},{1,25},{... | collective-permute-start | bytes 2359304 | tf_op jit(solution)/shard_map/ppermute | solution.py:436
  554.7 21.6 %collective-permute-start.61 = (f32[12,512]{1,0:T(8,128)S(1)}, f32[12,512]{1,0:T(8,128)S(1)}, u32[]{:S(2)}, u32[]{:S(2)}) collective-permute-start(f32[12,512]{1,0:T(8,128)S(1)} %concatenate.27), channel_id=1, source_target_pairs={{0,8},{4,12},{8,0},{12,4},{16,24},{20,28},{24,16},{28,20},{1,9},{5... | collective-permute-start | bytes 73736 | tf_op jit(solution)/shard_map/ppermute | solution.py:431
  556.4 24.6 %collective-permute-start.64 = (f32[2,1024]{1,0:T(2,128)S(1)}, f32[2,1024]{1,0:T(2,128)S(1)}, u32[]{:S(2)}, u32[]{:S(2)}) collective-permute-start(f32[2,1024]{1,0:T(2,128)S(1)} %fusion.18), channel_id=1, source_target_pairs={{0,2},{1,3},{2,0},{3,1},{4,6},{5,7},{6,4},{7,5},{8,10},{9,11},{10,... | collective-permute-start | bytes 24584 | tf_op jit(solution)/shard_map/ppermute | solution.py:431
  576.4 25.1 %collective-permute-start.67 = (bf16[256,1536]{1,0:T(8,128)(2,1)}, bf16[256,1536]{1,0:T(8,128)(2,1)}, u32[]{:S(2)}, u32[]{:S(2)}) collective-permute-start(bf16[256,1536]{1,0:T(8,128)(2,1)} %get-tuple-element.258), channel_id=1, source_target_pairs={{0,4},{4,0},{8,12},{12,8},{16,20},{20,16},{24,28},{28,24},{1,5},{5... | collective-permute-start | bytes 2359304 | tf_op jit(solution)/shard_map/ppermute | solution.py:431
  579.1 22.4 %collective-permute-start.66 = (bf16[256,1536]{1,0:T(8,128)(2,1)}, bf16[256,1536]{1,0:T(8,128)(2,1)}, u32[]{:S(2)}, u32[]{:S(2)}) collective-permute-start(bf16[256,1536]{1,0:T(8,128)(2,1)} %add_convert_fusion.9), channel_id=1, source_target_pairs={{0,24},{4,28},{8,0},{12,4},{16,8},{20,12},{24,16},{28,20},{1,25},{... | collective-permute-start | bytes 2359304 | tf_op jit(solution)/shard_map/ppermute | solution.py:436
  581.0 18.5 %collective-permute-start.65 = (f32[12,512]{1,0:T(8,128)S(1)}, f32[12,512]{1,0:T(8,128)S(1)}, u32[]{:S(2)}, u32[]{:S(2)}) collective-permute-start(f32[12,512]{1,0:T(8,128)S(1)} %add.341), channel_id=1, source_target_pairs={{0,16},{4,20},{8,24},{12,28},{16,0},{20,4},{24,8},{28,12},{1,17},{... | collective-permute-start | bytes 73736 | tf_op jit(solution)/shard_map/ppermute | solution.py:431
  581.6 39.9 %collective-permute-start.62 = (bf16[1024,512]{1,0:T(8,128)(2,1)}, bf16[1024,512]{1,0:T(8,128)(2,1)}, u32[]{:S(2)}, u32[]{:S(2)}) collective-permute-start(bf16[1024,512]{1,0:T(8,128)(2,1)} %contract_part.1), channel_id=1, source_target_pairs={{0,2},{1,3},{2,0},{3,1},{4,6},{5,7},{6,4},{7,5},{8,10},{9,11},{10,... | collective-permute-start | bytes 3145736 | tf_op jit(solution)/shard_map/ppermute | solution.py:431
  601.5 22.9 %collective-permute-start.69 = (bf16[256,1536]{1,0:T(8,128)(2,1)}, bf16[256,1536]{1,0:T(8,128)(2,1)S(1)}, u32[]{:S(2)}, u32[]{:S(2)}) collective-permute-start(bf16[256,1536]{1,0:T(8,128)(2,1)} %copy-done.114), channel_id=1, source_target_pairs={{0,4},{4,0},{8,12},{12,8},{16,20},{20,16},{24,28},{28,24},{1,5},{5... | collective-permute-start | bytes 2359304 | tf_op jit(solution)/shard_map/ppermute | solution.py:431
  602.0 17.6 %collective-permute-start.68 = (f32[12,512]{1,0:T(8,128)S(1)}, f32[12,512]{1,0:T(8,128)S(1)}, u32[]{:S(2)}, u32[]{:S(2)}) collective-permute-start(f32[12,512]{1,0:T(8,128)S(1)} %add.350), channel_id=1, source_target_pairs={{0,4},{4,0},{8,12},{12,8},{16,20},{20,16},{24,28},{28,24},{1,5},{5... | collective-permute-start | bytes 73736 | tf_op jit(solution)/shard_map/ppermute | solution.py:431
  605.2 19.6 %collective-permute-start.70 = (bf16[256,1536]{1,0:T(8,128)(2,1)S(1)}, bf16[256,1536]{1,0:T(8,128)(2,1)S(1)}, u32[]{:S(2)}, u32[]{:S(2)}) collective-permute-start(bf16[256,1536]{1,0:T(8,128)(2,1)S(1)} %add_convert_fusion.8), channel_id=1, source_target_pairs={{0,24},{4,28},{8,0},{12,4},{16,8},{20,12},{24,16},{28,20},{1,25},{... | collective-permute-start | bytes 2359304 | tf_op jit(solution)/shard_map/ppermute | solution.py:436
  (138 other events, 1187.0 us)
Sparse Core Ops, SparseCore 0:
  173.0 153.9 all-gather.1
  535.4 32.3 reduce-scatter.1
